TPU v7x, 256 devices: a whole 4x4x8 slice. The times are simulated.
256 devices in a mesh: layer: 32 (over z, x), batch: 8 (over y, core).
Axes of the slice: x: 4, y: 4, z: 8, core: 2. Of those that a mesh axis runs over, the one named last changes fastest.
Arguments:
- inputs: float32 [8, 8, 8, 8, 128], P('batch'), parts along dimension 0, may hold values from -6 to 6
- guess_states: float32 [128, 8, 8, 8, 8, 128], P('layer', 'batch'), parts along dimension 1, may hold values from -6 to 6
- kernels: bfloat16 [128, 3, 3, 3, 128, 128], P('layer'), may hold values from -0.109375 to 0.109375
- biases: float32 [128, 128], P('layer'), may hold values from -4 to 4
Outputs:
- states: float32 [128, 8, 8, 8, 8, 128], P('layer', 'batch'), parts along dimension 1
- coarse_residual: float32 [32, 8, 8, 8, 8, 128], P('layer', 'batch'), parts along dimension 1
There are 8 independent parts, one for each index of `batch`. A program takes and returns all parts, laid end to end along the dimension named above; an argument that names none is the same for every part. Nothing has to cross between parts.
All inputs are finite; a program needn't handle non-finite values.
Results may differ from a plain program's by a relative error of at most 0.0008.
Values may be sent and summed in bfloat16 or wider, within the bound.
No kernel may reach another device: no remote copies, remote signals or barrier semaphores. Data moves between devices by JAX's collectives and lax.ppermute only.
A program may use at most 128 MiB of HBM per device.

v0:
```python
import jax
import jax.numpy as jnp
from jax import lax
from jax.sharding import Mesh
from jax.sharding import PartitionSpec as P

COARSEN = 4
LAYER = ("layer_0", "layer_1")


def passed_along(value, axis, steps):
    count = lax.axis_size(axis)
    initial, last = (max(0, -steps), min(count, count - steps))
    return lax.ppermute(value, axis, [(source, source + steps) for source in range(initial, last)])


def gathered_by_axis(x, axes, dim):
    out = x
    for number in range(len(axes) - 1, -1, -1):
        out = lax.all_gather(out, axes[number], axis=dim, tiled=True)
    return out


def joined_along(pieces, dim):
    dims = list(pieces.shape[1:])
    dims[dim] *= pieces.shape[0]
    return jnp.moveaxis(pieces, 0, dim).reshape(dims)


def gather_packed(arrays, axis, dims):
    vector = jnp.concatenate([a.reshape(-1) for a in arrays])
    lines, at, done = (lax.all_gather(vector, axis), 0, [])
    for a, dim in zip(arrays, dims):
        pieces = lines[:, at : at + a.size].reshape(-1, *a.shape)
        done.append(joined_along(pieces, dim))
        at += a.size
    return tuple(done)


def advance(state, kernel, offset_row, step_size):
    squashed = jnp.tanh(state).astype(jnp.bfloat16)
    mixed = lax.conv_general_dilated(
        squashed,
        kernel,
        (1, 1, 1),
        "SAME",
        dimension_numbers=("NDHWC", "DHWIO", "NDHWC"),
        preferred_element_type=jnp.float32,
    )
    return state + step_size * (mixed + offset_row)


def shards(inputs, guess_states, kernels, biases):
    device_index = lax.axis_index(LAYER)
    sections = lax.axis_size(LAYER)
    depth = guess_states.shape[0]
    fine_size = 2.0 / (depth * sections)
    coarse_size = depth * fine_size
    top_size = COARSEN * coarse_size
    group_pos = device_index % COARSEN
    first_device = device_index == 0
    is_owner = group_pos == COARSEN - 1
    lead_kernel = kernels[0]
    lead_bias = biases[0]
    groups = sections // COARSEN
    owner_group = device_index // COARSEN
    channels = lead_kernel.shape[3]
    share = channels // COARSEN
    held_kernel = lead_kernel
    for reach in range(1, COARSEN):
        got_kernel = passed_along(held_kernel, LAYER, -1)
        held_kernel = jnp.where(group_pos == COARSEN - 1 - reach, got_kernel, held_kernel)
    kernel_share = lax.dynamic_slice_in_dim(held_kernel, group_pos * share, share, 3)
    all_shares = gathered_by_axis(kernel_share[None], LAYER, 0)
    share_grid = all_shares.reshape((groups, COARSEN) + kernel_share.shape)

    def heads_of(corner):
        arrived = passed_along(corner, LAYER, 1)
        return jnp.where(first_device, inputs, arrived)

    def relax_fine(current, heads):
        chain_rows = [heads]
        for layer_row in range(1, depth):
            chain_rows.append(
                advance(chain_rows[-1], kernels[layer_row - 1], biases[layer_row - 1], fine_size)
            )
        return jnp.stack(chain_rows[1:] + [current[-1]], 0)

    states = relax_fine(guess_states, heads_of(guess_states[-1]))
    new_corner = advance(states[-2], kernels[-1], biases[-1], fine_size)
    states = states.at[-1].set(new_corner)
    heads = heads_of(new_corner)
    states = relax_fine(states, heads)
    fine_defect = advance(states[-2], kernels[-1], biases[-1], fine_size) - advance(
        heads, lead_kernel, lead_bias, coarse_size
    )
    coarse_value = states[-1]

    def update(active, before, current):
        return lax.cond(
            active,
            lambda: advance(before, lead_kernel, lead_bias, coarse_size) + fine_defect,
            lambda: current,
        )

    def pass_on(current):
        return passed_along(current, LAYER, 1)

    def relax_coarse(current):
        for turn in range(COARSEN - 1):
            before = jnp.where(first_device, inputs, pass_on(current))
            current = update(group_pos == turn, before, current)
        return current

    current = relax_coarse(coarse_value)
    coarse_value = update(is_owner, pass_on(current), current)
    current = coarse_value
    anchor = jnp.zeros_like(current)
    arrived = current
    handed = anchor
    for turn in range(COARSEN):
        arrived, handed = passed_along((current, anchor), LAYER, 1)
        if turn < COARSEN - 1:
            before = jnp.where(first_device, inputs, arrived)
            active = group_pos == turn
            current = update(active, before, current)
            anchor = jnp.where(active, before if turn == 0 else handed, anchor)
    coarse_value, arrived, group_before = (current, arrived, handed)
    fine_before = jnp.where(first_device, inputs, arrived)
    corner = advance(fine_before, lead_kernel, lead_bias, coarse_size) + fine_defect
    coarse_residual = corner - coarse_value
    level_defect = lax.cond(
        is_owner,
        lambda: corner - advance(group_before, lead_kernel, lead_bias, top_size),
        lambda: jnp.zeros_like(coarse_value),
    )
    slab = level_defect.shape[1] // COARSEN
    held_defect, held_bias = (level_defect, lead_bias)
    for reach in range(1, COARSEN):
        got_defect, got_bias = passed_along((held_defect, held_bias), LAYER, -1)
        taking = group_pos == COARSEN - 1 - reach
        held_defect = jnp.where(taking, got_defect, held_defect)
        held_bias = jnp.where(taking, got_bias, held_bias)
    defect_share = lax.dynamic_slice_in_dim(held_defect, group_pos * slab, slab, 1)
    bias_share = lax.dynamic_slice_in_dim(held_bias, group_pos * share, share, 0)
    all_defects, all_biases = gather_packed((defect_share[None], bias_share[None]), LAYER, (0, 0))
    defect_grid = all_defects.reshape((groups, COARSEN) + defect_share.shape)
    bias_grid = all_biases.reshape((groups, COARSEN, share))

    def local_round(turn, carry):
        running, kept = carry
        block = lax.dynamic_index_in_dim(share_grid, turn, 0, keepdims=False)
        whole_kernel = jnp.moveaxis(block, 0, 3).reshape(lead_kernel.shape)
        bias_row = lax.dynamic_index_in_dim(bias_grid, turn, 0, keepdims=False).reshape((channels,))
        defect_block = lax.dynamic_index_in_dim(defect_grid, turn, 0, keepdims=False)
        defect_row = jnp.moveaxis(defect_block, 0, 1).reshape(level_defect.shape)
        running = advance(running, whole_kernel, bias_row, top_size) + defect_row
        kept = jnp.where(owner_group == turn, running, kept)
        return (running, kept)

    unused, level_two = lax.fori_loop(
        0, groups, local_round, (inputs, jnp.zeros_like(coarse_value))
    )
    coarse_value = jnp.where(is_owner, level_two, coarse_value)
    coarse_value = relax_coarse(coarse_value)
    states = states.at[-1].set(coarse_value)
    states = relax_fine(states, heads_of(coarse_value))
    return (states, coarse_residual[None])


def solution(mesh):
    finer = Mesh(mesh.devices.reshape(8, 4, mesh.shape["batch"]), ("layer_0", "layer_1", "batch"))
    return jax.shard_map(
        shards,
        mesh=finer,
        in_specs=(
            P("batch", None, None, None, None),
            P(LAYER, "batch", None, None, None, None),
            P(LAYER, None, None, None, None, None),
            P(LAYER, None),
        ),
        out_specs=(
            P(LAYER, "batch", None, None, None, None),
            P(LAYER, "batch", None, None, None, None),
        ),
        check_vma=False,
    )
```

profile of v0, /device:TPU:128, one launch (start us, length us, event | category | flops | bytes accessed | tf_op | source)
XLA Modules:
  0.0 507.3 jit_solution(2235113815713005103)
XLA Ops:
  9.1 3.4 collective-permute-start.3
  14.7 7.6 %collective-permute-done.3 = f32[1,8,8,8,128]{4,3,2,1,0:T(8,128)S(1)} collective-permute-done((f32[1,8,8,8,128]{4,3,2,1,0:T(8,128)S(1)}, f32[1,8,8,8,128]{4,3,2,1,0:T(8,128)S(1)}, u32[]{:S(2)}, u32[]{:S(2)}) %collective-permute-start.3) | collective-permute-done | bytes 262176 | tf_op jit(solution)/shard_map/ppermute | solution.py:14
  22.4 2.6 fusion.58
  25.0 2.6 fusion.40
  27.7 2.6 fusion.43
  30.4 2.6 fusion.37
  33.0 2.1 collective-permute-start.4
  35.1 10.3 %collective-permute-done.4 = f32[1,8,8,8,128]{4,3,2,1,0:T(8,128)S(1)} collective-permute-done((f32[1,8,8,8,128]{4,3,2,1,0:T(8,128)S(1)}, f32[1,8,8,8,128]{4,3,2,1,0:T(8,128)S(1)}, u32[]{:S(2)}, u32[]{:S(2)}) %collective-permute-start.4) | collective-permute-done | bytes 262176 | tf_op jit(solution)/shard_map/ppermute | solution.py:14
  45.4 2.6 fusion.53
  48.1 2.6 fusion.39
  50.7 2.6 fusion.42
  53.4 2.6 fusion.36
  56.1 3.1 conditional.11
  56.3 2.9 fusion.2
  59.2 1.9 collective-permute-start.5
  61.2 9.7 %collective-permute-done.5 = f32[1,8,8,8,128]{4,0,3,2,1:T(1,128)S(1)} collective-permute-done((f32[1,8,8,8,128]{4,0,3,2,1:T(1,128)S(1)}, f32[1,8,8,8,128]{4,0,3,2,1:T(1,128)S(1)}, u32[]{:S(2)}, u32[]{:S(2)}) %collective-permute-start.5) | collective-permute-done | bytes 262176 | tf_op jit(solution)/shard_map/ppermute | solution.py:14
  72.7 9.7 %collective-permute-done.6 = f32[1,8,8,8,128]{4,0,3,2,1:T(1,128)S(1)} collective-permute-done((f32[1,8,8,8,128]{4,0,3,2,1:T(1,128)S(1)}, f32[1,8,8,8,128]{4,0,3,2,1:T(1,128)S(1)}, u32[]{:S(2)}, u32[]{:S(2)}) %collective-permute-start.6) | collective-permute-done | bytes 262176 | tf_op jit(solution)/shard_map/ppermute | solution.py:14
  84.3 9.7 %collective-permute-done.7 = f32[1,8,8,8,128]{4,0,3,2,1:T(1,128)S(1)} collective-permute-done((f32[1,8,8,8,128]{4,0,3,2,1:T(1,128)S(1)}, f32[1,8,8,8,128]{4,0,3,2,1:T(1,128)S(1)}, u32[]{:S(2)}, u32[]{:S(2)}) %collective-permute-start.7) | collective-permute-done | bytes 262176 | tf_op jit(solution)/shard_map/ppermute | solution.py:14
  96.3 9.7 %collective-permute-done.8 = f32[1,8,8,8,128]{4,3,2,1,0:T(8,128)S(1)} collective-permute-done((f32[1,8,8,8,128]{4,3,2,1,0:T(8,128)S(1)}, f32[1,8,8,8,128]{4,3,2,1,0:T(8,128)S(1)}, u32[]{:S(2)}, u32[]{:S(2)}) %collective-permute-start.8) | collective-permute-done | bytes 262176 | tf_op jit(solution)/shard_map/ppermute | solution.py:14
  106.0 2.9 conditional.15
  106.0 2.9 fusion.14
  108.9 1.9 collective-permute-start.12
  110.9 1.9 collective-permute-start.9
  112.8 7.7 %collective-permute-done.12 = f32[1,8,8,8,128]{4,0,3,2,1:T(1,128)S(1)} collective-permute-done((f32[1,8,8,8,128]{4,0,3,2,1:T(1,128)S(1)}, f32[1,8,8,8,128]{4,0,3,2,1:T(1,128)S(1)}, u32[]{:S(2)}, u32[]{:S(2)}) %collective-permute-start.12) | collective-permute-done | bytes 262176 | tf_op jit(solution)/shard_map/ppermute | solution.py:14
  122.4 3.6 collective-permute-done.9
  126.1 1.9 collective-permute-start.10
  128.0 4.0 collective-permute-done.13
  134.2 6.4 %collective-permute-done.10 = f32[1,8,8,8,128]{4,3,2,1,0:T(8,128)} collective-permute-done((f32[1,8,8,8,128]{4,3,2,1,0:T(8,128)S(1)}, f32[1,8,8,8,128]{4,3,2,1,0:T(8,128)}, u32[]{:S(2)}, u32[]{:S(2)}) %collective-permute-start.10) | collective-permute-done | bytes 262176 | tf_op jit(solution)/shard_map/ppermute | solution.py:14
  142.5 2.9 collective-permute-done.14
  145.5 2.6 fusion.48
  149.0 3.2 collective-permute-done.11
  152.4 4.2 collective-permute-start.15
  160.5 3.0 collective-permute-done.15
  163.5 7.5 %collective-permute-start.16 = (f32[1,8,8,8,128]{4,3,2,1,0:T(8,128)S(1)}, f32[1,8,8,8,128]{4,3,2,1,0:T(8,128)S(1)}, u32[]{:S(2)}, u32[]{:S(2)}) collective-permute-start(f32[1,8,8,8,128]{4,3,2,1,0:T(8,128)S(1)} %broadcast_select_fusion.20), channel_id=1, source_target_pairs={{8,0},{16,8},{24,16},{32,24},{40,32},{48,40},{56,48},{64,56},{72,6... | collective-permute-start | bytes 786440 | tf_op jit(solution)/shard_map/ppermute | solution.py:14
  174.9 7.3 %collective-permute-done.19 = f32[128]{0:T(128)S(1)} collective-permute-done((f32[128]{0:T(128)S(1)}, f32[128]{0:T(128)S(1)}, u32[]{:S(2)}, u32[]{:S(2)}) %collective-permute-start.19) | collective-permute-done | bytes 544 | tf_op jit(solution)/shard_map/ppermute | solution.py:14
  182.2 5.5 %collective-permute-start.20 = (f32[128]{0:T(128)S(1)}, f32[128]{0:T(128)S(1)}, u32[]{:S(2)}, u32[]{:S(2)}) collective-permute-start(f32[128]{0:T(128)S(1)} %broadcast_select_fusion.30), channel_id=1, source_target_pairs={{8,0},{16,8},{24,16},{32,24},{40,32},{48,40},{56,48},{64,56},{72,6... | collective-permute-start | bytes 1544 | tf_op jit(solution)/shard_map/ppermute | solution.py:14
  191.0 1.9 collective-permute-start.1
  193.0 5.9 %collective-permute-done.17 = f32[1,8,8,8,128]{4,3,2,1,0:T(8,128)S(1)} collective-permute-done((f32[1,8,8,8,128]{4,3,2,1,0:T(8,128)S(1)}, f32[1,8,8,8,128]{4,3,2,1,0:T(8,128)S(1)}, u32[]{:S(2)}, u32[]{:S(2)}) %collective-permute-start.17) | collective-permute-done | bytes 262176 | tf_op jit(solution)/shard_map/ppermute | solution.py:14
  200.7 9.1 %collective-permute-done.1 = bf16[3,3,3,128,128]{4,3,2,1,0:T(8,128)(2,1)} collective-permute-done((bf16[3,3,3,128,128]{4,3,2,1,0:T(8,128)(2,1)S(1)}, bf16[3,3,3,128,128]{4,3,2,1,0:T(8,128)(2,1)}, u32[]{:S(2)}, u32[]{:S(2)}) %collective-permute-start.1) | collective-permute-done | bytes 884768 | tf_op jit(solution)/shard_map/ppermute | solution.py:14
  209.9 5.2 %collective-permute-start.2 = (bf16[3,3,3,128,128]{4,3,2,1,0:T(8,128)(2,1)S(1)}, bf16[3,3,3,128,128]{4,3,2,1,0:T(8,128)(2,1)S(1)}, u32[]{:S(2)}, u32[]{:S(2)}) collective-permute-start(bf16[3,3,3,128,128]{4,3,2,1,0:T(8,128)(2,1)S(1)} %broadcast_select_fusion.17), channel_id=1, source_target_pairs={{8,0},{16,8},{24,16},{32,24},{40,32},{48,40},{56,48},{64,56},{72,6... | collective-permute-start | bytes 2654216 | tf_op jit(solution)/shard_map/ppermute | solution.py:14
  215.1 24.1 %collective-permute-done.2 = bf16[3,3,3,128,128]{4,3,2,1,0:T(8,128)(2,1)S(1)} collective-permute-done((bf16[3,3,3,128,128]{4,3,2,1,0:T(8,128)(2,1)S(1)}, bf16[3,3,3,128,128]{4,3,2,1,0:T(8,128)(2,1)S(1)}, u32[]{:S(2)}, u32[]{:S(2)}) %collective-permute-start.2) | collective-permute-done | bytes 884768 | tf_op jit(solution)/shard_map/ppermute | solution.py:14
  239.3 18.1 %all-gather = bf16[12,3,3,32,128]{4,3,2,1,0:T(8,128)(2,1)} all-gather(bf16[3,3,3,32,128]{4,3,2,1,0:T(8,128)(2,1)S(1)} %dynamic-slice_select_fusion), channel_id=2, replica_groups=mesh['layer_0'=8,'layer_1'=4,'batch'=8] {'layer_1'}, dimensions={0}, use_global_device_ids=true | all-gather | bytes 1105920 | tf_op jit(solution)/shard_map/all_gather | solution.py:20
  257.5 132.7 %all-reduce.3.cloned.1.call-done = f32[525312]{0:T(1024)} async-done(((f32[525312]{0:T(1024)}), f32[525312]{0:T(1024)}) %all-reduce.3.cloned.1.call-update) | async-done | bytes 2101264
  390.2 2.9 reshape.168
  395.0 45.4 %while.18 = (s32[]{:T(128)}, f32[1,8,8,8,128]{4,0,3,2,1:T(1,128)S(1)}, f32[1,8,8,8,128]{4,0,3,2,1:T(1,128)S(1)}, bf16[8,4,3,3,3,32,128]{6,5,4,3,2,1,0:T(8,128)(2...) while((s32[]{:T(128)}, ...), condition=%wide.region_17.18_spmd.clone, body=%wide.region_16.17_spmd.clone.sunk | while | flops 349372416 | bytes 6785661 | solution.py:161
  397.5 3.2 broadcast_select_fusion.35
  403.2 3.2 broadcast_select_fusion.35
  408.9 3.2 broadcast_select_fusion.35
  414.5 3.2 broadcast_select_fusion.35
  420.2 3.2 broadcast_select_fusion.35
  425.9 3.2 broadcast_select_fusion.35
  431.5 3.2 broadcast_select_fusion.35
  437.2 3.2 broadcast_select_fusion.35
  440.5 2.0 collective-permute-start.21
  442.5 9.6 %collective-permute-done.21 = f32[1,8,8,8,128]{4,0,3,2,1:T(1,128)S(1)} collective-permute-done((f32[1,8,8,8,128]{4,0,3,2,1:T(1,128)S(1)}, f32[1,8,8,8,128]{4,0,3,2,1:T(1,128)S(1)}, u32[]{:S(2)}, u32[]{:S(2)}) %collective-permute-start.21) | collective-permute-done | bytes 262176 | tf_op jit(solution)/shard_map/ppermute | solution.py:14
  452.1 3.1 conditional.19
  452.1 3.1 fusion.26
  457.1 9.7 %collective-permute-done.22 = f32[1,8,8,8,128]{4,0,3,2,1:T(1,128)S(1)} collective-permute-done((f32[1,8,8,8,128]{4,0,3,2,1:T(1,128)S(1)}, f32[1,8,8,8,128]{4,0,3,2,1:T(1,128)S(1)}, u32[]{:S(2)}, u32[]{:S(2)}) %collective-permute-start.22) | collective-permute-done | bytes 262176 | tf_op jit(solution)/shard_map/ppermute | solution.py:14
  468.6 9.7 %collective-permute-done.23 = f32[1,8,8,8,128]{4,0,3,2,1:T(1,128)S(1)} collective-permute-done((f32[1,8,8,8,128]{4,0,3,2,1:T(1,128)S(1)}, f32[1,8,8,8,128]{4,0,3,2,1:T(1,128)S(1)}, u32[]{:S(2)}, u32[]{:S(2)}) %collective-permute-start.23) | collective-permute-done | bytes 262176 | tf_op jit(solution)/shard_map/ppermute | solution.py:14
  478.5 2.2 collective-permute-start.24
  480.7 9.7 %collective-permute-done.24 = f32[1,8,8,8,128]{4,3,2,1,0:T(8,128)S(1)} collective-permute-done((f32[1,8,8,8,128]{4,3,2,1,0:T(8,128)S(1)}, f32[1,8,8,8,128]{4,3,2,1,0:T(8,128)S(1)}, u32[]{:S(2)}, u32[]{:S(2)}) %collective-permute-start.24) | collective-permute-done | bytes 262176 | tf_op jit(solution)/shard_map/ppermute | solution.py:14
  490.4 2.6 fusion.46
  493.1 2.6 fusion.38
  495.7 2.6 fusion.41
  (140 shorter events, 56.4 us)
Async XLA Ops:
  8.0 17.0 %copy-start = (f32[1,8,8,8,128]{4,3,2,1,0:T(8,128)S(1)}, f32[1,8,8,8,128]{4,3,2,1,0:T(8,128)}, u32[]{:S(2)}) copy-start(f32[1,8,8,8,128]{4,3,2,1,0:T(8,128)} %param.32) | copy-start | bytes 786436
  8.0 382.2 %all-reduce.3.cloned.1.call-start = ((), (), s32[]{:S(2)}) async-start(), calls=%async_computation.1 | async-start | bytes 4202496
  9.1 13.3 %collective-permute-start.3 = (f32[1,8,8,8,128]{4,3,2,1,0:T(8,128)S(1)}, f32[1,8,8,8,128]{4,3,2,1,0:T(8,128)S(1)}, u32[]{:S(2)}, u32[]{:S(2)}) collective-permute-start(f32[1,8,8,8,128]{4,3,2,1,0:T(8,128)S(1)} %slice_bitcast_fusion.13), channel_id=1, source_target_pairs={{0,8},{8,16},{16,24},{24,32},{32,40},{40,48},{48,56},{56,64},{64,7... | collective-permute-start | bytes 786440 | tf_op jit(solution)/shard_map/ppermute | solution.py:14
  13.3 11.7 %copy-start.2 = (bf16[4,3,3,3,128,128]{5,4,3,2,1,0:T(8,128)(2,1)S(1)}, bf16[4,3,3,3,128,128]{5,4,3,2,1,0:T(8,128)(2,1)}, u32[]{:S(2)}) copy-start(bf16[4,3,3,3,128,128]{5,4,3,2,1,0:T(8,128)(2,1)} %param.34) | copy-start | bytes 10616836
  14.7 143.8 %copy-start.5 = (bf16[3,3,3,128,128]{4,3,2,1,0:T(8,128)(2,1)}, bf16[3,3,3,128,128]{4,3,2,1,0:T(8,128)(2,1)S(1)}, u32[]{:S(2)}) copy-start(bf16[3,3,3,128,128]{4,3,2,1,0:T(8,128)(2,1)S(1)} %slice_bitcast_fusion.4) | copy-start | bytes 2654212
  33.0 12.4 %collective-permute-start.4 = (f32[1,8,8,8,128]{4,3,2,1,0:T(8,128)S(1)}, f32[1,8,8,8,128]{4,3,2,1,0:T(8,128)S(1)}, u32[]{:S(2)}, u32[]{:S(2)}) collective-permute-start(f32[1,8,8,8,128]{4,3,2,1,0:T(8,128)S(1)} %multiply_add_fusion.6), channel_id=1, source_target_pairs={{0,8},{8,16},{16,24},{24,32},{32,40},{40,48},{48,56},{56,64},{64,7... | collective-permute-start | bytes 786440 | tf_op jit(solution)/shard_map/ppermute | solution.py:14
  35.1 13.0 %copy-start.3 = (bf16[4,3,3,3,128,128]{5,4,3,2,1,0:T(8,128)(2,1)S(1)}, bf16[4,3,3,3,128,128]{5,4,3,2,1,0:T(8,128)(2,1)}, u32[]{:S(2)}) copy-start(bf16[4,3,3,3,128,128]{5,4,3,2,1,0:T(8,128)(2,1)} %param.34) | copy-start | bytes 10616836
  56.1 76.0 %copy-start.7 = (f32[1,8,8,8,128]{4,3,2,1,0:T(8,128)}, f32[1,8,8,8,128]{4,3,2,1,0:T(8,128)S(1)}, u32[]{:S(2)}) copy-start(f32[1,8,8,8,128]{4,3,2,1,0:T(8,128)S(1)} %add_subtract_fusion) | copy-start | bytes 786436
  59.2 11.6 %collective-permute-start.5 = (f32[1,8,8,8,128]{4,0,3,2,1:T(1,128)S(1)}, f32[1,8,8,8,128]{4,0,3,2,1:T(1,128)S(1)}, u32[]{:S(2)}, u32[]{:S(2)}) collective-permute-start(f32[1,8,8,8,128]{4,0,3,2,1:T(1,128)S(1)} %get-tuple-element.745), channel_id=1, source_target_pairs={{0,8},{8,16},{16,24},{24,32},{32,40},{40,48},{48,56},{56,64},{64,7... | collective-permute-start | bytes 786440 | tf_op jit(solution)/shard_map/ppermute | solution.py:14
  70.8 11.6 %collective-permute-start.6 = (f32[1,8,8,8,128]{4,0,3,2,1:T(1,128)S(1)}, f32[1,8,8,8,128]{4,0,3,2,1:T(1,128)S(1)}, u32[]{:S(2)}, u32[]{:S(2)}) collective-permute-start(f32[1,8,8,8,128]{4,0,3,2,1:T(1,128)S(1)} %get-tuple-element.746), channel_id=1, source_target_pairs={{0,8},{8,16},{16,24},{24,32},{32,40},{40,48},{48,56},{56,64},{64,7... | collective-permute-start | bytes 786440 | tf_op jit(solution)/shard_map/ppermute | solution.py:14
  82.4 11.6 %collective-permute-start.7 = (f32[1,8,8,8,128]{4,0,3,2,1:T(1,128)S(1)}, f32[1,8,8,8,128]{4,0,3,2,1:T(1,128)S(1)}, u32[]{:S(2)}, u32[]{:S(2)}) collective-permute-start(f32[1,8,8,8,128]{4,0,3,2,1:T(1,128)S(1)} %get-tuple-element.747), channel_id=1, source_target_pairs={{0,8},{8,16},{16,24},{24,32},{32,40},{40,48},{48,56},{56,64},{64,7... | collective-permute-start | bytes 786440 | tf_op jit(solution)/shard_map/ppermute | solution.py:14
  94.4 11.6 %collective-permute-start.8 = (f32[1,8,8,8,128]{4,3,2,1,0:T(8,128)S(1)}, f32[1,8,8,8,128]{4,3,2,1,0:T(8,128)S(1)}, u32[]{:S(2)}, u32[]{:S(2)}) collective-permute-start(f32[1,8,8,8,128]{4,3,2,1,0:T(8,128)S(1)} %bitcast.150), channel_id=1, source_target_pairs={{0,8},{8,16},{16,24},{24,32},{32,40},{40,48},{48,56},{56,64},{64,7... | collective-permute-start | bytes 786440 | tf_op jit(solution)/shard_map/ppermute | solution.py:14
  108.9 11.6 %collective-permute-start.12 = (f32[1,8,8,8,128]{4,0,3,2,1:T(1,128)S(1)}, f32[1,8,8,8,128]{4,0,3,2,1:T(1,128)S(1)}, u32[]{:S(2)}, u32[]{:S(2)}) collective-permute-start(f32[1,8,8,8,128]{4,0,3,2,1:T(1,128)S(1)} %get-tuple-element.749), channel_id=1, source_target_pairs={{0,8},{8,16},{16,24},{24,32},{32,40},{40,48},{48,56},{56,64},{64,7... | collective-permute-start | bytes 786440 | tf_op jit(solution)/shard_map/ppermute | solution.py:14
  110.9 15.2 %collective-permute-start.9 = (f32[1,8,8,8,128]{4,3,2,1,0:T(8,128)S(1)}, f32[1,8,8,8,128]{4,3,2,1,0:T(8,128)}, u32[]{:S(2)}, u32[]{:S(2)}) collective-permute-start(f32[1,8,8,8,128]{4,3,2,1,0:T(8,128)S(1)} %get-tuple-element.651), channel_id=1, source_target_pairs={{0,8},{8,16},{16,24},{24,32},{32,40},{40,48},{48,56},{56,64},{64,7... | collective-permute-start | bytes 786440 | tf_op jit(solution)/shard_map/ppermute | solution.py:14
  120.5 11.6 %collective-permute-start.13 = (f32[1,8,8,8,128]{4,0,3,2,1:T(1,128)S(1)}, f32[1,8,8,8,128]{4,0,3,2,1:T(1,128)S(1)}, u32[]{:S(2)}, u32[]{:S(2)}) collective-permute-start(f32[1,8,8,8,128]{4,0,3,2,1:T(1,128)S(1)} %get-tuple-element.750), channel_id=1, source_target_pairs={{0,8},{8,16},{16,24},{24,32},{32,40},{40,48},{48,56},{56,64},{64,7... | collective-permute-start | bytes 786440 | tf_op jit(solution)/shard_map/ppermute | solution.py:14
  126.1 14.5 %collective-permute-start.10 = (f32[1,8,8,8,128]{4,3,2,1,0:T(8,128)S(1)}, f32[1,8,8,8,128]{4,3,2,1,0:T(8,128)}, u32[]{:S(2)}, u32[]{:S(2)}) collective-permute-start(f32[1,8,8,8,128]{4,3,2,1,0:T(8,128)S(1)} %broadcast_select_fusion.23), channel_id=1, source_target_pairs={{0,8},{8,16},{16,24},{24,32},{32,40},{40,48},{48,56},{56,64},{64,7... | collective-permute-start | bytes 786440 | tf_op jit(solution)/shard_map/ppermute | solution.py:14
  132.3 13.1 %collective-permute-start.14 = (f32[1,8,8,8,128]{4,3,2,1,0:T(8,128)S(1)}, f32[1,8,8,8,128]{4,3,2,1,0:T(8,128)S(1)}, u32[]{:S(2)}, u32[]{:S(2)}) collective-permute-start(f32[1,8,8,8,128]{4,3,2,1,0:T(8,128)S(1)} %bitcast.151), channel_id=1, source_target_pairs={{0,8},{8,16},{16,24},{24,32},{32,40},{40,48},{48,56},{56,64},{64,7... | collective-permute-start | bytes 786440 | tf_op jit(solution)/shard_map/ppermute | solution.py:14
  140.6 11.6 %collective-permute-start.11 = (f32[1,8,8,8,128]{4,3,2,1,0:T(8,128)S(1)}, f32[1,8,8,8,128]{4,3,2,1,0:T(8,128)S(1)}, u32[]{:S(2)}, u32[]{:S(2)}) collective-permute-start(f32[1,8,8,8,128]{4,3,2,1,0:T(8,128)S(1)} %broadcast_select_fusion.21), channel_id=1, source_target_pairs={{0,8},{8,16},{16,24},{24,32},{32,40},{40,48},{48,56},{56,64},{64,7... | collective-permute-start | bytes 786440 | tf_op jit(solution)/shard_map/ppermute | solution.py:14
  149.0 24.7 %copy-start.10 = (u32[256]{0:T(256)S(1)}, u32[256]{0:T(256)}, u32[]{:S(2)}) copy-start(u32[256]{0:T(256)} %constant.167) | copy-start | bytes 3076
  152.4 11.1 %collective-permute-start.15 = (f32[1,8,8,8,128]{4,3,2,1,0:T(8,128)S(1)}, f32[1,8,8,8,128]{4,3,2,1,0:T(8,128)S(1)}, u32[]{:S(2)}, u32[]{:S(2)}) collective-permute-start(f32[1,8,8,8,128]{4,3,2,1,0:T(8,128)S(1)} %get-tuple-element.630), channel_id=1, source_target_pairs={{8,0},{16,8},{24,16},{32,24},{40,32},{48,40},{56,48},{64,56},{72,6... | collective-permute-start | bytes 786440 | tf_op jit(solution)/shard_map/ppermute | solution.py:14
  156.6 14.5 %collective-permute-start.18 = (f32[128]{0:T(128)S(1)}, f32[128]{0:T(128)S(1)}, u32[]{:S(2)}, u32[]{:S(2)}) collective-permute-start(f32[128]{0:T(128)S(1)} %get-tuple-element.664), channel_id=1, source_target_pairs={{8,0},{16,8},{24,16},{32,24},{40,32},{48,40},{56,48},{64,56},{72,6... | collective-permute-start | bytes 1544 | tf_op jit(solution)/shard_map/ppermute | solution.py:14
  158.5 31.2 %collective-permute-start = (bf16[3,3,3,128,128]{4,3,2,1,0:T(8,128)(2,1)S(1)}, bf16[3,3,3,128,128]{4,3,2,1,0:T(8,128)(2,1)S(1)}, u32[]{:S(2)}, u32[]{:S(2)}) collective-permute-start(bf16[3,3,3,128,128]{4,3,2,1,0:T(8,128)(2,1)S(1)} %slice_bitcast_fusion.4), channel_id=1, source_target_pairs={{8,0},{16,8},{24,16},{32,24},{40,32},{48,40},{56,48},{64,56},{72,6... | collective-permute-start | bytes 2654216 | tf_op jit(solution)/shard_map/ppermute | solution.py:14
  163.5 24.2 %collective-permute-start.16 = (f32[1,8,8,8,128]{4,3,2,1,0:T(8,128)S(1)}, f32[1,8,8,8,128]{4,3,2,1,0:T(8,128)S(1)}, u32[]{:S(2)}, u32[]{:S(2)}) collective-permute-start(f32[1,8,8,8,128]{4,3,2,1,0:T(8,128)S(1)} %broadcast_select_fusion.20), channel_id=1, source_target_pairs={{8,0},{16,8},{24,16},{32,24},{40,32},{48,40},{56,48},{64,56},{72,6... | collective-permute-start | bytes 786440 | tf_op jit(solution)/shard_map/ppermute | solution.py:14
  171.8 10.4 %collective-permute-start.19 = (f32[128]{0:T(128)S(1)}, f32[128]{0:T(128)S(1)}, u32[]{:S(2)}, u32[]{:S(2)}) collective-permute-start(f32[128]{0:T(128)S(1)} %broadcast_select_fusion.29), channel_id=1, source_target_pairs={{8,0},{16,8},{24,16},{32,24},{40,32},{48,40},{56,48},{64,56},{72,6... | collective-permute-start | bytes 1544 | tf_op jit(solution)/shard_map/ppermute | solution.py:14
  182.2 10.7 %collective-permute-start.20 = (f32[128]{0:T(128)S(1)}, f32[128]{0:T(128)S(1)}, u32[]{:S(2)}, u32[]{:S(2)}) collective-permute-start(f32[128]{0:T(128)S(1)} %broadcast_select_fusion.30), channel_id=1, source_target_pairs={{8,0},{16,8},{24,16},{32,24},{40,32},{48,40},{56,48},{64,56},{72,6... | collective-permute-start | bytes 1544 | tf_op jit(solution)/shard_map/ppermute | solution.py:14
  187.8 11.1 %collective-permute-start.17 = (f32[1,8,8,8,128]{4,3,2,1,0:T(8,128)S(1)}, f32[1,8,8,8,128]{4,3,2,1,0:T(8,128)S(1)}, u32[]{:S(2)}, u32[]{:S(2)}) collective-permute-start(f32[1,8,8,8,128]{4,3,2,1,0:T(8,128)S(1)} %broadcast_select_fusion.22), channel_id=1, source_target_pairs={{8,0},{16,8},{24,16},{32,24},{40,32},{48,40},{56,48},{64,56},{72,6... | collective-permute-start | bytes 786440 | tf_op jit(solution)/shard_map/ppermute | solution.py:14
  191.0 18.8 %collective-permute-start.1 = (bf16[3,3,3,128,128]{4,3,2,1,0:T(8,128)(2,1)S(1)}, bf16[3,3,3,128,128]{4,3,2,1,0:T(8,128)(2,1)}, u32[]{:S(2)}, u32[]{:S(2)}) collective-permute-start(bf16[3,3,3,128,128]{4,3,2,1,0:T(8,128)(2,1)S(1)} %broadcast_select_fusion.16), channel_id=1, source_target_pairs={{8,0},{16,8},{24,16},{32,24},{40,32},{48,40},{56,48},{64,56},{72,6... | collective-permute-start | bytes 2654216 | tf_op jit(solution)/shard_map/ppermute | solution.py:14
  199.4 1.3 copy-start.1
  200.7 194.3 %all-gather.4.cloned.1.call-start = ((), (), s32[]{:S(2)}) async-start(), calls=%async_computation | async-start | bytes 7962624 | tf_op jit(solution)/shard_map/all_gather | solution.py:20
  209.9 29.3 %collective-permute-start.2 = (bf16[3,3,3,128,128]{4,3,2,1,0:T(8,128)(2,1)S(1)}, bf16[3,3,3,128,128]{4,3,2,1,0:T(8,128)(2,1)S(1)}, u32[]{:S(2)}, u32[]{:S(2)}) collective-permute-start(bf16[3,3,3,128,128]{4,3,2,1,0:T(8,128)(2,1)S(1)} %broadcast_select_fusion.17), channel_id=1, source_target_pairs={{8,0},{16,8},{24,16},{32,24},{40,32},{48,40},{56,48},{64,56},{72,6... | collective-permute-start | bytes 2654216 | tf_op jit(solution)/shard_map/ppermute | solution.py:14
  395.0 57.1 %copy-start.6 = (bf16[3,3,3,128,128]{4,3,2,1,0:T(8,128)(2,1)S(1)}, bf16[3,3,3,128,128]{4,3,2,1,0:T(8,128)(2,1)}, u32[]{:S(2)}) copy-start(bf16[3,3,3,128,128]{4,3,2,1,0:T(8,128)(2,1)} %copy-done.5) | copy-start | bytes 2654212
  395.0 57.1 %copy-start.8 = (f32[1,8,8,8,128]{4,3,2,1,0:T(8,128)S(1)}, f32[1,8,8,8,128]{4,3,2,1,0:T(8,128)}, u32[]{:S(2)}) copy-start(f32[1,8,8,8,128]{4,3,2,1,0:T(8,128)} %copy-done.7) | copy-start | bytes 786436
  440.5 11.6 %collective-permute-start.21 = (f32[1,8,8,8,128]{4,0,3,2,1:T(1,128)S(1)}, f32[1,8,8,8,128]{4,0,3,2,1:T(1,128)S(1)}, u32[]{:S(2)}, u32[]{:S(2)}) collective-permute-start(f32[1,8,8,8,128]{4,0,3,2,1:T(1,128)S(1)} %bitcast.162), channel_id=1, source_target_pairs={{0,8},{8,16},{16,24},{24,32},{32,40},{40,48},{48,56},{56,64},{64,7... | collective-permute-start | bytes 786440 | tf_op jit(solution)/shard_map/ppermute | solution.py:14
  455.1 11.6 %collective-permute-start.22 = (f32[1,8,8,8,128]{4,0,3,2,1:T(1,128)S(1)}, f32[1,8,8,8,128]{4,0,3,2,1:T(1,128)S(1)}, u32[]{:S(2)}, u32[]{:S(2)}) collective-permute-start(f32[1,8,8,8,128]{4,0,3,2,1:T(1,128)S(1)} %get-tuple-element.752), channel_id=1, source_target_pairs={{0,8},{8,16},{16,24},{24,32},{32,40},{40,48},{48,56},{56,64},{64,7... | collective-permute-start | bytes 786440 | tf_op jit(solution)/shard_map/ppermute | solution.py:14
  466.7 11.6 %collective-permute-start.23 = (f32[1,8,8,8,128]{4,0,3,2,1:T(1,128)S(1)}, f32[1,8,8,8,128]{4,0,3,2,1:T(1,128)S(1)}, u32[]{:S(2)}, u32[]{:S(2)}) collective-permute-start(f32[1,8,8,8,128]{4,0,3,2,1:T(1,128)S(1)} %get-tuple-element.753), channel_id=1, source_target_pairs={{0,8},{8,16},{16,24},{24,32},{32,40},{40,48},{48,56},{56,64},{64,7... | collective-permute-start | bytes 786440 | tf_op jit(solution)/shard_map/ppermute | solution.py:14
  478.5 14.6 %copy-start.4 = (bf16[4,3,3,3,128,128]{5,4,3,2,1,0:T(8,128)(2,1)S(1)}, bf16[4,3,3,3,128,128]{5,4,3,2,1,0:T(8,128)(2,1)}, u32[]{:S(2)}) copy-start(bf16[4,3,3,3,128,128]{5,4,3,2,1,0:T(8,128)(2,1)} %param.34) | copy-start | bytes 10616836
  478.5 11.8 %collective-permute-start.24 = (f32[1,8,8,8,128]{4,3,2,1,0:T(8,128)S(1)}, f32[1,8,8,8,128]{4,3,2,1,0:T(8,128)S(1)}, u32[]{:S(2)}, u32[]{:S(2)}) collective-permute-start(f32[1,8,8,8,128]{4,3,2,1,0:T(8,128)S(1)} %bitcast.164), channel_id=1, source_target_pairs={{0,8},{8,16},{16,24},{24,32},{32,40},{40,48},{48,56},{56,64},{64,7... | collective-permute-start | bytes 786440 | tf_op jit(solution)/shard_map/ppermute | solution.py:14
Sparse Core Ops, SparseCore 0:
  200.8 189.3 all-reduce.2
Sparse Core Ops, SparseCore 1:
  257.5 82.5 all-gather.3
where the time goes:
time: 517 us; the launch traced here: 507 us
  waiting for transfers between devices  305 us (59%)
  matrix products  65.4 us (13%)
  starting transfers between devices  64.8 us (13%)
  local copies, waits for them, and re-layouts  29.7 us (6%)
  blocking collectives  18.1 us (4%)
  between operations  17.3 us (3%)
  other arithmetic  5.56 us (1%)
    ppermute x25, waiting for transfers between devices, passed_along(): lax.ppermute(value, axis, [(source, source + steps) for source in range(i...  172 us
    unnamed x3, waiting for transfers between devices  133 us
    conv_general_dilated x23, matrix products, advance(): lax.conv_general_dilated(squashed, kernel, (1, 1, 1), 'SAME', dimension_n...  65.4 us
    ppermute x25, starting transfers between devices, passed_along(): lax.ppermute(value, axis, [(source, source + steps) for source in range(i...  64.7 us
    all_gather x1, blocking collectives, gathered_by_axis(): out = lax.all_gather(out, axes[number], axis=dim, tiled=True)  18.1 us
    dynamic_slice x16, local copies, waits for them, and re-layouts, local_round(): block = lax.dynamic_index_in_dim(share_grid, turn, 0, keepdims=False)  10.7 us
  transfers between devices with their start and end apart: 27, of which 22 were waited for; matrix products, arithmetic and copies ran while one was open for 3% of the time, Pallas kernels for 0%

commit v1 on v0

v1 whole, which is shorter than its diff:
```python
import functools

import jax
import jax.numpy as jnp
from jax import lax
from jax.experimental import pallas as pl
from jax.experimental.pallas import tpu as pltpu
from jax.sharding import Mesh
from jax.sharding import PartitionSpec as P

X, Z = 4, 8
LAYER, BATCH = ("z", "x"), ("y", "core")
ROWS, CH = 512, 128
TAPS, DEEP = 9, 384
SHARE = TAPS * DEEP // 8
FINE = 2.0 / 128
COARSE = 4 * FINE
TOP = 4 * COARSE


def conv(v, weights):
    t = jnp.tanh(v).reshape(64, 8, CH)
    at = lax.broadcasted_iota(jnp.int32, (64, 8, CH), 1)
    before = jnp.where(at == 0, 0.0, pltpu.roll(t, 1, 1))
    after = jnp.where(at == 7, 0.0, pltpu.roll(t, 7, 1))
    lhs = jnp.concatenate(
        [s.reshape(ROWS, CH).astype(jnp.bfloat16) for s in (before, t, after)], 1
    )
    rhs = jnp.concatenate([weights[n * DEEP : (n + 1) * DEEP] for n in range(TAPS)], 1)
    out = jnp.dot(lhs, rhs, preferred_element_type=jnp.float32)
    edge_y = jnp.zeros((8, 1, 8, CH), jnp.float32)
    edge_x = jnp.zeros((1, 8, 8, CH), jnp.float32)
    total = None
    for dx in range(3):
        for dy in range(3):
            n = dx * 3 + dy
            part = out[:, n * CH : (n + 1) * CH].reshape(8, 8, 8, CH)
            if dy == 0:
                part = jnp.concatenate([edge_y, part[:, :7]], 1)
            if dy == 2:
                part = jnp.concatenate([part[:, 1:], edge_y], 1)
            if dx == 0:
                part = jnp.concatenate([edge_x, part[:7]], 0)
            if dx == 2:
                part = jnp.concatenate([part[1:], edge_x], 0)
            total = part if total is None else total + part
    return total.reshape(ROWS, CH)


def own_weights(ref, index):
    return ref[pl.ds(index, 1)].reshape(TAPS * DEEP, CH)


def group_weights(ref, pos, q):
    turn = lax.rem(q - pos[0] + X, X)
    return ref[:, pl.ds(turn, 1)].reshape(TAPS * DEEP, CH)


def add_term(buf, pos, q, terms):
    turn = lax.rem(q - pos[0] + X, X)
    for r, term in enumerate(terms):

        @pl.when(turn == r)
        def _():
            buf[...] += term[...]


def first_kernel(pos, guess, head, inputs, kernels, biases, out):
    out[...] = jnp.where((pos[0] == 0) & (pos[1] == 0), inputs[...], head[...])

    def body(i, carry):
        v = out[...]
        out[...] = v + FINE * (conv(v, own_weights(kernels, i)) + biases[pl.ds(i, 1)])
        return carry

    lax.fori_loop(0, 4, body, 0)


def second_kernel(pos, head, inputs, kernels, biases, message, term, buf):
    start = jnp.where((pos[0] == 0) & (pos[1] == 0), inputs[...], head[...])
    buf[...] = start
    term[...] = start

    def body(i, carry):
        v = buf[...]
        mixed = conv(v, own_weights(kernels, i))
        buf[...] = v + FINE * (mixed + biases[pl.ds(i, 1)])

        @pl.when(i == 0)
        def _():
            term[...] += COARSE * mixed

        return carry

    lax.fori_loop(0, 4, body, 0)
    term[...] = buf[...] - term[...]

    @pl.when(pos[0] == 0)
    def _():
        message[...] = buf[...]

    @pl.when(pos[0] != 0)
    def _():
        message[...] = term[...]


def third_kernel(pos, m0, m1, m2, m3, weights, out):
    messages = (m0, m1, m2, m3)
    out[...] = jnp.zeros((ROWS, CH), jnp.float32)
    add_term(out, pos, 0, messages)

    def body(q, carry):
        out[...] += COARSE * conv(out[...], group_weights(weights, pos, q))
        add_term(out, pos, q, messages)
        return carry

    lax.fori_loop(1, 4, body, 0)


def first_term(pos, buf, own, f1, f2, f3):
    for x, term in enumerate((own, f1, f2, f3)):

        @pl.when(pos[0] == x)
        def _():
            buf[...] += term[...]


def fourth_kernel(
    pos, hop, inputs, point, own, f1, f2, f3, m1, m2, m3, weights, residual, corner, defect
):
    start = jnp.where(pos[1] == 0, inputs[...], hop[...])
    corner[...] = start
    residual[...] = jnp.zeros((ROWS, CH), jnp.float32)

    def body(q, carry):
        corner[...] += COARSE * conv(corner[...], group_weights(weights, pos, q))

        @pl.when(q == 0)
        def _():
            first_term(pos, corner, own, f1, f2, f3)

        @pl.when(q > 0)
        def _():
            add_term(corner, pos, q, (own, m1, m2, m3))

        return carry

    lax.fori_loop(0, 4, body, 0)

    @pl.when(pos[0] == 3)
    def _():
        residual[...] = corner[...] - point[...]

    start = jnp.where(pos[1] == 0, inputs[...], hop[...])
    defect[...] = corner[...] - start - TOP * conv(start, group_weights(weights, pos, 3))


def chain_kernel(step, pos, arrived, before, value, defect, weights, out_before, out_value):
    @pl.when(pos[1] == step)
    def _():
        v = arrived[...]
        out_before[...] = v
        out_value[...] = v + TOP * conv(v, group_weights(weights, pos, 3)) + defect[...]

    @pl.when(pos[1] != step)
    def _():
        out_before[...] = before[...]
        out_value[...] = value[...]


def last_kernel(
    pos, start, value, own, f1, f2, f3, m1, m2, m3, weights, kernels, biases, states, buf
):
    buf[...] = start[...]

    def coarse(q, carry):
        buf[...] += COARSE * conv(buf[...], group_weights(weights, pos, q))

        @pl.when(q == 0)
        def _():
            first_term(pos, buf, own, f1, f2, f3)

        @pl.when(q > 0)
        def _():
            add_term(buf, pos, q, (own, m1, m2, m3))

        return carry

    lax.fori_loop(0, pos[0], coarse, 0)

    def fine(i, carry):
        v = buf[...]
        mixed = conv(v, own_weights(kernels, i))

        @pl.when((i == 0) & (pos[0] < 3))
        def _():
            states[3] = v + COARSE * mixed + own[...]

        new = v + FINE * (mixed + biases[pl.ds(i, 1)])
        states[pl.ds(i, 1)] = new.reshape(1, ROWS, CH)
        buf[...] = new
        return carry

    lax.fori_loop(0, 3, fine, 0)

    @pl.when(pos[0] == 3)
    def _():
        states[3] = value[...]


STATE = jax.ShapeDtypeStruct((ROWS, CH), jnp.float32)


def call(body, name, outs, convs, *args, scratch=()):
    vmem = pl.BlockSpec(memory_space=pltpu.VMEM)
    smem = pl.BlockSpec(memory_space=pltpu.SMEM)
    return pl.pallas_call(
        body,
        name=name,
        out_shape=outs,
        in_specs=[smem] + [vmem] * (len(args) - 1),
        out_specs=jax.tree.map(lambda _: vmem, outs),
        scratch_shapes=scratch,
        compiler_params=pltpu.CompilerParams(vmem_limit_bytes=24 << 20),
        cost_estimate=pl.CostEstimate(
            flops=convs * 2 * ROWS * CH * CH * 27,
            bytes_accessed=convs * 27 * CH * CH * 2,
            transcendentals=convs * ROWS * CH,
        ),
    )(*args)


def shards(inputs, guess_states, kernels, biases):
    x, z = lax.axis_index("x"), lax.axis_index("z")
    pos = jnp.stack([x, z]).astype(jnp.int32)
    share_index = lax.axis_index(BATCH)
    state = jax.ShapeDtypeStruct((ROWS, CH), jnp.float32)
    buffer = pltpu.VMEM((ROWS, CH), jnp.float32)
    inputs = inputs.reshape(ROWS, CH)
    guess = guess_states[-1].reshape(ROWS, CH)
    kernels = kernels.reshape(4, TAPS * DEEP, CH)

    along = [(i, i + 1) for i in range(X * Z - 1)]
    ring = [[(i, (i - r) % X) for i in range(X)] for r in range(X)]

    def next_layer(v):
        return lax.ppermute(v, LAYER, along)

    def from_ahead(v, r):
        return lax.ppermute(v, "x", ring[r])

    head = next_layer(guess)
    share = lax.dynamic_slice_in_dim(kernels[0], share_index * SHARE, SHARE, 0)
    shares = jnp.stack([share] + [from_ahead(share, r) for r in (1, 2, 3)])
    group = lax.all_gather(shares, BATCH)

    point = call(first_kernel, "first", state, 4, pos, guess, head, inputs, kernels, biases)
    head = next_layer(point)
    message, term = call(
        second_kernel, "second", (state, state), 4, pos, head, inputs, kernels, biases,
        scratch=[buffer],
    )
    m1, m2, m3 = (from_ahead(message, r) for r in (1, 2, 3))
    point = call(third_kernel, "third", state, 3, pos, message, m1, m2, m3, group)
    hop = lax.ppermute(point, "z", [(i, i + 1) for i in range(Z - 1)])
    f1, f2, f3 = (lax.ppermute(term, "x", [(0, i)]) for i in (1, 2, 3))
    residual, corner, defect = call(
        fourth_kernel, "fourth", (state,) * 3, 5,
        pos, hop, inputs, point, term, f1, f2, f3, m1, m2, m3, group,
    )
    before = jnp.where(z == 0, inputs, hop)
    value = corner
    for step in range(2, Z):
        arrived = lax.ppermute(value, "z", [(step - 1, step)])
        before, value = call(
            functools.partial(chain_kernel, step), "chain", (state, state), 1,
            pos, arrived, before, value, defect, group,
        )
    states = call(
        last_kernel, "last", jax.ShapeDtypeStruct((4, ROWS, CH), jnp.float32), 6,
        pos, before, value, term, f1, f2, f3, m1, m2, m3, group, kernels, biases,
        scratch=[buffer],
    )
    volume = (8, 8, 8, CH)
    return states.reshape((4, 1) + volume), residual.reshape((1, 1) + volume)


def solution(mesh):
    finer = Mesh(mesh.devices.reshape(Z, X, 4, 2), LAYER + BATCH)
    return jax.shard_map(
        shards,
        mesh=finer,
        in_specs=(P(BATCH), P(LAYER, BATCH), P(LAYER), P(LAYER)),
        out_specs=(P(LAYER, BATCH), P(LAYER, BATCH)),
        check_vma=False,
    )
```

time: 517 us -> 159 us (0.31)
  the two profiles are of different devices: /device:TPU:128 before, /device:TPU:230 now
where the time goes in v1:
time: 159 us; the launch traced here: 158 us
  waiting for transfers between devices  69.5 us (44%)
  Pallas kernels  30.6 us (19%)
  starting transfers between devices  23.2 us (15%)
  local copies, waits for them, and re-layouts  18.1 us (11%)
  between operations  14.4 us (9%)
  other arithmetic  2 us (1%)
    ppermute x6, waiting for transfers between devices, shards(): arrived = lax.ppermute(value, 'z', [(step - 1, step)])  37.2 us
    pallas_call x11, Pallas kernels, call(): pl.pallas_call(body, name=name, out_shape=outs, in_specs=[smem] + [vmem]...  30.6 us
    ppermute x2, waiting for transfers between devices, next_layer(): return lax.ppermute(v, LAYER, along)  16 us
    unnamed x50, local copies, waits for them, and re-layouts  12.2 us
    ppermute x6, starting transfers between devices, from_ahead(): return lax.ppermute(v, 'x', ring[r])  9.77 us
    ppermute x6, waiting for transfers between devices, from_ahead(): return lax.ppermute(v, 'x', ring[r])  9.38 us
    ppermute x1, waiting for transfers between devices, shards(): hop = lax.ppermute(point, 'z', [(i, i + 1) for i in range(Z - 1)])  6.93 us
    ppermute x6, starting transfers between devices, shards(): arrived = lax.ppermute(value, 'z', [(step - 1, step)])  5.49 us
  transfers between devices with their start and end apart: 19, of which 8 were waited for; matrix products, arithmetic and copies ran while one was open for 2% of the time, Pallas kernels for 8%

profile of v1, /device:TPU:230, one launch (start us, length us, event | category | flops | bytes accessed | tf_op | source)
XLA Modules:
  0.0 157.7 jit_solution(17567706304681966849)
XLA Ops:
  7.2 0.0 copy-start.5
  7.2 0.0 all-gather.3.cloned.1.call-start
  7.2 2.3 %slice.8 = bf16[1,3,3,3,128,128]{5,4,3,2,1,0:T(8,128)(2,1)} slice(bf16[4,3,3,3,128,128]{5,4,3,2,1,0:T(8,128)(2,1)} %param.6), slice={[0:1], [0:3], [0:3], [0:3], [0:128], [0:128]} | slice | bytes 1769472 | tf_op jit(solution)/shard_map/slice | solution.py:253
  9.6 0.9 constant_dynamic-slice_fusion
  10.5 1.4 collective-permute-start.6
  11.9 3.2 %collective-permute-start.7 = (bf16[432,128]{1,0:T(8,128)(2,1)S(1)}, bf16[432,128]{1,0:T(8,128)(2,1)S(1)}, u32[]{:S(2)}, u32[]{:S(2)}) collective-permute-start(bf16[432,128]{1,0:T(8,128)(2,1)S(1)} %constant_dynamic-slice_fusion), channel_id=1, source_target_pairs={{0,8},{8,16},{16,24},{24,0},{1,9},{9,17},{17,25},{25,1},{2,10},{10... | collective-permute-start | bytes 331784 | tf_op jit(solution)/shard_map/ppermute | solution.py:250
  15.1 0.9 fusion
  16.0 1.9 %collective-permute-done.6 = bf16[432,128]{1,0:T(8,128)(2,1)S(1)} collective-permute-done((bf16[432,128]{1,0:T(8,128)(2,1)S(1)}, bf16[432,128]{1,0:T(8,128)(2,1)S(1)}, u32[]{:S(2)}, u32[]{:S(2)}) %collective-permute-start.6) | collective-permute-done | bytes 110624 | tf_op jit(solution)/shard_map/ppermute | solution.py:250
  17.9 1.2 collective-permute-done.5
  19.1 0.8 pad_maximum_fusion
  20.0 0.0 all-gather.3.cloned.1.call-update
  20.0 1.7 %slice.7 = f32[1,1,8,8,8,128]{5,4,3,2,1,0:T(8,128)} slice(f32[4,1,8,8,8,128]{5,4,3,2,1,0:T(8,128)} %param.5), slice={[3:4], [0:1], [0:8], [0:8], [0:8], [0:128]} | slice | bytes 524288 | tf_op jit(solution)/shard_map/slice | solution.py:240
  21.7 1.3 collective-permute-start
  23.0 0.1 pad_add_fusion.pos
  23.0 8.6 %collective-permute-done.head = f32[512,128]{1,0:T(8,128)} collective-permute-done((f32[512,128]{1,0:T(8,128)}, f32[512,128]{1,0:T(8,128)}, u32[]{:S(2)}, u32[]{:S(2)}) %collective-permute-start) | collective-permute-done | bytes 262176 | tf_op jit(solution)/shard_map/ppermute | solution.py:247
  31.6 1.0 copy-done.19
  32.6 4.3 %first.1 = f32[512,128]{1,0:T(8,128)S(1)} custom-call(s32[2]{0:T(128)S(1)} %pad_add_fusion.pos, f32[512,128]{1,0:T(8,128)} %bitcast.2.guess, f32[512,128]{1,0:T(8,128)} %collective-permute-done.head, f32[512,128]{1,0:T(8,128)S(1)} %bitcast.29, bf16[4,3456,128]{2,1,0:T(8,128)(2,1)S(1)} %bitcast.26, f32[4,128]{1,0:T(4,128)S(1)} %copy-done.22), custom_call_target="tpu_custom_call" | custom-call | flops 1811939328 | bytes 3538944 | tf_op jit(solution)/shard_map/first/pallas_call | solution.py:217
  36.9 1.3 collective-permute-start.1
  38.2 7.4 %collective-permute-done.1.head = f32[512,128]{1,0:T(8,128)S(1)} collective-permute-done((f32[512,128]{1,0:T(8,128)S(1)}, f32[512,128]{1,0:T(8,128)S(1)}, u32[]{:S(2)}, u32[]{:S(2)}) %collective-permute-start.1) | collective-permute-done | bytes 262176 | tf_op jit(solution)/shard_map/ppermute | solution.py:247
  45.7 4.6 %second.1 = (f32[512,128]{1,0:T(8,128)S(1)}, f32[512,128]{1,0:T(8,128)}) custom-call(s32[2]{0:T(128)S(1)} %pad_add_fusion.pos, f32[512,128]{1,0:T(8,128)S(1)} %collective-permute-done.1.head, f32[512,128]{1,0:T(8,128)S(1)} %bitcast.30, bf16[4,3456,128]{2,1,0:T(8,128)(2,1)S(1)} %bitcast.27, f32[4,128]{1,0:T(4,128)S(1)} %copy-done.22), custom_call_target="tpu_custom_call" | custom-call | flops 1811939328 | bytes 3538944 | tf_op jit(solution)/shard_map/second/pallas_call | solution.py:217
  50.3 4.3 %collective-permute-start.4 = (f32[512,128]{1,0:T(8,128)S(1)}, f32[512,128]{1,0:T(8,128)S(1)}, u32[]{:S(2)}, u32[]{:S(2)}) collective-permute-start(f32[512,128]{1,0:T(8,128)S(1)} %get-tuple-element.19.m0), channel_id=1, source_target_pairs={{0,8},{8,16},{16,24},{24,0},{1,9},{9,17},{17,25},{25,1},{2,10},{10... | collective-permute-start | bytes 786440 | tf_op jit(solution)/shard_map/ppermute | solution.py:250
  54.5 0.9 collective-permute-start.2
  55.4 0.7 copy-done.23
  56.1 1.3 collective-permute-start.11
  57.4 1.4 collective-permute-start.10
  58.8 3.5 %collective-permute-done.4.m3 = f32[512,128]{1,0:T(8,128)S(1)} collective-permute-done((f32[512,128]{1,0:T(8,128)S(1)}, f32[512,128]{1,0:T(8,128)S(1)}, u32[]{:S(2)}, u32[]{:S(2)}) %collective-permute-start.4) | collective-permute-done | bytes 262176 | tf_op jit(solution)/shard_map/ppermute | solution.py:250
  62.3 0.7 copy-done.7
  63.0 1.4 collective-permute-start.9
  64.3 0.7 copy-done.11
  65.1 2.7 %collective-permute-done.2.m1 = f32[512,128]{1,0:T(8,128)S(1)} collective-permute-done((f32[512,128]{1,0:T(8,128)S(1)}, f32[512,128]{1,0:T(8,128)S(1)}, u32[]{:S(2)}, u32[]{:S(2)}) %collective-permute-start.2) | collective-permute-done | bytes 262176 | tf_op jit(solution)/shard_map/ppermute | solution.py:250
  67.8 0.7 copy-done.15
  68.5 2.0 %copy-done = bf16[32,432,128]{2,1,0:T(8,128)(2,1)S(1)} copy-done((bf16[32,432,128]{2,1,0:T(8,128)(2,1)S(1)}, bf16[32,432,128]{2,1,0:T(8,128)(2,1)}, u32[]{:S(2)}) %copy-start) | copy-done | bytes 3538968
  70.5 0.9 copy-done.8
  71.5 0.9 copy-done.12
  72.4 0.9 copy-done.16
  73.4 0.9 copy-done.24
  74.3 3.2 %third.1.point = f32[512,128]{1,0:T(8,128)S(1)} custom-call(s32[2]{0:T(128)S(1)} %pad_add_fusion.pos, f32[512,128]{1,0:T(8,128)S(1)} %copy-done.24, f32[512,128]{1,0:T(8,128)S(1)} %copy-done.16, f32[512,128]{1,0:T(8,128)S(1)} %copy-done.12, f32[512,128]{1,0:T(8,128)S(1)} %copy-done.8, bf16[8,4,432,128]{3,2,1,0:T(8,128)(2,1)S(1)} %bitcast.17), custom_call_target="tpu_custom_call" | custom-call | flops 1358954496 | bytes 2654208 | tf_op jit(solution)/shard_map/third/pallas_call | solution.py:217
  77.5 1.3 collective-permute-start.8
  78.8 0.0 collective-permute-done.11.f3
  78.8 0.0 collective-permute-done.10.f2
  78.8 6.9 %collective-permute-done.8.hop = f32[512,128]{1,0:T(8,128)S(1)} collective-permute-done((f32[512,128]{1,0:T(8,128)S(1)}, f32[512,128]{1,0:T(8,128)S(1)}, u32[]{:S(2)}, u32[]{:S(2)}) %collective-permute-start.8) | collective-permute-done | bytes 262176 | tf_op jit(solution)/shard_map/ppermute | solution.py:265
  85.8 0.0 copy-start.20
  85.8 0.9 copy-done.20
  86.7 6.1 %fourth.1 = (f32[512,128]{1,0:T(8,128)}, f32[512,128]{1,0:T(8,128)}, f32[512,128]{1,0:T(8,128)S(1)}) custom-call(s32[2]{0:T(128)S(1)} %pad_add_fusion.pos, f32[512,128]{1,0:T(8,128)S(1)} %collective-permute-done.8.hop, f32[512,128]{1,0:T(8,128)S(1)} %bitcast.31, f32[512,128]{1,0:T(8,128)S(1)} %third.1.point, f32[512,128]{1,0:T(8,128)} %get-tuple-element.20.own, ...), custom_call_target="tpu_custom_call" | custom-call | flops 2264924160 | bytes 4423680 | tf_op jit(solution)/shard_map/fourth/pallas_call | solution.py:217
  92.9 0.7 copy-done.2
  93.6 1.4 collective-permute-start.12
  94.9 1.1 broadcast_select_fusion.before
  96.0 0.9 copy-done.3
  97.0 1.1 chain.6
  98.1 0.7 collective-permute-start.13
  98.8 0.6 chain.7
  99.4 0.7 collective-permute-start.14
  100.1 0.0 collective-permute-done.14.arrived
  100.1 0.8 chain.8
  100.9 0.7 collective-permute-start.15
  101.5 0.0 collective-permute-done.15.arrived
  101.5 0.6 chain.9
  102.1 0.7 collective-permute-start.16
  102.8 0.0 copy-start.6
  102.9 0.6 chain.10
  103.5 1.4 collective-permute-start.17
  104.9 37.2 %collective-permute-done.17.arrived = f32[512,128]{1,0:T(8,128)S(1)} collective-permute-done((f32[512,128]{1,0:T(8,128)S(1)}, f32[512,128]{1,0:T(8,128)S(1)}, u32[]{:S(2)}, u32[]{:S(2)}) %collective-permute-start.17) | collective-permute-done | bytes 262176 | tf_op jit(solution)/shard_map/ppermute | solution.py:274
  142.1 1.4 chain.11
  143.5 7.4 %last.1 = f32[4,512,128]{2,1,0:T(8,128)} custom-call(s32[2]{0:T(128)S(1)} %pad_add_fusion.pos, f32[512,128]{1,0:T(8,128)S(1)} %get-tuple-element.33.start, f32[512,128]{1,0:T(8,128)S(1)} %get-tuple-element.34.value, f32[512,128]{1,0:T(8,128)} %get-tuple-element.20.own, f32[512,128]{1,0:T(8,128)} %collective-permute-done.9.f1, ...), custom_call_target="tpu_custom_call" | custom-call | flops 2717908992 | bytes 5308416 | tf_op jit(solution)/shard_map/last/pallas_call | solution.py:217
  (43 shorter events, 0.1 us)
Async XLA Ops:
  7.2 24.5 %copy-start.5 = (bf16[4,3,3,3,128,128]{5,4,3,2,1,0:T(8,128)(2,1)S(1)}, bf16[4,3,3,3,128,128]{5,4,3,2,1,0:T(8,128)(2,1)}, u32[]{:S(2)}) copy-start(bf16[4,3,3,3,128,128]{5,4,3,2,1,0:T(8,128)(2,1)} %param.6) | copy-start | bytes 10616836
  7.2 24.5 %copy-start.22 = (f32[4,128]{1,0:T(4,128)S(1)}, f32[4,128]{1,0:T(4,128)}, u32[]{:S(2)}) copy-start(f32[4,128]{1,0:T(4,128)} %biases.5) | copy-start | bytes 6148
  7.2 61.3 %all-gather.3.cloned.1.call-start = ((), (), s32[]{:S(2)}) async-start(), calls=%async_computation | async-start | bytes 3981312 | tf_op jit(solution)/shard_map/all_gather | solution.py:255
  10.5 7.4 %collective-permute-start.6 = (bf16[432,128]{1,0:T(8,128)(2,1)S(1)}, bf16[432,128]{1,0:T(8,128)(2,1)S(1)}, u32[]{:S(2)}, u32[]{:S(2)}) collective-permute-start(bf16[432,128]{1,0:T(8,128)(2,1)S(1)} %constant_dynamic-slice_fusion), channel_id=1, source_target_pairs={{0,16},{8,24},{16,0},{24,8},{1,17},{9,25},{17,1},{25,9},{2,18},{10... | collective-permute-start | bytes 331784 | tf_op jit(solution)/shard_map/ppermute | solution.py:250
  11.9 7.3 %collective-permute-start.5 = (bf16[432,128]{1,0:T(8,128)(2,1)S(1)}, bf16[432,128]{1,0:T(8,128)(2,1)S(1)}, u32[]{:S(2)}, u32[]{:S(2)}) collective-permute-start(bf16[432,128]{1,0:T(8,128)(2,1)S(1)} %constant_dynamic-slice_fusion), channel_id=1, source_target_pairs={{0,24},{8,0},{16,8},{24,16},{1,25},{9,1},{17,9},{25,17},{2,26},{10... | collective-permute-start | bytes 331784 | tf_op jit(solution)/shard_map/ppermute | solution.py:250
  11.9 7.3 %collective-permute-start.7 = (bf16[432,128]{1,0:T(8,128)(2,1)S(1)}, bf16[432,128]{1,0:T(8,128)(2,1)S(1)}, u32[]{:S(2)}, u32[]{:S(2)}) collective-permute-start(bf16[432,128]{1,0:T(8,128)(2,1)S(1)} %constant_dynamic-slice_fusion), channel_id=1, source_target_pairs={{0,8},{8,16},{16,24},{24,0},{1,9},{9,17},{17,25},{25,1},{2,10},{10... | collective-permute-start | bytes 331784 | tf_op jit(solution)/shard_map/ppermute | solution.py:250
  21.7 10.0 %collective-permute-start = (f32[512,128]{1,0:T(8,128)}, f32[512,128]{1,0:T(8,128)}, u32[]{:S(2)}, u32[]{:S(2)}) collective-permute-start(f32[512,128]{1,0:T(8,128)} %bitcast.2.guess), channel_id=1, source_target_pairs={{0,8},{8,16},{16,24},{24,32},{32,40},{40,48},{48,56},{56,64},{64,7... | collective-permute-start | bytes 786440 | tf_op jit(solution)/shard_map/ppermute | solution.py:247
  31.6 1.0 copy-start.19
  36.9 8.7 %collective-permute-start.1 = (f32[512,128]{1,0:T(8,128)S(1)}, f32[512,128]{1,0:T(8,128)S(1)}, u32[]{:S(2)}, u32[]{:S(2)}) collective-permute-start(f32[512,128]{1,0:T(8,128)S(1)} %first.1), channel_id=1, source_target_pairs={{0,8},{8,16},{16,24},{24,32},{32,40},{40,48},{48,56},{56,64},{64,7... | collective-permute-start | bytes 786440 | tf_op jit(solution)/shard_map/ppermute | solution.py:247
  50.3 12.0 %collective-permute-start.4 = (f32[512,128]{1,0:T(8,128)S(1)}, f32[512,128]{1,0:T(8,128)S(1)}, u32[]{:S(2)}, u32[]{:S(2)}) collective-permute-start(f32[512,128]{1,0:T(8,128)S(1)} %get-tuple-element.19.m0), channel_id=1, source_target_pairs={{0,8},{8,16},{16,24},{24,0},{1,9},{9,17},{17,25},{25,1},{2,10},{10... | collective-permute-start | bytes 786440 | tf_op jit(solution)/shard_map/ppermute | solution.py:250
  54.5 9.8 %collective-permute-start.3 = (f32[512,128]{1,0:T(8,128)S(1)}, f32[512,128]{1,0:T(8,128)S(1)}, u32[]{:S(2)}, u32[]{:S(2)}) collective-permute-start(f32[512,128]{1,0:T(8,128)S(1)} %get-tuple-element.19.m0), channel_id=1, source_target_pairs={{0,16},{8,24},{16,0},{24,8},{1,17},{9,25},{17,1},{25,9},{2,18},{10... | collective-permute-start | bytes 786440 | tf_op jit(solution)/shard_map/ppermute | solution.py:250
  54.5 13.3 %collective-permute-start.2 = (f32[512,128]{1,0:T(8,128)S(1)}, f32[512,128]{1,0:T(8,128)S(1)}, u32[]{:S(2)}, u32[]{:S(2)}) collective-permute-start(f32[512,128]{1,0:T(8,128)S(1)} %get-tuple-element.19.m0), channel_id=1, source_target_pairs={{0,24},{8,0},{16,8},{24,16},{1,25},{9,1},{17,9},{25,17},{2,26},{10... | collective-permute-start | bytes 786440 | tf_op jit(solution)/shard_map/ppermute | solution.py:250
  55.4 0.7 copy-start.23
  56.1 22.7 %collective-permute-start.11 = (f32[512,128]{1,0:T(8,128)}, f32[512,128]{1,0:T(8,128)}, u32[]{:S(2)}, u32[]{:S(2)}) collective-permute-start(f32[512,128]{1,0:T(8,128)} %get-tuple-element.20.own), channel_id=1, source_target_pairs={{0,24},{1,25},{2,26},{3,27},{4,28},{5,29},{6,30},{7,31},{32,56},{3... | collective-permute-start | bytes 786440 | tf_op jit(solution)/shard_map/ppermute | solution.py:266
  57.4 21.4 %collective-permute-start.10 = (f32[512,128]{1,0:T(8,128)}, f32[512,128]{1,0:T(8,128)}, u32[]{:S(2)}, u32[]{:S(2)}) collective-permute-start(f32[512,128]{1,0:T(8,128)} %get-tuple-element.20.own), channel_id=1, source_target_pairs={{0,16},{1,17},{2,18},{3,19},{4,20},{5,21},{6,22},{7,23},{32,48},{3... | collective-permute-start | bytes 786440 | tf_op jit(solution)/shard_map/ppermute | solution.py:266
  62.3 0.7 copy-start.7
  63.0 15.8 %collective-permute-start.9 = (f32[512,128]{1,0:T(8,128)}, f32[512,128]{1,0:T(8,128)}, u32[]{:S(2)}, u32[]{:S(2)}) collective-permute-start(f32[512,128]{1,0:T(8,128)} %get-tuple-element.20.own), channel_id=1, source_target_pairs={{0,8},{1,9},{2,10},{3,11},{4,12},{5,13},{6,14},{7,15},{32,40},{33,... | collective-permute-start | bytes 786440 | tf_op jit(solution)/shard_map/ppermute | solution.py:266
  64.3 0.7 copy-start.11
  67.8 0.7 copy-start.15
  68.5 2.0 %copy-start = (bf16[32,432,128]{2,1,0:T(8,128)(2,1)S(1)}, bf16[32,432,128]{2,1,0:T(8,128)(2,1)}, u32[]{:S(2)}) copy-start(bf16[32,432,128]{2,1,0:T(8,128)(2,1)} %all-gather.3.cloned.1.call-done) | copy-start | bytes 10616836
  70.5 0.9 copy-start.8
  71.5 0.9 copy-start.12
  72.4 0.9 copy-start.16
  73.4 0.9 copy-start.24
  74.3 11.4 %copy-start.1 = (bf16[32,432,128]{2,1,0:T(8,128)(2,1)S(1)}, bf16[32,432,128]{2,1,0:T(8,128)(2,1)}, u32[]{:S(2)}) copy-start(bf16[32,432,128]{2,1,0:T(8,128)(2,1)} %all-gather.3.cloned.1.call-done) | copy-start | bytes 10616836
  74.3 11.4 %copy-start.9 = (f32[512,128]{1,0:T(8,128)S(1)}, f32[512,128]{1,0:T(8,128)}, u32[]{:S(2)}) copy-start(f32[512,128]{1,0:T(8,128)} %copy-done.7) | copy-start | bytes 786436
  74.3 11.4 %copy-start.13 = (f32[512,128]{1,0:T(8,128)S(1)}, f32[512,128]{1,0:T(8,128)}, u32[]{:S(2)}) copy-start(f32[512,128]{1,0:T(8,128)} %copy-done.11) | copy-start | bytes 786436
  74.3 11.5 %copy-start.17 = (f32[512,128]{1,0:T(8,128)S(1)}, f32[512,128]{1,0:T(8,128)}, u32[]{:S(2)}) copy-start(f32[512,128]{1,0:T(8,128)} %copy-done.15) | copy-start | bytes 786436
  77.5 8.3 %collective-permute-start.8 = (f32[512,128]{1,0:T(8,128)S(1)}, f32[512,128]{1,0:T(8,128)S(1)}, u32[]{:S(2)}, u32[]{:S(2)}) collective-permute-start(f32[512,128]{1,0:T(8,128)S(1)} %third.1.point), channel_id=1, source_target_pairs={{0,32},{32,64},{64,96},{96,128},{128,160},{160,192},{192,224},{1,3... | collective-permute-start | bytes 786440 | tf_op jit(solution)/shard_map/ppermute | solution.py:265
  85.8 1.0 copy-start.20
  86.7 6.1 %copy-start.21 = (f32[512,128]{1,0:T(8,128)}, f32[512,128]{1,0:T(8,128)S(1)}, u32[]{:S(2)}) copy-start(f32[512,128]{1,0:T(8,128)S(1)} %collective-permute-done.8.hop) | copy-start | bytes 786436
  92.9 0.7 copy-start.2
  93.6 2.5 %collective-permute-start.12 = (f32[512,128]{1,0:T(8,128)}, f32[512,128]{1,0:T(8,128)}, u32[]{:S(2)}, u32[]{:S(2)}) collective-permute-start(f32[512,128]{1,0:T(8,128)} %get-tuple-element.21.value), channel_id=1, source_target_pairs={{32,64},{33,65},{34,66},{35,67},{36,68},{37,69},{38,70},{39,71},{4... | collective-permute-start | bytes 786440 | tf_op jit(solution)/shard_map/ppermute | solution.py:274
  94.9 3.9 %copy-start.4 = (f32[512,128]{1,0:T(8,128)S(1)}, f32[512,128]{1,0:T(8,128)}, u32[]{:S(2)}) copy-start(f32[512,128]{1,0:T(8,128)} %copy-done.2) | copy-start | bytes 786436
  96.0 1.0 copy-start.3
  98.1 0.7 collective-permute-start.13
  99.4 0.7 collective-permute-start.14
  100.9 0.7 collective-permute-start.15
  102.1 0.7 collective-permute-start.16
  102.8 40.6 %copy-start.6 = (bf16[4,3,3,3,128,128]{5,4,3,2,1,0:T(8,128)(2,1)S(1)}, bf16[4,3,3,3,128,128]{5,4,3,2,1,0:T(8,128)(2,1)}, u32[]{:S(2)}) copy-start(bf16[4,3,3,3,128,128]{5,4,3,2,1,0:T(8,128)(2,1)} %param.6) | copy-start | bytes 10616836
  102.9 40.6 %copy-start.10 = (f32[512,128]{1,0:T(8,128)S(1)}, f32[512,128]{1,0:T(8,128)}, u32[]{:S(2)}) copy-start(f32[512,128]{1,0:T(8,128)} %copy-done.7) | copy-start | bytes 786436
  102.9 40.6 %copy-start.14 = (f32[512,128]{1,0:T(8,128)S(1)}, f32[512,128]{1,0:T(8,128)}, u32[]{:S(2)}) copy-start(f32[512,128]{1,0:T(8,128)} %copy-done.11) | copy-start | bytes 786436
  102.9 40.6 %copy-start.18 = (f32[512,128]{1,0:T(8,128)S(1)}, f32[512,128]{1,0:T(8,128)}, u32[]{:S(2)}) copy-start(f32[512,128]{1,0:T(8,128)} %copy-done.15) | copy-start | bytes 786436
  103.5 38.6 %collective-permute-start.17 = (f32[512,128]{1,0:T(8,128)S(1)}, f32[512,128]{1,0:T(8,128)S(1)}, u32[]{:S(2)}, u32[]{:S(2)}) collective-permute-start(f32[512,128]{1,0:T(8,128)S(1)} %get-tuple-element.31.value), channel_id=1, source_target_pairs={{192,224},{193,225},{194,226},{195,227},{196,228},{197,229},{198,2... | collective-permute-start | bytes 786440 | tf_op jit(solution)/shard_map/ppermute | solution.py:274
Sparse Core Ops, SparseCore 0:
  20.1 32.3 all-gather.2

commit v2 on v1

v2 whole, which is shorter than its diff:
```python
import functools

import jax
import jax.numpy as jnp
from jax import lax
from jax.experimental import pallas as pl
from jax.experimental.pallas import tpu as pltpu
from jax.sharding import Mesh
from jax.sharding import PartitionSpec as P

X, Z = 4, 8
LAYER, BATCH = ("z", "x"), ("y", "core")
ROWS, CH = 512, 128
TAPS, DEEP = 9, 384
HALF = TAPS * DEEP // 2
WHOLE = (2, HALF, CH)
FINE = 2.0 / 128
COARSE = 4 * FINE
TOP = 4 * COARSE


def conv(v, weights):
    t = jnp.tanh(v).reshape(64, 8, CH)
    at = lax.broadcasted_iota(jnp.int32, (64, 8, CH), 1)
    before = jnp.where(at == 0, 0.0, pltpu.roll(t, 1, 1))
    after = jnp.where(at == 7, 0.0, pltpu.roll(t, 7, 1))
    lhs = jnp.concatenate(
        [s.reshape(ROWS, CH).astype(jnp.bfloat16) for s in (before, t, after)], 1
    )
    rhs = jnp.concatenate([weights[n * DEEP : (n + 1) * DEEP] for n in range(TAPS)], 1)
    out = jnp.dot(lhs, rhs, preferred_element_type=jnp.float32)
    edge_y = jnp.zeros((8, 1, 8, CH), jnp.float32)
    edge_x = jnp.zeros((1, 8, 8, CH), jnp.float32)
    total = None
    for dx in range(3):
        for dy in range(3):
            n = dx * 3 + dy
            part = out[:, n * CH : (n + 1) * CH].reshape(8, 8, 8, CH)
            if dy == 0:
                part = jnp.concatenate([edge_y, part[:, :7]], 1)
            if dy == 2:
                part = jnp.concatenate([part[:, 1:], edge_y], 1)
            if dx == 0:
                part = jnp.concatenate([edge_x, part[:7]], 0)
            if dx == 2:
                part = jnp.concatenate([part[1:], edge_x], 0)
            total = part if total is None else total + part
    return total.reshape(ROWS, CH)


def flat(weights):
    return weights.reshape(TAPS * DEEP, CH)


def relative(q):
    return lax.rem(q - lax.axis_index("x") + X, X)


def start_own(kernels, layer, slot, sem):
    for half in range(2):
        pltpu.make_async_copy(kernels.at[layer, half], slot.at[half], sem.at[half]).start()


def start_lead(q, slot, sem, mine, other):
    core = lax.axis_index("core")
    pltpu.make_async_copy(mine.at[q], slot.at[core], sem.at[core]).start()
    pltpu.make_async_copy(other.at[q], slot.at[1 - core], sem.at[1 - core]).start()


def arrived(slot, sem, source):
    for half in range(2):
        pltpu.make_async_copy(source.at[0], slot.at[half], sem.at[half]).wait()


def copied(source, target, sem):
    copy = pltpu.make_async_copy(source, target, sem)
    copy.start()
    copy.wait()


def add_relative(buf, q, terms):
    turn = relative(q)
    for r, term in enumerate(terms):

        @pl.when(turn == r)
        def _():
            buf[...] += term[...]


def last_device():
    return (lax.axis_index("x") == X - 1) & (lax.axis_index("z") == Z - 1)


def first_device():
    return (lax.axis_index("x") == 0) & (lax.axis_index("z") == 0)


def prepare_kernel(guess, inputs, kernels, corner, half, sem):
    two = pltpu.make_async_copy(kernels.at[0, lax.axis_index("core")], half, sem.at[1])
    two.start()

    @pl.when(last_device())
    def _():
        pltpu.make_async_copy(inputs, corner, sem.at[0]).start()

    @pl.when(jnp.logical_not(last_device()))
    def _():
        pltpu.make_async_copy(guess.at[3], corner, sem.at[0]).start()

    pltpu.make_async_copy(inputs, corner, sem.at[0]).wait()
    two.wait()


def first_kernel(head, kernels, biases, out):
    out[...] = head[...]

    def body(i, carry):
        v = out[...]
        out[...] = v + FINE * (conv(v, flat(kernels[pl.ds(i, 1)])) + biases[pl.ds(i, 1)])
        return carry

    lax.fori_loop(0, 4, body, 0)


def second_kernel(head, guess_head, kernels, biases, message, term, buf):
    @pl.when(first_device())
    def _():
        buf[...] = guess_head[...]

    @pl.when(jnp.logical_not(first_device()))
    def _():
        buf[...] = head[...]

    term[...] = buf[...]

    def body(i, carry):
        v = buf[...]
        mixed = conv(v, flat(kernels[pl.ds(i, 1)]))
        buf[...] = v + FINE * (mixed + biases[pl.ds(i, 1)])

        @pl.when(i == 0)
        def _():
            term[...] += COARSE * mixed

        return carry

    lax.fori_loop(0, 4, body, 0)
    term[...] = buf[...] - term[...]
    x = lax.axis_index("x")

    @pl.when(x == 0)
    def _():
        message[...] = buf[...]

    @pl.when(x != 0)
    def _():
        message[...] = term[...]


def third_kernel(m0, m1, m2, m3, mine, other, out, top, stack, wbuf, sem, ssem):
    x = lax.axis_index("x")
    for q in range(1, 4):
        start_lead(q, wbuf.at[q - 1], sem.at[q - 1], mine, other)
    start_lead(3, top, sem.at[3], mine, other)
    messages = (m0, m1, m2, m3)
    for r, message in enumerate(messages):
        q = lax.rem(x + r, X)

        @pl.when(q > 0)
        def _():
            pltpu.make_async_copy(message, stack.at[q - 1], ssem.at[q - 1]).start()

    out[...] = jnp.zeros((ROWS, CH), jnp.float32)
    add_relative(out, 0, messages)

    def body(q, carry):
        arrived(wbuf.at[q - 1], sem.at[q - 1], mine)
        out[...] += COARSE * conv(out[...], flat(wbuf[pl.ds(q - 1, 1)]))
        add_relative(out, q, messages)
        return carry

    lax.fori_loop(1, 4, body, 0)
    arrived(top, sem.at[3], mine)
    for q in range(3):
        pltpu.make_async_copy(m0, stack.at[q], ssem.at[q]).wait()


def start_terms(own, f1, f2, f3, stack, tbuf, sem):
    x = lax.axis_index("x")
    for r, term in enumerate((own, f1, f2, f3)):

        @pl.when(x == r)
        def _():
            pltpu.make_async_copy(term, tbuf.at[0], sem.at[0]).start()

    pltpu.make_async_copy(stack, tbuf.at[pl.ds(1, 3)], sem.at[1]).start()


def terms_arrived(own, stack, tbuf, sem):
    pltpu.make_async_copy(own, tbuf.at[0], sem.at[0]).wait()
    pltpu.make_async_copy(stack, tbuf.at[pl.ds(1, 3)], sem.at[1]).wait()


def fourth_kernel(
    hop, point, inputs, own, f1, f2, f3, stack, mine, other,
    residual, corner, start, wbuf, tbuf, sem, tsem, isem,
):
    for q in range(4):
        start_lead(q, wbuf.at[q], sem.at[q], mine, other)
    start_terms(own, f1, f2, f3, stack, tbuf, tsem)
    z = lax.axis_index("z")

    @pl.when(z == 0)
    def _():
        copied(inputs, start, isem)

    @pl.when(z != 0)
    def _():
        start[...] = hop[...]

    corner[...] = start[...]
    terms_arrived(own, stack, tbuf, tsem)

    def body(q, carry):
        arrived(wbuf.at[q], sem.at[q], mine)
        v = corner[...]
        mixed = conv(v, flat(wbuf[pl.ds(q, 1)]))
        corner[...] = v + COARSE * mixed + tbuf[pl.ds(q, 1)].reshape(ROWS, CH)
        return carry

    lax.fori_loop(0, 4, body, 0)
    x = lax.axis_index("x")

    @pl.when(x == 3)
    def _():
        residual[...] = corner[...] - point[...]

    @pl.when(x != 3)
    def _():
        residual[...] = jnp.zeros((ROWS, CH), jnp.float32)


def defect_kernel(corner, start, top, defect):
    v = start[...]
    defect[...] = corner[...] - v - TOP * conv(v, flat(top[...]))


def one_kernel(z, came, before, value, top, defect, out_before, out_value):
    @pl.when(lax.axis_index("z") == z)
    def _():
        v = came[...]
        out_before[...] = v
        out_value[...] = v + TOP * conv(v, flat(top[...])) + defect[...]


def two_kernel(
    z, came, before, value, top, defect, next_top, next_defect, out_before, out_value, ahead
):
    @pl.when(lax.axis_index("z") == z)
    def _():
        v = came[...]
        out_before[...] = v
        v = v + TOP * conv(v, flat(top[...])) + defect[...]
        out_value[...] = v
        ahead[...] = v + TOP * conv(v, flat(next_top[...])) + next_defect[...]


def last_kernel(
    w4, w7, before, value, defect, biases, own, f1, f2, f3, stack, mine, other, kernels,
    states, buf, sbuf, wbuf, tbuf, sem, tsem, ssem,
):
    x, z = lax.axis_index("x"), lax.axis_index("z")
    late = (z == 4) | (z == 6) | (z == 7)
    extra = (x == 3) & late
    for q in range(3):

        @pl.when(q < x)
        def _():
            start_lead(q, wbuf.at[q], sem.at[q], mine, other)

        start_own(kernels, q, wbuf.at[4 + q], sem.at[4 + q])

    @pl.when(extra)
    def _():
        start_lead(3, wbuf.at[3], sem.at[3], mine, other)

    start_terms(own, f1, f2, f3, stack, tbuf, tsem)

    @pl.when((z == 4) | (z == 6))
    def _():
        buf[...] = w4[...]

    @pl.when(z == 7)
    def _():
        buf[...] = w7[...]

    @pl.when(jnp.logical_not(late))
    def _():
        buf[...] = before[...]

    @pl.when((x == 3) & jnp.logical_not(late))
    def _():
        sbuf[3] = value[...]

    terms_arrived(own, stack, tbuf, tsem)

    def body(i, carry):
        slot = jnp.where(i < 0, 3, jnp.where(i < x, i, i - x + 4))
        arrived(wbuf.at[slot], sem.at[slot], mine)
        v = buf[...]
        mixed = conv(v, flat(wbuf[pl.ds(slot, 1)]))

        @pl.when(i < 0)
        def _():
            sbuf[3] = v + TOP * mixed + defect[...]

        @pl.when((i >= 0) & (i < x))
        def _():
            buf[...] = v + COARSE * mixed + tbuf[pl.ds(i, 1)].reshape(ROWS, CH)

        @pl.when((i == x) & (x < 3))
        def _():
            sbuf[3] = v + COARSE * mixed + tbuf[pl.ds(x, 1)].reshape(ROWS, CH)

        @pl.when(i >= x)
        def _():
            new = v + FINE * (mixed + biases[pl.ds(i - x, 1)])
            buf[...] = new
            sbuf[pl.ds(i - x, 1)] = new.reshape(1, ROWS, CH)
            pltpu.make_async_copy(sbuf.at[i - x], states.at[i - x], ssem.at[i - x]).start()

        @pl.when(i == x)
        def _():
            pltpu.make_async_copy(sbuf.at[3], states.at[3], ssem.at[3]).start()

        return carry

    lax.fori_loop(jnp.where(extra, -1, 0), x + 3, body, 0)
    for i in range(4):
        pltpu.make_async_copy(sbuf.at[i], states.at[i], ssem.at[i]).wait()


def call(body, name, outs, convs, args, places, scratch=(), alias=None, out_places=None, limit=16):
    specs = {
        "v": pl.BlockSpec(memory_space=pltpu.VMEM),
        "h": pl.BlockSpec(memory_space=pltpu.HBM),
    }
    out_places = out_places or "v" * len(outs)
    return pl.pallas_call(
        body,
        name=name,
        out_shape=outs,
        in_specs=[specs[p] for p in places],
        out_specs=tuple(specs[p] for p in out_places),
        scratch_shapes=scratch,
        input_output_aliases=alias or {},
        compiler_params=pltpu.CompilerParams(vmem_limit_bytes=limit << 20),
        cost_estimate=pl.CostEstimate(
            flops=convs * 2 * ROWS * CH * CH * 27,
            bytes_accessed=convs * 27 * CH * CH * 2,
            transcendentals=convs * ROWS * CH,
        ),
    )(*args)


def shards(inputs, guess_states, kernels, biases):
    state = jax.ShapeDtypeStruct((ROWS, CH), jnp.float32)
    weight = jax.ShapeDtypeStruct(WHOLE, jnp.bfloat16)
    buffer = pltpu.VMEM((ROWS, CH), jnp.float32)
    dma = pltpu.SemaphoreType.DMA
    inputs = inputs.reshape(ROWS, CH)
    guess = guess_states.reshape(4, ROWS, CH)
    kernels = kernels.reshape((4,) + WHOLE)
    barrier = lax.optimization_barrier

    def weights(slots):
        return [pltpu.VMEM((slots,) + WHOLE, jnp.bfloat16)], [dma((slots, 2))]

    def next_layer(v):
        return lax.ppermute(v, LAYER, [(i, (i + 1) % (X * Z)) for i in range(X * Z)])

    def from_ahead(v, r):
        return lax.ppermute(v, "x", [(i, (i - r) % X) for i in range(X)])

    def along_z(v, *pairs):
        return lax.ppermute(v, "z", pairs)

    guess_corner, half = call(
        prepare_kernel, "prepare",
        (state, jax.ShapeDtypeStruct((HALF, CH), jnp.bfloat16)), 0,
        (guess, inputs, kernels), "hhh", [dma((2,))], limit=63,
    )
    mine = lax.all_gather(half, "x")
    guess_head = next_layer(guess_corner)
    (point,) = call(
        first_kernel, "first", (state,), 4, (guess_head, kernels, biases), "vvv",
    )
    head = next_layer(point)
    message, term = call(
        second_kernel, "second", (state, state), 4, (head, guess_head, kernels, biases),
        "vvvv", [buffer],
    )
    m1, m2, m3 = (from_ahead(message, r) for r in (1, 2, 3))
    mine, _ = barrier((mine, message))
    other = lax.ppermute(mine, "core", [(0, 1), (1, 0)])
    group = (mine, other)
    wbuf, wsem = weights(4)
    wbuf3, _ = weights(3)
    point, top, stack = call(
        third_kernel, "third",
        (state, weight, jax.ShapeDtypeStruct((3, ROWS, CH), jnp.float32)), 3,
        (message, m1, m2, m3) + group, "vvvvhh", wbuf3 + wsem + [dma((3,))],
        out_places="vvh",
    )
    point, term = barrier((point, term))
    hop = along_z(point, *((i, i + 1) for i in range(Z - 1)))
    terms = (term, *(lax.ppermute(term, "x", [(0, i)]) for i in (1, 2, 3)), stack)
    tbuf = [pltpu.VMEM((4, ROWS, CH), jnp.float32)]
    residual, corner, start = call(
        fourth_kernel, "fourth", (state,) * 3, 4,
        (hop, point, inputs) + terms + group, "vvh" + "h" * 7,
        wbuf + tbuf + wsem + [dma((2,)), dma(())],
    )
    w2 = along_z(corner, (1, 2))
    next_top = along_z(barrier((top, corner))[0], (4, 3), (6, 5))
    (defect,) = call(defect_kernel, "defect", (state,), 1, (corner, start, top), "vvv")
    next_defect = along_z(defect, (4, 3), (6, 5))
    before, value = call(
        functools.partial(one_kernel, 2), "one", (state, state), 1,
        (w2, start, corner, top, defect), "vvvvv", alias={1: 0, 2: 1},
    )
    for z, distance in ((3, 1), (5, 2)):
        came = along_z(value if z == 3 else ahead, (z - distance, z))
        before, value, ahead = call(
            functools.partial(two_kernel, z), f"two{z}", (state,) * 3, 2,
            (came, before, value, top, defect, next_top, next_defect), "v" * 7,
            alias={1: 0, 2: 1},
        )
    w7 = along_z(ahead, (5, 7))
    w4 = along_z(value, (3, 4), (5, 6))
    wbuf7, wsem7 = weights(7)
    (states,) = call(
        last_kernel, "last", (jax.ShapeDtypeStruct((4, ROWS, CH), jnp.float32),), 6,
        (w4, w7, before, value, defect, biases) + terms + group + (kernels,),
        "v" * 6 + "h" * 8, [buffer] + tbuf + wbuf7 + tbuf + wsem7 + [dma((2,)), dma((4,))],
        out_places="h",
    )
    volume = (8, 8, 8, CH)
    return states.reshape((4, 1) + volume), residual.reshape((1, 1) + volume)


def solution(mesh):
    finer = Mesh(mesh.devices.reshape(Z, X, 4, 2), LAYER + BATCH)
    return jax.shard_map(
        shards,
        mesh=finer,
        in_specs=(P(BATCH), P(LAYER, BATCH), P(LAYER), P(LAYER)),
        out_specs=(P(LAYER, BATCH), P(LAYER, BATCH)),
        check_vma=False,
    )
```

time: 159 us -> 163 us (1.025)
  the two profiles are of different devices: /device:TPU:230 before, /device:TPU:194 now
where the time goes in v2:
time: 163 us
  waiting for transfers between devices  95.6 us (59%)
  Pallas kernels  27.4 us (17%)
  starting transfers between devices  21.9 us (13%)
  between operations  14.3 us (9%)
  local copies, waits for them, and re-layouts  3.49 us (2%)
    ppermute x8, waiting for transfers between devices, along_z(): return lax.ppermute(v, 'z', pairs)  47.7 us
    pallas_call x10, Pallas kernels, call(): pl.pallas_call(body, name=name, out_shape=outs, in_specs=[specs[p] for p...  27.4 us
    ppermute x2, waiting for transfers between devices, next_layer(): lax.ppermute(v, LAYER, [(i, (i + 1) % (X * Z)) for i in range(X * Z)])  19 us
    ppermute x3, waiting for transfers between devices, from_ahead(): return lax.ppermute(v, 'x', [(i, (i - r) % X) for i in range(X)])  11.8 us
    ppermute x8, starting transfers between devices, along_z(): return lax.ppermute(v, 'z', pairs)  11.3 us
    ppermute x3, waiting for transfers between devices, shards(): lax.ppermute(term, 'x', [(0, i)])  11.1 us
    all_gather x1, waiting for transfers between devices, shards(): mine = lax.all_gather(half, 'x')  5.98 us
    ppermute x3, starting transfers between devices, from_ahead(): return lax.ppermute(v, 'x', [(i, (i - r) % X) for i in range(X)])  4.7 us
  transfers between devices with their start and end apart: 18, of which 10 were waited for; matrix products, arithmetic and copies ran while one was open for 0% of the time, Pallas kernels for 5%

profile of v2, /device:TPU:194, one launch (start us, length us, event | category | flops | bytes accessed | tf_op | source)
XLA Modules:
  0.0 162.6 jit_solution(18260312672508320989)
XLA Ops:
  7.2 0.0 all-gather.3.cloned.1.call-start
  7.2 0.0 copy-start.5
  7.2 2.0 %prepare.1 = (f32[512,128]{1,0:T(8,128)}, bf16[1728,128]{1,0:T(8,128)(2,1)}) custom-call(f32[4,512,128]{2,1,0:T(8,128)} %bitcast.18, f32[512,128]{1,0:T(8,128)} %bitcast.16, bf16[4,2,1728,128]{3,2,1,0:T(8,128)(2,1)} %bitcast.8), custom_call_target="tpu_custom_call" | custom-call | tf_op jit(solution)/shard_map/prepare/pallas_call | solution.py:349
  9.2 0.0 all-gather.3.cloned.1.call-update
  9.2 1.6 collective-permute-start
  10.8 6.8 %collective-permute-done.head.guess_head = f32[512,128]{1,0:T(8,128)S(1)} collective-permute-done((f32[512,128]{1,0:T(8,128)}, f32[512,128]{1,0:T(8,128)S(1)}, u32[]{:S(2)}, u32[]{:S(2)}) %collective-permute-start) | collective-permute-done | bytes 262176 | tf_op jit(solution)/shard_map/ppermute | solution.py:380
  17.5 0.0 copy-done.5
  17.5 0.0 copy-start
  17.5 2.0 %copy-done = bf16[4,3,3,3,128,128]{5,4,3,2,1,0:T(8,128)(2,1)S(1)} copy-done((bf16[4,3,3,3,128,128]{5,4,3,2,1,0:T(8,128)(2,1)S(1)}, bf16[4,3,3,3,128,128]{5,4,3,2,1,0:T(8,128)(2,1)}, u32[]{:S(2)}) %copy-start) | copy-done | bytes 3538968
  19.5 3.2 %first.1 = f32[512,128]{1,0:T(8,128)S(1)} custom-call(f32[512,128]{1,0:T(8,128)S(1)} %collective-permute-done.head.guess_head, bf16[4,2,1728,128]{3,2,1,0:T(8,128)(2,1)S(1)} %bitcast.9, f32[4,128]{1,0:T(4,128)S(1)} %copy-done.5), custom_call_target="tpu_custom_call" | custom-call | flops 1811939328 | bytes 3538944 | tf_op jit(solution)/shard_map/first/pallas_call | solution.py:349
  22.8 1.6 collective-permute-start.1
  24.4 12.3 %collective-permute-done.1.head = f32[512,128]{1,0:T(8,128)S(1)} collective-permute-done((f32[512,128]{1,0:T(8,128)S(1)}, f32[512,128]{1,0:T(8,128)S(1)}, u32[]{:S(2)}, u32[]{:S(2)}) %collective-permute-start.1) | collective-permute-done | bytes 262176 | tf_op jit(solution)/shard_map/ppermute | solution.py:380
  36.6 0.0 copy-start.4
  36.6 3.3 %second.1 = (f32[512,128]{1,0:T(8,128)S(1)}, f32[512,128]{1,0:T(8,128)S(1)}) custom-call(f32[512,128]{1,0:T(8,128)S(1)} %collective-permute-done.1.head, f32[512,128]{1,0:T(8,128)S(1)} %collective-permute-done.head.guess_head, bf16[4,2,1728,128]{3,2,1,0:T(8,128)(2,1)S(1)} %bitcast.10, f32[4,128]{1,0:T(4,128)S(1)} %copy-done.5), custom_call_target="tpu_custom_call" | custom-call | flops 1811939328 | bytes 3538944 | tf_op jit(solution)/shard_map/second/pallas_call | solution.py:349
  40.0 6.0 %all-gather.3.cloned.1.call-done = bf16[6912,128]{1,0:T(8,128)(2,1)} async-done(((bf16[1728,128]{1,0:T(8,128)(2,1)}), bf16[6912,128]{1,0:T(8,128)(2,1)}) %all-gather.3.cloned.1.call-update) | async-done | bytes 1769488 | tf_op jit(solution)/shard_map/all_gather | solution.py:393
  46.0 0.0 collective-permute-start.5
  46.0 0.9 collective-permute-start.4
  46.9 3.2 %collective-permute-start.3 = (f32[512,128]{1,0:T(8,128)S(1)}, f32[512,128]{1,0:T(8,128)S(1)}, u32[]{:S(2)}, u32[]{:S(2)}) collective-permute-start(f32[512,128]{1,0:T(8,128)S(1)} %get-tuple-element.25.m0), channel_id=1, source_target_pairs={{0,16},{8,24},{16,0},{24,8},{1,17},{9,25},{17,1},{25,9},{2,18},{10... | collective-permute-start | bytes 786440 | tf_op jit(solution)/shard_map/ppermute | solution.py:383
  50.1 0.6 collective-permute-start.2
  50.7 4.5 %collective-permute-done.4.m3 = f32[512,128]{1,0:T(8,128)S(1)} collective-permute-done((f32[512,128]{1,0:T(8,128)S(1)}, f32[512,128]{1,0:T(8,128)S(1)}, u32[]{:S(2)}, u32[]{:S(2)}) %collective-permute-start.4) | collective-permute-done | bytes 262176 | tf_op jit(solution)/shard_map/ppermute | solution.py:383
  55.2 2.4 %collective-permute-done.3.m2 = f32[512,128]{1,0:T(8,128)S(1)} collective-permute-done((f32[512,128]{1,0:T(8,128)S(1)}, f32[512,128]{1,0:T(8,128)S(1)}, u32[]{:S(2)}, u32[]{:S(2)}) %collective-permute-start.3) | collective-permute-done | bytes 262176 | tf_op jit(solution)/shard_map/ppermute | solution.py:383
  57.6 4.9 %collective-permute-done.2.m1 = f32[512,128]{1,0:T(8,128)S(1)} collective-permute-done((f32[512,128]{1,0:T(8,128)S(1)}, f32[512,128]{1,0:T(8,128)S(1)}, u32[]{:S(2)}, u32[]{:S(2)}) %collective-permute-start.2) | collective-permute-done | bytes 262176 | tf_op jit(solution)/shard_map/ppermute | solution.py:383
  62.5 0.0 collective-permute-done.5.other
  62.5 0.0 copy-start.2
  62.5 1.5 copy-done.2
  64.0 0.0 copy-start.3
  64.0 4.9 %third.1 = (f32[512,128]{1,0:T(8,128)S(1)}, bf16[2,1728,128]{2,1,0:T(8,128)(2,1)S(1)}, f32[3,512,128]{2,1,0:T(8,128)S(1)}) custom-call(f32[512,128]{1,0:T(8,128)S(1)} %get-tuple-element.25.m0, f32[512,128]{1,0:T(8,128)S(1)} %collective-permute-done.2.m1, f32[512,128]{1,0:T(8,128)S(1)} %collective-permute-done.3.m2, ...), custom_call_target="tpu_custom_call" | custom-call | flops 1358954496 | bytes 2654208 | tf_op jit(solution)/shard_map/third/pallas_call | solution.py:349
  68.9 2.6 %collective-permute-start.6 = (f32[512,128]{1,0:T(8,128)S(1)}, f32[512,128]{1,0:T(8,128)S(1)}, u32[]{:S(2)}, u32[]{:S(2)}) collective-permute-start(f32[512,128]{1,0:T(8,128)S(1)} %get-tuple-element.30.point), channel_id=1, source_target_pairs={{0,32},{32,64},{64,96},{96,128},{128,160},{160,192},{192,224},{1,3... | collective-permute-start | bytes 786440 | tf_op jit(solution)/shard_map/ppermute | solution.py:386
  71.4 0.7 collective-permute-start.9
  72.1 0.7 collective-permute-start.8
  72.8 1.3 collective-permute-start.7
  74.1 4.9 %collective-permute-done.6.hop = f32[512,128]{1,0:T(8,128)S(1)} collective-permute-done((f32[512,128]{1,0:T(8,128)S(1)}, f32[512,128]{1,0:T(8,128)S(1)}, u32[]{:S(2)}, u32[]{:S(2)}) %collective-permute-start.6) | collective-permute-done | bytes 262176 | tf_op jit(solution)/shard_map/ppermute | solution.py:386
  79.0 0.0 collective-permute-done.9.f3
  79.0 0.0 collective-permute-done.8.f2
  79.0 11.1 %collective-permute-done.7.f1 = f32[512,128]{1,0:T(8,128)S(1)} collective-permute-done((f32[512,128]{1,0:T(8,128)S(1)}, f32[512,128]{1,0:T(8,128)S(1)}, u32[]{:S(2)}, u32[]{:S(2)}) %collective-permute-start.7) | collective-permute-done | bytes 262176 | tf_op jit(solution)/shard_map/ppermute | solution.py:417
  90.1 0.0 copy-done.4
  90.1 0.0 copy-done.3
  90.1 6.3 %fourth.1 = (f32[512,128]{1,0:T(8,128)}, f32[512,128]{1,0:T(8,128)S(1)}, f32[512,128]{1,0:T(8,128)S(1)}) custom-call(f32[512,128]{1,0:T(8,128)S(1)} %collective-permute-done.6.hop, f32[512,128]{1,0:T(8,128)S(1)} %get-tuple-element.30.point, f32[512,128]{1,0:T(8,128)S(1)} %bitcast.17, f32[512,128]{1,0:T(8,128)S(1)} %get-tuple-element.31.own, ...), custom_call_target="tpu_custom_call" | custom-call | flops 1811939328 | bytes 3538944 | tf_op jit(solution)/shard_map/fourth/pallas_call | solution.py:349
  96.4 3.3 %collective-permute-start.12 = (bf16[2,1728,128]{2,1,0:T(8,128)(2,1)S(1)}, bf16[2,1728,128]{2,1,0:T(8,128)(2,1)S(1)}, u32[]{:S(2)}, u32[]{:S(2)}) collective-permute-start(bf16[2,1728,128]{2,1,0:T(8,128)(2,1)S(1)} %get-tuple-element.38.top), channel_id=1, source_target_pairs={{128,96},{192,160},{129,97},{193,161},{130,98},{194,162},{131,99},... | collective-permute-start | bytes 2654216 | tf_op jit(solution)/shard_map/ppermute | solution.py:386
  99.7 0.7 collective-permute-start.10
  100.4 0.8 defect.1
  101.2 1.3 collective-permute-start.13
  102.6 0.0 collective-permute-done.10.came
  102.6 0.7 collective-permute-start.11
  103.3 19.7 %collective-permute-done.13.next_defect = f32[512,128]{1,0:T(8,128)S(1)} collective-permute-done((f32[512,128]{1,0:T(8,128)S(1)}, f32[512,128]{1,0:T(8,128)S(1)}, u32[]{:S(2)}, u32[]{:S(2)}) %collective-permute-start.13) | collective-permute-done | bytes 262176 | tf_op jit(solution)/shard_map/ppermute | solution.py:386
  122.9 0.0 collective-permute-done.11.came
  122.9 0.0 collective-permute-done.12.next_top
  122.9 0.0 copy-start.1
  122.9 0.2 two3.1
  123.1 0.8 collective-permute-start.14
  124.0 0.0 collective-permute-done.14.came
  124.0 0.7 collective-permute-start.16
  124.7 1.3 collective-permute-start.15
  126.0 0.0 collective-permute-done.16.w7
  126.0 23.2 %collective-permute-done.15.w4 = f32[512,128]{1,0:T(8,128)S(1)} collective-permute-done((f32[512,128]{1,0:T(8,128)S(1)}, f32[512,128]{1,0:T(8,128)S(1)}, u32[]{:S(2)}, u32[]{:S(2)}) %collective-permute-start.15) | collective-permute-done | bytes 262176 | tf_op jit(solution)/shard_map/ppermute | solution.py:386
  149.2 0.0 copy-done.1
  149.2 6.6 %last.1 = f32[4,512,128]{2,1,0:T(8,128)} custom-call(f32[512,128]{1,0:T(8,128)S(1)} %collective-permute-done.15.w4, f32[512,128]{1,0:T(8,128)S(1)} %collective-permute-done.16.w7, f32[512,128]{1,0:T(8,128)S(1)} %get-tuple-element.44.before, f32[512,128]{1,0:T(8,128)S(1)} %get-tuple-element.42.value, f32[512,128]{1,0:T(8,128)S(1)} %defect.1, ...), custom_call_target="tpu_custom_call" | custom-call | flops 2717908992 | bytes 5308416 | tf_op jit(solution)/shard_map/last/pallas_call | solution.py:349
  (2 shorter events, 0.0 us)
Async XLA Ops:
  7.2 38.8 %all-gather.3.cloned.1.call-start = ((), (), s32[]{:S(2)}) async-start(), calls=%async_computation | async-start | bytes 2211840 | tf_op jit(solution)/shard_map/all_gather | solution.py:393
  7.2 10.3 %copy-start.5 = (f32[4,128]{1,0:T(4,128)S(1)}, f32[4,128]{1,0:T(4,128)}, u32[]{:S(2)}) copy-start(f32[4,128]{1,0:T(4,128)} %biases.5) | copy-start | bytes 6148
  9.2 8.3 %collective-permute-start = (f32[512,128]{1,0:T(8,128)}, f32[512,128]{1,0:T(8,128)S(1)}, u32[]{:S(2)}, u32[]{:S(2)}) collective-permute-start(f32[512,128]{1,0:T(8,128)} %get-tuple-element.24), channel_id=1, source_target_pairs={{0,8},{8,16},{16,24},{24,32},{32,40},{40,48},{48,56},{56,64},{64,7... | collective-permute-start | bytes 786440 | tf_op jit(solution)/shard_map/ppermute | solution.py:380
  17.5 2.0 %copy-start = (bf16[4,3,3,3,128,128]{5,4,3,2,1,0:T(8,128)(2,1)S(1)}, bf16[4,3,3,3,128,128]{5,4,3,2,1,0:T(8,128)(2,1)}, u32[]{:S(2)}) copy-start(bf16[4,3,3,3,128,128]{5,4,3,2,1,0:T(8,128)(2,1)} %param.6) | copy-start | bytes 10616836
  22.8 13.8 %collective-permute-start.1 = (f32[512,128]{1,0:T(8,128)S(1)}, f32[512,128]{1,0:T(8,128)S(1)}, u32[]{:S(2)}, u32[]{:S(2)}) collective-permute-start(f32[512,128]{1,0:T(8,128)S(1)} %first.1), channel_id=1, source_target_pairs={{0,8},{8,16},{16,24},{24,32},{32,40},{40,48},{48,56},{56,64},{64,7... | collective-permute-start | bytes 786440 | tf_op jit(solution)/shard_map/ppermute | solution.py:380
  36.6 53.4 %copy-start.4 = (f32[1,8,8,8,128]{4,3,2,1,0:T(8,128)S(1)}, f32[1,8,8,8,128]{4,3,2,1,0:T(8,128)}, u32[]{:S(2)}) copy-start(f32[1,8,8,8,128]{4,3,2,1,0:T(8,128)} %param.4) | copy-start | bytes 786436
  46.0 16.5 %collective-permute-start.5 = (bf16[4,1728,128]{2,1,0:T(8,128)(2,1)}, bf16[4,1728,128]{2,1,0:T(8,128)(2,1)S(1)}, u32[]{:S(2)}, u32[]{:S(2)}) collective-permute-start(bf16[4,1728,128]{2,1,0:T(8,128)(2,1)} %bitcast.12), channel_id=1, source_target_pairs={{0,1},{1,0},{2,3},{3,2},{4,5},{5,4},{6,7},{7,6},{8,9},{9,8},{10,11... | collective-permute-start | bytes 5308424 | tf_op jit(solution)/shard_map/ppermute | solution.py:405
  46.0 9.2 %collective-permute-start.4 = (f32[512,128]{1,0:T(8,128)S(1)}, f32[512,128]{1,0:T(8,128)S(1)}, u32[]{:S(2)}, u32[]{:S(2)}) collective-permute-start(f32[512,128]{1,0:T(8,128)S(1)} %get-tuple-element.25.m0), channel_id=1, source_target_pairs={{0,8},{8,16},{16,24},{24,0},{1,9},{9,17},{17,25},{25,1},{2,10},{10... | collective-permute-start | bytes 786440 | tf_op jit(solution)/shard_map/ppermute | solution.py:383
  46.9 10.7 %collective-permute-start.3 = (f32[512,128]{1,0:T(8,128)S(1)}, f32[512,128]{1,0:T(8,128)S(1)}, u32[]{:S(2)}, u32[]{:S(2)}) collective-permute-start(f32[512,128]{1,0:T(8,128)S(1)} %get-tuple-element.25.m0), channel_id=1, source_target_pairs={{0,16},{8,24},{16,0},{24,8},{1,17},{9,25},{17,1},{25,9},{2,18},{10... | collective-permute-start | bytes 786440 | tf_op jit(solution)/shard_map/ppermute | solution.py:383
  50.1 12.4 %collective-permute-start.2 = (f32[512,128]{1,0:T(8,128)S(1)}, f32[512,128]{1,0:T(8,128)S(1)}, u32[]{:S(2)}, u32[]{:S(2)}) collective-permute-start(f32[512,128]{1,0:T(8,128)S(1)} %get-tuple-element.25.m0), channel_id=1, source_target_pairs={{0,24},{8,0},{16,8},{24,16},{1,25},{9,1},{17,9},{25,17},{2,26},{10... | collective-permute-start | bytes 786440 | tf_op jit(solution)/shard_map/ppermute | solution.py:383
  62.5 1.5 copy-start.2
  64.0 26.1 %copy-start.3 = (bf16[6912,128]{1,0:T(8,128)(2,1)S(1)}, bf16[6912,128]{1,0:T(8,128)(2,1)}, u32[]{:S(2)}) copy-start(bf16[6912,128]{1,0:T(8,128)(2,1)} %all-gather.3.cloned.1.call-done) | copy-start | bytes 5308420
  68.9 10.1 %collective-permute-start.6 = (f32[512,128]{1,0:T(8,128)S(1)}, f32[512,128]{1,0:T(8,128)S(1)}, u32[]{:S(2)}, u32[]{:S(2)}) collective-permute-start(f32[512,128]{1,0:T(8,128)S(1)} %get-tuple-element.30.point), channel_id=1, source_target_pairs={{0,32},{32,64},{64,96},{96,128},{128,160},{160,192},{192,224},{1,3... | collective-permute-start | bytes 786440 | tf_op jit(solution)/shard_map/ppermute | solution.py:386
  71.4 7.6 %collective-permute-start.9 = (f32[512,128]{1,0:T(8,128)S(1)}, f32[512,128]{1,0:T(8,128)S(1)}, u32[]{:S(2)}, u32[]{:S(2)}) collective-permute-start(f32[512,128]{1,0:T(8,128)S(1)} %get-tuple-element.31.own), channel_id=1, source_target_pairs={{0,24},{1,25},{2,26},{3,27},{4,28},{5,29},{6,30},{7,31},{32,56},{3... | collective-permute-start | bytes 786440 | tf_op jit(solution)/shard_map/ppermute | solution.py:417
  72.1 6.9 %collective-permute-start.8 = (f32[512,128]{1,0:T(8,128)S(1)}, f32[512,128]{1,0:T(8,128)S(1)}, u32[]{:S(2)}, u32[]{:S(2)}) collective-permute-start(f32[512,128]{1,0:T(8,128)S(1)} %get-tuple-element.31.own), channel_id=1, source_target_pairs={{0,16},{1,17},{2,18},{3,19},{4,20},{5,21},{6,22},{7,23},{32,48},{3... | collective-permute-start | bytes 786440 | tf_op jit(solution)/shard_map/ppermute | solution.py:417
  72.8 17.3 %collective-permute-start.7 = (f32[512,128]{1,0:T(8,128)S(1)}, f32[512,128]{1,0:T(8,128)S(1)}, u32[]{:S(2)}, u32[]{:S(2)}) collective-permute-start(f32[512,128]{1,0:T(8,128)S(1)} %get-tuple-element.31.own), channel_id=1, source_target_pairs={{0,8},{1,9},{2,10},{3,11},{4,12},{5,13},{6,14},{7,15},{32,40},{33,... | collective-permute-start | bytes 786440 | tf_op jit(solution)/shard_map/ppermute | solution.py:417
  96.4 26.5 %collective-permute-start.12 = (bf16[2,1728,128]{2,1,0:T(8,128)(2,1)S(1)}, bf16[2,1728,128]{2,1,0:T(8,128)(2,1)S(1)}, u32[]{:S(2)}, u32[]{:S(2)}) collective-permute-start(bf16[2,1728,128]{2,1,0:T(8,128)(2,1)S(1)} %get-tuple-element.38.top), channel_id=1, source_target_pairs={{128,96},{192,160},{129,97},{193,161},{130,98},{194,162},{131,99},... | collective-permute-start | bytes 2654216 | tf_op jit(solution)/shard_map/ppermute | solution.py:386
  99.7 2.8 %collective-permute-start.10 = (f32[512,128]{1,0:T(8,128)S(1)}, f32[512,128]{1,0:T(8,128)S(1)}, u32[]{:S(2)}, u32[]{:S(2)}) collective-permute-start(f32[512,128]{1,0:T(8,128)S(1)} %get-tuple-element.33.corner.value), channel_id=1, source_target_pairs={{32,64},{33,65},{34,66},{35,67},{36,68},{37,69},{38,70},{39,71},{4... | collective-permute-start | bytes 786440 | tf_op jit(solution)/shard_map/ppermute | solution.py:386
  101.2 21.7 %collective-permute-start.13 = (f32[512,128]{1,0:T(8,128)S(1)}, f32[512,128]{1,0:T(8,128)S(1)}, u32[]{:S(2)}, u32[]{:S(2)}) collective-permute-start(f32[512,128]{1,0:T(8,128)S(1)} %defect.1), channel_id=1, source_target_pairs={{128,96},{192,160},{129,97},{193,161},{130,98},{194,162},{131,99},... | collective-permute-start | bytes 786440 | tf_op jit(solution)/shard_map/ppermute | solution.py:386
  102.6 20.3 %collective-permute-start.11 = (f32[512,128]{1,0:T(8,128)S(1)}, f32[512,128]{1,0:T(8,128)S(1)}, u32[]{:S(2)}, u32[]{:S(2)}) collective-permute-start(f32[512,128]{1,0:T(8,128)S(1)} %get-tuple-element.36.value), channel_id=1, source_target_pairs={{64,96},{65,97},{66,98},{67,99},{68,100},{69,101},{70,102},{71,103... | collective-permute-start | bytes 786440 | tf_op jit(solution)/shard_map/ppermute | solution.py:386
  122.9 26.2 %copy-start.1 = (bf16[4,3,3,3,128,128]{5,4,3,2,1,0:T(8,128)(2,1)S(1)}, bf16[4,3,3,3,128,128]{5,4,3,2,1,0:T(8,128)(2,1)}, u32[]{:S(2)}) copy-start(bf16[4,3,3,3,128,128]{5,4,3,2,1,0:T(8,128)(2,1)} %param.6) | copy-start | bytes 10616836
  123.1 0.8 collective-permute-start.14
  124.0 2.0 %collective-permute-start.16 = (f32[512,128]{1,0:T(8,128)S(1)}, f32[512,128]{1,0:T(8,128)S(1)}, u32[]{:S(2)}, u32[]{:S(2)}) collective-permute-start(f32[512,128]{1,0:T(8,128)S(1)} %get-tuple-element.43), channel_id=1, source_target_pairs={{160,224},{161,225},{162,226},{163,227},{164,228},{165,229},{166,2... | collective-permute-start | bytes 786440 | tf_op jit(solution)/shard_map/ppermute | solution.py:386
  124.7 24.5 %collective-permute-start.15 = (f32[512,128]{1,0:T(8,128)S(1)}, f32[512,128]{1,0:T(8,128)S(1)}, u32[]{:S(2)}, u32[]{:S(2)}) collective-permute-start(f32[512,128]{1,0:T(8,128)S(1)} %get-tuple-element.42.value), channel_id=1, source_target_pairs={{96,128},{160,192},{97,129},{161,193},{98,130},{162,194},{99,131},... | collective-permute-start | bytes 786440 | tf_op jit(solution)/shard_map/ppermute | solution.py:386
Sparse Core Ops, SparseCore 0:
  10.4 35.5 all-gather.2

commit v3 on v2

v3 whole, which is shorter than its diff:
```python
import functools

import jax
import jax.numpy as jnp
from jax import lax
from jax.experimental import pallas as pl
from jax.experimental.pallas import tpu as pltpu
from jax.sharding import Mesh
from jax.sharding import PartitionSpec as P

X, Z = 4, 8
LAYER, BATCH = ("z", "x"), ("y", "core")
ROWS, CH = 512, 128
TAPS, DEEP = 9, 384
SHARE = TAPS * DEEP // 8
WHOLE = (8, SHARE, CH)
FINE = 2.0 / 128
COARSE = 4 * FINE
TOP = 4 * COARSE


def conv(v, weights):
    t = jnp.tanh(v).reshape(64, 8, CH)
    at = lax.broadcasted_iota(jnp.int32, (64, 8, CH), 1)
    before = jnp.where(at == 0, 0.0, pltpu.roll(t, 1, 1))
    after = jnp.where(at == 7, 0.0, pltpu.roll(t, 7, 1))
    lhs = jnp.concatenate(
        [s.reshape(ROWS, CH).astype(jnp.bfloat16) for s in (before, t, after)], 1
    )
    rhs = jnp.concatenate([weights[n * DEEP : (n + 1) * DEEP] for n in range(TAPS)], 1)
    out = jnp.dot(lhs, rhs, preferred_element_type=jnp.float32)
    edge_y = jnp.zeros((8, 1, 8, CH), jnp.float32)
    edge_x = jnp.zeros((1, 8, 8, CH), jnp.float32)
    total = None
    for dx in range(3):
        for dy in range(3):
            n = dx * 3 + dy
            part = out[:, n * CH : (n + 1) * CH].reshape(8, 8, 8, CH)
            if dy == 0:
                part = jnp.concatenate([edge_y, part[:, :7]], 1)
            if dy == 2:
                part = jnp.concatenate([part[:, 1:], edge_y], 1)
            if dx == 0:
                part = jnp.concatenate([edge_x, part[:7]], 0)
            if dx == 2:
                part = jnp.concatenate([part[1:], edge_x], 0)
            total = part if total is None else total + part
    return total.reshape(ROWS, CH)


def flat(weights):
    return weights.reshape(TAPS * DEEP, CH)


def last_device():
    return (lax.axis_index("x") == X - 1) & (lax.axis_index("z") == Z - 1)


def first_device():
    return (lax.axis_index("x") == 0) & (lax.axis_index("z") == 0)


def prepare_kernel(guess, inputs, kernels, corner, share, sem):
    two = pltpu.make_async_copy(
        kernels.at[0, lax.axis_index("y") * 2 + lax.axis_index("core")], share, sem.at[1]
    )
    two.start()

    @pl.when(last_device())
    def _():
        pltpu.make_async_copy(inputs, corner, sem.at[0]).start()

    @pl.when(jnp.logical_not(last_device()))
    def _():
        pltpu.make_async_copy(guess.at[3], corner, sem.at[0]).start()

    pltpu.make_async_copy(inputs, corner, sem.at[0]).wait()
    two.wait()


def first_kernel(head, biases, kernels, out, kept, lead, sem, lsem):
    for i in range(4):
        pltpu.make_async_copy(kernels.at[i], kept.at[i], sem.at[i]).start()
    pltpu.make_async_copy(kernels.at[0], lead, lsem).start()
    out[...] = head[...]

    def body(i, carry):
        pltpu.make_async_copy(kernels.at[i], kept.at[i], sem.at[i]).wait()
        v = out[...]
        out[...] = v + FINE * (conv(v, flat(kept[pl.ds(i, 1)])) + biases[pl.ds(i, 1)])
        return carry

    lax.fori_loop(0, 4, body, 0)
    pltpu.make_async_copy(kernels.at[0], lead, lsem).wait()


def second_kernel(head, guess_head, kernels, biases, term, buf):
    @pl.when(first_device())
    def _():
        buf[...] = guess_head[...]

    @pl.when(jnp.logical_not(first_device()))
    def _():
        buf[...] = head[...]

    term[...] = buf[...]

    def body(i, carry):
        v = buf[...]
        mixed = conv(v, flat(kernels[pl.ds(i, 1)]))
        buf[...] = v + FINE * (mixed + biases[pl.ds(i, 1)])

        @pl.when(i == 0)
        def _():
            term[...] += COARSE * mixed

        return carry

    lax.fori_loop(0, 4, body, 0)
    term[...] = buf[...] - term[...]


def coarse_steps(out, stack, lead, ready=lambda q: None):
    def body(q, carry):
        ready(q)
        v = out[...]
        mixed = conv(v, flat(lead[pl.ds(q, 1)]))
        out[...] = v + COARSE * mixed + stack[pl.ds(q, 1)].reshape(ROWS, CH)
        return carry

    lax.fori_loop(0, X, body, 0)


def third_kernel(
    inputs, head, b1, b2, b3, m0, m1, m2, m3, own, others, out, stack, lead, top, part, sem
):
    x, z = lax.axis_index("x"), lax.axis_index("z")

    def copy(q, wait):
        turn = lax.rem(q - x + X, X)

        @pl.when(turn == 0)
        def _():
            one = pltpu.make_async_copy(own, lead.at[q], sem.at[q])
            one.wait() if wait else one.start()

        @pl.when(turn != 0)
        def _():
            one = pltpu.make_async_copy(others.at[:, turn - 1], lead.at[q], sem.at[q])
            one.wait() if wait else one.start()

    for q in range(X):
        copy(q, False)
    for r, term in enumerate((m0, m1, m2, m3)):
        stack[pl.ds(lax.rem(x + r, X), 1)] = term[...].reshape(1, ROWS, CH)
    for r, start in enumerate((head, b1, b2, b3)):

        @pl.when((z > 0) & (x == r))
        def _():
            out[...] = start[...]

    @pl.when(z == 0)
    def _():
        out[...] = inputs[...]

    coarse_steps(out, stack, lead, lambda q: copy(q, True))
    top[...] = lead[X - 1]
    part[...] = lead[X - 1, pl.ds(lax.axis_index("core") * 4, 4)]


def fourth_kernel(inputs, hop, point, stack, lead, residual, corner, start):
    x, z = lax.axis_index("x"), lax.axis_index("z")

    @pl.when(z == 0)
    def _():
        start[...] = inputs[...]

    @pl.when(z > 0)
    def _():
        start[...] = hop[...]

    corner[...] = start[...]
    coarse_steps(corner, stack, lead)

    @pl.when(x == X - 1)
    def _():
        residual[...] = corner[...] - point[...]

    @pl.when(x != X - 1)
    def _():
        residual[...] = jnp.zeros((ROWS, CH), jnp.float32)


def defect_kernel(corner, start, top, defect):
    v = start[...]
    defect[...] = corner[...] - v - TOP * conv(v, flat(top[...]))


def one_kernel(z, came, before, value, top, defect, out_before, out_value):
    @pl.when(lax.axis_index("z") == z)
    def _():
        v = came[...]
        out_before[...] = v
        out_value[...] = v + TOP * conv(v, flat(top[...])) + defect[...]


def two_kernel(
    z, came, before, value, top, defect, mine, other, next_defect,
    out_before, out_value, ahead, wbuf,
):
    @pl.when(lax.axis_index("z") == z)
    def _():
        v = came[...]
        out_before[...] = v
        v = v + TOP * conv(v, flat(top[...])) + defect[...]
        out_value[...] = v
        core = lax.axis_index("core")
        wbuf[pl.ds(core * 4, 4)] = mine[...]
        wbuf[pl.ds(4 - core * 4, 4)] = other[...]
        ahead[...] = v + TOP * conv(v, flat(wbuf[...])) + next_defect[...]


def last_kernel(
    w4, w7, before, value, defect, biases, stack, lead, kernels, states, buf, sbuf, sem
):
    x, z = lax.axis_index("x"), lax.axis_index("z")
    late = (z == 4) | (z == 6) | (z == 7)
    extra = (x == X - 1) & late

    @pl.when((z == 4) | (z == 6))
    def _():
        buf[...] = w4[...]

    @pl.when(z == 7)
    def _():
        buf[...] = w7[...]

    @pl.when(jnp.logical_not(late))
    def _():
        buf[...] = before[...]

    @pl.when((x == X - 1) & jnp.logical_not(late))
    def _():
        sbuf[3] = value[...]

    @pl.when(extra)
    def _():
        v = buf[...]
        sbuf[3] = v + TOP * conv(v, flat(lead[3])) + defect[...]

    def coarse(q, carry):
        v = buf[...]
        mixed = conv(v, flat(lead[pl.ds(q, 1)]))
        buf[...] = v + COARSE * mixed + stack[pl.ds(q, 1)].reshape(ROWS, CH)
        return carry

    lax.fori_loop(0, x, coarse, 0)

    def fine(i, carry):
        v = buf[...]
        mixed = conv(v, flat(kernels[pl.ds(i, 1)]))

        @pl.when((i == 0) & (x < X - 1))
        def _():
            sbuf[3] = v + COARSE * mixed + stack[pl.ds(x, 1)].reshape(ROWS, CH)

        @pl.when(i == 0)
        def _():
            pltpu.make_async_copy(sbuf.at[3], states.at[3], sem.at[3]).start()

        new = v + FINE * (mixed + biases[pl.ds(i, 1)])
        buf[...] = new
        sbuf[pl.ds(i, 1)] = new.reshape(1, ROWS, CH)
        pltpu.make_async_copy(sbuf.at[i], states.at[i], sem.at[i]).start()
        return carry

    lax.fori_loop(0, 3, fine, 0)
    for i in range(4):
        pltpu.make_async_copy(sbuf.at[i], states.at[i], sem.at[i]).wait()


def call(body, name, outs, convs, args, places, scratch=(), alias=None, out_places=None, limit=16):
    specs = {
        "v": pl.BlockSpec(memory_space=pltpu.VMEM),
        "h": pl.BlockSpec(memory_space=pltpu.HBM),
    }
    out_places = out_places or "v" * len(outs)
    return pl.pallas_call(
        body,
        name=name,
        out_shape=outs,
        in_specs=[specs[p] for p in places],
        out_specs=tuple(specs[p] for p in out_places),
        scratch_shapes=scratch,
        input_output_aliases=alias or {},
        compiler_params=pltpu.CompilerParams(vmem_limit_bytes=limit << 20),
        cost_estimate=pl.CostEstimate(
            flops=convs,
            bytes_accessed=convs,
            transcendentals=0,
        ),
    )(*args)


def shards(inputs, guess_states, kernels, biases):
    state = jax.ShapeDtypeStruct((ROWS, CH), jnp.float32)
    weight = jax.ShapeDtypeStruct(WHOLE, jnp.bfloat16)
    buffer = pltpu.VMEM((ROWS, CH), jnp.float32)
    dma = pltpu.SemaphoreType.DMA
    inputs = inputs.reshape(ROWS, CH)
    guess = guess_states.reshape(4, ROWS, CH)
    kernels = kernels.reshape((4,) + WHOLE)
    barrier = lax.optimization_barrier

    def next_layer(v):
        return lax.ppermute(v, LAYER, [(i, (i + 1) % (X * Z)) for i in range(X * Z)])

    def from_ahead(v, r):
        return lax.ppermute(v, "x", [(i, (i - r) % X) for i in range(X)])

    def along_z(v, *pairs):
        return lax.ppermute(v, "z", pairs)

    guess_corner, share = call(
        prepare_kernel, "prepare",
        (state, jax.ShapeDtypeStruct((SHARE, CH), jnp.bfloat16)), 0,
        (guess, inputs, kernels), "hhh", [dma((2,))], limit=63,
    )
    guess_head = next_layer(guess_corner)
    shares = [from_ahead(share, r) for r in (1, 2, 3)]
    guess_head, *shares = barrier((guess_head, *shares))
    others = lax.all_gather(jnp.stack(shares), BATCH)
    point, kept, own = call(
        first_kernel, "first",
        (state, jax.ShapeDtypeStruct((4,) + WHOLE, jnp.bfloat16), weight), 4,
        (guess_head, biases, kernels), "vvh", [dma((4,)), dma(())],
        out_places="vvh", limit=16,
    )
    head = next_layer(point)
    starts = [
        lax.ppermute(point, LAYER, [(X * z - 1, X * z + r) for z in range(1, Z)])
        for r in (1, 2, 3)
    ]
    (term,) = call(
        second_kernel, "second", (state,), 4, (head, guess_head, kept, biases),
        "vvvv", [buffer],
    )
    terms = [from_ahead(term, r) for r in (1, 2, 3)]
    others, *come = barrier((others, *starts, *terms))
    point, stack, lead, top, part = call(
        third_kernel, "third",
        (state, jax.ShapeDtypeStruct((X, ROWS, CH), jnp.float32))
        + tuple(jax.ShapeDtypeStruct(d + (SHARE, CH), jnp.bfloat16) for d in ((X, 8), (8,), (4,))),
        4, (inputs, head, *come[:3], term, *come[3:], own, others), "v" * 9 + "hh",
        [dma((X,))],
    )
    hop = along_z(point, *((i, i + 1) for i in range(Z - 1)))
    residual, corner, start = call(
        fourth_kernel, "fourth", (state,) * 3, 4, (inputs, hop, point, stack, lead), "vvvvv",
    )
    w2 = along_z(corner, (1, 2))
    (defect,) = call(defect_kernel, "defect", (state,), 1, (corner, start, top), "vvv")
    next_defect = along_z(defect, (4, 3), (6, 5))
    next_mine = along_z(part, (4, 3), (6, 5))
    next_mine, _ = barrier((next_mine, defect))
    next_other = lax.ppermute(next_mine, "core", [(0, 1), (1, 0)])
    before, value = call(
        functools.partial(one_kernel, 2), "one", (state, state), 1,
        (w2, start, corner, top, defect), "vvvvv", alias={1: 0, 2: 1},
    )
    for z, distance in ((3, 1), (5, 2)):
        came = along_z(value if z == 3 else ahead, (z - distance, z))
        before, value, ahead = call(
            functools.partial(two_kernel, z), f"two{z}", (state,) * 3, 2,
            (came, before, value, top, defect, next_mine, next_other, next_defect), "v" * 8,
            [pltpu.VMEM(WHOLE, jnp.bfloat16)],
            alias={1: 0, 2: 1},
        )
    w7 = along_z(ahead, (5, 7))
    w4 = along_z(value, (3, 4), (5, 6))
    (states,) = call(
        last_kernel, "last", (jax.ShapeDtypeStruct((4, ROWS, CH), jnp.float32),), 6,
        (w4, w7, before, value, defect, biases, stack, lead, kernels), "v" * 9,
        [buffer, pltpu.VMEM((4, ROWS, CH), jnp.float32), dma((4,))], out_places="h",
    )
    volume = (8, 8, 8, CH)
    return states.reshape((4, 1) + volume), residual.reshape((1, 1) + volume)


def solution(mesh):
    finer = Mesh(mesh.devices.reshape(Z, X, 4, 2), LAYER + BATCH)
    return jax.shard_map(
        shards,
        mesh=finer,
        in_specs=(P(BATCH), P(LAYER, BATCH), P(LAYER), P(LAYER)),
        out_specs=(P(LAYER, BATCH), P(LAYER, BATCH)),
        check_vma=False,
    )
```

time: 163 us -> 138 us (0.85)
  the two profiles are of different devices: /device:TPU:194 before, /device:TPU:204 now
where the time goes in v3:
time: 138 us; the launch traced here: 137 us
  waiting for transfers between devices  67.5 us (49%)
  starting transfers between devices  27.8 us (20%)
  Pallas kernels  23.2 us (17%)
  between operations  14.3 us (10%)
  local copies, waits for them, and re-layouts  3.76 us (3%)
    ppermute x8, waiting for transfers between devices, along_z(): return lax.ppermute(v, 'z', pairs)  37.9 us
    pallas_call x10, Pallas kernels, call(): pl.pallas_call(body, name=name, out_shape=outs, in_specs=[specs[p] for p...  23.2 us
    ppermute x6, waiting for transfers between devices, from_ahead(): return lax.ppermute(v, 'x', [(i, (i - r) % X) for i in range(X)])  21.9 us
    ppermute x6, starting transfers between devices, from_ahead(): return lax.ppermute(v, 'x', [(i, (i - r) % X) for i in range(X)])  13 us
    ppermute x8, starting transfers between devices, along_z(): return lax.ppermute(v, 'z', pairs)  10.6 us
    ppermute x2, waiting for transfers between devices, next_layer(): lax.ppermute(v, LAYER, [(i, (i + 1) % (X * Z)) for i in range(X * Z)])  4.46 us
    unnamed x10, local copies, waits for them, and re-layouts  3.76 us
    ppermute x3, waiting for transfers between devices, shards(): lax.ppermute(point, LAYER, [(X * z - 1, X * z + r) for z in range(1, Z)])  3.24 us
  transfers between devices with their start and end apart: 21, of which 9 were waited for; matrix products, arithmetic and copies ran while one was open for 0% of the time, Pallas kernels for 9%

profile of v3, /device:TPU:204, one launch (start us, length us, event | category | flops | bytes accessed | tf_op | source)
XLA Modules:
  0.0 137.4 jit_solution(12760042692087011159)
XLA Ops:
  7.2 0.0 copy-start.4
  7.2 0.0 all-gather.3.cloned.1.call-start
  7.2 1.8 %prepare.1 = (f32[512,128]{1,0:T(8,128)}, bf16[432,128]{1,0:T(8,128)(2,1)}) custom-call(f32[4,512,128]{2,1,0:T(8,128)} %bitcast.18, f32[512,128]{1,0:T(8,128)} %bitcast.15, bf16[4,8,432,128]{3,2,1,0:T(8,128)(2,1)} %bitcast.11), custom_call_target="tpu_custom_call" | custom-call | tf_op jit(solution)/shard_map/prepare/pallas_call | solution.py:288
  9.0 1.3 collective-permute-start
  10.3 0.9 collective-permute-start.3
  11.2 1.4 collective-permute-start.2
  12.6 1.1 collective-permute-start.1
  13.7 7.2 %collective-permute-done.3 = bf16[432,128]{1,0:T(8,128)(2,1)S(1)} collective-permute-done((bf16[432,128]{1,0:T(8,128)(2,1)}, bf16[432,128]{1,0:T(8,128)(2,1)S(1)}, u32[]{:S(2)}, u32[]{:S(2)}) %collective-permute-start.3) | collective-permute-done | bytes 110624 | tf_op jit(solution)/shard_map/ppermute | solution.py:319
  20.9 1.2 collective-permute-done.2
  22.1 0.0 collective-permute-done.1
  22.1 0.0 collective-permute-done.head.guess_head
  22.1 0.8 pad_maximum_fusion
  22.8 0.0 all-gather.3.cloned.1.call-update
  22.9 0.0 copy-done.4
  22.9 0.0 copy-start
  22.9 2.0 %copy-done = bf16[4,3,3,3,128,128]{5,4,3,2,1,0:T(8,128)(2,1)S(1)} copy-done((bf16[4,3,3,3,128,128]{5,4,3,2,1,0:T(8,128)(2,1)S(1)}, bf16[4,3,3,3,128,128]{5,4,3,2,1,0:T(8,128)(2,1)}, u32[]{:S(2)}) %copy-start) | copy-done | bytes 3538968
  24.9 0.0 copy-start.3
  24.9 4.2 %first.1 = (f32[512,128]{1,0:T(8,128)S(1)}, bf16[4,8,432,128]{3,2,1,0:T(8,128)(2,1)S(1)}, bf16[8,432,128]{2,1,0:T(8,128)(2,1)S(1)}) custom-call(f32[512,128]{1,0:T(8,128)S(1)} %collective-permute-done.head.guess_head, f32[4,128]{1,0:T(4,128)S(1)} %copy-done.4, bf16[4,8,432,128]{3,2,1,0:T(8,128)(2,1)S(1)} %bitcast.12), custom_call_target="tpu_custom_call" | custom-call | flops 4 | bytes 4 | tf_op jit(solution)/shard_map/first/pallas_call | solution.py:288
  29.1 0.1 collective-permute-start.4
  29.2 0.7 collective-permute-start.7
  29.9 1.3 collective-permute-start.6
  31.2 0.7 collective-permute-start.5
  31.9 4.5 %collective-permute-done.4.head = f32[512,128]{1,0:T(8,128)S(1)} collective-permute-done((f32[512,128]{1,0:T(8,128)S(1)}, f32[512,128]{1,0:T(8,128)S(1)}, u32[]{:S(2)}, u32[]{:S(2)}) %collective-permute-start.4) | collective-permute-done | bytes 262176 | tf_op jit(solution)/shard_map/ppermute | solution.py:316
  36.4 3.3 %second.1.m0 = f32[512,128]{1,0:T(8,128)S(1)} custom-call(f32[512,128]{1,0:T(8,128)S(1)} %collective-permute-done.4.head, f32[512,128]{1,0:T(8,128)S(1)} %collective-permute-done.head.guess_head, bf16[4,8,432,128]{3,2,1,0:T(8,128)(2,1)S(1)} %get-tuple-element.42.kernels, f32[4,128]{1,0:T(4,128)S(1)} %copy-done.4), custom_call_target="tpu_custom_call" | custom-call | flops 4 | bytes 4 | tf_op jit(solution)/shard_map/second/pallas_call | solution.py:288
  39.7 4.0 %collective-permute-start.10 = (f32[512,128]{1,0:T(8,128)S(1)}, f32[512,128]{1,0:T(8,128)S(1)}, u32[]{:S(2)}, u32[]{:S(2)}) collective-permute-start(f32[512,128]{1,0:T(8,128)S(1)} %second.1.m0), channel_id=1, source_target_pairs={{0,8},{8,16},{16,24},{24,0},{1,9},{9,17},{17,25},{25,1},{2,10},{10... | collective-permute-start | bytes 786440 | tf_op jit(solution)/shard_map/ppermute | solution.py:319
  43.7 3.1 %collective-permute-start.9 = (f32[512,128]{1,0:T(8,128)S(1)}, f32[512,128]{1,0:T(8,128)S(1)}, u32[]{:S(2)}, u32[]{:S(2)}) collective-permute-start(f32[512,128]{1,0:T(8,128)S(1)} %second.1.m0), channel_id=1, source_target_pairs={{0,16},{8,24},{16,0},{24,8},{1,17},{9,25},{17,1},{25,9},{2,18},{10... | collective-permute-start | bytes 786440 | tf_op jit(solution)/shard_map/ppermute | solution.py:319
  46.8 0.0 collective-permute-done.7.b3
  46.8 2.5 %collective-permute-start.8 = (f32[512,128]{1,0:T(8,128)S(1)}, f32[512,128]{1,0:T(8,128)S(1)}, u32[]{:S(2)}, u32[]{:S(2)}) collective-permute-start(f32[512,128]{1,0:T(8,128)S(1)} %second.1.m0), channel_id=1, source_target_pairs={{0,24},{8,0},{16,8},{24,16},{1,25},{9,1},{17,9},{25,17},{2,26},{10... | collective-permute-start | bytes 786440 | tf_op jit(solution)/shard_map/ppermute | solution.py:319
  49.3 3.2 %collective-permute-done.6.b2 = f32[512,128]{1,0:T(8,128)S(1)} collective-permute-done((f32[512,128]{1,0:T(8,128)S(1)}, f32[512,128]{1,0:T(8,128)S(1)}, u32[]{:S(2)}, u32[]{:S(2)}) %collective-permute-start.6) | collective-permute-done | bytes 262176 | tf_op jit(solution)/shard_map/ppermute | solution.py:341
  52.5 0.0 collective-permute-done.5.b1
  52.5 0.0 collective-permute-done.10.m3
  52.5 2.2 %collective-permute-done.9.m2 = f32[512,128]{1,0:T(8,128)S(1)} collective-permute-done((f32[512,128]{1,0:T(8,128)S(1)}, f32[512,128]{1,0:T(8,128)S(1)}, u32[]{:S(2)}, u32[]{:S(2)}) %collective-permute-start.9) | collective-permute-done | bytes 262176 | tf_op jit(solution)/shard_map/ppermute | solution.py:319
  54.7 11.3 %collective-permute-done.8.m1 = f32[512,128]{1,0:T(8,128)S(1)} collective-permute-done((f32[512,128]{1,0:T(8,128)S(1)}, f32[512,128]{1,0:T(8,128)S(1)}, u32[]{:S(2)}, u32[]{:S(2)}) %collective-permute-start.8) | collective-permute-done | bytes 262176 | tf_op jit(solution)/shard_map/ppermute | solution.py:319
  66.0 0.0 all-gather.3.cloned.1.call-done
  66.0 0.0 copy-done.3
  66.1 0.0 copy-start.2
  66.1 1.7 %copy-done.2 = bf16[24,432,128]{2,1,0:T(8,128)(2,1)S(1)} copy-done((bf16[24,432,128]{2,1,0:T(8,128)(2,1)S(1)}, bf16[24,432,128]{2,1,0:T(8,128)(2,1)}, u32[]{:S(2)}) %copy-start.2) | copy-done | bytes 2654232
  67.8 3.9 %third.1 = (f32[512,128]{1,0:T(8,128)S(1)}, f32[4,512,128]{2,1,0:T(8,128)S(1)}, bf16[4,8,432,128]{3,2,1,0:T(8,128)(2,1)S(1)}, bf16[8,432,128]{2,1,0:T(8,128)(2,1)S(1)}, bf16[4,432,128]{2,1,0:T(8,128)(2,1)S(1)}) custom-call(f32[512,128]{1,0:T(8,128)S(1)} %bitcast.16, f32[512,128]{1,0:T(8,128)S(1)} %collective-permute-done.4.head, ...), custom_call_target="tpu_custom_call" | custom-call | flops 4 | bytes 4 | tf_op jit(solution)/shard_map/third/pallas_call | solution.py:288
  71.7 2.9 %collective-permute-start.14 = (bf16[4,432,128]{2,1,0:T(8,128)(2,1)S(1)}, bf16[4,432,128]{2,1,0:T(8,128)(2,1)S(1)}, u32[]{:S(2)}, u32[]{:S(2)}) collective-permute-start(bf16[4,432,128]{2,1,0:T(8,128)(2,1)S(1)} %get-tuple-element.59), channel_id=1, source_target_pairs={{128,96},{192,160},{129,97},{193,161},{130,98},{194,162},{131,99},... | collective-permute-start | bytes 1327112 | tf_op jit(solution)/shard_map/ppermute | solution.py:322
  74.7 1.9 %collective-permute-start.11 = (f32[512,128]{1,0:T(8,128)S(1)}, f32[512,128]{1,0:T(8,128)S(1)}, u32[]{:S(2)}, u32[]{:S(2)}) collective-permute-start(f32[512,128]{1,0:T(8,128)S(1)} %get-tuple-element.51.point), channel_id=1, source_target_pairs={{0,32},{32,64},{64,96},{96,128},{128,160},{160,192},{192,224},{1,3... | collective-permute-start | bytes 786440 | tf_op jit(solution)/shard_map/ppermute | solution.py:322
  76.6 6.6 %collective-permute-done.11.hop = f32[512,128]{1,0:T(8,128)S(1)} collective-permute-done((f32[512,128]{1,0:T(8,128)S(1)}, f32[512,128]{1,0:T(8,128)S(1)}, u32[]{:S(2)}, u32[]{:S(2)}) %collective-permute-start.11) | collective-permute-done | bytes 262176 | tf_op jit(solution)/shard_map/ppermute | solution.py:322
  83.2 4.0 %fourth.1 = (f32[512,128]{1,0:T(8,128)}, f32[512,128]{1,0:T(8,128)S(1)}, f32[512,128]{1,0:T(8,128)S(1)}) custom-call(f32[512,128]{1,0:T(8,128)S(1)} %bitcast.17, f32[512,128]{1,0:T(8,128)S(1)} %collective-permute-done.11.hop, f32[512,128]{1,0:T(8,128)S(1)} %get-tuple-element.51.point, f32[4,512,128]{2,1,0:T(8,128)S(1)} %get-tuple-element.52.stack, ...), custom_call_target="tpu_custom_call" | custom-call | flops 4 | bytes 4 | tf_op jit(solution)/shard_map/fourth/pallas_call | solution.py:288
  87.2 0.7 collective-permute-start.12
  87.9 0.8 defect.1
  88.7 0.0 collective-permute-done.14.mine
  88.7 0.1 collective-permute-start.15
  88.8 1.7 %collective-permute-start.16 = (f32[512,128]{1,0:T(8,128)S(1)}, f32[512,128]{1,0:T(8,128)S(1)}, u32[]{:S(2)}, u32[]{:S(2)}) collective-permute-start(f32[512,128]{1,0:T(8,128)S(1)} %defect.1), channel_id=1, source_target_pairs={{128,96},{192,160},{129,97},{193,161},{130,98},{194,162},{131,99},... | collective-permute-start | bytes 786440 | tf_op jit(solution)/shard_map/ppermute | solution.py:322
  90.5 0.0 collective-permute-done.12.came
  90.5 0.2 one.1
  90.7 0.0 copy-start.1
  90.8 0.8 collective-permute-start.13
  91.6 5.1 %collective-permute-done.16.next_defect = f32[512,128]{1,0:T(8,128)S(1)} collective-permute-done((f32[512,128]{1,0:T(8,128)S(1)}, f32[512,128]{1,0:T(8,128)S(1)}, u32[]{:S(2)}, u32[]{:S(2)}) %collective-permute-start.16) | collective-permute-done | bytes 262176 | tf_op jit(solution)/shard_map/ppermute | solution.py:322
  96.7 0.0 collective-permute-done.13.came
  96.7 0.0 collective-permute-done.15.other
  96.7 0.7 collective-permute-start.17
  97.4 0.0 collective-permute-done.17.came
  97.4 0.7 collective-permute-start.19
  98.1 1.3 collective-permute-start.18
  99.4 0.0 collective-permute-done.19.w7
  99.4 26.1 %collective-permute-done.18.w4 = f32[512,128]{1,0:T(8,128)S(1)} collective-permute-done((f32[512,128]{1,0:T(8,128)S(1)}, f32[512,128]{1,0:T(8,128)S(1)}, u32[]{:S(2)}, u32[]{:S(2)}) %collective-permute-start.18) | collective-permute-done | bytes 262176 | tf_op jit(solution)/shard_map/ppermute | solution.py:322
  125.5 0.0 copy-done.1
  125.5 5.0 %last.1 = f32[4,512,128]{2,1,0:T(8,128)} custom-call(f32[512,128]{1,0:T(8,128)S(1)} %collective-permute-done.18.w4, f32[512,128]{1,0:T(8,128)S(1)} %collective-permute-done.19.w7, f32[512,128]{1,0:T(8,128)S(1)} %get-tuple-element.66.before, f32[512,128]{1,0:T(8,128)S(1)} %get-tuple-element.64.value, f32[512,128]{1,0:T(8,128)S(1)} %defect.1, ...), custom_call_target="tpu_custom_call" | custom-call | flops 6 | bytes 6 | tf_op jit(solution)/shard_map/last/pallas_call | solution.py:288
  (2 shorter events, 0.0 us)
Async XLA Ops:
  7.2 15.7 %copy-start.4 = (f32[4,128]{1,0:T(4,128)S(1)}, f32[4,128]{1,0:T(4,128)}, u32[]{:S(2)}) copy-start(f32[4,128]{1,0:T(4,128)} %biases.5) | copy-start | bytes 6148
  7.2 58.9 %all-gather.3.cloned.1.call-start = ((), (), s32[]{:S(2)}) async-start(), calls=%async_computation | async-start | bytes 2985984 | tf_op jit(solution)/shard_map/all_gather | solution.py:332
  9.0 13.1 %collective-permute-start = (f32[512,128]{1,0:T(8,128)}, f32[512,128]{1,0:T(8,128)S(1)}, u32[]{:S(2)}, u32[]{:S(2)}) collective-permute-start(f32[512,128]{1,0:T(8,128)} %get-tuple-element.35), channel_id=1, source_target_pairs={{0,8},{8,16},{16,24},{24,32},{32,40},{40,48},{48,56},{56,64},{64,7... | collective-permute-start | bytes 786440 | tf_op jit(solution)/shard_map/ppermute | solution.py:316
  10.3 10.6 %collective-permute-start.3 = (bf16[432,128]{1,0:T(8,128)(2,1)}, bf16[432,128]{1,0:T(8,128)(2,1)S(1)}, u32[]{:S(2)}, u32[]{:S(2)}) collective-permute-start(bf16[432,128]{1,0:T(8,128)(2,1)} %get-tuple-element.36), channel_id=1, source_target_pairs={{0,8},{8,16},{16,24},{24,0},{1,9},{9,17},{17,25},{25,1},{2,10},{10... | collective-permute-start | bytes 331784 | tf_op jit(solution)/shard_map/ppermute | solution.py:319
  11.2 10.9 %collective-permute-start.2 = (bf16[432,128]{1,0:T(8,128)(2,1)}, bf16[432,128]{1,0:T(8,128)(2,1)S(1)}, u32[]{:S(2)}, u32[]{:S(2)}) collective-permute-start(bf16[432,128]{1,0:T(8,128)(2,1)} %get-tuple-element.36), channel_id=1, source_target_pairs={{0,16},{8,24},{16,0},{24,8},{1,17},{9,25},{17,1},{25,9},{2,18},{10... | collective-permute-start | bytes 331784 | tf_op jit(solution)/shard_map/ppermute | solution.py:319
  12.6 9.5 %collective-permute-start.1 = (bf16[432,128]{1,0:T(8,128)(2,1)}, bf16[432,128]{1,0:T(8,128)(2,1)S(1)}, u32[]{:S(2)}, u32[]{:S(2)}) collective-permute-start(bf16[432,128]{1,0:T(8,128)(2,1)} %get-tuple-element.36), channel_id=1, source_target_pairs={{0,24},{8,0},{16,8},{24,16},{1,25},{9,1},{17,9},{25,17},{2,26},{10... | collective-permute-start | bytes 331784 | tf_op jit(solution)/shard_map/ppermute | solution.py:319
  22.9 2.0 %copy-start = (bf16[4,3,3,3,128,128]{5,4,3,2,1,0:T(8,128)(2,1)S(1)}, bf16[4,3,3,3,128,128]{5,4,3,2,1,0:T(8,128)(2,1)}, u32[]{:S(2)}) copy-start(bf16[4,3,3,3,128,128]{5,4,3,2,1,0:T(8,128)(2,1)} %param.6) | copy-start | bytes 10616836
  24.9 41.2 %copy-start.3 = (f32[1,8,8,8,128]{4,3,2,1,0:T(8,128)S(1)}, f32[1,8,8,8,128]{4,3,2,1,0:T(8,128)}, u32[]{:S(2)}) copy-start(f32[1,8,8,8,128]{4,3,2,1,0:T(8,128)} %param.4) | copy-start | bytes 786436
  29.1 7.2 %collective-permute-start.4 = (f32[512,128]{1,0:T(8,128)S(1)}, f32[512,128]{1,0:T(8,128)S(1)}, u32[]{:S(2)}, u32[]{:S(2)}) collective-permute-start(f32[512,128]{1,0:T(8,128)S(1)} %get-tuple-element.38), channel_id=1, source_target_pairs={{0,8},{8,16},{16,24},{24,32},{32,40},{40,48},{48,56},{56,64},{64,7... | collective-permute-start | bytes 786440 | tf_op jit(solution)/shard_map/ppermute | solution.py:316
  29.2 17.5 %collective-permute-start.7 = (f32[512,128]{1,0:T(8,128)S(1)}, f32[512,128]{1,0:T(8,128)S(1)}, u32[]{:S(2)}, u32[]{:S(2)}) collective-permute-start(f32[512,128]{1,0:T(8,128)S(1)} %get-tuple-element.38), channel_id=1, source_target_pairs={{24,56},{56,88},{88,120},{120,152},{152,184},{184,216},{216,248},{... | collective-permute-start | bytes 786440 | tf_op jit(solution)/shard_map/ppermute | solution.py:341
  29.9 22.6 %collective-permute-start.6 = (f32[512,128]{1,0:T(8,128)S(1)}, f32[512,128]{1,0:T(8,128)S(1)}, u32[]{:S(2)}, u32[]{:S(2)}) collective-permute-start(f32[512,128]{1,0:T(8,128)S(1)} %get-tuple-element.38), channel_id=1, source_target_pairs={{24,48},{56,80},{88,112},{120,144},{152,176},{184,208},{216,240},{... | collective-permute-start | bytes 786440 | tf_op jit(solution)/shard_map/ppermute | solution.py:341
  31.2 21.3 %collective-permute-start.5 = (f32[512,128]{1,0:T(8,128)S(1)}, f32[512,128]{1,0:T(8,128)S(1)}, u32[]{:S(2)}, u32[]{:S(2)}) collective-permute-start(f32[512,128]{1,0:T(8,128)S(1)} %get-tuple-element.38), channel_id=1, source_target_pairs={{24,40},{56,72},{88,104},{120,136},{152,168},{184,200},{216,232},{... | collective-permute-start | bytes 786440 | tf_op jit(solution)/shard_map/ppermute | solution.py:341
  39.7 12.9 %collective-permute-start.10 = (f32[512,128]{1,0:T(8,128)S(1)}, f32[512,128]{1,0:T(8,128)S(1)}, u32[]{:S(2)}, u32[]{:S(2)}) collective-permute-start(f32[512,128]{1,0:T(8,128)S(1)} %second.1.m0), channel_id=1, source_target_pairs={{0,8},{8,16},{16,24},{24,0},{1,9},{9,17},{17,25},{25,1},{2,10},{10... | collective-permute-start | bytes 786440 | tf_op jit(solution)/shard_map/ppermute | solution.py:319
  43.7 11.0 %collective-permute-start.9 = (f32[512,128]{1,0:T(8,128)S(1)}, f32[512,128]{1,0:T(8,128)S(1)}, u32[]{:S(2)}, u32[]{:S(2)}) collective-permute-start(f32[512,128]{1,0:T(8,128)S(1)} %second.1.m0), channel_id=1, source_target_pairs={{0,16},{8,24},{16,0},{24,8},{1,17},{9,25},{17,1},{25,9},{2,18},{10... | collective-permute-start | bytes 786440 | tf_op jit(solution)/shard_map/ppermute | solution.py:319
  46.8 19.3 %collective-permute-start.8 = (f32[512,128]{1,0:T(8,128)S(1)}, f32[512,128]{1,0:T(8,128)S(1)}, u32[]{:S(2)}, u32[]{:S(2)}) collective-permute-start(f32[512,128]{1,0:T(8,128)S(1)} %second.1.m0), channel_id=1, source_target_pairs={{0,24},{8,0},{16,8},{24,16},{1,25},{9,1},{17,9},{25,17},{2,26},{10... | collective-permute-start | bytes 786440 | tf_op jit(solution)/shard_map/ppermute | solution.py:319
  66.1 1.8 %copy-start.2 = (bf16[24,432,128]{2,1,0:T(8,128)(2,1)S(1)}, bf16[24,432,128]{2,1,0:T(8,128)(2,1)}, u32[]{:S(2)}) copy-start(bf16[24,432,128]{2,1,0:T(8,128)(2,1)} %all-gather.3.cloned.1.call-done) | copy-start | bytes 7962628
  71.7 17.0 %collective-permute-start.14 = (bf16[4,432,128]{2,1,0:T(8,128)(2,1)S(1)}, bf16[4,432,128]{2,1,0:T(8,128)(2,1)S(1)}, u32[]{:S(2)}, u32[]{:S(2)}) collective-permute-start(bf16[4,432,128]{2,1,0:T(8,128)(2,1)S(1)} %get-tuple-element.59), channel_id=1, source_target_pairs={{128,96},{192,160},{129,97},{193,161},{130,98},{194,162},{131,99},... | collective-permute-start | bytes 1327112 | tf_op jit(solution)/shard_map/ppermute | solution.py:322
  74.7 8.6 %collective-permute-start.11 = (f32[512,128]{1,0:T(8,128)S(1)}, f32[512,128]{1,0:T(8,128)S(1)}, u32[]{:S(2)}, u32[]{:S(2)}) collective-permute-start(f32[512,128]{1,0:T(8,128)S(1)} %get-tuple-element.51.point), channel_id=1, source_target_pairs={{0,32},{32,64},{64,96},{96,128},{128,160},{160,192},{192,224},{1,3... | collective-permute-start | bytes 786440 | tf_op jit(solution)/shard_map/ppermute | solution.py:322
  87.2 3.3 %collective-permute-start.12 = (f32[512,128]{1,0:T(8,128)S(1)}, f32[512,128]{1,0:T(8,128)S(1)}, u32[]{:S(2)}, u32[]{:S(2)}) collective-permute-start(f32[512,128]{1,0:T(8,128)S(1)} %get-tuple-element.54.corner.value), channel_id=1, source_target_pairs={{32,64},{33,65},{34,66},{35,67},{36,68},{37,69},{38,70},{39,71},{4... | collective-permute-start | bytes 786440 | tf_op jit(solution)/shard_map/ppermute | solution.py:322
  88.7 8.0 %collective-permute-start.15 = (bf16[4,432,128]{2,1,0:T(8,128)(2,1)S(1)}, bf16[4,432,128]{2,1,0:T(8,128)(2,1)S(1)}, u32[]{:S(2)}, u32[]{:S(2)}) collective-permute-start(bf16[4,432,128]{2,1,0:T(8,128)(2,1)S(1)} %collective-permute-done.14.mine), channel_id=1, source_target_pairs={{0,1},{1,0},{2,3},{3,2},{4,5},{5,4},{6,7},{7,6},{8,9},{9,8},{10,11... | collective-permute-start | bytes 1327112 | tf_op jit(solution)/shard_map/ppermute | solution.py:366
  88.8 7.9 %collective-permute-start.16 = (f32[512,128]{1,0:T(8,128)S(1)}, f32[512,128]{1,0:T(8,128)S(1)}, u32[]{:S(2)}, u32[]{:S(2)}) collective-permute-start(f32[512,128]{1,0:T(8,128)S(1)} %defect.1), channel_id=1, source_target_pairs={{128,96},{192,160},{129,97},{193,161},{130,98},{194,162},{131,99},... | collective-permute-start | bytes 786440 | tf_op jit(solution)/shard_map/ppermute | solution.py:322
  90.7 34.8 %copy-start.1 = (bf16[4,3,3,3,128,128]{5,4,3,2,1,0:T(8,128)(2,1)S(1)}, bf16[4,3,3,3,128,128]{5,4,3,2,1,0:T(8,128)(2,1)}, u32[]{:S(2)}) copy-start(bf16[4,3,3,3,128,128]{5,4,3,2,1,0:T(8,128)(2,1)} %param.6) | copy-start | bytes 10616836
  90.8 6.0 %collective-permute-start.13 = (f32[512,128]{1,0:T(8,128)S(1)}, f32[512,128]{1,0:T(8,128)S(1)}, u32[]{:S(2)}, u32[]{:S(2)}) collective-permute-start(f32[512,128]{1,0:T(8,128)S(1)} %get-tuple-element.57.value), channel_id=1, source_target_pairs={{64,96},{65,97},{66,98},{67,99},{68,100},{69,101},{70,102},{71,103... | collective-permute-start | bytes 786440 | tf_op jit(solution)/shard_map/ppermute | solution.py:322
  96.7 0.7 collective-permute-start.17
  97.4 2.0 %collective-permute-start.19 = (f32[512,128]{1,0:T(8,128)S(1)}, f32[512,128]{1,0:T(8,128)S(1)}, u32[]{:S(2)}, u32[]{:S(2)}) collective-permute-start(f32[512,128]{1,0:T(8,128)S(1)} %get-tuple-element.65), channel_id=1, source_target_pairs={{160,224},{161,225},{162,226},{163,227},{164,228},{165,229},{166,2... | collective-permute-start | bytes 786440 | tf_op jit(solution)/shard_map/ppermute | solution.py:322
  98.1 27.4 %collective-permute-start.18 = (f32[512,128]{1,0:T(8,128)S(1)}, f32[512,128]{1,0:T(8,128)S(1)}, u32[]{:S(2)}, u32[]{:S(2)}) collective-permute-start(f32[512,128]{1,0:T(8,128)S(1)} %get-tuple-element.64.value), channel_id=1, source_target_pairs={{96,128},{160,192},{97,129},{161,193},{98,130},{162,194},{99,131},... | collective-permute-start | bytes 786440 | tf_op jit(solution)/shard_map/ppermute | solution.py:322
Sparse Core Ops, SparseCore 0:
  23.0 28.4 all-gather.2

commit v4 on v3

--- a/solution.py
+++ b/solution.py
@@ -78,7 +78,7 @@
     two.wait()
 
 
-def first_kernel(head, biases, kernels, out, kept, lead, sem, lsem):
+def first_kernel(head, biases, kernels, out, lead, kept, sem, lsem):
     for i in range(4):
         pltpu.make_async_copy(kernels.at[i], kept.at[i], sem.at[i]).start()
     pltpu.make_async_copy(kernels.at[0], lead, lsem).start()
@@ -94,7 +94,7 @@
     pltpu.make_async_copy(kernels.at[0], lead, lsem).wait()
 
 
-def second_kernel(head, guess_head, kernels, biases, term, buf):
+def second_kernel(head, guess_head, kernels, biases, message, buf):
     @pl.when(first_device())
     def _():
         buf[...] = guess_head[...]
@@ -103,7 +103,7 @@
     def _():
         buf[...] = head[...]
 
-    term[...] = buf[...]
+    message[...] = buf[...]
 
     def body(i, carry):
         v = buf[...]
@@ -112,15 +112,23 @@
 
         @pl.when(i == 0)
         def _():
-            term[...] += COARSE * mixed
+            message[...] += COARSE * mixed
 
         return carry
 
     lax.fori_loop(0, 4, body, 0)
-    term[...] = buf[...] - term[...]
-
-
-def coarse_steps(out, stack, lead, ready=lambda q: None):
+    x = lax.axis_index("x")
+
+    @pl.when(x == 0)
+    def _():
+        message[...] = buf[...]
+
+    @pl.when(x > 0)
+    def _():
+        message[...] = buf[...] - message[...]
+
+
+def coarse_steps(out, stack, lead, first=0, ready=lambda q: None):
     def body(q, carry):
         ready(q)
         v = out[...]
@@ -128,13 +136,11 @@
         out[...] = v + COARSE * mixed + stack[pl.ds(q, 1)].reshape(ROWS, CH)
         return carry
 
-    lax.fori_loop(0, X, body, 0)
-
-
-def third_kernel(
-    inputs, head, b1, b2, b3, m0, m1, m2, m3, own, others, out, stack, lead, top, part, sem
-):
-    x, z = lax.axis_index("x"), lax.axis_index("z")
+    lax.fori_loop(first, X, body, 0)
+
+
+def third_kernel(m0, m1, m2, m3, own, others, out, stack, lead, sem):
+    x = lax.axis_index("x")
 
     def copy(q, wait):
         turn = lax.rem(q - x + X, X)
@@ -149,21 +155,30 @@
             one = pltpu.make_async_copy(others.at[:, turn - 1], lead.at[q], sem.at[q])
             one.wait() if wait else one.start()
 
-    for q in range(X):
+    for q in (1, 2, 3, 0):
         copy(q, False)
     for r, term in enumerate((m0, m1, m2, m3)):
         stack[pl.ds(lax.rem(x + r, X), 1)] = term[...].reshape(1, ROWS, CH)
+    out[...] = stack[0]
+    coarse_steps(out, stack, lead, 1, lambda q: copy(q, True))
+    copy(0, True)
+
+
+def head_kernel(inputs, head, b1, b2, b3, lead, stack, out, top, part, buf):
+    x, z = lax.axis_index("x"), lax.axis_index("z")
     for r, start in enumerate((head, b1, b2, b3)):
 
         @pl.when((z > 0) & (x == r))
         def _():
-            out[...] = start[...]
+            buf[...] = start[...]
 
     @pl.when(z == 0)
     def _():
-        out[...] = inputs[...]
-
-    coarse_steps(out, stack, lead, lambda q: copy(q, True))
+        buf[...] = inputs[...]
+
+    v = buf[...]
+    out[0] = stack[0] - v - COARSE * conv(v, flat(lead[0]))
+    out[1:] = stack[1:]
     top[...] = lead[X - 1]
     part[...] = lead[X - 1, pl.ds(lax.axis_index("core") * 4, 4)]
 
@@ -204,36 +219,24 @@
         out_value[...] = v + TOP * conv(v, flat(top[...])) + defect[...]
 
 
-def two_kernel(
-    z, came, before, value, top, defect, mine, other, next_defect,
-    out_before, out_value, ahead, wbuf,
-):
+def next_kernel(z, value, mine, other, defect, ahead, wbuf):
     @pl.when(lax.axis_index("z") == z)
     def _():
-        v = came[...]
-        out_before[...] = v
-        v = v + TOP * conv(v, flat(top[...])) + defect[...]
-        out_value[...] = v
         core = lax.axis_index("core")
         wbuf[pl.ds(core * 4, 4)] = mine[...]
         wbuf[pl.ds(4 - core * 4, 4)] = other[...]
-        ahead[...] = v + TOP * conv(v, flat(wbuf[...])) + next_defect[...]
-
-
-def last_kernel(
-    w4, w7, before, value, defect, biases, stack, lead, kernels, states, buf, sbuf, sem
-):
+        v = value[...]
+        ahead[...] = v + TOP * conv(v, flat(wbuf[...])) + defect[...]
+
+
+def last_kernel(came, before, value, defect, biases, stack, lead, kernels, states, buf, sbuf, sem):
     x, z = lax.axis_index("x"), lax.axis_index("z")
-    late = (z == 4) | (z == 6) | (z == 7)
+    late = (z == 3) | (z == 5) | (z == 7)
     extra = (x == X - 1) & late
 
-    @pl.when((z == 4) | (z == 6))
-    def _():
-        buf[...] = w4[...]
-
-    @pl.when(z == 7)
-    def _():
-        buf[...] = w7[...]
+    @pl.when(late)
+    def _():
+        buf[...] = came[...]
 
     @pl.when(jnp.logical_not(late))
     def _():
@@ -295,8 +298,8 @@
         input_output_aliases=alias or {},
         compiler_params=pltpu.CompilerParams(vmem_limit_bytes=limit << 20),
         cost_estimate=pl.CostEstimate(
-            flops=convs,
-            bytes_accessed=convs,
+            flops=convs if convs != 1 else 6 * 10**9,
+            bytes_accessed=convs if convs != 1 else 20 * 10**6,
             transcendentals=0,
         ),
     )(*args)
@@ -327,60 +330,65 @@
         (guess, inputs, kernels), "hhh", [dma((2,))], limit=63,
     )
     guess_head = next_layer(guess_corner)
-    shares = [from_ahead(share, r) for r in (1, 2, 3)]
+    shares = [from_ahead(share, 1), None, from_ahead(share, 3)]
+    shares[1] = from_ahead(shares[0], 1)
     guess_head, *shares = barrier((guess_head, *shares))
     others = lax.all_gather(jnp.stack(shares), BATCH)
-    point, kept, own = call(
-        first_kernel, "first",
-        (state, jax.ShapeDtypeStruct((4,) + WHOLE, jnp.bfloat16), weight), 4,
-        (guess_head, biases, kernels), "vvh", [dma((4,)), dma(())],
-        out_places="vvh", limit=16,
+    point, own = call(
+        first_kernel, "first", (state, weight), 4, (guess_head, biases, kernels), "vvh",
+        [pltpu.VMEM((4,) + WHOLE, jnp.bfloat16), dma((4,)), dma(())], out_places="vh", limit=48,
     )
     head = next_layer(point)
-    starts = [
-        lax.ppermute(point, LAYER, [(X * z - 1, X * z + r) for z in range(1, Z)])
-        for r in (1, 2, 3)
-    ]
-    (term,) = call(
-        second_kernel, "second", (state,), 4, (head, guess_head, kept, biases),
+    b2, b3 = (
+        lax.ppermute(point, LAYER, [(X * z - 1, X * z + r) for z in range(1, Z)]) for r in (2, 3)
+    )
+    (message,) = call(
+        second_kernel, "second", (state,), 4,
+        (head, guess_head, barrier((kernels, point))[0], biases),
         "vvvv", [buffer],
     )
-    terms = [from_ahead(term, r) for r in (1, 2, 3)]
-    others, *come = barrier((others, *starts, *terms))
-    point, stack, lead, top, part = call(
+    m1, m2, m3 = (from_ahead(message, r) for r in (1, 2, 3))
+    b1 = lax.ppermute(b2, "x", [(2, 1)])
+    others, b2, b3, m1, m2, m3 = barrier((others, b2, b3, m1, m2, m3))
+    point, stack, lead = call(
         third_kernel, "third",
-        (state, jax.ShapeDtypeStruct((X, ROWS, CH), jnp.float32))
-        + tuple(jax.ShapeDtypeStruct(d + (SHARE, CH), jnp.bfloat16) for d in ((X, 8), (8,), (4,))),
-        4, (inputs, head, *come[:3], term, *come[3:], own, others), "v" * 9 + "hh",
-        [dma((X,))],
+        (state, jax.ShapeDtypeStruct((X, ROWS, CH), jnp.float32),
+         jax.ShapeDtypeStruct((X,) + WHOLE, jnp.bfloat16)),
+        3, (message, m1, m2, m3, own, others), "vvvvhh", [dma((X,))],
     )
     hop = along_z(point, *((i, i + 1) for i in range(Z - 1)))
+    stack, top, part = call(
+        head_kernel, "head",
+        (jax.ShapeDtypeStruct((X, ROWS, CH), jnp.float32), weight,
+         jax.ShapeDtypeStruct((4, SHARE, CH), jnp.bfloat16)), 1,
+        (inputs, head, b1, b2, b3, lead, barrier((stack, point))[0]), "v" * 7, [buffer],
+    )
+    next_mine = along_z(part, (3, 2), (5, 4))
     residual, corner, start = call(
         fourth_kernel, "fourth", (state,) * 3, 4, (inputs, hop, point, stack, lead), "vvvvv",
     )
-    w2 = along_z(corner, (1, 2))
+    came = along_z(corner, (1, 2))
     (defect,) = call(defect_kernel, "defect", (state,), 1, (corner, start, top), "vvv")
-    next_defect = along_z(defect, (4, 3), (6, 5))
-    next_mine = along_z(part, (4, 3), (6, 5))
+    next_defect = along_z(defect, (3, 2), (5, 4))
     next_mine, _ = barrier((next_mine, defect))
     next_other = lax.ppermute(next_mine, "core", [(0, 1), (1, 0)])
-    before, value = call(
-        functools.partial(one_kernel, 2), "one", (state, state), 1,
-        (w2, start, corner, top, defect), "vvvvv", alias={1: 0, 2: 1},
-    )
-    for z, distance in ((3, 1), (5, 2)):
-        came = along_z(value if z == 3 else ahead, (z - distance, z))
-        before, value, ahead = call(
-            functools.partial(two_kernel, z), f"two{z}", (state,) * 3, 2,
-            (came, before, value, top, defect, next_mine, next_other, next_defect), "v" * 8,
-            [pltpu.VMEM(WHOLE, jnp.bfloat16)],
-            alias={1: 0, 2: 1},
+    before, value = start, corner
+    for z in (2, 4, 6):
+        before, value = call(
+            functools.partial(one_kernel, z), f"one{z}", (state, state), 1,
+            (came, before, value, top, defect), "vvvvv", alias={1: 0, 2: 1},
         )
-    w7 = along_z(ahead, (5, 7))
-    w4 = along_z(value, (3, 4), (5, 6))
+        if z < 6:
+            (ahead,) = call(
+                functools.partial(next_kernel, z), f"next{z}", (state,), 0,
+                (value, next_mine, next_other, next_defect), "vvvv",
+                [pltpu.VMEM(WHOLE, jnp.bfloat16)],
+            )
+            came = along_z(ahead, (z, z + 2))
+    came = along_z(value, (2, 3), (4, 5), (6, 7))
     (states,) = call(
         last_kernel, "last", (jax.ShapeDtypeStruct((4, ROWS, CH), jnp.float32),), 6,
-        (w4, w7, before, value, defect, biases, stack, lead, kernels), "v" * 9,
+        (came, before, value, defect, biases, stack, lead, kernels), "v" * 8,
         [buffer, pltpu.VMEM((4, ROWS, CH), jnp.float32), dma((4,))], out_places="h",
     )
     volume = (8, 8, 8, CH)

time: 138 us -> 130 us (0.942)
  the two profiles are of different devices: /device:TPU:204 before, /device:TPU:230 now
where the time goes in v4:
time: 130 us; the launch traced here: 129 us
  waiting for transfers between devices  63.7 us (49%)
  Pallas kernels  24.7 us (19%)
  starting transfers between devices  21.6 us (17%)
  between operations  14.3 us (11%)
  local copies, waits for them, and re-layouts  3.76 us (3%)
    ppermute x7, waiting for transfers between devices, along_z(): return lax.ppermute(v, 'z', pairs)  40.8 us
    pallas_call x13, Pallas kernels, call(): pl.pallas_call(body, name=name, out_shape=outs, in_specs=[specs[p] for p...  24.7 us
    ppermute x6, waiting for transfers between devices, from_ahead(): return lax.ppermute(v, 'x', [(i, (i - r) % X) for i in range(X)])  15.5 us
    ppermute x6, starting transfers between devices, from_ahead(): return lax.ppermute(v, 'x', [(i, (i - r) % X) for i in range(X)])  11.4 us
    ppermute x7, starting transfers between devices, along_z(): return lax.ppermute(v, 'z', pairs)  6.4 us
    unnamed x10, local copies, waits for them, and re-layouts  3.76 us
    ppermute x2, waiting for transfers between devices, next_layer(): lax.ppermute(v, LAYER, [(i, (i + 1) % (X * Z)) for i in range(X * Z)])  3.5 us
  transfers between devices with their start and end apart: 20, of which 10 were waited for; matrix products, arithmetic and copies ran while one was open for 0% of the time, Pallas kernels for 13%

profile of v4, /device:TPU:230, one launch (start us, length us, event | category | flops | bytes accessed | tf_op | source)
XLA Modules:
  0.0 128.8 jit_solution(5851322508723596715)
XLA Ops:
  7.2 0.0 copy-start.4
  7.2 0.0 all-gather.3.cloned.1.call-start
  7.2 1.8 %prepare.1 = (f32[512,128]{1,0:T(8,128)}, bf16[432,128]{1,0:T(8,128)(2,1)}) custom-call(f32[4,512,128]{2,1,0:T(8,128)} %bitcast.19, f32[512,128]{1,0:T(8,128)} %bitcast.16, bf16[4,8,432,128]{3,2,1,0:T(8,128)(2,1)} %bitcast.11), custom_call_target="tpu_custom_call" | custom-call | tf_op jit(solution)/shard_map/prepare/pallas_call | solution.py:291
  9.0 0.1 collective-permute-start
  9.1 2.0 %collective-permute-start.1 = (bf16[432,128]{1,0:T(8,128)(2,1)}, bf16[432,128]{1,0:T(8,128)(2,1)S(1)}, u32[]{:S(2)}, u32[]{:S(2)}) collective-permute-start(bf16[432,128]{1,0:T(8,128)(2,1)} %get-tuple-element.35), channel_id=1, source_target_pairs={{0,24},{8,0},{16,8},{24,16},{1,25},{9,1},{17,9},{25,17},{2,26},{10... | collective-permute-start | bytes 331784 | tf_op jit(solution)/shard_map/ppermute | solution.py:322
  11.1 1.3 %collective-permute-start.3 = (bf16[432,128]{1,0:T(8,128)(2,1)}, bf16[432,128]{1,0:T(8,128)(2,1)S(1)}, u32[]{:S(2)}, u32[]{:S(2)}) collective-permute-start(bf16[432,128]{1,0:T(8,128)(2,1)} %get-tuple-element.35), channel_id=1, source_target_pairs={{0,8},{8,16},{16,24},{24,0},{1,9},{9,17},{17,25},{25,1},{2,10},{10... | collective-permute-start | bytes 331784 | tf_op jit(solution)/shard_map/ppermute | solution.py:322
  12.4 3.0 %collective-permute-done.1 = bf16[432,128]{1,0:T(8,128)(2,1)S(1)} collective-permute-done((bf16[432,128]{1,0:T(8,128)(2,1)}, bf16[432,128]{1,0:T(8,128)(2,1)S(1)}, u32[]{:S(2)}, u32[]{:S(2)}) %collective-permute-start.1) | collective-permute-done | bytes 110624 | tf_op jit(solution)/shard_map/ppermute | solution.py:322
  15.4 0.7 collective-permute-start.2
  16.1 3.6 %collective-permute-done.3 = bf16[432,128]{1,0:T(8,128)(2,1)S(1)} collective-permute-done((bf16[432,128]{1,0:T(8,128)(2,1)}, bf16[432,128]{1,0:T(8,128)(2,1)S(1)}, u32[]{:S(2)}, u32[]{:S(2)}) %collective-permute-start.3) | collective-permute-done | bytes 110624 | tf_op jit(solution)/shard_map/ppermute | solution.py:322
  19.7 1.6 %collective-permute-done.2 = bf16[432,128]{1,0:T(8,128)(2,1)S(1)} collective-permute-done((bf16[432,128]{1,0:T(8,128)(2,1)S(1)}, bf16[432,128]{1,0:T(8,128)(2,1)S(1)}, u32[]{:S(2)}, u32[]{:S(2)}) %collective-permute-start.2) | collective-permute-done | bytes 110624 | tf_op jit(solution)/shard_map/ppermute | solution.py:322
  21.3 0.0 collective-permute-done.head.guess_head
  21.3 0.8 pad_maximum_fusion
  22.1 0.0 all-gather.3.cloned.1.call-update
  22.1 0.0 copy-done.4
  22.1 0.0 copy-start
  22.2 2.0 %copy-done = bf16[4,3,3,3,128,128]{5,4,3,2,1,0:T(8,128)(2,1)S(1)} copy-done((bf16[4,3,3,3,128,128]{5,4,3,2,1,0:T(8,128)(2,1)S(1)}, bf16[4,3,3,3,128,128]{5,4,3,2,1,0:T(8,128)(2,1)}, u32[]{:S(2)}) %copy-start) | copy-done | bytes 3538968
  24.2 4.2 %first.1 = (f32[512,128]{1,0:T(8,128)S(1)}, bf16[8,432,128]{2,1,0:T(8,128)(2,1)S(1)}) custom-call(f32[512,128]{1,0:T(8,128)S(1)} %collective-permute-done.head.guess_head, f32[4,128]{1,0:T(4,128)S(1)} %copy-done.4, bf16[4,8,432,128]{3,2,1,0:T(8,128)(2,1)S(1)} %bitcast.12), custom_call_target="tpu_custom_call" | custom-call | flops 4 | bytes 4 | tf_op jit(solution)/shard_map/first/pallas_call | solution.py:291
  28.4 0.0 copy-start.3
  28.4 1.0 collective-permute-start.4
  29.4 0.7 collective-permute-start.5
  30.1 1.3 %collective-permute-start.6 = (f32[512,128]{1,0:T(8,128)S(1)}, f32[512,128]{1,0:T(8,128)S(1)}, u32[]{:S(2)}, u32[]{:S(2)}) collective-permute-start(f32[512,128]{1,0:T(8,128)S(1)} %get-tuple-element.37), channel_id=1, source_target_pairs={{24,56},{56,88},{88,120},{120,152},{152,184},{184,216},{216,248},{... | collective-permute-start | bytes 786440 | tf_op jit(solution)/shard_map/ppermute | solution.py:343
  31.4 3.5 %collective-permute-done.4.head = f32[512,128]{1,0:T(8,128)S(1)} collective-permute-done((f32[512,128]{1,0:T(8,128)S(1)}, f32[512,128]{1,0:T(8,128)S(1)}, u32[]{:S(2)}, u32[]{:S(2)}) %collective-permute-start.4) | collective-permute-done | bytes 262176 | tf_op jit(solution)/shard_map/ppermute | solution.py:319
  34.9 3.3 %second.1.m0 = f32[512,128]{1,0:T(8,128)S(1)} custom-call(f32[512,128]{1,0:T(8,128)S(1)} %collective-permute-done.4.head, f32[512,128]{1,0:T(8,128)S(1)} %collective-permute-done.head.guess_head, bf16[4,8,432,128]{3,2,1,0:T(8,128)(2,1)S(1)} %bitcast.13, f32[4,128]{1,0:T(4,128)S(1)} %copy-done.4), custom_call_target="tpu_custom_call" | custom-call | flops 4 | bytes 4 | tf_op jit(solution)/shard_map/second/pallas_call | solution.py:291
  38.2 0.1 collective-permute-start.7
  38.3 7.3 %collective-permute-start.8 = (f32[512,128]{1,0:T(8,128)S(1)}, f32[512,128]{1,0:T(8,128)S(1)}, u32[]{:S(2)}, u32[]{:S(2)}) collective-permute-start(f32[512,128]{1,0:T(8,128)S(1)} %second.1.m0), channel_id=1, source_target_pairs={{0,16},{8,24},{16,0},{24,8},{1,17},{9,25},{17,1},{25,9},{2,18},{10... | collective-permute-start | bytes 786440 | tf_op jit(solution)/shard_map/ppermute | solution.py:322
  45.6 0.0 collective-permute-start.9
  45.6 0.0 collective-permute-done.5.b2
  45.6 0.7 collective-permute-start.11
  46.2 2.1 %collective-permute-done.6.b3 = f32[512,128]{1,0:T(8,128)S(1)} collective-permute-done((f32[512,128]{1,0:T(8,128)S(1)}, f32[512,128]{1,0:T(8,128)S(1)}, u32[]{:S(2)}, u32[]{:S(2)}) %collective-permute-start.6) | collective-permute-done | bytes 262176 | tf_op jit(solution)/shard_map/ppermute | solution.py:343
  48.4 2.1 %collective-permute-done.7.m1 = f32[512,128]{1,0:T(8,128)S(1)} collective-permute-done((f32[512,128]{1,0:T(8,128)S(1)}, f32[512,128]{1,0:T(8,128)S(1)}, u32[]{:S(2)}, u32[]{:S(2)}) %collective-permute-start.7) | collective-permute-done | bytes 262176 | tf_op jit(solution)/shard_map/ppermute | solution.py:322
  50.4 5.2 %collective-permute-done.8.m2 = f32[512,128]{1,0:T(8,128)S(1)} collective-permute-done((f32[512,128]{1,0:T(8,128)S(1)}, f32[512,128]{1,0:T(8,128)S(1)}, u32[]{:S(2)}, u32[]{:S(2)}) %collective-permute-start.8) | collective-permute-done | bytes 262176 | tf_op jit(solution)/shard_map/ppermute | solution.py:322
  55.6 0.0 collective-permute-done.9.m3
  55.6 0.0 all-gather.3.cloned.1.call-done
  55.6 0.0 copy-start.2
  55.6 1.7 %copy-done.2 = bf16[24,432,128]{2,1,0:T(8,128)(2,1)S(1)} copy-done((bf16[24,432,128]{2,1,0:T(8,128)(2,1)S(1)}, bf16[24,432,128]{2,1,0:T(8,128)(2,1)}, u32[]{:S(2)}) %copy-start.2) | copy-done | bytes 2654232
  57.3 3.0 %third.1 = (f32[512,128]{1,0:T(8,128)S(1)}, f32[4,512,128]{2,1,0:T(8,128)S(1)}, bf16[4,8,432,128]{3,2,1,0:T(8,128)(2,1)S(1)}) custom-call(f32[512,128]{1,0:T(8,128)S(1)} %second.1.m0, f32[512,128]{1,0:T(8,128)S(1)} %collective-permute-done.7.m1, f32[512,128]{1,0:T(8,128)S(1)} %collective-permute-done.8.m2, f32[512,128]{1,0:T(8,128)S(1)} %collective-permute-done.9.m3, ...), custom_call_target="tpu_custom_call" | custom-call | flops 3 | bytes 3 | tf_op jit(solution)/shard_map/third/pallas_call | solution.py:291
  60.4 1.3 %collective-permute-start.10 = (f32[512,128]{1,0:T(8,128)S(1)}, f32[512,128]{1,0:T(8,128)S(1)}, u32[]{:S(2)}, u32[]{:S(2)}) collective-permute-start(f32[512,128]{1,0:T(8,128)S(1)} %get-tuple-element.47.point), channel_id=1, source_target_pairs={{0,32},{32,64},{64,96},{96,128},{128,160},{160,192},{192,224},{1,3... | collective-permute-start | bytes 786440 | tf_op jit(solution)/shard_map/ppermute | solution.py:325
  61.7 0.0 collective-permute-done.11.b1
  61.7 0.0 copy-done.3
  61.7 1.0 head.1
  62.6 0.7 collective-permute-start.13
  63.3 5.3 %collective-permute-done.10.hop = f32[512,128]{1,0:T(8,128)S(1)} collective-permute-done((f32[512,128]{1,0:T(8,128)S(1)}, f32[512,128]{1,0:T(8,128)S(1)}, u32[]{:S(2)}, u32[]{:S(2)}) %collective-permute-start.10) | collective-permute-done | bytes 262176 | tf_op jit(solution)/shard_map/ppermute | solution.py:325
  68.6 4.0 %fourth.1 = (f32[512,128]{1,0:T(8,128)}, f32[512,128]{1,0:T(8,128)S(1)}, f32[512,128]{1,0:T(8,128)S(1)}) custom-call(f32[512,128]{1,0:T(8,128)S(1)} %bitcast.18, f32[512,128]{1,0:T(8,128)S(1)} %collective-permute-done.10.hop, f32[512,128]{1,0:T(8,128)S(1)} %get-tuple-element.47.point, f32[4,512,128]{2,1,0:T(8,128)S(1)} %get-tuple-element.53.stack, ...), custom_call_target="tpu_custom_call" | custom-call | flops 4 | bytes 4 | tf_op jit(solution)/shard_map/fourth/pallas_call | solution.py:291
  72.6 0.8 collective-permute-start.12
  73.5 0.8 defect.1
  74.3 0.7 collective-permute-start.15
  75.0 0.0 collective-permute-done.13.mine
  75.0 0.1 collective-permute-start.14
  75.1 0.0 collective-permute-done.12.came
  75.2 0.0 collective-permute-done.15.defect
  75.2 1.7 %collective-permute-done.14.other = bf16[4,432,128]{2,1,0:T(8,128)(2,1)S(1)} collective-permute-done((bf16[4,432,128]{2,1,0:T(8,128)(2,1)S(1)}, bf16[4,432,128]{2,1,0:T(8,128)(2,1)S(1)}, u32[]{:S(2)}, u32[]{:S(2)}) %collective-permute-start.14) | collective-permute-done | bytes 442400 | tf_op jit(solution)/shard_map/ppermute | solution.py:374
  76.9 0.7 collective-permute-start.16
  77.6 0.0 collective-permute-done.16.came
  77.6 0.7 collective-permute-start.17
  78.3 0.0 collective-permute-done.17.came
  78.3 0.0 copy-start.1
  78.4 1.6 %collective-permute-start.18 = (f32[512,128]{1,0:T(8,128)S(1)}, f32[512,128]{1,0:T(8,128)S(1)}, u32[]{:S(2)}, u32[]{:S(2)}) collective-permute-start(f32[512,128]{1,0:T(8,128)S(1)} %get-tuple-element.63.value), channel_id=1, source_target_pairs={{64,96},{128,160},{192,224},{65,97},{129,161},{193,225},{66,98},{1... | collective-permute-start | bytes 786440 | tf_op jit(solution)/shard_map/ppermute | solution.py:325
  79.9 35.5 %collective-permute-done.18.came = f32[512,128]{1,0:T(8,128)S(1)} collective-permute-done((f32[512,128]{1,0:T(8,128)S(1)}, f32[512,128]{1,0:T(8,128)S(1)}, u32[]{:S(2)}, u32[]{:S(2)}) %collective-permute-start.18) | collective-permute-done | bytes 262176 | tf_op jit(solution)/shard_map/ppermute | solution.py:325
  115.4 0.0 copy-done.1
  115.4 6.5 %last.1 = f32[4,512,128]{2,1,0:T(8,128)} custom-call(f32[512,128]{1,0:T(8,128)S(1)} %collective-permute-done.18.came, f32[512,128]{1,0:T(8,128)S(1)} %get-tuple-element.64.before, f32[512,128]{1,0:T(8,128)S(1)} %get-tuple-element.63.value, f32[512,128]{1,0:T(8,128)S(1)} %defect.1, f32[4,128]{1,0:T(4,128)S(1)} %copy-done.4, ...), custom_call_target="tpu_custom_call" | custom-call | flops 6 | bytes 6 | tf_op jit(solution)/shard_map/last/pallas_call | solution.py:291
  (5 shorter events, 0.1 us)
Async XLA Ops:
  7.2 15.0 %copy-start.4 = (f32[4,128]{1,0:T(4,128)S(1)}, f32[4,128]{1,0:T(4,128)}, u32[]{:S(2)}) copy-start(f32[4,128]{1,0:T(4,128)} %biases.5) | copy-start | bytes 6148
  7.2 48.4 %all-gather.3.cloned.1.call-start = ((), (), s32[]{:S(2)}) async-start(), calls=%async_computation | async-start | bytes 2985984 | tf_op jit(solution)/shard_map/all_gather | solution.py:336
  9.0 12.3 %collective-permute-start = (f32[512,128]{1,0:T(8,128)}, f32[512,128]{1,0:T(8,128)S(1)}, u32[]{:S(2)}, u32[]{:S(2)}) collective-permute-start(f32[512,128]{1,0:T(8,128)} %get-tuple-element.34), channel_id=1, source_target_pairs={{0,8},{8,16},{16,24},{24,32},{32,40},{40,48},{48,56},{56,64},{64,7... | collective-permute-start | bytes 786440 | tf_op jit(solution)/shard_map/ppermute | solution.py:319
  9.1 6.3 %collective-permute-start.1 = (bf16[432,128]{1,0:T(8,128)(2,1)}, bf16[432,128]{1,0:T(8,128)(2,1)S(1)}, u32[]{:S(2)}, u32[]{:S(2)}) collective-permute-start(bf16[432,128]{1,0:T(8,128)(2,1)} %get-tuple-element.35), channel_id=1, source_target_pairs={{0,24},{8,0},{16,8},{24,16},{1,25},{9,1},{17,9},{25,17},{2,26},{10... | collective-permute-start | bytes 331784 | tf_op jit(solution)/shard_map/ppermute | solution.py:322
  11.1 8.6 %collective-permute-start.3 = (bf16[432,128]{1,0:T(8,128)(2,1)}, bf16[432,128]{1,0:T(8,128)(2,1)S(1)}, u32[]{:S(2)}, u32[]{:S(2)}) collective-permute-start(bf16[432,128]{1,0:T(8,128)(2,1)} %get-tuple-element.35), channel_id=1, source_target_pairs={{0,8},{8,16},{16,24},{24,0},{1,9},{9,17},{17,25},{25,1},{2,10},{10... | collective-permute-start | bytes 331784 | tf_op jit(solution)/shard_map/ppermute | solution.py:322
  15.4 6.0 %collective-permute-start.2 = (bf16[432,128]{1,0:T(8,128)(2,1)S(1)}, bf16[432,128]{1,0:T(8,128)(2,1)S(1)}, u32[]{:S(2)}, u32[]{:S(2)}) collective-permute-start(bf16[432,128]{1,0:T(8,128)(2,1)S(1)} %collective-permute-done.1), channel_id=1, source_target_pairs={{0,24},{8,0},{16,8},{24,16},{1,25},{9,1},{17,9},{25,17},{2,26},{10... | collective-permute-start | bytes 331784 | tf_op jit(solution)/shard_map/ppermute | solution.py:322
  22.1 2.0 %copy-start = (bf16[4,3,3,3,128,128]{5,4,3,2,1,0:T(8,128)(2,1)S(1)}, bf16[4,3,3,3,128,128]{5,4,3,2,1,0:T(8,128)(2,1)}, u32[]{:S(2)}) copy-start(bf16[4,3,3,3,128,128]{5,4,3,2,1,0:T(8,128)(2,1)} %param.6) | copy-start | bytes 10616836
  28.4 33.3 %copy-start.3 = (f32[1,8,8,8,128]{4,3,2,1,0:T(8,128)S(1)}, f32[1,8,8,8,128]{4,3,2,1,0:T(8,128)}, u32[]{:S(2)}) copy-start(f32[1,8,8,8,128]{4,3,2,1,0:T(8,128)} %param.4) | copy-start | bytes 786436
  28.4 6.4 %collective-permute-start.4 = (f32[512,128]{1,0:T(8,128)S(1)}, f32[512,128]{1,0:T(8,128)S(1)}, u32[]{:S(2)}, u32[]{:S(2)}) collective-permute-start(f32[512,128]{1,0:T(8,128)S(1)} %get-tuple-element.37), channel_id=1, source_target_pairs={{0,8},{8,16},{16,24},{24,32},{32,40},{40,48},{48,56},{56,64},{64,7... | collective-permute-start | bytes 786440 | tf_op jit(solution)/shard_map/ppermute | solution.py:319
  29.4 16.2 %collective-permute-start.5 = (f32[512,128]{1,0:T(8,128)S(1)}, f32[512,128]{1,0:T(8,128)S(1)}, u32[]{:S(2)}, u32[]{:S(2)}) collective-permute-start(f32[512,128]{1,0:T(8,128)S(1)} %get-tuple-element.37), channel_id=1, source_target_pairs={{24,48},{56,80},{88,112},{120,144},{152,176},{184,208},{216,240},{... | collective-permute-start | bytes 786440 | tf_op jit(solution)/shard_map/ppermute | solution.py:343
  30.1 18.3 %collective-permute-start.6 = (f32[512,128]{1,0:T(8,128)S(1)}, f32[512,128]{1,0:T(8,128)S(1)}, u32[]{:S(2)}, u32[]{:S(2)}) collective-permute-start(f32[512,128]{1,0:T(8,128)S(1)} %get-tuple-element.37), channel_id=1, source_target_pairs={{24,56},{56,88},{88,120},{120,152},{152,184},{184,216},{216,248},{... | collective-permute-start | bytes 786440 | tf_op jit(solution)/shard_map/ppermute | solution.py:343
  38.2 12.3 %collective-permute-start.7 = (f32[512,128]{1,0:T(8,128)S(1)}, f32[512,128]{1,0:T(8,128)S(1)}, u32[]{:S(2)}, u32[]{:S(2)}) collective-permute-start(f32[512,128]{1,0:T(8,128)S(1)} %second.1.m0), channel_id=1, source_target_pairs={{0,24},{8,0},{16,8},{24,16},{1,25},{9,1},{17,9},{25,17},{2,26},{10... | collective-permute-start | bytes 786440 | tf_op jit(solution)/shard_map/ppermute | solution.py:322
  38.3 17.3 %collective-permute-start.8 = (f32[512,128]{1,0:T(8,128)S(1)}, f32[512,128]{1,0:T(8,128)S(1)}, u32[]{:S(2)}, u32[]{:S(2)}) collective-permute-start(f32[512,128]{1,0:T(8,128)S(1)} %second.1.m0), channel_id=1, source_target_pairs={{0,16},{8,24},{16,0},{24,8},{1,17},{9,25},{17,1},{25,9},{2,18},{10... | collective-permute-start | bytes 786440 | tf_op jit(solution)/shard_map/ppermute | solution.py:322
  45.6 10.0 %collective-permute-start.9 = (f32[512,128]{1,0:T(8,128)S(1)}, f32[512,128]{1,0:T(8,128)S(1)}, u32[]{:S(2)}, u32[]{:S(2)}) collective-permute-start(f32[512,128]{1,0:T(8,128)S(1)} %second.1.m0), channel_id=1, source_target_pairs={{0,8},{8,16},{16,24},{24,0},{1,9},{9,17},{17,25},{25,1},{2,10},{10... | collective-permute-start | bytes 786440 | tf_op jit(solution)/shard_map/ppermute | solution.py:322
  45.6 16.1 %collective-permute-start.11 = (f32[512,128]{1,0:T(8,128)S(1)}, f32[512,128]{1,0:T(8,128)S(1)}, u32[]{:S(2)}, u32[]{:S(2)}) collective-permute-start(f32[512,128]{1,0:T(8,128)S(1)} %collective-permute-done.5.b2), channel_id=1, source_target_pairs={{16,8},{17,9},{18,10},{19,11},{20,12},{21,13},{22,14},{23,15},{48,... | collective-permute-start | bytes 786440 | tf_op jit(solution)/shard_map/ppermute | solution.py:351
  55.6 1.8 %copy-start.2 = (bf16[24,432,128]{2,1,0:T(8,128)(2,1)S(1)}, bf16[24,432,128]{2,1,0:T(8,128)(2,1)}, u32[]{:S(2)}) copy-start(bf16[24,432,128]{2,1,0:T(8,128)(2,1)} %all-gather.3.cloned.1.call-done) | copy-start | bytes 7962628
  60.4 8.3 %collective-permute-start.10 = (f32[512,128]{1,0:T(8,128)S(1)}, f32[512,128]{1,0:T(8,128)S(1)}, u32[]{:S(2)}, u32[]{:S(2)}) collective-permute-start(f32[512,128]{1,0:T(8,128)S(1)} %get-tuple-element.47.point), channel_id=1, source_target_pairs={{0,32},{32,64},{64,96},{96,128},{128,160},{160,192},{192,224},{1,3... | collective-permute-start | bytes 786440 | tf_op jit(solution)/shard_map/ppermute | solution.py:325
  62.6 12.4 %collective-permute-start.13 = (bf16[4,432,128]{2,1,0:T(8,128)(2,1)S(1)}, bf16[4,432,128]{2,1,0:T(8,128)(2,1)S(1)}, u32[]{:S(2)}, u32[]{:S(2)}) collective-permute-start(bf16[4,432,128]{2,1,0:T(8,128)(2,1)S(1)} %get-tuple-element.58), channel_id=1, source_target_pairs={{96,64},{160,128},{97,65},{161,129},{98,66},{162,130},{99,67},{163... | collective-permute-start | bytes 1327112 | tf_op jit(solution)/shard_map/ppermute | solution.py:325
  72.6 2.5 %collective-permute-start.12 = (f32[512,128]{1,0:T(8,128)S(1)}, f32[512,128]{1,0:T(8,128)S(1)}, u32[]{:S(2)}, u32[]{:S(2)}) collective-permute-start(f32[512,128]{1,0:T(8,128)S(1)} %get-tuple-element.54.corner.value), channel_id=1, source_target_pairs={{32,64},{33,65},{34,66},{35,67},{36,68},{37,69},{38,70},{39,71},{4... | collective-permute-start | bytes 786440 | tf_op jit(solution)/shard_map/ppermute | solution.py:325
  74.3 0.8 collective-permute-start.15
  75.0 1.9 %collective-permute-start.14 = (bf16[4,432,128]{2,1,0:T(8,128)(2,1)S(1)}, bf16[4,432,128]{2,1,0:T(8,128)(2,1)S(1)}, u32[]{:S(2)}, u32[]{:S(2)}) collective-permute-start(bf16[4,432,128]{2,1,0:T(8,128)(2,1)S(1)} %collective-permute-done.13.mine), channel_id=1, source_target_pairs={{0,1},{1,0},{2,3},{3,2},{4,5},{5,4},{6,7},{7,6},{8,9},{9,8},{10,11... | collective-permute-start | bytes 1327112 | tf_op jit(solution)/shard_map/ppermute | solution.py:374
  76.9 0.7 collective-permute-start.16
  77.6 0.7 collective-permute-start.17
  78.3 37.1 %copy-start.1 = (bf16[4,3,3,3,128,128]{5,4,3,2,1,0:T(8,128)(2,1)S(1)}, bf16[4,3,3,3,128,128]{5,4,3,2,1,0:T(8,128)(2,1)}, u32[]{:S(2)}) copy-start(bf16[4,3,3,3,128,128]{5,4,3,2,1,0:T(8,128)(2,1)} %param.6) | copy-start | bytes 10616836
  78.4 37.1 %collective-permute-start.18 = (f32[512,128]{1,0:T(8,128)S(1)}, f32[512,128]{1,0:T(8,128)S(1)}, u32[]{:S(2)}, u32[]{:S(2)}) collective-permute-start(f32[512,128]{1,0:T(8,128)S(1)} %get-tuple-element.63.value), channel_id=1, source_target_pairs={{64,96},{128,160},{192,224},{65,97},{129,161},{193,225},{66,98},{1... | collective-permute-start | bytes 786440 | tf_op jit(solution)/shard_map/ppermute | solution.py:325
Sparse Core Ops, SparseCore 0:
  22.3 29.6 all-gather.2

commit v5 on v4

--- a/solution.py
+++ b/solution.py
@@ -94,7 +94,7 @@
     pltpu.make_async_copy(kernels.at[0], lead, lsem).wait()
 
 
-def second_kernel(head, guess_head, kernels, biases, message, buf):
+def second_kernel(head, guess_head, kernels, biases, message, term, buf):
     @pl.when(first_device())
     def _():
         buf[...] = guess_head[...]
@@ -103,7 +103,7 @@
     def _():
         buf[...] = head[...]
 
-    message[...] = buf[...]
+    term[...] = buf[...]
 
     def body(i, carry):
         v = buf[...]
@@ -112,11 +112,12 @@
 
         @pl.when(i == 0)
         def _():
-            message[...] += COARSE * mixed
+            term[...] += COARSE * mixed
 
         return carry
 
     lax.fori_loop(0, 4, body, 0)
+    term[...] = buf[...] - term[...]
     x = lax.axis_index("x")
 
     @pl.when(x == 0)
@@ -125,7 +126,7 @@
 
     @pl.when(x > 0)
     def _():
-        message[...] = buf[...] - message[...]
+        message[...] = term[...]
 
 
 def coarse_steps(out, stack, lead, first=0, ready=lambda q: None):
@@ -139,7 +140,7 @@
     lax.fori_loop(first, X, body, 0)
 
 
-def third_kernel(m0, m1, m2, m3, own, others, out, stack, lead, sem):
+def third_kernel(m0, m1, m2, m3, own, others, out, stack, lead, top, part, sem):
     x = lax.axis_index("x")
 
     def copy(q, wait):
@@ -162,29 +163,21 @@
     out[...] = stack[0]
     coarse_steps(out, stack, lead, 1, lambda q: copy(q, True))
     copy(0, True)
-
-
-def head_kernel(inputs, head, b1, b2, b3, lead, stack, out, top, part, buf):
-    x, z = lax.axis_index("x"), lax.axis_index("z")
-    for r, start in enumerate((head, b1, b2, b3)):
-
-        @pl.when((z > 0) & (x == r))
-        def _():
-            buf[...] = start[...]
-
-    @pl.when(z == 0)
-    def _():
-        buf[...] = inputs[...]
-
-    v = buf[...]
-    out[0] = stack[0] - v - COARSE * conv(v, flat(lead[0]))
-    out[1:] = stack[1:]
     top[...] = lead[X - 1]
     part[...] = lead[X - 1, pl.ds(lax.axis_index("core") * 4, 4)]
 
 
-def fourth_kernel(inputs, hop, point, stack, lead, residual, corner, start):
+def fourth_kernel(
+    inputs, hop, point, term, f1, f2, f3, stack, lead, residual, corner, start, out_stack
+):
     x, z = lax.axis_index("x"), lax.axis_index("z")
+    out_stack[1:] = stack[1:]
+    for r, first in enumerate((term, f1, f2, f3)):
+
+        @pl.when(x == r)
+        def _():
+            out_stack[0] = first[...]
+
 
     @pl.when(z == 0)
     def _():
@@ -195,7 +188,7 @@
         start[...] = hop[...]
 
     corner[...] = start[...]
-    coarse_steps(corner, stack, lead)
+    coarse_steps(corner, out_stack, lead)
 
     @pl.when(x == X - 1)
     def _():
@@ -339,37 +332,31 @@
         [pltpu.VMEM((4,) + WHOLE, jnp.bfloat16), dma((4,)), dma(())], out_places="vh", limit=48,
     )
     head = next_layer(point)
-    b2, b3 = (
-        lax.ppermute(point, LAYER, [(X * z - 1, X * z + r) for z in range(1, Z)]) for r in (2, 3)
-    )
-    (message,) = call(
-        second_kernel, "second", (state,), 4,
+    message, term = call(
+        second_kernel, "second", (state, state), 4,
         (head, guess_head, barrier((kernels, point))[0], biases),
         "vvvv", [buffer],
     )
     m1, m2, m3 = (from_ahead(message, r) for r in (1, 2, 3))
-    b1 = lax.ppermute(b2, "x", [(2, 1)])
-    others, b2, b3, m1, m2, m3 = barrier((others, b2, b3, m1, m2, m3))
-    point, stack, lead = call(
+    others, term, m1, m2, m3 = barrier((others, term, m1, m2, m3))
+    f1, f3 = (lax.ppermute(term, "x", [(0, r)]) for r in (1, 3))
+    stacked = jax.ShapeDtypeStruct((X, ROWS, CH), jnp.float32)
+    point, stack, lead, top, part = call(
         third_kernel, "third",
-        (state, jax.ShapeDtypeStruct((X, ROWS, CH), jnp.float32),
-         jax.ShapeDtypeStruct((X,) + WHOLE, jnp.bfloat16)),
+        (state, stacked, jax.ShapeDtypeStruct((X,) + WHOLE, jnp.bfloat16), weight,
+         jax.ShapeDtypeStruct((4, SHARE, CH), jnp.bfloat16)),
         3, (message, m1, m2, m3, own, others), "vvvvhh", [dma((X,))],
     )
     hop = along_z(point, *((i, i + 1) for i in range(Z - 1)))
-    stack, top, part = call(
-        head_kernel, "head",
-        (jax.ShapeDtypeStruct((X, ROWS, CH), jnp.float32), weight,
-         jax.ShapeDtypeStruct((4, SHARE, CH), jnp.bfloat16)), 1,
-        (inputs, head, b1, b2, b3, lead, barrier((stack, point))[0]), "v" * 7, [buffer],
-    )
+    f2 = lax.ppermute(f1, "x", [(1, 2)])
     next_mine = along_z(part, (3, 2), (5, 4))
-    residual, corner, start = call(
-        fourth_kernel, "fourth", (state,) * 3, 4, (inputs, hop, point, stack, lead), "vvvvv",
+    residual, corner, start, stack = call(
+        fourth_kernel, "fourth", (state,) * 3 + (stacked,), 1,
+        (inputs, hop, point, term, f1, f2, f3, stack, lead), "v" * 9,
     )
     came = along_z(corner, (1, 2))
     (defect,) = call(defect_kernel, "defect", (state,), 1, (corner, start, top), "vvv")
-    next_defect = along_z(defect, (3, 2), (5, 4))
+    next_defect = {2: along_z(defect, (3, 2)), 4: along_z(defect, (5, 4))}
     next_mine, _ = barrier((next_mine, defect))
     next_other = lax.ppermute(next_mine, "core", [(0, 1), (1, 0)])
     before, value = start, corner
@@ -381,7 +368,7 @@
         if z < 6:
             (ahead,) = call(
                 functools.partial(next_kernel, z), f"next{z}", (state,), 0,
-                (value, next_mine, next_other, next_defect), "vvvv",
+                (value, next_mine, next_other, next_defect[z]), "vvvv",
                 [pltpu.VMEM(WHOLE, jnp.bfloat16)],
             )
             came = along_z(ahead, (z, z + 2))

time: 130 us -> 128 us (0.985)
  waiting for transfers between devices: 63.7 us -> 61.8 us
    ppermute x7 -> x8, waiting for transfers between devices: 40.8 us -> 35.3 us  [along_z(): return lax.ppermute(v, 'z', pairs)]
    ppermute x6, waiting for transfers between devices: 15.5 us -> 19.2 us  [from_ahead(): return lax.ppermute(v, 'x', [(i, (i - r) % X) for i in range(X)])]
    ppermute x3, waiting for transfers between devices: 2.13 us -> 0.01 us  [the longest x2 0.01 us: shards(): f1, f3 = (lax.ppermute(term, 'x', [(0, r)]) for r in (1, 3))]
    ppermute x2, waiting for transfers between devices: 3.5 us -> 5.47 us  [next_layer(): lax.ppermute(v, LAYER, [(i, (i + 1) % (X * Z)) for i in range(X * Z)])]
    pallas_call x13 -> x12, Pallas kernels: 24.7 us -> 24 us  [call(): pl.pallas_call(body, name=name, out_shape=outs, in_specs=[specs[p] for p...]
    ppermute x7 -> x8, starting transfers between devices: 6.4 us -> 6.9 us  [along_z(): return lax.ppermute(v, 'z', pairs)]
  transfers between devices with their start and end apart: 20 -> 21, of which waited for: 10 -> 9; matrix products, arithmetic and copies ran while one was open for 0% -> 0% of each run, Pallas kernels for 13% -> 12%
where the time goes in v5:
time: 128 us; the launch traced here: 126 us
  waiting for transfers between devices  61.8 us (48%)
  Pallas kernels  24 us (19%)
  starting transfers between devices  21.3 us (17%)
  between operations  14.3 us (11%)
  local copies, waits for them, and re-layouts  3.76 us (3%)
    ppermute x8, waiting for transfers between devices, along_z(): return lax.ppermute(v, 'z', pairs)  35.3 us
    pallas_call x12, Pallas kernels, call(): pl.pallas_call(body, name=name, out_shape=outs, in_specs=[specs[p] for p...  24 us
    ppermute x6, waiting for transfers between devices, from_ahead(): return lax.ppermute(v, 'x', [(i, (i - r) % X) for i in range(X)])  19.2 us
    ppermute x6, starting transfers between devices, from_ahead(): return lax.ppermute(v, 'x', [(i, (i - r) % X) for i in range(X)])  10.4 us
    ppermute x8, starting transfers between devices, along_z(): return lax.ppermute(v, 'z', pairs)  6.9 us
    ppermute x2, waiting for transfers between devices, next_layer(): lax.ppermute(v, LAYER, [(i, (i + 1) % (X * Z)) for i in range(X * Z)])  5.47 us
    unnamed x10, local copies, waits for them, and re-layouts  3.76 us
  transfers between devices with their start and end apart: 21, of which 9 were waited for; matrix products, arithmetic and copies ran while one was open for 0% of the time, Pallas kernels for 12%

profile of v5, /device:TPU:230, one launch (start us, length us, event | category | flops | bytes accessed | tf_op | source)
XLA Modules:
  0.0 126.0 jit_solution(8915907131338218655)
XLA Ops:
  7.2 0.0 copy-start.4
  7.2 0.0 all-gather.3.cloned.1.call-start
  7.2 1.8 %prepare.1 = (f32[512,128]{1,0:T(8,128)}, bf16[432,128]{1,0:T(8,128)(2,1)}) custom-call(f32[4,512,128]{2,1,0:T(8,128)} %bitcast.18, f32[512,128]{1,0:T(8,128)} %bitcast.16, bf16[4,8,432,128]{3,2,1,0:T(8,128)(2,1)} %bitcast.11), custom_call_target="tpu_custom_call" | custom-call | tf_op jit(solution)/shard_map/prepare/pallas_call | solution.py:284
  9.0 0.1 collective-permute-start
  9.1 2.0 %collective-permute-start.1 = (bf16[432,128]{1,0:T(8,128)(2,1)}, bf16[432,128]{1,0:T(8,128)(2,1)S(1)}, u32[]{:S(2)}, u32[]{:S(2)}) collective-permute-start(bf16[432,128]{1,0:T(8,128)(2,1)} %get-tuple-element.35), channel_id=1, source_target_pairs={{0,24},{8,0},{16,8},{24,16},{1,25},{9,1},{17,9},{25,17},{2,26},{10... | collective-permute-start | bytes 331784 | tf_op jit(solution)/shard_map/ppermute | solution.py:315
  11.1 1.3 %collective-permute-start.3 = (bf16[432,128]{1,0:T(8,128)(2,1)}, bf16[432,128]{1,0:T(8,128)(2,1)S(1)}, u32[]{:S(2)}, u32[]{:S(2)}) collective-permute-start(bf16[432,128]{1,0:T(8,128)(2,1)} %get-tuple-element.35), channel_id=1, source_target_pairs={{0,8},{8,16},{16,24},{24,0},{1,9},{9,17},{17,25},{25,1},{2,10},{10... | collective-permute-start | bytes 331784 | tf_op jit(solution)/shard_map/ppermute | solution.py:315
  12.4 3.0 %collective-permute-done.1 = bf16[432,128]{1,0:T(8,128)(2,1)S(1)} collective-permute-done((bf16[432,128]{1,0:T(8,128)(2,1)}, bf16[432,128]{1,0:T(8,128)(2,1)S(1)}, u32[]{:S(2)}, u32[]{:S(2)}) %collective-permute-start.1) | collective-permute-done | bytes 110624 | tf_op jit(solution)/shard_map/ppermute | solution.py:315
  15.4 0.7 collective-permute-start.2
  16.1 3.6 %collective-permute-done.3 = bf16[432,128]{1,0:T(8,128)(2,1)S(1)} collective-permute-done((bf16[432,128]{1,0:T(8,128)(2,1)}, bf16[432,128]{1,0:T(8,128)(2,1)S(1)}, u32[]{:S(2)}, u32[]{:S(2)}) %collective-permute-start.3) | collective-permute-done | bytes 110624 | tf_op jit(solution)/shard_map/ppermute | solution.py:315
  19.7 1.6 %collective-permute-done.2 = bf16[432,128]{1,0:T(8,128)(2,1)S(1)} collective-permute-done((bf16[432,128]{1,0:T(8,128)(2,1)S(1)}, bf16[432,128]{1,0:T(8,128)(2,1)S(1)}, u32[]{:S(2)}, u32[]{:S(2)}) %collective-permute-start.2) | collective-permute-done | bytes 110624 | tf_op jit(solution)/shard_map/ppermute | solution.py:315
  21.3 0.0 collective-permute-done.head.guess_head
  21.3 0.8 pad_maximum_fusion
  22.1 0.0 all-gather.3.cloned.1.call-update
  22.1 0.0 copy-done.4
  22.1 0.0 copy-start
  22.2 2.0 %copy-done = bf16[4,3,3,3,128,128]{5,4,3,2,1,0:T(8,128)(2,1)S(1)} copy-done((bf16[4,3,3,3,128,128]{5,4,3,2,1,0:T(8,128)(2,1)S(1)}, bf16[4,3,3,3,128,128]{5,4,3,2,1,0:T(8,128)(2,1)}, u32[]{:S(2)}) %copy-start) | copy-done | bytes 3538968
  24.2 4.2 %first.1 = (f32[512,128]{1,0:T(8,128)S(1)}, bf16[8,432,128]{2,1,0:T(8,128)(2,1)S(1)}) custom-call(f32[512,128]{1,0:T(8,128)S(1)} %collective-permute-done.head.guess_head, f32[4,128]{1,0:T(4,128)S(1)} %copy-done.4, bf16[4,8,432,128]{3,2,1,0:T(8,128)(2,1)S(1)} %bitcast.12), custom_call_target="tpu_custom_call" | custom-call | flops 4 | bytes 4 | tf_op jit(solution)/shard_map/first/pallas_call | solution.py:284
  28.4 0.0 copy-start.3
  28.4 1.0 collective-permute-start.4
  29.4 5.5 %collective-permute-done.4.head = f32[512,128]{1,0:T(8,128)S(1)} collective-permute-done((f32[512,128]{1,0:T(8,128)S(1)}, f32[512,128]{1,0:T(8,128)S(1)}, u32[]{:S(2)}, u32[]{:S(2)}) %collective-permute-start.4) | collective-permute-done | bytes 262176 | tf_op jit(solution)/shard_map/ppermute | solution.py:312
  34.9 3.3 %second.1 = (f32[512,128]{1,0:T(8,128)S(1)}, f32[512,128]{1,0:T(8,128)S(1)}) custom-call(f32[512,128]{1,0:T(8,128)S(1)} %collective-permute-done.4.head, f32[512,128]{1,0:T(8,128)S(1)} %collective-permute-done.head.guess_head, bf16[4,8,432,128]{3,2,1,0:T(8,128)(2,1)S(1)} %bitcast.13, f32[4,128]{1,0:T(4,128)S(1)} %copy-done.4), custom_call_target="tpu_custom_call" | custom-call | flops 4 | bytes 4 | tf_op jit(solution)/shard_map/second/pallas_call | solution.py:284
  38.2 0.1 collective-permute-start.5
  38.3 6.4 %collective-permute-start.6 = (f32[512,128]{1,0:T(8,128)S(1)}, f32[512,128]{1,0:T(8,128)S(1)}, u32[]{:S(2)}, u32[]{:S(2)}) collective-permute-start(f32[512,128]{1,0:T(8,128)S(1)} %get-tuple-element.39.m0), channel_id=1, source_target_pairs={{0,16},{8,24},{16,0},{24,8},{1,17},{9,25},{17,1},{25,9},{2,18},{10... | collective-permute-start | bytes 786440 | tf_op jit(solution)/shard_map/ppermute | solution.py:315
  44.7 0.0 collective-permute-start.7
  44.7 4.9 %collective-permute-done.5.m1 = f32[512,128]{1,0:T(8,128)S(1)} collective-permute-done((f32[512,128]{1,0:T(8,128)S(1)}, f32[512,128]{1,0:T(8,128)S(1)}, u32[]{:S(2)}, u32[]{:S(2)}) %collective-permute-start.5) | collective-permute-done | bytes 262176 | tf_op jit(solution)/shard_map/ppermute | solution.py:315
  49.5 6.1 %collective-permute-done.6.m2 = f32[512,128]{1,0:T(8,128)S(1)} collective-permute-done((f32[512,128]{1,0:T(8,128)S(1)}, f32[512,128]{1,0:T(8,128)S(1)}, u32[]{:S(2)}, u32[]{:S(2)}) %collective-permute-start.6) | collective-permute-done | bytes 262176 | tf_op jit(solution)/shard_map/ppermute | solution.py:315
  55.6 0.0 collective-permute-done.7.m3
  55.6 0.0 all-gather.3.cloned.1.call-done
  55.6 0.7 collective-permute-start.9
  56.3 1.3 %collective-permute-start.11 = (f32[512,128]{1,0:T(8,128)S(1)}, f32[512,128]{1,0:T(8,128)S(1)}, u32[]{:S(2)}, u32[]{:S(2)}) collective-permute-start(f32[512,128]{1,0:T(8,128)S(1)} %get-tuple-element.50.term), channel_id=1, source_target_pairs={{0,24},{1,25},{2,26},{3,27},{4,28},{5,29},{6,30},{7,31},{32,56},{3... | collective-permute-start | bytes 786440 | tf_op jit(solution)/shard_map/ppermute | solution.py:342
  57.6 0.0 copy-start.2
  57.6 1.7 %copy-done.2 = bf16[24,432,128]{2,1,0:T(8,128)(2,1)S(1)} copy-done((bf16[24,432,128]{2,1,0:T(8,128)(2,1)S(1)}, bf16[24,432,128]{2,1,0:T(8,128)(2,1)}, u32[]{:S(2)}) %copy-start.2) | copy-done | bytes 2654232
  59.3 3.1 %third.1 = (f32[512,128]{1,0:T(8,128)S(1)}, f32[4,512,128]{2,1,0:T(8,128)S(1)}, bf16[4,8,432,128]{3,2,1,0:T(8,128)(2,1)S(1)}, bf16[8,432,128]{2,1,0:T(8,128)(2,1)S(1)}, bf16[4,432,128]{2,1,0:T(8,128)(2,1)S(1)}) custom-call(f32[512,128]{1,0:T(8,128)S(1)} %get-tuple-element.39.m0, f32[512,128]{1,0:T(8,128)S(1)} %collective-permute-done.5.m1, ...), custom_call_target="tpu_custom_call" | custom-call | flops 3 | bytes 3 | tf_op jit(solution)/shard_map/third/pallas_call | solution.py:284
  62.5 1.3 %collective-permute-start.8 = (f32[512,128]{1,0:T(8,128)S(1)}, f32[512,128]{1,0:T(8,128)S(1)}, u32[]{:S(2)}, u32[]{:S(2)}) collective-permute-start(f32[512,128]{1,0:T(8,128)S(1)} %get-tuple-element.49.point), channel_id=1, source_target_pairs={{0,32},{32,64},{64,96},{96,128},{128,160},{160,192},{192,224},{1,3... | collective-permute-start | bytes 786440 | tf_op jit(solution)/shard_map/ppermute | solution.py:318
  63.8 0.0 collective-permute-done.9.f1
  63.8 0.7 collective-permute-start.10
  64.5 0.7 collective-permute-start.13
  65.1 5.9 %collective-permute-done.8.hop = f32[512,128]{1,0:T(8,128)S(1)} collective-permute-done((f32[512,128]{1,0:T(8,128)S(1)}, f32[512,128]{1,0:T(8,128)S(1)}, u32[]{:S(2)}, u32[]{:S(2)}) %collective-permute-start.8) | collective-permute-done | bytes 262176 | tf_op jit(solution)/shard_map/ppermute | solution.py:318
  71.0 0.0 collective-permute-done.11.f3
  71.1 0.0 collective-permute-done.10.f2
  71.1 0.0 copy-done.3
  71.1 4.1 %fourth.1 = (f32[512,128]{1,0:T(8,128)}, f32[512,128]{1,0:T(8,128)S(1)}, f32[512,128]{1,0:T(8,128)S(1)}, f32[4,512,128]{2,1,0:T(8,128)S(1)}) custom-call(f32[512,128]{1,0:T(8,128)S(1)} %bitcast.17, f32[512,128]{1,0:T(8,128)S(1)} %collective-permute-done.8.hop, f32[512,128]{1,0:T(8,128)S(1)} %get-tuple-element.49.point, ...), custom_call_target="tpu_custom_call" | custom-call | flops 6000000000 | bytes 20000000 | tf_op jit(solution)/shard_map/fourth/pallas_call | solution.py:284
  75.2 0.7 collective-permute-start.12
  75.9 0.8 defect.1
  76.7 0.7 collective-permute-start.15
  77.4 0.0 collective-permute-done.13.mine
  77.4 0.3 collective-permute-start.14
  77.7 0.0 collective-permute-done.12.came
  77.7 0.0 collective-permute-done.15.defect
  77.7 1.7 %collective-permute-done.14.other = bf16[4,432,128]{2,1,0:T(8,128)(2,1)S(1)} collective-permute-done((bf16[4,432,128]{2,1,0:T(8,128)(2,1)S(1)}, bf16[4,432,128]{2,1,0:T(8,128)(2,1)S(1)}, u32[]{:S(2)}, u32[]{:S(2)}) %collective-permute-start.14) | collective-permute-done | bytes 442400 | tf_op jit(solution)/shard_map/ppermute | solution.py:361
  79.4 0.7 collective-permute-start.16
  80.1 0.7 collective-permute-start.17
  80.8 0.0 collective-permute-done.16.came
  80.8 0.0 collective-permute-done.17.defect
  80.9 0.7 collective-permute-start.18
  81.5 0.0 collective-permute-done.18.came
  81.6 0.0 copy-start.1
  81.6 1.6 %collective-permute-start.19 = (f32[512,128]{1,0:T(8,128)S(1)}, f32[512,128]{1,0:T(8,128)S(1)}, u32[]{:S(2)}, u32[]{:S(2)}) collective-permute-start(f32[512,128]{1,0:T(8,128)S(1)} %get-tuple-element.62.value), channel_id=1, source_target_pairs={{64,96},{128,160},{192,224},{65,97},{129,161},{193,225},{66,98},{1... | collective-permute-start | bytes 786440 | tf_op jit(solution)/shard_map/ppermute | solution.py:318
  83.2 29.4 %collective-permute-done.19.came = f32[512,128]{1,0:T(8,128)S(1)} collective-permute-done((f32[512,128]{1,0:T(8,128)S(1)}, f32[512,128]{1,0:T(8,128)S(1)}, u32[]{:S(2)}, u32[]{:S(2)}) %collective-permute-start.19) | collective-permute-done | bytes 262176 | tf_op jit(solution)/shard_map/ppermute | solution.py:318
  112.6 0.0 copy-done.1
  112.6 6.5 %last.1 = f32[4,512,128]{2,1,0:T(8,128)} custom-call(f32[512,128]{1,0:T(8,128)S(1)} %collective-permute-done.19.came, f32[512,128]{1,0:T(8,128)S(1)} %get-tuple-element.63.before, f32[512,128]{1,0:T(8,128)S(1)} %get-tuple-element.62.value, f32[512,128]{1,0:T(8,128)S(1)} %defect.1, f32[4,128]{1,0:T(4,128)S(1)} %copy-done.4, ...), custom_call_target="tpu_custom_call" | custom-call | flops 6 | bytes 6 | tf_op jit(solution)/shard_map/last/pallas_call | solution.py:284
  (5 shorter events, 0.1 us)
Async XLA Ops:
  7.2 15.0 %copy-start.4 = (f32[4,128]{1,0:T(4,128)S(1)}, f32[4,128]{1,0:T(4,128)}, u32[]{:S(2)}) copy-start(f32[4,128]{1,0:T(4,128)} %biases.5) | copy-start | bytes 6148
  7.2 48.4 %all-gather.3.cloned.1.call-start = ((), (), s32[]{:S(2)}) async-start(), calls=%async_computation | async-start | bytes 2985984 | tf_op jit(solution)/shard_map/all_gather | solution.py:329
  9.0 12.3 %collective-permute-start = (f32[512,128]{1,0:T(8,128)}, f32[512,128]{1,0:T(8,128)S(1)}, u32[]{:S(2)}, u32[]{:S(2)}) collective-permute-start(f32[512,128]{1,0:T(8,128)} %get-tuple-element.34), channel_id=1, source_target_pairs={{0,8},{8,16},{16,24},{24,32},{32,40},{40,48},{48,56},{56,64},{64,7... | collective-permute-start | bytes 786440 | tf_op jit(solution)/shard_map/ppermute | solution.py:312
  9.1 6.3 %collective-permute-start.1 = (bf16[432,128]{1,0:T(8,128)(2,1)}, bf16[432,128]{1,0:T(8,128)(2,1)S(1)}, u32[]{:S(2)}, u32[]{:S(2)}) collective-permute-start(bf16[432,128]{1,0:T(8,128)(2,1)} %get-tuple-element.35), channel_id=1, source_target_pairs={{0,24},{8,0},{16,8},{24,16},{1,25},{9,1},{17,9},{25,17},{2,26},{10... | collective-permute-start | bytes 331784 | tf_op jit(solution)/shard_map/ppermute | solution.py:315
  11.1 8.6 %collective-permute-start.3 = (bf16[432,128]{1,0:T(8,128)(2,1)}, bf16[432,128]{1,0:T(8,128)(2,1)S(1)}, u32[]{:S(2)}, u32[]{:S(2)}) collective-permute-start(bf16[432,128]{1,0:T(8,128)(2,1)} %get-tuple-element.35), channel_id=1, source_target_pairs={{0,8},{8,16},{16,24},{24,0},{1,9},{9,17},{17,25},{25,1},{2,10},{10... | collective-permute-start | bytes 331784 | tf_op jit(solution)/shard_map/ppermute | solution.py:315
  15.4 6.0 %collective-permute-start.2 = (bf16[432,128]{1,0:T(8,128)(2,1)S(1)}, bf16[432,128]{1,0:T(8,128)(2,1)S(1)}, u32[]{:S(2)}, u32[]{:S(2)}) collective-permute-start(bf16[432,128]{1,0:T(8,128)(2,1)S(1)} %collective-permute-done.1), channel_id=1, source_target_pairs={{0,24},{8,0},{16,8},{24,16},{1,25},{9,1},{17,9},{25,17},{2,26},{10... | collective-permute-start | bytes 331784 | tf_op jit(solution)/shard_map/ppermute | solution.py:315
  22.1 2.0 %copy-start = (bf16[4,3,3,3,128,128]{5,4,3,2,1,0:T(8,128)(2,1)S(1)}, bf16[4,3,3,3,128,128]{5,4,3,2,1,0:T(8,128)(2,1)}, u32[]{:S(2)}) copy-start(bf16[4,3,3,3,128,128]{5,4,3,2,1,0:T(8,128)(2,1)} %param.6) | copy-start | bytes 10616836
  28.4 42.7 %copy-start.3 = (f32[1,8,8,8,128]{4,3,2,1,0:T(8,128)S(1)}, f32[1,8,8,8,128]{4,3,2,1,0:T(8,128)}, u32[]{:S(2)}) copy-start(f32[1,8,8,8,128]{4,3,2,1,0:T(8,128)} %param.4) | copy-start | bytes 786436
  28.4 6.4 %collective-permute-start.4 = (f32[512,128]{1,0:T(8,128)S(1)}, f32[512,128]{1,0:T(8,128)S(1)}, u32[]{:S(2)}, u32[]{:S(2)}) collective-permute-start(f32[512,128]{1,0:T(8,128)S(1)} %get-tuple-element.37), channel_id=1, source_target_pairs={{0,8},{8,16},{16,24},{24,32},{32,40},{40,48},{48,56},{56,64},{64,7... | collective-permute-start | bytes 786440 | tf_op jit(solution)/shard_map/ppermute | solution.py:312
  38.2 11.3 %collective-permute-start.5 = (f32[512,128]{1,0:T(8,128)S(1)}, f32[512,128]{1,0:T(8,128)S(1)}, u32[]{:S(2)}, u32[]{:S(2)}) collective-permute-start(f32[512,128]{1,0:T(8,128)S(1)} %get-tuple-element.39.m0), channel_id=1, source_target_pairs={{0,24},{8,0},{16,8},{24,16},{1,25},{9,1},{17,9},{25,17},{2,26},{10... | collective-permute-start | bytes 786440 | tf_op jit(solution)/shard_map/ppermute | solution.py:315
  38.3 17.3 %collective-permute-start.6 = (f32[512,128]{1,0:T(8,128)S(1)}, f32[512,128]{1,0:T(8,128)S(1)}, u32[]{:S(2)}, u32[]{:S(2)}) collective-permute-start(f32[512,128]{1,0:T(8,128)S(1)} %get-tuple-element.39.m0), channel_id=1, source_target_pairs={{0,16},{8,24},{16,0},{24,8},{1,17},{9,25},{17,1},{25,9},{2,18},{10... | collective-permute-start | bytes 786440 | tf_op jit(solution)/shard_map/ppermute | solution.py:315
  44.7 11.0 %collective-permute-start.7 = (f32[512,128]{1,0:T(8,128)S(1)}, f32[512,128]{1,0:T(8,128)S(1)}, u32[]{:S(2)}, u32[]{:S(2)}) collective-permute-start(f32[512,128]{1,0:T(8,128)S(1)} %get-tuple-element.39.m0), channel_id=1, source_target_pairs={{0,8},{8,16},{16,24},{24,0},{1,9},{9,17},{17,25},{25,1},{2,10},{10... | collective-permute-start | bytes 786440 | tf_op jit(solution)/shard_map/ppermute | solution.py:315
  55.6 8.1 %collective-permute-start.9 = (f32[512,128]{1,0:T(8,128)S(1)}, f32[512,128]{1,0:T(8,128)S(1)}, u32[]{:S(2)}, u32[]{:S(2)}) collective-permute-start(f32[512,128]{1,0:T(8,128)S(1)} %get-tuple-element.50.term), channel_id=1, source_target_pairs={{0,8},{1,9},{2,10},{3,11},{4,12},{5,13},{6,14},{7,15},{32,40},{33,... | collective-permute-start | bytes 786440 | tf_op jit(solution)/shard_map/ppermute | solution.py:342
  56.3 14.8 %collective-permute-start.11 = (f32[512,128]{1,0:T(8,128)S(1)}, f32[512,128]{1,0:T(8,128)S(1)}, u32[]{:S(2)}, u32[]{:S(2)}) collective-permute-start(f32[512,128]{1,0:T(8,128)S(1)} %get-tuple-element.50.term), channel_id=1, source_target_pairs={{0,24},{1,25},{2,26},{3,27},{4,28},{5,29},{6,30},{7,31},{32,56},{3... | collective-permute-start | bytes 786440 | tf_op jit(solution)/shard_map/ppermute | solution.py:342
  57.6 1.8 %copy-start.2 = (bf16[24,432,128]{2,1,0:T(8,128)(2,1)S(1)}, bf16[24,432,128]{2,1,0:T(8,128)(2,1)}, u32[]{:S(2)}) copy-start(bf16[24,432,128]{2,1,0:T(8,128)(2,1)} %all-gather.3.cloned.1.call-done) | copy-start | bytes 7962628
  62.5 8.6 %collective-permute-start.8 = (f32[512,128]{1,0:T(8,128)S(1)}, f32[512,128]{1,0:T(8,128)S(1)}, u32[]{:S(2)}, u32[]{:S(2)}) collective-permute-start(f32[512,128]{1,0:T(8,128)S(1)} %get-tuple-element.49.point), channel_id=1, source_target_pairs={{0,32},{32,64},{64,96},{96,128},{128,160},{160,192},{192,224},{1,3... | collective-permute-start | bytes 786440 | tf_op jit(solution)/shard_map/ppermute | solution.py:318
  63.8 7.3 %collective-permute-start.10 = (f32[512,128]{1,0:T(8,128)S(1)}, f32[512,128]{1,0:T(8,128)S(1)}, u32[]{:S(2)}, u32[]{:S(2)}) collective-permute-start(f32[512,128]{1,0:T(8,128)S(1)} %collective-permute-done.9.f1), channel_id=1, source_target_pairs={{8,16},{9,17},{10,18},{11,19},{12,20},{13,21},{14,22},{15,23},{40,... | collective-permute-start | bytes 786440 | tf_op jit(solution)/shard_map/ppermute | solution.py:351
  64.5 12.9 %collective-permute-start.13 = (bf16[4,432,128]{2,1,0:T(8,128)(2,1)S(1)}, bf16[4,432,128]{2,1,0:T(8,128)(2,1)S(1)}, u32[]{:S(2)}, u32[]{:S(2)}) collective-permute-start(bf16[4,432,128]{2,1,0:T(8,128)(2,1)S(1)} %get-tuple-element.57), channel_id=1, source_target_pairs={{96,64},{160,128},{97,65},{161,129},{98,66},{162,130},{99,67},{163... | collective-permute-start | bytes 1327112 | tf_op jit(solution)/shard_map/ppermute | solution.py:318
  75.2 2.5 %collective-permute-start.12 = (f32[512,128]{1,0:T(8,128)S(1)}, f32[512,128]{1,0:T(8,128)S(1)}, u32[]{:S(2)}, u32[]{:S(2)}) collective-permute-start(f32[512,128]{1,0:T(8,128)S(1)} %get-tuple-element.53.corner.value), channel_id=1, source_target_pairs={{32,64},{33,65},{34,66},{35,67},{36,68},{37,69},{38,70},{39,71},{4... | collective-permute-start | bytes 786440 | tf_op jit(solution)/shard_map/ppermute | solution.py:318
  76.7 1.0 collective-permute-start.15
  77.4 2.1 %collective-permute-start.14 = (bf16[4,432,128]{2,1,0:T(8,128)(2,1)S(1)}, bf16[4,432,128]{2,1,0:T(8,128)(2,1)S(1)}, u32[]{:S(2)}, u32[]{:S(2)}) collective-permute-start(bf16[4,432,128]{2,1,0:T(8,128)(2,1)S(1)} %collective-permute-done.13.mine), channel_id=1, source_target_pairs={{0,1},{1,0},{2,3},{3,2},{4,5},{5,4},{6,7},{7,6},{8,9},{9,8},{10,11... | collective-permute-start | bytes 1327112 | tf_op jit(solution)/shard_map/ppermute | solution.py:361
  79.4 1.4 %collective-permute-start.16 = (f32[512,128]{1,0:T(8,128)S(1)}, f32[512,128]{1,0:T(8,128)S(1)}, u32[]{:S(2)}, u32[]{:S(2)}) collective-permute-start(f32[512,128]{1,0:T(8,128)S(1)} %next2.1), channel_id=1, source_target_pairs={{64,128},{65,129},{66,130},{67,131},{68,132},{69,133},{70,134},{71... | collective-permute-start | bytes 786440 | tf_op jit(solution)/shard_map/ppermute | solution.py:318
  80.1 0.7 collective-permute-start.17
  80.9 0.7 collective-permute-start.18
  81.6 31.0 %copy-start.1 = (bf16[4,3,3,3,128,128]{5,4,3,2,1,0:T(8,128)(2,1)S(1)}, bf16[4,3,3,3,128,128]{5,4,3,2,1,0:T(8,128)(2,1)}, u32[]{:S(2)}) copy-start(bf16[4,3,3,3,128,128]{5,4,3,2,1,0:T(8,128)(2,1)} %param.6) | copy-start | bytes 10616836
  81.6 31.0 %collective-permute-start.19 = (f32[512,128]{1,0:T(8,128)S(1)}, f32[512,128]{1,0:T(8,128)S(1)}, u32[]{:S(2)}, u32[]{:S(2)}) collective-permute-start(f32[512,128]{1,0:T(8,128)S(1)} %get-tuple-element.62.value), channel_id=1, source_target_pairs={{64,96},{128,160},{192,224},{65,97},{129,161},{193,225},{66,98},{1... | collective-permute-start | bytes 786440 | tf_op jit(solution)/shard_map/ppermute | solution.py:318
Sparse Core Ops, SparseCore 0:
  22.3 29.6 all-gather.2

commit v6 on v5

--- a/solution.py
+++ b/solution.py
@@ -78,20 +78,21 @@
     two.wait()
 
 
-def first_kernel(head, biases, kernels, out, lead, kept, sem, lsem):
-    for i in range(4):
-        pltpu.make_async_copy(kernels.at[i], kept.at[i], sem.at[i]).start()
-    pltpu.make_async_copy(kernels.at[0], lead, lsem).start()
+def load_kernel(kernels, kept, sem):
+    copy = pltpu.make_async_copy(kernels, kept, sem)
+    copy.start()
+    copy.wait()
+
+
+def first_kernel(head, kernels, biases, out):
     out[...] = head[...]
 
     def body(i, carry):
-        pltpu.make_async_copy(kernels.at[i], kept.at[i], sem.at[i]).wait()
         v = out[...]
-        out[...] = v + FINE * (conv(v, flat(kept[pl.ds(i, 1)])) + biases[pl.ds(i, 1)])
+        out[...] = v + FINE * (conv(v, flat(kernels[pl.ds(i, 1)])) + biases[pl.ds(i, 1)])
         return carry
 
     lax.fori_loop(0, 4, body, 0)
-    pltpu.make_async_copy(kernels.at[0], lead, lsem).wait()
 
 
 def second_kernel(head, guess_head, kernels, biases, message, term, buf):
@@ -140,31 +141,23 @@
     lax.fori_loop(first, X, body, 0)
 
 
-def third_kernel(m0, m1, m2, m3, own, others, out, stack, lead, top, part, sem):
-    x = lax.axis_index("x")
-
-    def copy(q, wait):
-        turn = lax.rem(q - x + X, X)
-
-        @pl.when(turn == 0)
-        def _():
-            one = pltpu.make_async_copy(own, lead.at[q], sem.at[q])
-            one.wait() if wait else one.start()
-
-        @pl.when(turn != 0)
-        def _():
-            one = pltpu.make_async_copy(others.at[:, turn - 1], lead.at[q], sem.at[q])
-            one.wait() if wait else one.start()
-
-    for q in (1, 2, 3, 0):
-        copy(q, False)
+def third_kernel(
+    m0, m1, m2, m3, kernels, p0, p1, p2, p3, o0, o1, o2, o3, out, stack, lead, top, part
+):
+    x, y, core = lax.axis_index("x"), lax.axis_index("y"), lax.axis_index("core")
+    lead[pl.ds(x, 1)] = kernels[pl.ds(0, 1)]
+    for offset, mine, other in ((0, p0, o0), (3, p1, o1), (1, p2, o2), (2, p3, o3)):
+        at = lax.rem(y + offset, 4) * 2
+        for r in range(1, X):
+            q = pl.ds(lax.rem(x + r, X), 1)
+            lead[q, pl.ds(at + core, 1)] = mine[r - 1].reshape(1, 1, SHARE, CH)
+            lead[q, pl.ds(at + 1 - core, 1)] = other[r - 1].reshape(1, 1, SHARE, CH)
     for r, term in enumerate((m0, m1, m2, m3)):
         stack[pl.ds(lax.rem(x + r, X), 1)] = term[...].reshape(1, ROWS, CH)
     out[...] = stack[0]
-    coarse_steps(out, stack, lead, 1, lambda q: copy(q, True))
-    copy(0, True)
+    coarse_steps(out, stack, lead, 1)
     top[...] = lead[X - 1]
-    part[...] = lead[X - 1, pl.ds(lax.axis_index("core") * 4, 4)]
+    part[...] = lead[X - 1, pl.ds(core * 4, 4)]
 
 
 def fourth_kernel(
@@ -325,27 +318,34 @@
     guess_head = next_layer(guess_corner)
     shares = [from_ahead(share, 1), None, from_ahead(share, 3)]
     shares[1] = from_ahead(shares[0], 1)
-    guess_head, *shares = barrier((guess_head, *shares))
-    others = lax.all_gather(jnp.stack(shares), BATCH)
-    point, own = call(
-        first_kernel, "first", (state, weight), 4, (guess_head, biases, kernels), "vvh",
-        [pltpu.VMEM((4,) + WHOLE, jnp.bfloat16), dma((4,)), dma(())], out_places="vh", limit=48,
+    (kept,) = call(
+        load_kernel, "load", (jax.ShapeDtypeStruct((4,) + WHOLE, jnp.bfloat16),), 0,
+        (barrier((kernels, guess_corner))[0],), "h", [dma(())],
+    )
+    (point,) = call(
+        first_kernel, "first", (state,), 4, (guess_head, kept, biases), "vvv",
     )
     head = next_layer(point)
+    first_piece = jnp.stack(barrier((point, *shares))[1:])
+    pieces = [first_piece] + [
+        lax.ppermute(first_piece, "y", [(i, (i + r) % 4) for i in range(4)]) for r in (1, 3, 2)
+    ]
     message, term = call(
         second_kernel, "second", (state, state), 4,
-        (head, guess_head, barrier((kernels, point))[0], biases),
+        (head, guess_head, kept, biases),
         "vvvv", [buffer],
     )
-    m1, m2, m3 = (from_ahead(message, r) for r in (1, 2, 3))
-    others, term, m1, m2, m3 = barrier((others, term, m1, m2, m3))
+    m2, m3, m1 = (from_ahead(message, r) for r in (2, 3, 1))
+    pieces, m2, m3 = barrier((pieces, m2, m3))
+    pieces += [lax.ppermute(p, "core", [(0, 1), (1, 0)]) for p in pieces]
+    term, m1, m2, m3 = barrier((term, m1, m2, m3))
     f1, f3 = (lax.ppermute(term, "x", [(0, r)]) for r in (1, 3))
     stacked = jax.ShapeDtypeStruct((X, ROWS, CH), jnp.float32)
     point, stack, lead, top, part = call(
         third_kernel, "third",
         (state, stacked, jax.ShapeDtypeStruct((X,) + WHOLE, jnp.bfloat16), weight,
          jax.ShapeDtypeStruct((4, SHARE, CH), jnp.bfloat16)),
-        3, (message, m1, m2, m3, own, others), "vvvvhh", [dma((X,))],
+        3, (message, m1, m2, m3, kept, *pieces), "v" * 13,
     )
     hop = along_z(point, *((i, i + 1) for i in range(Z - 1)))
     f2 = lax.ppermute(f1, "x", [(1, 2)])
@@ -375,7 +375,7 @@
     came = along_z(value, (2, 3), (4, 5), (6, 7))
     (states,) = call(
         last_kernel, "last", (jax.ShapeDtypeStruct((4, ROWS, CH), jnp.float32),), 6,
-        (came, before, value, defect, biases, stack, lead, kernels), "v" * 8,
+        (came, before, value, defect, biases, stack, lead, kept), "v" * 8,
         [buffer, pltpu.VMEM((4, ROWS, CH), jnp.float32), dma((4,))], out_places="h",
     )
     volume = (8, 8, 8, CH)

time: 128 us -> 111 us (0.87)
  the two profiles are of different devices: /device:TPU:230 before, /device:TPU:226 now
where the time goes in v6:
time: 111 us
  waiting for transfers between devices  59.1 us (53%)
  starting transfers between devices  28.1 us (25%)
  Pallas kernels  20.8 us (19%)
  local copies, waits for them, and re-layouts  2.01 us (2%)
    ppermute x8, waiting for transfers between devices, along_z(): return lax.ppermute(v, 'z', pairs)  36.3 us
    pallas_call x13, Pallas kernels, call(): pl.pallas_call(body, name=name, out_shape=outs, in_specs=[specs[p] for p...  20.8 us
    ppermute x6, waiting for transfers between devices, from_ahead(): return lax.ppermute(v, 'x', [(i, (i - r) % X) for i in range(X)])  9.57 us
    ppermute x2, waiting for transfers between devices, shards(): f1, f3 = (lax.ppermute(term, 'x', [(0, r)]) for r in (1, 3))  8.66 us
    ppermute x6, starting transfers between devices, from_ahead(): return lax.ppermute(v, 'x', [(i, (i - r) % X) for i in range(X)])  8.56 us
    ppermute x8, starting transfers between devices, along_z(): return lax.ppermute(v, 'z', pairs)  6.64 us
    ppermute x3, starting transfers between devices, shards(): lax.ppermute(first_piece, 'y', [(i, (i + r) % 4) for i in range(4)])  5.3 us
    ppermute x2, starting transfers between devices, next_layer(): lax.ppermute(v, LAYER, [(i, (i + 1) % (X * Z)) for i in range(X * Z)])  3.13 us
  transfers between devices with their start and end apart: 27, of which 11 were waited for; matrix products, arithmetic and copies ran while one was open for 0% of the time, Pallas kernels for 13%

profile of v6, /device:TPU:226, one launch (start us, length us, event | category | flops | bytes accessed | tf_op | source)
XLA Modules:
  0.0 111.2 jit_solution(861399016897675558)
XLA Ops:
  0.6 1.8 %prepare.1 = (f32[512,128]{1,0:T(8,128)}, bf16[432,128]{1,0:T(8,128)(2,1)}) custom-call(f32[4,512,128]{2,1,0:T(8,128)} %bitcast.14, f32[512,128]{1,0:T(8,128)} %bitcast.12, bf16[4,8,432,128]{3,2,1,0:T(8,128)(2,1)} %bitcast.10), custom_call_target="tpu_custom_call" | custom-call | tf_op jit(solution)/shard_map/prepare/pallas_call | solution.py:277
  2.4 0.0 copy-start.2
  2.4 1.6 %collective-permute-start = (f32[512,128]{1,0:T(8,128)}, f32[512,128]{1,0:T(8,128)S(1)}, u32[]{:S(2)}, u32[]{:S(2)}) collective-permute-start(f32[512,128]{1,0:T(8,128)} %get-tuple-element.36), channel_id=1, source_target_pairs={{0,8},{8,16},{16,24},{24,32},{32,40},{40,48},{48,56},{56,64},{64,7... | collective-permute-start | bytes 786440 | tf_op jit(solution)/shard_map/ppermute | solution.py:305
  4.0 0.5 collective-permute-start.3
  4.5 1.5 %collective-permute-start.5 = (bf16[432,128]{1,0:T(8,128)(2,1)}, bf16[432,128]{1,0:T(8,128)(2,1)S(1)}, u32[]{:S(2)}, u32[]{:S(2)}) collective-permute-start(bf16[432,128]{1,0:T(8,128)(2,1)} %get-tuple-element.40), channel_id=1, source_target_pairs={{0,8},{8,16},{16,24},{24,0},{1,9},{9,17},{17,25},{25,1},{2,10},{10... | collective-permute-start | bytes 331784 | tf_op jit(solution)/shard_map/ppermute | solution.py:308
  6.0 2.9 %collective-permute-done.3 = bf16[432,128]{1,0:T(8,128)(2,1)S(1)} collective-permute-done((bf16[432,128]{1,0:T(8,128)(2,1)}, bf16[432,128]{1,0:T(8,128)(2,1)S(1)}, u32[]{:S(2)}, u32[]{:S(2)}) %collective-permute-start.3) | collective-permute-done | bytes 110624 | tf_op jit(solution)/shard_map/ppermute | solution.py:308
  8.9 0.5 collective-permute-start.4
  9.5 2.0 %copy-done = bf16[4,3,3,3,128,128]{5,4,3,2,1,0:T(8,128)(2,1)S(1)} copy-done((bf16[4,3,3,3,128,128]{5,4,3,2,1,0:T(8,128)(2,1)S(1)}, bf16[4,3,3,3,128,128]{5,4,3,2,1,0:T(8,128)(2,1)}, u32[]{:S(2)}) %copy-start) | copy-done | bytes 3538968
  11.5 0.4 load.1.kernels
  11.9 0.0 collective-permute-done.head.guess_head
  11.9 3.3 %first.1 = f32[512,128]{1,0:T(8,128)S(1)} custom-call(f32[512,128]{1,0:T(8,128)S(1)} %collective-permute-done.head.guess_head, bf16[4,8,432,128]{3,2,1,0:T(8,128)(2,1)S(1)} %load.1.kernels, f32[4,128]{1,0:T(4,128)S(1)} %copy-done.2), custom_call_target="tpu_custom_call" | custom-call | flops 4 | bytes 4 | tf_op jit(solution)/shard_map/first/pallas_call | solution.py:277
  15.2 1.6 %collective-permute-start.1 = (f32[512,128]{1,0:T(8,128)S(1)}, f32[512,128]{1,0:T(8,128)S(1)}, u32[]{:S(2)}, u32[]{:S(2)}) collective-permute-start(f32[512,128]{1,0:T(8,128)S(1)} %first.1), channel_id=1, source_target_pairs={{0,8},{8,16},{16,24},{24,32},{32,40},{40,48},{48,56},{56,64},{64,7... | collective-permute-start | bytes 786440 | tf_op jit(solution)/shard_map/ppermute | solution.py:305
  16.8 0.0 collective-permute-done.5
  16.8 0.0 collective-permute-done.4
  16.8 1.7 %collective-permute-start.6 = (bf16[3,432,128]{2,1,0:T(8,128)(2,1)S(1)}, bf16[3,432,128]{2,1,0:T(8,128)(2,1)S(1)}, u32[]{:S(2)}, u32[]{:S(2)}) collective-permute-start(bf16[3,432,128]{2,1,0:T(8,128)(2,1)S(1)} %pad_maximum_fusion.p0), channel_id=1, source_target_pairs={{0,2},{2,4},{4,6},{6,0},{1,3},{3,5},{5,7},{7,1},{8,10},{10,12},{12... | collective-permute-start | bytes 995336 | tf_op jit(solution)/shard_map/ppermute | solution.py:331
  18.5 1.7 %collective-permute-start.7 = (bf16[3,432,128]{2,1,0:T(8,128)(2,1)S(1)}, bf16[3,432,128]{2,1,0:T(8,128)(2,1)S(1)}, u32[]{:S(2)}, u32[]{:S(2)}) collective-permute-start(bf16[3,432,128]{2,1,0:T(8,128)(2,1)S(1)} %pad_maximum_fusion.p0), channel_id=1, source_target_pairs={{0,6},{2,0},{4,2},{6,4},{1,7},{3,1},{5,3},{7,5},{8,14},{10,8},{12,... | collective-permute-start | bytes 995336 | tf_op jit(solution)/shard_map/ppermute | solution.py:331
  20.1 2.0 %collective-permute-start.8 = (bf16[3,432,128]{2,1,0:T(8,128)(2,1)S(1)}, bf16[3,432,128]{2,1,0:T(8,128)(2,1)S(1)}, u32[]{:S(2)}, u32[]{:S(2)}) collective-permute-start(bf16[3,432,128]{2,1,0:T(8,128)(2,1)S(1)} %pad_maximum_fusion.p0), channel_id=1, source_target_pairs={{0,4},{2,6},{4,0},{6,2},{1,5},{3,7},{5,1},{7,3},{8,12},{10,14},{12... | collective-permute-start | bytes 995336 | tf_op jit(solution)/shard_map/ppermute | solution.py:331
  22.1 0.9 collective-permute-done.1.head
  23.0 3.3 %second.1 = (f32[512,128]{1,0:T(8,128)S(1)}, f32[512,128]{1,0:T(8,128)S(1)}) custom-call(f32[512,128]{1,0:T(8,128)S(1)} %collective-permute-done.1.head, f32[512,128]{1,0:T(8,128)S(1)} %collective-permute-done.head.guess_head, bf16[4,8,432,128]{3,2,1,0:T(8,128)(2,1)S(1)} %load.1.kernels, f32[4,128]{1,0:T(4,128)S(1)} %copy-done.2), custom_call_target="tpu_custom_call" | custom-call | flops 4 | bytes 4 | tf_op jit(solution)/shard_map/second/pallas_call | solution.py:277
  26.4 0.4 collective-permute-start.10
  26.8 5.6 %collective-permute-start.9 = (f32[512,128]{1,0:T(8,128)S(1)}, f32[512,128]{1,0:T(8,128)S(1)}, u32[]{:S(2)}, u32[]{:S(2)}) collective-permute-start(f32[512,128]{1,0:T(8,128)S(1)} %get-tuple-element.38.m0), channel_id=1, source_target_pairs={{0,16},{8,24},{16,0},{24,8},{1,17},{9,25},{17,1},{25,9},{2,18},{10... | collective-permute-start | bytes 786440 | tf_op jit(solution)/shard_map/ppermute | solution.py:308
  32.4 0.0 collective-permute-done.6.p1
  32.4 0.0 collective-permute-start.2
  32.4 0.1 collective-permute-done.7.p2
  32.5 1.8 %collective-permute-done.8.p3 = bf16[3,432,128]{2,1,0:T(8,128)(2,1)S(1)} collective-permute-done((bf16[3,432,128]{2,1,0:T(8,128)(2,1)S(1)}, bf16[3,432,128]{2,1,0:T(8,128)(2,1)S(1)}, u32[]{:S(2)}, u32[]{:S(2)}) %collective-permute-start.8) | collective-permute-done | bytes 331808 | tf_op jit(solution)/shard_map/ppermute | solution.py:331
  34.3 3.1 %collective-permute-done.10.m3 = f32[512,128]{1,0:T(8,128)S(1)} collective-permute-done((f32[512,128]{1,0:T(8,128)S(1)}, f32[512,128]{1,0:T(8,128)S(1)}, u32[]{:S(2)}, u32[]{:S(2)}) %collective-permute-start.10) | collective-permute-done | bytes 262176 | tf_op jit(solution)/shard_map/ppermute | solution.py:308
  37.3 1.8 %collective-permute-done.9.m2 = f32[512,128]{1,0:T(8,128)S(1)} collective-permute-done((f32[512,128]{1,0:T(8,128)S(1)}, f32[512,128]{1,0:T(8,128)S(1)}, u32[]{:S(2)}, u32[]{:S(2)}) %collective-permute-start.9) | collective-permute-done | bytes 262176 | tf_op jit(solution)/shard_map/ppermute | solution.py:308
  39.2 0.0 collective-permute-start.11
  39.2 0.5 collective-permute-start.12
  39.7 0.0 collective-permute-start.13
  39.7 0.5 collective-permute-start.14
  40.2 1.7 %collective-permute-done.2.m1 = f32[512,128]{1,0:T(8,128)S(1)} collective-permute-done((f32[512,128]{1,0:T(8,128)S(1)}, f32[512,128]{1,0:T(8,128)S(1)}, u32[]{:S(2)}, u32[]{:S(2)}) %collective-permute-start.2) | collective-permute-done | bytes 262176 | tf_op jit(solution)/shard_map/ppermute | solution.py:308
  41.9 1.4 %collective-permute-start.16 = (f32[512,128]{1,0:T(8,128)S(1)}, f32[512,128]{1,0:T(8,128)S(1)}, u32[]{:S(2)}, u32[]{:S(2)}) collective-permute-start(f32[512,128]{1,0:T(8,128)S(1)} %get-tuple-element.54.term), channel_id=1, source_target_pairs={{0,8},{1,9},{2,10},{3,11},{4,12},{5,13},{6,14},{7,15},{32,40},{33,... | collective-permute-start | bytes 786440 | tf_op jit(solution)/shard_map/ppermute | solution.py:342
  43.4 8.7 %collective-permute-done.16.f1 = f32[512,128]{1,0:T(8,128)S(1)} collective-permute-done((f32[512,128]{1,0:T(8,128)S(1)}, f32[512,128]{1,0:T(8,128)S(1)}, u32[]{:S(2)}, u32[]{:S(2)}) %collective-permute-start.16) | collective-permute-done | bytes 262176 | tf_op jit(solution)/shard_map/ppermute | solution.py:342
  52.0 0.7 collective-permute-start.18
  52.7 0.0 collective-permute-done.11.o0
  52.7 1.3 %collective-permute-start.17 = (f32[512,128]{1,0:T(8,128)S(1)}, f32[512,128]{1,0:T(8,128)S(1)}, u32[]{:S(2)}, u32[]{:S(2)}) collective-permute-start(f32[512,128]{1,0:T(8,128)S(1)} %collective-permute-done.16.f1), channel_id=1, source_target_pairs={{8,16},{9,17},{10,18},{11,19},{12,20},{13,21},{14,22},{15,23},{40,... | collective-permute-start | bytes 786440 | tf_op jit(solution)/shard_map/ppermute | solution.py:351
  54.0 0.0 collective-permute-done.12.o1
  54.0 0.0 collective-permute-done.13.o2
  54.0 0.0 collective-permute-done.14.o3
  54.0 2.9 %third.1 = (f32[512,128]{1,0:T(8,128)S(1)}, f32[4,512,128]{2,1,0:T(8,128)S(1)}, bf16[4,8,432,128]{3,2,1,0:T(8,128)(2,1)S(1)}, bf16[8,432,128]{2,1,0:T(8,128)(2,1)S(1)}, bf16[4,432,128]{2,1,0:T(8,128)(2,1)S(1)}) custom-call(f32[512,128]{1,0:T(8,128)S(1)} %get-tuple-element.38.m0, f32[512,128]{1,0:T(8,128)S(1)} %collective-permute-done.2.m1, ...), custom_call_target="tpu_custom_call" | custom-call | flops 3 | bytes 3 | tf_op jit(solution)/shard_map/third/pallas_call | solution.py:277
  56.9 1.3 %collective-permute-start.15 = (f32[512,128]{1,0:T(8,128)S(1)}, f32[512,128]{1,0:T(8,128)S(1)}, u32[]{:S(2)}, u32[]{:S(2)}) collective-permute-start(f32[512,128]{1,0:T(8,128)S(1)} %get-tuple-element.53.point), channel_id=1, source_target_pairs={{0,32},{32,64},{64,96},{96,128},{128,160},{160,192},{192,224},{1,3... | collective-permute-start | bytes 786440 | tf_op jit(solution)/shard_map/ppermute | solution.py:311
  58.2 0.7 collective-permute-start.20
  58.9 0.0 collective-permute-done.18.f3
  58.9 0.0 collective-permute-done.17.f2
  59.0 7.0 %collective-permute-done.15.hop = f32[512,128]{1,0:T(8,128)S(1)} collective-permute-done((f32[512,128]{1,0:T(8,128)S(1)}, f32[512,128]{1,0:T(8,128)S(1)}, u32[]{:S(2)}, u32[]{:S(2)}) %collective-permute-start.15) | collective-permute-done | bytes 262176 | tf_op jit(solution)/shard_map/ppermute | solution.py:311
  66.0 4.1 %fourth.1 = (f32[512,128]{1,0:T(8,128)}, f32[512,128]{1,0:T(8,128)S(1)}, f32[512,128]{1,0:T(8,128)S(1)}, f32[4,512,128]{2,1,0:T(8,128)S(1)}) custom-call(f32[512,128]{1,0:T(8,128)S(1)} %bitcast.13, f32[512,128]{1,0:T(8,128)S(1)} %collective-permute-done.15.hop, f32[512,128]{1,0:T(8,128)S(1)} %get-tuple-element.53.point, ...), custom_call_target="tpu_custom_call" | custom-call | flops 6000000000 | bytes 20000000 | tf_op jit(solution)/shard_map/fourth/pallas_call | solution.py:277
  70.1 0.7 collective-permute-start.19
  70.8 0.8 defect.1
  71.6 0.7 collective-permute-start.22
  72.3 0.0 collective-permute-done.20.mine
  72.3 0.1 collective-permute-start.21
  72.4 0.0 collective-permute-done.19.came
  72.4 0.0 collective-permute-done.22.defect
  72.4 1.7 %collective-permute-done.21.other = bf16[4,432,128]{2,1,0:T(8,128)(2,1)S(1)} collective-permute-done((bf16[4,432,128]{2,1,0:T(8,128)(2,1)S(1)}, bf16[4,432,128]{2,1,0:T(8,128)(2,1)S(1)}, u32[]{:S(2)}, u32[]{:S(2)}) %collective-permute-start.21) | collective-permute-done | bytes 442400 | tf_op jit(solution)/shard_map/ppermute | solution.py:361
  74.2 0.7 collective-permute-start.23
  74.8 0.7 collective-permute-start.24
  75.5 0.0 collective-permute-done.23.came
  75.6 0.0 collective-permute-done.24.defect
  75.6 0.7 collective-permute-start.25
  76.3 0.0 collective-permute-done.25.came
  76.3 1.3 %collective-permute-start.26 = (f32[512,128]{1,0:T(8,128)S(1)}, f32[512,128]{1,0:T(8,128)S(1)}, u32[]{:S(2)}, u32[]{:S(2)}) collective-permute-start(f32[512,128]{1,0:T(8,128)S(1)} %get-tuple-element.66.value), channel_id=1, source_target_pairs={{64,96},{128,160},{192,224},{65,97},{129,161},{193,225},{66,98},{1... | collective-permute-start | bytes 786440 | tf_op jit(solution)/shard_map/ppermute | solution.py:311
  77.6 29.2 %collective-permute-done.26.came = f32[512,128]{1,0:T(8,128)S(1)} collective-permute-done((f32[512,128]{1,0:T(8,128)S(1)}, f32[512,128]{1,0:T(8,128)S(1)}, u32[]{:S(2)}, u32[]{:S(2)}) %collective-permute-start.26) | collective-permute-done | bytes 262176 | tf_op jit(solution)/shard_map/ppermute | solution.py:311
  106.9 4.2 %last.1 = f32[4,512,128]{2,1,0:T(8,128)} custom-call(f32[512,128]{1,0:T(8,128)S(1)} %collective-permute-done.26.came, f32[512,128]{1,0:T(8,128)S(1)} %get-tuple-element.67.before, f32[512,128]{1,0:T(8,128)S(1)} %get-tuple-element.66.value, f32[512,128]{1,0:T(8,128)S(1)} %defect.1, f32[4,128]{1,0:T(4,128)S(1)} %copy-done.2, ...), custom_call_target="tpu_custom_call" | custom-call | flops 6 | bytes 6 | tf_op jit(solution)/shard_map/last/pallas_call | solution.py:277
  (10 shorter events, 0.1 us)
Async XLA Ops:
  2.4 9.5 %copy-start.2 = (f32[4,128]{1,0:T(4,128)S(1)}, f32[4,128]{1,0:T(4,128)}, u32[]{:S(2)}) copy-start(f32[4,128]{1,0:T(4,128)} %biases.5) | copy-start | bytes 6148
  2.4 9.5 %collective-permute-start = (f32[512,128]{1,0:T(8,128)}, f32[512,128]{1,0:T(8,128)S(1)}, u32[]{:S(2)}, u32[]{:S(2)}) collective-permute-start(f32[512,128]{1,0:T(8,128)} %get-tuple-element.36), channel_id=1, source_target_pairs={{0,8},{8,16},{16,24},{24,32},{32,40},{40,48},{48,56},{56,64},{64,7... | collective-permute-start | bytes 786440 | tf_op jit(solution)/shard_map/ppermute | solution.py:305
  4.0 5.0 %collective-permute-start.3 = (bf16[432,128]{1,0:T(8,128)(2,1)}, bf16[432,128]{1,0:T(8,128)(2,1)S(1)}, u32[]{:S(2)}, u32[]{:S(2)}) collective-permute-start(bf16[432,128]{1,0:T(8,128)(2,1)} %get-tuple-element.40), channel_id=1, source_target_pairs={{0,24},{8,0},{16,8},{24,16},{1,25},{9,1},{17,9},{25,17},{2,26},{10... | collective-permute-start | bytes 331784 | tf_op jit(solution)/shard_map/ppermute | solution.py:308
  4.5 12.2 %collective-permute-start.5 = (bf16[432,128]{1,0:T(8,128)(2,1)}, bf16[432,128]{1,0:T(8,128)(2,1)S(1)}, u32[]{:S(2)}, u32[]{:S(2)}) collective-permute-start(bf16[432,128]{1,0:T(8,128)(2,1)} %get-tuple-element.40), channel_id=1, source_target_pairs={{0,8},{8,16},{16,24},{24,0},{1,9},{9,17},{17,25},{25,1},{2,10},{10... | collective-permute-start | bytes 331784 | tf_op jit(solution)/shard_map/ppermute | solution.py:308
  8.9 7.8 %collective-permute-start.4 = (bf16[432,128]{1,0:T(8,128)(2,1)S(1)}, bf16[432,128]{1,0:T(8,128)(2,1)S(1)}, u32[]{:S(2)}, u32[]{:S(2)}) collective-permute-start(bf16[432,128]{1,0:T(8,128)(2,1)S(1)} %collective-permute-done.3), channel_id=1, source_target_pairs={{0,24},{8,0},{16,8},{24,16},{1,25},{9,1},{17,9},{25,17},{2,26},{10... | collective-permute-start | bytes 331784 | tf_op jit(solution)/shard_map/ppermute | solution.py:308
  9.5 2.0 %copy-start = (bf16[4,3,3,3,128,128]{5,4,3,2,1,0:T(8,128)(2,1)S(1)}, bf16[4,3,3,3,128,128]{5,4,3,2,1,0:T(8,128)(2,1)}, u32[]{:S(2)}) copy-start(bf16[4,3,3,3,128,128]{5,4,3,2,1,0:T(8,128)(2,1)} %param.6) | copy-start | bytes 10616836
  15.2 7.8 %collective-permute-start.1 = (f32[512,128]{1,0:T(8,128)S(1)}, f32[512,128]{1,0:T(8,128)S(1)}, u32[]{:S(2)}, u32[]{:S(2)}) collective-permute-start(f32[512,128]{1,0:T(8,128)S(1)} %first.1), channel_id=1, source_target_pairs={{0,8},{8,16},{16,24},{24,32},{32,40},{40,48},{48,56},{56,64},{64,7... | collective-permute-start | bytes 786440 | tf_op jit(solution)/shard_map/ppermute | solution.py:305
  16.8 15.6 %collective-permute-start.6 = (bf16[3,432,128]{2,1,0:T(8,128)(2,1)S(1)}, bf16[3,432,128]{2,1,0:T(8,128)(2,1)S(1)}, u32[]{:S(2)}, u32[]{:S(2)}) collective-permute-start(bf16[3,432,128]{2,1,0:T(8,128)(2,1)S(1)} %pad_maximum_fusion.p0), channel_id=1, source_target_pairs={{0,2},{2,4},{4,6},{6,0},{1,3},{3,5},{5,7},{7,1},{8,10},{10,12},{12... | collective-permute-start | bytes 995336 | tf_op jit(solution)/shard_map/ppermute | solution.py:331
  18.5 14.0 %collective-permute-start.7 = (bf16[3,432,128]{2,1,0:T(8,128)(2,1)S(1)}, bf16[3,432,128]{2,1,0:T(8,128)(2,1)S(1)}, u32[]{:S(2)}, u32[]{:S(2)}) collective-permute-start(bf16[3,432,128]{2,1,0:T(8,128)(2,1)S(1)} %pad_maximum_fusion.p0), channel_id=1, source_target_pairs={{0,6},{2,0},{4,2},{6,4},{1,7},{3,1},{5,3},{7,5},{8,14},{10,8},{12,... | collective-permute-start | bytes 995336 | tf_op jit(solution)/shard_map/ppermute | solution.py:331
  20.1 14.2 %collective-permute-start.8 = (bf16[3,432,128]{2,1,0:T(8,128)(2,1)S(1)}, bf16[3,432,128]{2,1,0:T(8,128)(2,1)S(1)}, u32[]{:S(2)}, u32[]{:S(2)}) collective-permute-start(bf16[3,432,128]{2,1,0:T(8,128)(2,1)S(1)} %pad_maximum_fusion.p0), channel_id=1, source_target_pairs={{0,4},{2,6},{4,0},{6,2},{1,5},{3,7},{5,1},{7,3},{8,12},{10,14},{12... | collective-permute-start | bytes 995336 | tf_op jit(solution)/shard_map/ppermute | solution.py:331
  26.4 11.0 %collective-permute-start.10 = (f32[512,128]{1,0:T(8,128)S(1)}, f32[512,128]{1,0:T(8,128)S(1)}, u32[]{:S(2)}, u32[]{:S(2)}) collective-permute-start(f32[512,128]{1,0:T(8,128)S(1)} %get-tuple-element.38.m0), channel_id=1, source_target_pairs={{0,8},{8,16},{16,24},{24,0},{1,9},{9,17},{17,25},{25,1},{2,10},{10... | collective-permute-start | bytes 786440 | tf_op jit(solution)/shard_map/ppermute | solution.py:308
  26.8 12.4 %collective-permute-start.9 = (f32[512,128]{1,0:T(8,128)S(1)}, f32[512,128]{1,0:T(8,128)S(1)}, u32[]{:S(2)}, u32[]{:S(2)}) collective-permute-start(f32[512,128]{1,0:T(8,128)S(1)} %get-tuple-element.38.m0), channel_id=1, source_target_pairs={{0,16},{8,24},{16,0},{24,8},{1,17},{9,25},{17,1},{25,9},{2,18},{10... | collective-permute-start | bytes 786440 | tf_op jit(solution)/shard_map/ppermute | solution.py:308
  32.4 9.6 %collective-permute-start.2 = (f32[512,128]{1,0:T(8,128)S(1)}, f32[512,128]{1,0:T(8,128)S(1)}, u32[]{:S(2)}, u32[]{:S(2)}) collective-permute-start(f32[512,128]{1,0:T(8,128)S(1)} %get-tuple-element.38.m0), channel_id=1, source_target_pairs={{0,24},{8,0},{16,8},{24,16},{1,25},{9,1},{17,9},{25,17},{2,26},{10... | collective-permute-start | bytes 786440 | tf_op jit(solution)/shard_map/ppermute | solution.py:308
  39.2 13.5 %collective-permute-start.11 = (bf16[3,432,128]{2,1,0:T(8,128)(2,1)S(1)}, bf16[3,432,128]{2,1,0:T(8,128)(2,1)S(1)}, u32[]{:S(2)}, u32[]{:S(2)}) collective-permute-start(bf16[3,432,128]{2,1,0:T(8,128)(2,1)S(1)} %pad_maximum_fusion.p0), channel_id=1, source_target_pairs={{0,1},{1,0},{2,3},{3,2},{4,5},{5,4},{6,7},{7,6},{8,9},{9,8},{10,11... | collective-permute-start | bytes 995336 | tf_op jit(solution)/shard_map/ppermute | solution.py:340
  39.2 14.8 %collective-permute-start.12 = (bf16[3,432,128]{2,1,0:T(8,128)(2,1)S(1)}, bf16[3,432,128]{2,1,0:T(8,128)(2,1)S(1)}, u32[]{:S(2)}, u32[]{:S(2)}) collective-permute-start(bf16[3,432,128]{2,1,0:T(8,128)(2,1)S(1)} %collective-permute-done.6.p1), channel_id=1, source_target_pairs={{0,1},{1,0},{2,3},{3,2},{4,5},{5,4},{6,7},{7,6},{8,9},{9,8},{10,11... | collective-permute-start | bytes 995336 | tf_op jit(solution)/shard_map/ppermute | solution.py:340
  39.7 14.3 %collective-permute-start.13 = (bf16[3,432,128]{2,1,0:T(8,128)(2,1)S(1)}, bf16[3,432,128]{2,1,0:T(8,128)(2,1)S(1)}, u32[]{:S(2)}, u32[]{:S(2)}) collective-permute-start(bf16[3,432,128]{2,1,0:T(8,128)(2,1)S(1)} %collective-permute-done.7.p2), channel_id=1, source_target_pairs={{0,1},{1,0},{2,3},{3,2},{4,5},{5,4},{6,7},{7,6},{8,9},{9,8},{10,11... | collective-permute-start | bytes 995336 | tf_op jit(solution)/shard_map/ppermute | solution.py:340
  39.7 14.3 %collective-permute-start.14 = (bf16[3,432,128]{2,1,0:T(8,128)(2,1)S(1)}, bf16[3,432,128]{2,1,0:T(8,128)(2,1)S(1)}, u32[]{:S(2)}, u32[]{:S(2)}) collective-permute-start(bf16[3,432,128]{2,1,0:T(8,128)(2,1)S(1)} %collective-permute-done.8.p3), channel_id=1, source_target_pairs={{0,1},{1,0},{2,3},{3,2},{4,5},{5,4},{6,7},{7,6},{8,9},{9,8},{10,11... | collective-permute-start | bytes 995336 | tf_op jit(solution)/shard_map/ppermute | solution.py:340
  41.9 24.1 %copy-start.1 = (f32[1,8,8,8,128]{4,3,2,1,0:T(8,128)S(1)}, f32[1,8,8,8,128]{4,3,2,1,0:T(8,128)}, u32[]{:S(2)}) copy-start(f32[1,8,8,8,128]{4,3,2,1,0:T(8,128)} %param.4) | copy-start | bytes 786436
  41.9 10.1 %collective-permute-start.16 = (f32[512,128]{1,0:T(8,128)S(1)}, f32[512,128]{1,0:T(8,128)S(1)}, u32[]{:S(2)}, u32[]{:S(2)}) collective-permute-start(f32[512,128]{1,0:T(8,128)S(1)} %get-tuple-element.54.term), channel_id=1, source_target_pairs={{0,8},{1,9},{2,10},{3,11},{4,12},{5,13},{6,14},{7,15},{32,40},{33,... | collective-permute-start | bytes 786440 | tf_op jit(solution)/shard_map/ppermute | solution.py:342
  52.0 6.9 %collective-permute-start.18 = (f32[512,128]{1,0:T(8,128)S(1)}, f32[512,128]{1,0:T(8,128)S(1)}, u32[]{:S(2)}, u32[]{:S(2)}) collective-permute-start(f32[512,128]{1,0:T(8,128)S(1)} %get-tuple-element.54.term), channel_id=1, source_target_pairs={{0,24},{1,25},{2,26},{3,27},{4,28},{5,29},{6,30},{7,31},{32,56},{3... | collective-permute-start | bytes 786440 | tf_op jit(solution)/shard_map/ppermute | solution.py:342
  52.7 6.3 %collective-permute-start.17 = (f32[512,128]{1,0:T(8,128)S(1)}, f32[512,128]{1,0:T(8,128)S(1)}, u32[]{:S(2)}, u32[]{:S(2)}) collective-permute-start(f32[512,128]{1,0:T(8,128)S(1)} %collective-permute-done.16.f1), channel_id=1, source_target_pairs={{8,16},{9,17},{10,18},{11,19},{12,20},{13,21},{14,22},{15,23},{40,... | collective-permute-start | bytes 786440 | tf_op jit(solution)/shard_map/ppermute | solution.py:351
  56.9 9.1 %collective-permute-start.15 = (f32[512,128]{1,0:T(8,128)S(1)}, f32[512,128]{1,0:T(8,128)S(1)}, u32[]{:S(2)}, u32[]{:S(2)}) collective-permute-start(f32[512,128]{1,0:T(8,128)S(1)} %get-tuple-element.53.point), channel_id=1, source_target_pairs={{0,32},{32,64},{64,96},{96,128},{128,160},{160,192},{192,224},{1,3... | collective-permute-start | bytes 786440 | tf_op jit(solution)/shard_map/ppermute | solution.py:311
  58.2 14.1 %collective-permute-start.20 = (bf16[4,432,128]{2,1,0:T(8,128)(2,1)S(1)}, bf16[4,432,128]{2,1,0:T(8,128)(2,1)S(1)}, u32[]{:S(2)}, u32[]{:S(2)}) collective-permute-start(bf16[4,432,128]{2,1,0:T(8,128)(2,1)S(1)} %get-tuple-element.61), channel_id=1, source_target_pairs={{96,64},{160,128},{97,65},{161,129},{98,66},{162,130},{99,67},{163... | collective-permute-start | bytes 1327112 | tf_op jit(solution)/shard_map/ppermute | solution.py:311
  70.1 2.3 %collective-permute-start.19 = (f32[512,128]{1,0:T(8,128)S(1)}, f32[512,128]{1,0:T(8,128)S(1)}, u32[]{:S(2)}, u32[]{:S(2)}) collective-permute-start(f32[512,128]{1,0:T(8,128)S(1)} %get-tuple-element.57.corner.value), channel_id=1, source_target_pairs={{32,64},{33,65},{34,66},{35,67},{36,68},{37,69},{38,70},{39,71},{4... | collective-permute-start | bytes 786440 | tf_op jit(solution)/shard_map/ppermute | solution.py:311
  71.6 0.8 collective-permute-start.22
  72.3 1.9 %collective-permute-start.21 = (bf16[4,432,128]{2,1,0:T(8,128)(2,1)S(1)}, bf16[4,432,128]{2,1,0:T(8,128)(2,1)S(1)}, u32[]{:S(2)}, u32[]{:S(2)}) collective-permute-start(bf16[4,432,128]{2,1,0:T(8,128)(2,1)S(1)} %collective-permute-done.20.mine), channel_id=1, source_target_pairs={{0,1},{1,0},{2,3},{3,2},{4,5},{5,4},{6,7},{7,6},{8,9},{9,8},{10,11... | collective-permute-start | bytes 1327112 | tf_op jit(solution)/shard_map/ppermute | solution.py:361
  74.2 1.4 %collective-permute-start.23 = (f32[512,128]{1,0:T(8,128)S(1)}, f32[512,128]{1,0:T(8,128)S(1)}, u32[]{:S(2)}, u32[]{:S(2)}) collective-permute-start(f32[512,128]{1,0:T(8,128)S(1)} %next2.1), channel_id=1, source_target_pairs={{64,128},{65,129},{66,130},{67,131},{68,132},{69,133},{70,134},{71... | collective-permute-start | bytes 786440 | tf_op jit(solution)/shard_map/ppermute | solution.py:311
  74.8 0.7 collective-permute-start.24
  75.6 0.7 collective-permute-start.25
  76.3 30.5 %collective-permute-start.26 = (f32[512,128]{1,0:T(8,128)S(1)}, f32[512,128]{1,0:T(8,128)S(1)}, u32[]{:S(2)}, u32[]{:S(2)}) collective-permute-start(f32[512,128]{1,0:T(8,128)S(1)} %get-tuple-element.66.value), channel_id=1, source_target_pairs={{64,96},{128,160},{192,224},{65,97},{129,161},{193,225},{66,98},{1... | collective-permute-start | bytes 786440 | tf_op jit(solution)/shard_map/ppermute | solution.py:311

commit v7 on v6

--- a/solution.py
+++ b/solution.py
@@ -317,11 +317,11 @@
     )
     guess_head = next_layer(guess_corner)
     shares = [from_ahead(share, 1), None, from_ahead(share, 3)]
-    shares[1] = from_ahead(shares[0], 1)
     (kept,) = call(
         load_kernel, "load", (jax.ShapeDtypeStruct((4,) + WHOLE, jnp.bfloat16),), 0,
         (barrier((kernels, guess_corner))[0],), "h", [dma(())],
     )
+    shares[1] = from_ahead(barrier((shares[0], kept))[0], 1)
     (point,) = call(
         first_kernel, "first", (state,), 4, (guess_head, kept, biases), "vvv",
     )
@@ -338,8 +338,8 @@
     m2, m3, m1 = (from_ahead(message, r) for r in (2, 3, 1))
     pieces, m2, m3 = barrier((pieces, m2, m3))
     pieces += [lax.ppermute(p, "core", [(0, 1), (1, 0)]) for p in pieces]
-    term, m1, m2, m3 = barrier((term, m1, m2, m3))
-    f1, f3 = (lax.ppermute(term, "x", [(0, r)]) for r in (1, 3))
+    term, m3 = barrier((term, m3))
+    f3 = lax.ppermute(term, "x", [(0, 3)])
     stacked = jax.ShapeDtypeStruct((X, ROWS, CH), jnp.float32)
     point, stack, lead, top, part = call(
         third_kernel, "third",
@@ -348,7 +348,9 @@
         3, (message, m1, m2, m3, kept, *pieces), "v" * 13,
     )
     hop = along_z(point, *((i, i + 1) for i in range(Z - 1)))
-    f2 = lax.ppermute(f1, "x", [(1, 2)])
+    f3, term, _ = barrier((f3, term, point))
+    f2 = lax.ppermute(f3, "x", [(3, 2)])
+    f1 = lax.ppermute(term, "x", [(0, 1)])
     next_mine = along_z(part, (3, 2), (5, 4))
     residual, corner, start, stack = call(
         fourth_kernel, "fourth", (state,) * 3 + (stacked,), 1,

time: 111 us -> 113 us (1.018)
  the two profiles are of different devices: /device:TPU:226 before, /device:TPU:230 now
where the time goes in v7:
time: 113 us
  waiting for transfers between devices  59.3 us (52%)
  starting transfers between devices  27.1 us (24%)
  Pallas kernels  23.2 us (21%)
  local copies, waits for them, and re-layouts  2.01 us (2%)
    ppermute x8, waiting for transfers between devices, along_z(): return lax.ppermute(v, 'z', pairs)  34.6 us
    pallas_call x13, Pallas kernels, call(): pl.pallas_call(body, name=name, out_shape=outs, in_specs=[specs[p] for p...  23.2 us
    ppermute x6, starting transfers between devices, from_ahead(): return lax.ppermute(v, 'x', [(i, (i - r) % X) for i in range(X)])  7.88 us
    ppermute x8, starting transfers between devices, along_z(): return lax.ppermute(v, 'z', pairs)  6.64 us
    ppermute x1, waiting for transfers between devices, shards(): f3 = lax.ppermute(term, 'x', [(0, 3)])  6.49 us
    ppermute x3, waiting for transfers between devices, shards(): lax.ppermute(first_piece, 'y', [(i, (i + r) % 4) for i in range(4)])  5.75 us
    ppermute x6, waiting for transfers between devices, from_ahead(): return lax.ppermute(v, 'x', [(i, (i - r) % X) for i in range(X)])  5.58 us
    ppermute x3, starting transfers between devices, shards(): lax.ppermute(first_piece, 'y', [(i, (i + r) % 4) for i in range(4)])  5.3 us
  transfers between devices with their start and end apart: 27, of which 12 were waited for; matrix products, arithmetic and copies ran while one was open for 0% of the time, Pallas kernels for 13%

profile of v7, /device:TPU:230, one launch (start us, length us, event | category | flops | bytes accessed | tf_op | source)
XLA Modules:
  0.0 112.7 jit_solution(1337758925626346279)
XLA Ops:
  0.6 1.8 %prepare.1 = (f32[512,128]{1,0:T(8,128)}, bf16[432,128]{1,0:T(8,128)(2,1)}) custom-call(f32[4,512,128]{2,1,0:T(8,128)} %bitcast.14, f32[512,128]{1,0:T(8,128)} %bitcast.12, bf16[4,8,432,128]{3,2,1,0:T(8,128)(2,1)} %bitcast.10), custom_call_target="tpu_custom_call" | custom-call | tf_op jit(solution)/shard_map/prepare/pallas_call | solution.py:277
  2.4 0.1 collective-permute-start
  2.5 2.0 %collective-permute-start.3 = (bf16[432,128]{1,0:T(8,128)(2,1)}, bf16[432,128]{1,0:T(8,128)(2,1)S(1)}, u32[]{:S(2)}, u32[]{:S(2)}) collective-permute-start(bf16[432,128]{1,0:T(8,128)(2,1)} %get-tuple-element.40), channel_id=1, source_target_pairs={{0,24},{8,0},{16,8},{24,16},{1,25},{9,1},{17,9},{25,17},{2,26},{10... | collective-permute-start | bytes 331784 | tf_op jit(solution)/shard_map/ppermute | solution.py:308
  4.5 1.3 %collective-permute-start.5 = (bf16[432,128]{1,0:T(8,128)(2,1)}, bf16[432,128]{1,0:T(8,128)(2,1)S(1)}, u32[]{:S(2)}, u32[]{:S(2)}) collective-permute-start(bf16[432,128]{1,0:T(8,128)(2,1)} %get-tuple-element.40), channel_id=1, source_target_pairs={{0,8},{8,16},{16,24},{24,0},{1,9},{9,17},{17,25},{25,1},{2,10},{10... | collective-permute-start | bytes 331784 | tf_op jit(solution)/shard_map/ppermute | solution.py:308
  5.8 2.0 %copy-done = bf16[4,3,3,3,128,128]{5,4,3,2,1,0:T(8,128)(2,1)S(1)} copy-done((bf16[4,3,3,3,128,128]{5,4,3,2,1,0:T(8,128)(2,1)S(1)}, bf16[4,3,3,3,128,128]{5,4,3,2,1,0:T(8,128)(2,1)}, u32[]{:S(2)}) %copy-start) | copy-done | bytes 3538968
  7.8 0.4 load.1.kernels
  8.2 0.6 collective-permute-done.3
  8.8 0.7 collective-permute-start.4
  9.5 2.4 %collective-permute-done.head.guess_head = f32[512,128]{1,0:T(8,128)S(1)} collective-permute-done((f32[512,128]{1,0:T(8,128)}, f32[512,128]{1,0:T(8,128)S(1)}, u32[]{:S(2)}, u32[]{:S(2)}) %collective-permute-start) | collective-permute-done | bytes 262176 | tf_op jit(solution)/shard_map/ppermute | solution.py:305
  11.9 0.0 copy-done.2
  11.9 3.3 %first.1 = f32[512,128]{1,0:T(8,128)S(1)} custom-call(f32[512,128]{1,0:T(8,128)S(1)} %collective-permute-done.head.guess_head, bf16[4,8,432,128]{3,2,1,0:T(8,128)(2,1)S(1)} %load.1.kernels, f32[4,128]{1,0:T(4,128)S(1)} %copy-done.2), custom_call_target="tpu_custom_call" | custom-call | flops 4 | bytes 4 | tf_op jit(solution)/shard_map/first/pallas_call | solution.py:277
  15.2 2.6 %collective-permute-start.1 = (f32[512,128]{1,0:T(8,128)S(1)}, f32[512,128]{1,0:T(8,128)S(1)}, u32[]{:S(2)}, u32[]{:S(2)}) collective-permute-start(f32[512,128]{1,0:T(8,128)S(1)} %first.1), channel_id=1, source_target_pairs={{0,8},{8,16},{16,24},{24,32},{32,40},{40,48},{48,56},{56,64},{64,7... | collective-permute-start | bytes 786440 | tf_op jit(solution)/shard_map/ppermute | solution.py:305
  17.8 0.0 collective-permute-done.5
  17.8 0.0 collective-permute-done.4
  17.9 1.7 %collective-permute-start.6 = (bf16[3,432,128]{2,1,0:T(8,128)(2,1)S(1)}, bf16[3,432,128]{2,1,0:T(8,128)(2,1)S(1)}, u32[]{:S(2)}, u32[]{:S(2)}) collective-permute-start(bf16[3,432,128]{2,1,0:T(8,128)(2,1)S(1)} %pad_maximum_fusion.p0), channel_id=1, source_target_pairs={{0,2},{2,4},{4,6},{6,0},{1,3},{3,5},{5,7},{7,1},{8,10},{10,12},{12... | collective-permute-start | bytes 995336 | tf_op jit(solution)/shard_map/ppermute | solution.py:331
  19.5 1.7 %collective-permute-start.7 = (bf16[3,432,128]{2,1,0:T(8,128)(2,1)S(1)}, bf16[3,432,128]{2,1,0:T(8,128)(2,1)S(1)}, u32[]{:S(2)}, u32[]{:S(2)}) collective-permute-start(bf16[3,432,128]{2,1,0:T(8,128)(2,1)S(1)} %pad_maximum_fusion.p0), channel_id=1, source_target_pairs={{0,6},{2,0},{4,2},{6,4},{1,7},{3,1},{5,3},{7,5},{8,14},{10,8},{12,... | collective-permute-start | bytes 995336 | tf_op jit(solution)/shard_map/ppermute | solution.py:331
  21.2 2.0 %collective-permute-start.8 = (bf16[3,432,128]{2,1,0:T(8,128)(2,1)S(1)}, bf16[3,432,128]{2,1,0:T(8,128)(2,1)S(1)}, u32[]{:S(2)}, u32[]{:S(2)}) collective-permute-start(bf16[3,432,128]{2,1,0:T(8,128)(2,1)S(1)} %pad_maximum_fusion.p0), channel_id=1, source_target_pairs={{0,4},{2,6},{4,0},{6,2},{1,5},{3,7},{5,1},{7,3},{8,12},{10,14},{12... | collective-permute-start | bytes 995336 | tf_op jit(solution)/shard_map/ppermute | solution.py:331
  23.1 0.0 collective-permute-done.1.head
  23.1 3.3 %second.1 = (f32[512,128]{1,0:T(8,128)S(1)}, f32[512,128]{1,0:T(8,128)S(1)}) custom-call(f32[512,128]{1,0:T(8,128)S(1)} %collective-permute-done.1.head, f32[512,128]{1,0:T(8,128)S(1)} %collective-permute-done.head.guess_head, bf16[4,8,432,128]{3,2,1,0:T(8,128)(2,1)S(1)} %load.1.kernels, f32[4,128]{1,0:T(4,128)S(1)} %copy-done.2), custom_call_target="tpu_custom_call" | custom-call | flops 4 | bytes 4 | tf_op jit(solution)/shard_map/second/pallas_call | solution.py:277
  26.5 2.9 %collective-permute-start.10 = (f32[512,128]{1,0:T(8,128)S(1)}, f32[512,128]{1,0:T(8,128)S(1)}, u32[]{:S(2)}, u32[]{:S(2)}) collective-permute-start(f32[512,128]{1,0:T(8,128)S(1)} %get-tuple-element.39.m0), channel_id=1, source_target_pairs={{0,8},{8,16},{16,24},{24,0},{1,9},{9,17},{17,25},{25,1},{2,10},{10... | collective-permute-start | bytes 786440 | tf_op jit(solution)/shard_map/ppermute | solution.py:308
  29.4 0.0 collective-permute-start.9
  29.4 0.0 collective-permute-done.6.p1
  29.4 1.0 collective-permute-start.2
  30.4 3.9 %collective-permute-done.7.p2 = bf16[3,432,128]{2,1,0:T(8,128)(2,1)S(1)} collective-permute-done((bf16[3,432,128]{2,1,0:T(8,128)(2,1)S(1)}, bf16[3,432,128]{2,1,0:T(8,128)(2,1)S(1)}, u32[]{:S(2)}, u32[]{:S(2)}) %collective-permute-start.7) | collective-permute-done | bytes 331808 | tf_op jit(solution)/shard_map/ppermute | solution.py:331
  34.3 1.8 %collective-permute-done.8.p3 = bf16[3,432,128]{2,1,0:T(8,128)(2,1)S(1)} collective-permute-done((bf16[3,432,128]{2,1,0:T(8,128)(2,1)S(1)}, bf16[3,432,128]{2,1,0:T(8,128)(2,1)S(1)}, u32[]{:S(2)}, u32[]{:S(2)}) %collective-permute-start.8) | collective-permute-done | bytes 331808 | tf_op jit(solution)/shard_map/ppermute | solution.py:331
  36.1 2.7 %collective-permute-done.10.m3 = f32[512,128]{1,0:T(8,128)S(1)} collective-permute-done((f32[512,128]{1,0:T(8,128)S(1)}, f32[512,128]{1,0:T(8,128)S(1)}, u32[]{:S(2)}, u32[]{:S(2)}) %collective-permute-start.10) | collective-permute-done | bytes 262176 | tf_op jit(solution)/shard_map/ppermute | solution.py:308
  38.8 1.0 collective-permute-done.9.m2
  39.7 0.0 collective-permute-start.11
  39.7 0.5 collective-permute-start.12
  40.3 0.0 collective-permute-start.13
  40.3 0.5 collective-permute-start.14
  40.8 1.4 %collective-permute-done.2.m1 = f32[512,128]{1,0:T(8,128)S(1)} collective-permute-done((f32[512,128]{1,0:T(8,128)S(1)}, f32[512,128]{1,0:T(8,128)S(1)}, u32[]{:S(2)}, u32[]{:S(2)}) %collective-permute-start.2) | collective-permute-done | bytes 262176 | tf_op jit(solution)/shard_map/ppermute | solution.py:308
  42.2 1.5 %collective-permute-start.16 = (f32[512,128]{1,0:T(8,128)S(1)}, f32[512,128]{1,0:T(8,128)S(1)}, u32[]{:S(2)}, u32[]{:S(2)}) collective-permute-start(f32[512,128]{1,0:T(8,128)S(1)} %get-tuple-element.55.term), channel_id=1, source_target_pairs={{0,24},{1,25},{2,26},{3,27},{4,28},{5,29},{6,30},{7,31},{32,56},{3... | collective-permute-start | bytes 786440 | tf_op jit(solution)/shard_map/ppermute | solution.py:342
  43.6 0.0 collective-permute-done.11.o0
  43.6 0.0 collective-permute-done.12.o1
  43.7 0.0 collective-permute-done.13.o2
  43.7 0.0 collective-permute-done.14.o3
  43.7 2.9 %third.1 = (f32[512,128]{1,0:T(8,128)S(1)}, f32[4,512,128]{2,1,0:T(8,128)S(1)}, bf16[4,8,432,128]{3,2,1,0:T(8,128)(2,1)S(1)}, bf16[8,432,128]{2,1,0:T(8,128)(2,1)S(1)}, bf16[4,432,128]{2,1,0:T(8,128)(2,1)S(1)}) custom-call(f32[512,128]{1,0:T(8,128)S(1)} %get-tuple-element.39.m0, f32[512,128]{1,0:T(8,128)S(1)} %collective-permute-done.2.m1, ...), custom_call_target="tpu_custom_call" | custom-call | flops 3 | bytes 3 | tf_op jit(solution)/shard_map/third/pallas_call | solution.py:277
  46.6 6.5 %collective-permute-done.16.f3 = f32[512,128]{1,0:T(8,128)S(1)} collective-permute-done((f32[512,128]{1,0:T(8,128)S(1)}, f32[512,128]{1,0:T(8,128)S(1)}, u32[]{:S(2)}, u32[]{:S(2)}) %collective-permute-start.16) | collective-permute-done | bytes 262176 | tf_op jit(solution)/shard_map/ppermute | solution.py:342
  53.1 0.7 collective-permute-start.17
  53.7 1.3 %collective-permute-start.18 = (f32[512,128]{1,0:T(8,128)S(1)}, f32[512,128]{1,0:T(8,128)S(1)}, u32[]{:S(2)}, u32[]{:S(2)}) collective-permute-start(f32[512,128]{1,0:T(8,128)S(1)} %collective-permute-done.16.f3), channel_id=1, source_target_pairs={{24,16},{25,17},{26,18},{27,19},{28,20},{29,21},{30,22},{31,23},{5... | collective-permute-start | bytes 786440 | tf_op jit(solution)/shard_map/ppermute | solution.py:352
  55.0 1.3 %collective-permute-start.15 = (f32[512,128]{1,0:T(8,128)S(1)}, f32[512,128]{1,0:T(8,128)S(1)}, u32[]{:S(2)}, u32[]{:S(2)}) collective-permute-start(f32[512,128]{1,0:T(8,128)S(1)} %get-tuple-element.53.point), channel_id=1, source_target_pairs={{0,32},{32,64},{64,96},{96,128},{128,160},{160,192},{192,224},{1,3... | collective-permute-start | bytes 786440 | tf_op jit(solution)/shard_map/ppermute | solution.py:311
  56.3 0.7 collective-permute-start.20
  57.0 0.0 collective-permute-done.17.f1
  57.1 2.6 %collective-permute-done.18.f2 = f32[512,128]{1,0:T(8,128)S(1)} collective-permute-done((f32[512,128]{1,0:T(8,128)S(1)}, f32[512,128]{1,0:T(8,128)S(1)}, u32[]{:S(2)}, u32[]{:S(2)}) %collective-permute-start.18) | collective-permute-done | bytes 262176 | tf_op jit(solution)/shard_map/ppermute | solution.py:352
  59.7 4.1 %collective-permute-done.15.hop = f32[512,128]{1,0:T(8,128)S(1)} collective-permute-done((f32[512,128]{1,0:T(8,128)S(1)}, f32[512,128]{1,0:T(8,128)S(1)}, u32[]{:S(2)}, u32[]{:S(2)}) %collective-permute-start.15) | collective-permute-done | bytes 262176 | tf_op jit(solution)/shard_map/ppermute | solution.py:311
  63.8 4.1 %fourth.1 = (f32[512,128]{1,0:T(8,128)}, f32[512,128]{1,0:T(8,128)S(1)}, f32[512,128]{1,0:T(8,128)S(1)}, f32[4,512,128]{2,1,0:T(8,128)S(1)}) custom-call(f32[512,128]{1,0:T(8,128)S(1)} %bitcast.13, f32[512,128]{1,0:T(8,128)S(1)} %collective-permute-done.15.hop, f32[512,128]{1,0:T(8,128)S(1)} %get-tuple-element.53.point, ...), custom_call_target="tpu_custom_call" | custom-call | flops 6000000000 | bytes 20000000 | tf_op jit(solution)/shard_map/fourth/pallas_call | solution.py:277
  67.9 0.7 collective-permute-start.19
  68.6 0.8 defect.1
  69.4 0.7 collective-permute-start.22
  70.1 0.0 collective-permute-done.20.mine
  70.1 0.1 collective-permute-start.21
  70.2 0.0 collective-permute-done.19.came
  70.3 0.0 collective-permute-done.22.defect
  70.3 1.7 %collective-permute-done.21.other = bf16[4,432,128]{2,1,0:T(8,128)(2,1)S(1)} collective-permute-done((bf16[4,432,128]{2,1,0:T(8,128)(2,1)S(1)}, bf16[4,432,128]{2,1,0:T(8,128)(2,1)S(1)}, u32[]{:S(2)}, u32[]{:S(2)}) %collective-permute-start.21) | collective-permute-done | bytes 442400 | tf_op jit(solution)/shard_map/ppermute | solution.py:363
  72.0 0.7 collective-permute-start.23
  72.7 0.7 collective-permute-start.24
  73.4 0.0 collective-permute-done.23.came
  73.4 0.0 collective-permute-done.24.defect
  73.4 0.7 collective-permute-start.25
  74.1 0.0 collective-permute-done.25.came
  74.2 1.3 %collective-permute-start.26 = (f32[512,128]{1,0:T(8,128)S(1)}, f32[512,128]{1,0:T(8,128)S(1)}, u32[]{:S(2)}, u32[]{:S(2)}) collective-permute-start(f32[512,128]{1,0:T(8,128)S(1)} %get-tuple-element.68.value), channel_id=1, source_target_pairs={{64,96},{128,160},{192,224},{65,97},{129,161},{193,225},{66,98},{1... | collective-permute-start | bytes 786440 | tf_op jit(solution)/shard_map/ppermute | solution.py:311
  75.5 30.5 %collective-permute-done.26.came = f32[512,128]{1,0:T(8,128)S(1)} collective-permute-done((f32[512,128]{1,0:T(8,128)S(1)}, f32[512,128]{1,0:T(8,128)S(1)}, u32[]{:S(2)}, u32[]{:S(2)}) %collective-permute-start.26) | collective-permute-done | bytes 262176 | tf_op jit(solution)/shard_map/ppermute | solution.py:311
  106.0 6.5 %last.1 = f32[4,512,128]{2,1,0:T(8,128)} custom-call(f32[512,128]{1,0:T(8,128)S(1)} %collective-permute-done.26.came, f32[512,128]{1,0:T(8,128)S(1)} %get-tuple-element.69.before, f32[512,128]{1,0:T(8,128)S(1)} %get-tuple-element.68.value, f32[512,128]{1,0:T(8,128)S(1)} %defect.1, f32[4,128]{1,0:T(4,128)S(1)} %copy-done.2, ...), custom_call_target="tpu_custom_call" | custom-call | flops 6 | bytes 6 | tf_op jit(solution)/shard_map/last/pallas_call | solution.py:277
  (10 shorter events, 0.1 us)
Async XLA Ops:
  2.4 9.5 %collective-permute-start = (f32[512,128]{1,0:T(8,128)}, f32[512,128]{1,0:T(8,128)S(1)}, u32[]{:S(2)}, u32[]{:S(2)}) collective-permute-start(f32[512,128]{1,0:T(8,128)} %get-tuple-element.37), channel_id=1, source_target_pairs={{0,8},{8,16},{16,24},{24,32},{32,40},{40,48},{48,56},{56,64},{64,7... | collective-permute-start | bytes 786440 | tf_op jit(solution)/shard_map/ppermute | solution.py:305
  2.5 6.3 %collective-permute-start.3 = (bf16[432,128]{1,0:T(8,128)(2,1)}, bf16[432,128]{1,0:T(8,128)(2,1)S(1)}, u32[]{:S(2)}, u32[]{:S(2)}) collective-permute-start(bf16[432,128]{1,0:T(8,128)(2,1)} %get-tuple-element.40), channel_id=1, source_target_pairs={{0,24},{8,0},{16,8},{24,16},{1,25},{9,1},{17,9},{25,17},{2,26},{10... | collective-permute-start | bytes 331784 | tf_op jit(solution)/shard_map/ppermute | solution.py:308
  4.5 13.3 %collective-permute-start.5 = (bf16[432,128]{1,0:T(8,128)(2,1)}, bf16[432,128]{1,0:T(8,128)(2,1)S(1)}, u32[]{:S(2)}, u32[]{:S(2)}) collective-permute-start(bf16[432,128]{1,0:T(8,128)(2,1)} %get-tuple-element.40), channel_id=1, source_target_pairs={{0,8},{8,16},{16,24},{24,0},{1,9},{9,17},{17,25},{25,1},{2,10},{10... | collective-permute-start | bytes 331784 | tf_op jit(solution)/shard_map/ppermute | solution.py:308
  5.8 2.0 %copy-start = (bf16[4,3,3,3,128,128]{5,4,3,2,1,0:T(8,128)(2,1)S(1)}, bf16[4,3,3,3,128,128]{5,4,3,2,1,0:T(8,128)(2,1)}, u32[]{:S(2)}) copy-start(bf16[4,3,3,3,128,128]{5,4,3,2,1,0:T(8,128)(2,1)} %param.6) | copy-start | bytes 10616836
  7.8 4.1 %copy-start.2 = (f32[4,128]{1,0:T(4,128)S(1)}, f32[4,128]{1,0:T(4,128)}, u32[]{:S(2)}) copy-start(f32[4,128]{1,0:T(4,128)} %biases.5) | copy-start | bytes 6148
  8.8 9.0 %collective-permute-start.4 = (bf16[432,128]{1,0:T(8,128)(2,1)S(1)}, bf16[432,128]{1,0:T(8,128)(2,1)S(1)}, u32[]{:S(2)}, u32[]{:S(2)}) collective-permute-start(bf16[432,128]{1,0:T(8,128)(2,1)S(1)} %collective-permute-done.3), channel_id=1, source_target_pairs={{0,24},{8,0},{16,8},{24,16},{1,25},{9,1},{17,9},{25,17},{2,26},{10... | collective-permute-start | bytes 331784 | tf_op jit(solution)/shard_map/ppermute | solution.py:308
  15.2 8.0 %collective-permute-start.1 = (f32[512,128]{1,0:T(8,128)S(1)}, f32[512,128]{1,0:T(8,128)S(1)}, u32[]{:S(2)}, u32[]{:S(2)}) collective-permute-start(f32[512,128]{1,0:T(8,128)S(1)} %first.1), channel_id=1, source_target_pairs={{0,8},{8,16},{16,24},{24,32},{32,40},{40,48},{48,56},{56,64},{64,7... | collective-permute-start | bytes 786440 | tf_op jit(solution)/shard_map/ppermute | solution.py:305
  17.9 11.6 %collective-permute-start.6 = (bf16[3,432,128]{2,1,0:T(8,128)(2,1)S(1)}, bf16[3,432,128]{2,1,0:T(8,128)(2,1)S(1)}, u32[]{:S(2)}, u32[]{:S(2)}) collective-permute-start(bf16[3,432,128]{2,1,0:T(8,128)(2,1)S(1)} %pad_maximum_fusion.p0), channel_id=1, source_target_pairs={{0,2},{2,4},{4,6},{6,0},{1,3},{3,5},{5,7},{7,1},{8,10},{10,12},{12... | collective-permute-start | bytes 995336 | tf_op jit(solution)/shard_map/ppermute | solution.py:331
  19.5 14.8 %collective-permute-start.7 = (bf16[3,432,128]{2,1,0:T(8,128)(2,1)S(1)}, bf16[3,432,128]{2,1,0:T(8,128)(2,1)S(1)}, u32[]{:S(2)}, u32[]{:S(2)}) collective-permute-start(bf16[3,432,128]{2,1,0:T(8,128)(2,1)S(1)} %pad_maximum_fusion.p0), channel_id=1, source_target_pairs={{0,6},{2,0},{4,2},{6,4},{1,7},{3,1},{5,3},{7,5},{8,14},{10,8},{12,... | collective-permute-start | bytes 995336 | tf_op jit(solution)/shard_map/ppermute | solution.py:331
  21.2 15.0 %collective-permute-start.8 = (bf16[3,432,128]{2,1,0:T(8,128)(2,1)S(1)}, bf16[3,432,128]{2,1,0:T(8,128)(2,1)S(1)}, u32[]{:S(2)}, u32[]{:S(2)}) collective-permute-start(bf16[3,432,128]{2,1,0:T(8,128)(2,1)S(1)} %pad_maximum_fusion.p0), channel_id=1, source_target_pairs={{0,4},{2,6},{4,0},{6,2},{1,5},{3,7},{5,1},{7,3},{8,12},{10,14},{12... | collective-permute-start | bytes 995336 | tf_op jit(solution)/shard_map/ppermute | solution.py:331
  26.5 12.3 %collective-permute-start.10 = (f32[512,128]{1,0:T(8,128)S(1)}, f32[512,128]{1,0:T(8,128)S(1)}, u32[]{:S(2)}, u32[]{:S(2)}) collective-permute-start(f32[512,128]{1,0:T(8,128)S(1)} %get-tuple-element.39.m0), channel_id=1, source_target_pairs={{0,8},{8,16},{16,24},{24,0},{1,9},{9,17},{17,25},{25,1},{2,10},{10... | collective-permute-start | bytes 786440 | tf_op jit(solution)/shard_map/ppermute | solution.py:308
  29.4 10.3 %collective-permute-start.9 = (f32[512,128]{1,0:T(8,128)S(1)}, f32[512,128]{1,0:T(8,128)S(1)}, u32[]{:S(2)}, u32[]{:S(2)}) collective-permute-start(f32[512,128]{1,0:T(8,128)S(1)} %get-tuple-element.39.m0), channel_id=1, source_target_pairs={{0,16},{8,24},{16,0},{24,8},{1,17},{9,25},{17,1},{25,9},{2,18},{10... | collective-permute-start | bytes 786440 | tf_op jit(solution)/shard_map/ppermute | solution.py:308
  29.4 12.7 %collective-permute-start.2 = (f32[512,128]{1,0:T(8,128)S(1)}, f32[512,128]{1,0:T(8,128)S(1)}, u32[]{:S(2)}, u32[]{:S(2)}) collective-permute-start(f32[512,128]{1,0:T(8,128)S(1)} %get-tuple-element.39.m0), channel_id=1, source_target_pairs={{0,24},{8,0},{16,8},{24,16},{1,25},{9,1},{17,9},{25,17},{2,26},{10... | collective-permute-start | bytes 786440 | tf_op jit(solution)/shard_map/ppermute | solution.py:308
  39.7 3.9 %collective-permute-start.11 = (bf16[3,432,128]{2,1,0:T(8,128)(2,1)S(1)}, bf16[3,432,128]{2,1,0:T(8,128)(2,1)S(1)}, u32[]{:S(2)}, u32[]{:S(2)}) collective-permute-start(bf16[3,432,128]{2,1,0:T(8,128)(2,1)S(1)} %pad_maximum_fusion.p0), channel_id=1, source_target_pairs={{0,1},{1,0},{2,3},{3,2},{4,5},{5,4},{6,7},{7,6},{8,9},{9,8},{10,11... | collective-permute-start | bytes 995336 | tf_op jit(solution)/shard_map/ppermute | solution.py:340
  39.7 3.9 %collective-permute-start.12 = (bf16[3,432,128]{2,1,0:T(8,128)(2,1)S(1)}, bf16[3,432,128]{2,1,0:T(8,128)(2,1)S(1)}, u32[]{:S(2)}, u32[]{:S(2)}) collective-permute-start(bf16[3,432,128]{2,1,0:T(8,128)(2,1)S(1)} %collective-permute-done.6.p1), channel_id=1, source_target_pairs={{0,1},{1,0},{2,3},{3,2},{4,5},{5,4},{6,7},{7,6},{8,9},{9,8},{10,11... | collective-permute-start | bytes 995336 | tf_op jit(solution)/shard_map/ppermute | solution.py:340
  40.3 3.4 %collective-permute-start.13 = (bf16[3,432,128]{2,1,0:T(8,128)(2,1)S(1)}, bf16[3,432,128]{2,1,0:T(8,128)(2,1)S(1)}, u32[]{:S(2)}, u32[]{:S(2)}) collective-permute-start(bf16[3,432,128]{2,1,0:T(8,128)(2,1)S(1)} %collective-permute-done.7.p2), channel_id=1, source_target_pairs={{0,1},{1,0},{2,3},{3,2},{4,5},{5,4},{6,7},{7,6},{8,9},{9,8},{10,11... | collective-permute-start | bytes 995336 | tf_op jit(solution)/shard_map/ppermute | solution.py:340
  40.3 3.4 %collective-permute-start.14 = (bf16[3,432,128]{2,1,0:T(8,128)(2,1)S(1)}, bf16[3,432,128]{2,1,0:T(8,128)(2,1)S(1)}, u32[]{:S(2)}, u32[]{:S(2)}) collective-permute-start(bf16[3,432,128]{2,1,0:T(8,128)(2,1)S(1)} %collective-permute-done.8.p3), channel_id=1, source_target_pairs={{0,1},{1,0},{2,3},{3,2},{4,5},{5,4},{6,7},{7,6},{8,9},{9,8},{10,11... | collective-permute-start | bytes 995336 | tf_op jit(solution)/shard_map/ppermute | solution.py:340
  40.8 23.1 %copy-start.1 = (f32[1,8,8,8,128]{4,3,2,1,0:T(8,128)S(1)}, f32[1,8,8,8,128]{4,3,2,1,0:T(8,128)}, u32[]{:S(2)}) copy-start(f32[1,8,8,8,128]{4,3,2,1,0:T(8,128)} %param.4) | copy-start | bytes 786436
  42.2 10.9 %collective-permute-start.16 = (f32[512,128]{1,0:T(8,128)S(1)}, f32[512,128]{1,0:T(8,128)S(1)}, u32[]{:S(2)}, u32[]{:S(2)}) collective-permute-start(f32[512,128]{1,0:T(8,128)S(1)} %get-tuple-element.55.term), channel_id=1, source_target_pairs={{0,24},{1,25},{2,26},{3,27},{4,28},{5,29},{6,30},{7,31},{32,56},{3... | collective-permute-start | bytes 786440 | tf_op jit(solution)/shard_map/ppermute | solution.py:342
  53.1 4.0 %collective-permute-start.17 = (f32[512,128]{1,0:T(8,128)S(1)}, f32[512,128]{1,0:T(8,128)S(1)}, u32[]{:S(2)}, u32[]{:S(2)}) collective-permute-start(f32[512,128]{1,0:T(8,128)S(1)} %get-tuple-element.55.term), channel_id=1, source_target_pairs={{0,8},{1,9},{2,10},{3,11},{4,12},{5,13},{6,14},{7,15},{32,40},{33,... | collective-permute-start | bytes 786440 | tf_op jit(solution)/shard_map/ppermute | solution.py:353
  53.7 6.0 %collective-permute-start.18 = (f32[512,128]{1,0:T(8,128)S(1)}, f32[512,128]{1,0:T(8,128)S(1)}, u32[]{:S(2)}, u32[]{:S(2)}) collective-permute-start(f32[512,128]{1,0:T(8,128)S(1)} %collective-permute-done.16.f3), channel_id=1, source_target_pairs={{24,16},{25,17},{26,18},{27,19},{28,20},{29,21},{30,22},{31,23},{5... | collective-permute-start | bytes 786440 | tf_op jit(solution)/shard_map/ppermute | solution.py:352
  55.0 8.8 %collective-permute-start.15 = (f32[512,128]{1,0:T(8,128)S(1)}, f32[512,128]{1,0:T(8,128)S(1)}, u32[]{:S(2)}, u32[]{:S(2)}) collective-permute-start(f32[512,128]{1,0:T(8,128)S(1)} %get-tuple-element.53.point), channel_id=1, source_target_pairs={{0,32},{32,64},{64,96},{96,128},{128,160},{160,192},{192,224},{1,3... | collective-permute-start | bytes 786440 | tf_op jit(solution)/shard_map/ppermute | solution.py:311
  56.3 13.8 %collective-permute-start.20 = (bf16[4,432,128]{2,1,0:T(8,128)(2,1)S(1)}, bf16[4,432,128]{2,1,0:T(8,128)(2,1)S(1)}, u32[]{:S(2)}, u32[]{:S(2)}) collective-permute-start(bf16[4,432,128]{2,1,0:T(8,128)(2,1)S(1)} %get-tuple-element.63), channel_id=1, source_target_pairs={{96,64},{160,128},{97,65},{161,129},{98,66},{162,130},{99,67},{163... | collective-permute-start | bytes 1327112 | tf_op jit(solution)/shard_map/ppermute | solution.py:311
  67.9 2.3 %collective-permute-start.19 = (f32[512,128]{1,0:T(8,128)S(1)}, f32[512,128]{1,0:T(8,128)S(1)}, u32[]{:S(2)}, u32[]{:S(2)}) collective-permute-start(f32[512,128]{1,0:T(8,128)S(1)} %get-tuple-element.59.corner.value), channel_id=1, source_target_pairs={{32,64},{33,65},{34,66},{35,67},{36,68},{37,69},{38,70},{39,71},{4... | collective-permute-start | bytes 786440 | tf_op jit(solution)/shard_map/ppermute | solution.py:311
  69.4 0.8 collective-permute-start.22
  70.1 1.9 %collective-permute-start.21 = (bf16[4,432,128]{2,1,0:T(8,128)(2,1)S(1)}, bf16[4,432,128]{2,1,0:T(8,128)(2,1)S(1)}, u32[]{:S(2)}, u32[]{:S(2)}) collective-permute-start(bf16[4,432,128]{2,1,0:T(8,128)(2,1)S(1)} %collective-permute-done.20.mine), channel_id=1, source_target_pairs={{0,1},{1,0},{2,3},{3,2},{4,5},{5,4},{6,7},{7,6},{8,9},{9,8},{10,11... | collective-permute-start | bytes 1327112 | tf_op jit(solution)/shard_map/ppermute | solution.py:363
  72.0 1.4 %collective-permute-start.23 = (f32[512,128]{1,0:T(8,128)S(1)}, f32[512,128]{1,0:T(8,128)S(1)}, u32[]{:S(2)}, u32[]{:S(2)}) collective-permute-start(f32[512,128]{1,0:T(8,128)S(1)} %next2.1), channel_id=1, source_target_pairs={{64,128},{65,129},{66,130},{67,131},{68,132},{69,133},{70,134},{71... | collective-permute-start | bytes 786440 | tf_op jit(solution)/shard_map/ppermute | solution.py:311
  72.7 0.7 collective-permute-start.24
  73.4 0.7 collective-permute-start.25
  74.2 31.8 %collective-permute-start.26 = (f32[512,128]{1,0:T(8,128)S(1)}, f32[512,128]{1,0:T(8,128)S(1)}, u32[]{:S(2)}, u32[]{:S(2)}) collective-permute-start(f32[512,128]{1,0:T(8,128)S(1)} %get-tuple-element.68.value), channel_id=1, source_target_pairs={{64,96},{128,160},{192,224},{65,97},{129,161},{193,225},{66,98},{1... | collective-permute-start | bytes 786440 | tf_op jit(solution)/shard_map/ppermute | solution.py:311

commit v8 on v7

--- a/solution.py
+++ b/solution.py
@@ -160,10 +160,23 @@
     part[...] = lead[X - 1, pl.ds(core * 4, 4)]
 
 
-def fourth_kernel(
-    inputs, hop, point, term, f1, f2, f3, stack, lead, residual, corner, start, out_stack
-):
-    x, z = lax.axis_index("x"), lax.axis_index("z")
+def begin_kernel(inputs, hop, lead, start, partial):
+    z = lax.axis_index("z")
+
+    @pl.when(z == 0)
+    def _():
+        start[...] = inputs[...]
+
+    @pl.when(z > 0)
+    def _():
+        start[...] = hop[...]
+
+    v = start[...]
+    partial[...] = v + COARSE * conv(v, flat(lead[0]))
+
+
+def fourth_kernel(partial, point, term, f1, f2, f3, stack, lead, residual, corner, out_stack):
+    x = lax.axis_index("x")
     out_stack[1:] = stack[1:]
     for r, first in enumerate((term, f1, f2, f3)):
 
@@ -171,17 +184,8 @@
         def _():
             out_stack[0] = first[...]
 
-
-    @pl.when(z == 0)
-    def _():
-        start[...] = inputs[...]
-
-    @pl.when(z > 0)
-    def _():
-        start[...] = hop[...]
-
-    corner[...] = start[...]
-    coarse_steps(corner, out_stack, lead)
+    corner[...] = partial[...] + out_stack[0]
+    coarse_steps(corner, out_stack, lead, 1)
 
     @pl.when(x == X - 1)
     def _():
@@ -284,8 +288,8 @@
         input_output_aliases=alias or {},
         compiler_params=pltpu.CompilerParams(vmem_limit_bytes=limit << 20),
         cost_estimate=pl.CostEstimate(
-            flops=convs if convs != 1 else 6 * 10**9,
-            bytes_accessed=convs if convs != 1 else 20 * 10**6,
+            flops=(0, 6, 30)[convs] * 10**9 if convs < 3 else 0,
+            bytes_accessed=(0, 20, 100)[convs] * 10**6 if convs < 3 else 0,
             transcendentals=0,
         ),
     )(*args)
@@ -322,6 +326,7 @@
         (barrier((kernels, guess_corner))[0],), "h", [dma(())],
     )
     shares[1] = from_ahead(barrier((shares[0], kept))[0], 1)
+    guess_head, *shares = barrier((guess_head, *shares))
     (point,) = call(
         first_kernel, "first", (state,), 4, (guess_head, kept, biases), "vvv",
     )
@@ -331,12 +336,13 @@
         lax.ppermute(first_piece, "y", [(i, (i + r) % 4) for i in range(4)]) for r in (1, 3, 2)
     ]
     message, term = call(
-        second_kernel, "second", (state, state), 4,
+        second_kernel, "second", (state, state), 1,
         (head, guess_head, kept, biases),
         "vvvv", [buffer],
     )
     m2, m3, m1 = (from_ahead(message, r) for r in (2, 3, 1))
     pieces, m2, m3 = barrier((pieces, m2, m3))
+    pieces[3], m1 = barrier((pieces[3], m1))
     pieces += [lax.ppermute(p, "core", [(0, 1), (1, 0)]) for p in pieces]
     term, m3 = barrier((term, m3))
     f3 = lax.ppermute(term, "x", [(0, 3)])
@@ -352,9 +358,12 @@
     f2 = lax.ppermute(f3, "x", [(3, 2)])
     f1 = lax.ppermute(term, "x", [(0, 1)])
     next_mine = along_z(part, (3, 2), (5, 4))
-    residual, corner, start, stack = call(
-        fourth_kernel, "fourth", (state,) * 3 + (stacked,), 1,
-        (inputs, hop, point, term, f1, f2, f3, stack, lead), "v" * 9,
+    start, partial = call(
+        begin_kernel, "begin", (state, state), 2, (inputs, hop, lead), "vvv",
+    )
+    residual, corner, stack = call(
+        fourth_kernel, "fourth", (state, state, stacked), 1,
+        (partial, point, term, f1, f2, f3, stack, lead), "v" * 8,
     )
     came = along_z(corner, (1, 2))
     (defect,) = call(defect_kernel, "defect", (state,), 1, (corner, start, top), "vvv")

time: 113 us -> 114 us (level)
    ppermute x6, waiting for transfers between devices: 5.58 us -> 13.6 us  [from_ahead(): return lax.ppermute(v, 'x', [(i, (i - r) % X) for i in range(X)])]
    ppermute x3, waiting for transfers between devices: 5.75 us -> 3.27 us  [shards(): lax.ppermute(first_piece, 'y', [(i, (i + r) % 4) for i in range(4)])]
    ppermute x2, waiting for transfers between devices: 2.42 us -> 0.13 us  [next_layer(): lax.ppermute(v, LAYER, [(i, (i + 1) % (X * Z)) for i in range(X * Z)])]
    ppermute x6, starting transfers between devices: 7.88 us -> 9.86 us  [from_ahead(): return lax.ppermute(v, 'x', [(i, (i - r) % X) for i in range(X)])]
    ppermute x2, starting transfers between devices: 2.72 us -> 1.06 us  [next_layer(): lax.ppermute(v, LAYER, [(i, (i + 1) % (X * Z)) for i in range(X * Z)])]
    ppermute x8, waiting for transfers between devices: 34.6 us -> 33.3 us  [along_z(): return lax.ppermute(v, 'z', pairs)]
    ppermute x1, waiting for transfers between devices: 6.49 us -> 5.23 us  [shards(): f3 = lax.ppermute(term, 'x', [(0, 3)])]
    pallas_call x13 -> x14, Pallas kernels: 23.2 us -> 23.2 us  [call(): pl.pallas_call(body, name=name, out_shape=outs, in_specs=[specs[p] for p...]
  transfers between devices with their start and end apart: 27 -> 27, of which waited for: 12 -> 14; matrix products, arithmetic and copies ran while one was open for 0% -> 0% of each run, Pallas kernels for 13% -> 10%
where the time goes in v8:
time: 114 us
  waiting for transfers between devices  60.2 us (53%)
  starting transfers between devices  27.5 us (24%)
  Pallas kernels  23.2 us (20%)
  local copies, waits for them, and re-layouts  2.01 us (2%)
    ppermute x8, waiting for transfers between devices, along_z(): return lax.ppermute(v, 'z', pairs)  33.3 us
    pallas_call x14, Pallas kernels, call(): pl.pallas_call(body, name=name, out_shape=outs, in_specs=[specs[p] for p...  23.2 us
    ppermute x6, waiting for transfers between devices, from_ahead(): return lax.ppermute(v, 'x', [(i, (i - r) % X) for i in range(X)])  13.6 us
    ppermute x6, starting transfers between devices, from_ahead(): return lax.ppermute(v, 'x', [(i, (i - r) % X) for i in range(X)])  9.86 us
    ppermute x8, starting transfers between devices, along_z(): return lax.ppermute(v, 'z', pairs)  6.64 us
    ppermute x3, starting transfers between devices, shards(): lax.ppermute(first_piece, 'y', [(i, (i + r) % 4) for i in range(4)])  5.3 us
    ppermute x1, waiting for transfers between devices, shards(): f3 = lax.ppermute(term, 'x', [(0, 3)])  5.23 us
    ppermute x3, waiting for transfers between devices, shards(): lax.ppermute(first_piece, 'y', [(i, (i + r) % 4) for i in range(4)])  3.27 us
  transfers between devices with their start and end apart: 27, of which 14 were waited for; matrix products, arithmetic and copies ran while one was open for 0% of the time, Pallas kernels for 10%

profile of v8, /device:TPU:230, one launch (start us, length us, event | category | flops | bytes accessed | tf_op | source)
XLA Modules:
  0.0 114.0 jit_solution(10284383275146420036)
XLA Ops:
  0.6 1.8 %prepare.1 = (f32[512,128]{1,0:T(8,128)}, bf16[432,128]{1,0:T(8,128)(2,1)}) custom-call(f32[4,512,128]{2,1,0:T(8,128)} %bitcast.14, f32[512,128]{1,0:T(8,128)} %bitcast.12, bf16[4,8,432,128]{3,2,1,0:T(8,128)(2,1)} %bitcast.10), custom_call_target="tpu_custom_call" | custom-call | tf_op jit(solution)/shard_map/prepare/pallas_call | solution.py:281
  2.4 0.1 collective-permute-start
  2.5 2.0 %collective-permute-start.1 = (bf16[432,128]{1,0:T(8,128)(2,1)}, bf16[432,128]{1,0:T(8,128)(2,1)S(1)}, u32[]{:S(2)}, u32[]{:S(2)}) collective-permute-start(bf16[432,128]{1,0:T(8,128)(2,1)} %get-tuple-element.45), channel_id=1, source_target_pairs={{0,24},{8,0},{16,8},{24,16},{1,25},{9,1},{17,9},{25,17},{2,26},{10... | collective-permute-start | bytes 331784 | tf_op jit(solution)/shard_map/ppermute | solution.py:312
  4.5 1.3 %collective-permute-start.3 = (bf16[432,128]{1,0:T(8,128)(2,1)}, bf16[432,128]{1,0:T(8,128)(2,1)S(1)}, u32[]{:S(2)}, u32[]{:S(2)}) collective-permute-start(bf16[432,128]{1,0:T(8,128)(2,1)} %get-tuple-element.45), channel_id=1, source_target_pairs={{0,8},{8,16},{16,24},{24,0},{1,9},{9,17},{17,25},{25,1},{2,10},{10... | collective-permute-start | bytes 331784 | tf_op jit(solution)/shard_map/ppermute | solution.py:312
  5.8 2.0 %copy-done = bf16[4,3,3,3,128,128]{5,4,3,2,1,0:T(8,128)(2,1)S(1)} copy-done((bf16[4,3,3,3,128,128]{5,4,3,2,1,0:T(8,128)(2,1)S(1)}, bf16[4,3,3,3,128,128]{5,4,3,2,1,0:T(8,128)(2,1)}, u32[]{:S(2)}) %copy-start) | copy-done | bytes 3538968
  7.8 0.4 load.1.kernels
  8.2 0.6 collective-permute-done.1
  8.8 0.7 collective-permute-start.2
  9.5 3.6 %collective-permute-done.3 = bf16[432,128]{1,0:T(8,128)(2,1)S(1)} collective-permute-done((bf16[432,128]{1,0:T(8,128)(2,1)}, bf16[432,128]{1,0:T(8,128)(2,1)S(1)}, u32[]{:S(2)}, u32[]{:S(2)}) %collective-permute-start.3) | collective-permute-done | bytes 110624 | tf_op jit(solution)/shard_map/ppermute | solution.py:312
  13.1 1.6 %collective-permute-done.2 = bf16[432,128]{1,0:T(8,128)(2,1)S(1)} collective-permute-done((bf16[432,128]{1,0:T(8,128)(2,1)S(1)}, bf16[432,128]{1,0:T(8,128)(2,1)S(1)}, u32[]{:S(2)}, u32[]{:S(2)}) %collective-permute-start.2) | collective-permute-done | bytes 110624 | tf_op jit(solution)/shard_map/ppermute | solution.py:312
  14.8 0.0 collective-permute-done.head.guess_head
  14.8 3.3 %first.1 = f32[512,128]{1,0:T(8,128)S(1)} custom-call(f32[512,128]{1,0:T(8,128)S(1)} %collective-permute-done.head.guess_head, bf16[4,8,432,128]{3,2,1,0:T(8,128)(2,1)S(1)} %load.1.kernels, f32[4,128]{1,0:T(4,128)S(1)} %copy-done.2), custom_call_target="tpu_custom_call" | custom-call | tf_op jit(solution)/shard_map/first/pallas_call | solution.py:281
  18.0 1.0 collective-permute-start.4
  19.0 1.7 %collective-permute-start.5 = (bf16[3,432,128]{2,1,0:T(8,128)(2,1)S(1)}, bf16[3,432,128]{2,1,0:T(8,128)(2,1)S(1)}, u32[]{:S(2)}, u32[]{:S(2)}) collective-permute-start(bf16[3,432,128]{2,1,0:T(8,128)(2,1)S(1)} %pad_maximum_fusion.p0), channel_id=1, source_target_pairs={{0,2},{2,4},{4,6},{6,0},{1,3},{3,5},{5,7},{7,1},{8,10},{10,12},{12... | collective-permute-start | bytes 995336 | tf_op jit(solution)/shard_map/ppermute | solution.py:336
  20.7 1.7 %collective-permute-start.6 = (bf16[3,432,128]{2,1,0:T(8,128)(2,1)S(1)}, bf16[3,432,128]{2,1,0:T(8,128)(2,1)S(1)}, u32[]{:S(2)}, u32[]{:S(2)}) collective-permute-start(bf16[3,432,128]{2,1,0:T(8,128)(2,1)S(1)} %pad_maximum_fusion.p0), channel_id=1, source_target_pairs={{0,6},{2,0},{4,2},{6,4},{1,7},{3,1},{5,3},{7,5},{8,14},{10,8},{12,... | collective-permute-start | bytes 995336 | tf_op jit(solution)/shard_map/ppermute | solution.py:336
  22.4 2.0 %collective-permute-start.7 = (bf16[3,432,128]{2,1,0:T(8,128)(2,1)S(1)}, bf16[3,432,128]{2,1,0:T(8,128)(2,1)S(1)}, u32[]{:S(2)}, u32[]{:S(2)}) collective-permute-start(bf16[3,432,128]{2,1,0:T(8,128)(2,1)S(1)} %pad_maximum_fusion.p0), channel_id=1, source_target_pairs={{0,4},{2,6},{4,0},{6,2},{1,5},{3,7},{5,1},{7,3},{8,12},{10,14},{12... | collective-permute-start | bytes 995336 | tf_op jit(solution)/shard_map/ppermute | solution.py:336
  24.3 0.1 collective-permute-done.4.head
  24.5 3.3 %second.1 = (f32[512,128]{1,0:T(8,128)S(1)}, f32[512,128]{1,0:T(8,128)S(1)}) custom-call(f32[512,128]{1,0:T(8,128)S(1)} %collective-permute-done.4.head, f32[512,128]{1,0:T(8,128)S(1)} %collective-permute-done.head.guess_head, bf16[4,8,432,128]{3,2,1,0:T(8,128)(2,1)S(1)} %load.1.kernels, f32[4,128]{1,0:T(4,128)S(1)} %copy-done.2), custom_call_target="tpu_custom_call" | custom-call | flops 6000000000 | bytes 20000000 | tf_op jit(solution)/shard_map/second/pallas_call | solution.py:281
  27.8 2.6 %collective-permute-start.8 = (f32[512,128]{1,0:T(8,128)S(1)}, f32[512,128]{1,0:T(8,128)S(1)}, u32[]{:S(2)}, u32[]{:S(2)}) collective-permute-start(f32[512,128]{1,0:T(8,128)S(1)} %get-tuple-element.49.m0), channel_id=1, source_target_pairs={{0,16},{8,24},{16,0},{24,8},{1,17},{9,25},{17,1},{25,9},{2,18},{10... | collective-permute-start | bytes 786440 | tf_op jit(solution)/shard_map/ppermute | solution.py:312
  30.4 2.5 %collective-permute-start.9 = (f32[512,128]{1,0:T(8,128)S(1)}, f32[512,128]{1,0:T(8,128)S(1)}, u32[]{:S(2)}, u32[]{:S(2)}) collective-permute-start(f32[512,128]{1,0:T(8,128)S(1)} %get-tuple-element.49.m0), channel_id=1, source_target_pairs={{0,8},{8,16},{16,24},{24,0},{1,9},{9,17},{17,25},{25,1},{2,10},{10... | collective-permute-start | bytes 786440 | tf_op jit(solution)/shard_map/ppermute | solution.py:312
  32.9 0.0 collective-permute-done.5.p1
  32.9 0.8 collective-permute-start.10
  33.7 1.5 %collective-permute-done.6.p2 = bf16[3,432,128]{2,1,0:T(8,128)(2,1)S(1)} collective-permute-done((bf16[3,432,128]{2,1,0:T(8,128)(2,1)S(1)}, bf16[3,432,128]{2,1,0:T(8,128)(2,1)S(1)}, u32[]{:S(2)}, u32[]{:S(2)}) %collective-permute-start.6) | collective-permute-done | bytes 331808 | tf_op jit(solution)/shard_map/ppermute | solution.py:336
  35.2 1.8 %collective-permute-done.7.p3 = bf16[3,432,128]{2,1,0:T(8,128)(2,1)S(1)} collective-permute-done((bf16[3,432,128]{2,1,0:T(8,128)(2,1)S(1)}, bf16[3,432,128]{2,1,0:T(8,128)(2,1)S(1)}, u32[]{:S(2)}, u32[]{:S(2)}) %collective-permute-start.7) | collective-permute-done | bytes 331808 | tf_op jit(solution)/shard_map/ppermute | solution.py:336
  37.0 0.5 collective-permute-done.8.m2
  37.5 7.2 %collective-permute-done.9.m3 = f32[512,128]{1,0:T(8,128)S(1)} collective-permute-done((f32[512,128]{1,0:T(8,128)S(1)}, f32[512,128]{1,0:T(8,128)S(1)}, u32[]{:S(2)}, u32[]{:S(2)}) %collective-permute-start.9) | collective-permute-done | bytes 262176 | tf_op jit(solution)/shard_map/ppermute | solution.py:312
  44.7 0.0 collective-permute-done.10.m1
  44.7 0.0 collective-permute-start.14
  44.7 0.5 collective-permute-start.11
  45.2 0.0 collective-permute-start.12
  45.2 0.5 collective-permute-start.13
  45.7 1.6 %collective-permute-start.16 = (f32[512,128]{1,0:T(8,128)S(1)}, f32[512,128]{1,0:T(8,128)S(1)}, u32[]{:S(2)}, u32[]{:S(2)}) collective-permute-start(f32[512,128]{1,0:T(8,128)S(1)} %get-tuple-element.70.term), channel_id=1, source_target_pairs={{0,24},{1,25},{2,26},{3,27},{4,28},{5,29},{6,30},{7,31},{32,56},{3... | collective-permute-start | bytes 786440 | tf_op jit(solution)/shard_map/ppermute | solution.py:348
  47.3 0.0 collective-permute-done.14.o3
  47.4 0.0 collective-permute-done.11.o0
  47.4 0.0 collective-permute-done.12.o1
  47.4 0.4 collective-permute-done.13.o2
  47.8 2.9 %third.1 = (f32[512,128]{1,0:T(8,128)S(1)}, f32[4,512,128]{2,1,0:T(8,128)S(1)}, bf16[4,8,432,128]{3,2,1,0:T(8,128)(2,1)S(1)}, bf16[8,432,128]{2,1,0:T(8,128)(2,1)S(1)}, bf16[4,432,128]{2,1,0:T(8,128)(2,1)S(1)}) custom-call(f32[512,128]{1,0:T(8,128)S(1)} %get-tuple-element.49.m0, f32[512,128]{1,0:T(8,128)S(1)} %collective-permute-done.10.m1, ...), custom_call_target="tpu_custom_call" | custom-call | tf_op jit(solution)/shard_map/third/pallas_call | solution.py:281
  50.7 1.3 %collective-permute-start.15 = (f32[512,128]{1,0:T(8,128)S(1)}, f32[512,128]{1,0:T(8,128)S(1)}, u32[]{:S(2)}, u32[]{:S(2)}) collective-permute-start(f32[512,128]{1,0:T(8,128)S(1)} %get-tuple-element.66.point), channel_id=1, source_target_pairs={{0,32},{32,64},{64,96},{96,128},{128,160},{160,192},{192,224},{1,3... | collective-permute-start | bytes 786440 | tf_op jit(solution)/shard_map/ppermute | solution.py:315
  52.0 5.2 %collective-permute-done.16.f3 = f32[512,128]{1,0:T(8,128)S(1)} collective-permute-done((f32[512,128]{1,0:T(8,128)S(1)}, f32[512,128]{1,0:T(8,128)S(1)}, u32[]{:S(2)}, u32[]{:S(2)}) %collective-permute-start.16) | collective-permute-done | bytes 262176 | tf_op jit(solution)/shard_map/ppermute | solution.py:348
  57.2 0.7 collective-permute-start.17
  57.9 1.3 %collective-permute-start.18 = (f32[512,128]{1,0:T(8,128)S(1)}, f32[512,128]{1,0:T(8,128)S(1)}, u32[]{:S(2)}, u32[]{:S(2)}) collective-permute-start(f32[512,128]{1,0:T(8,128)S(1)} %collective-permute-done.16.f3), channel_id=1, source_target_pairs={{24,16},{25,17},{26,18},{27,19},{28,20},{29,21},{30,22},{31,23},{5... | collective-permute-start | bytes 786440 | tf_op jit(solution)/shard_map/ppermute | solution.py:358
  59.2 0.7 collective-permute-start.20
  59.9 1.0 collective-permute-done.15.hop
  60.9 0.8 begin.1
  61.7 0.0 collective-permute-done.17.f1
  61.7 2.6 %collective-permute-done.18.f2 = f32[512,128]{1,0:T(8,128)S(1)} collective-permute-done((f32[512,128]{1,0:T(8,128)S(1)}, f32[512,128]{1,0:T(8,128)S(1)}, u32[]{:S(2)}, u32[]{:S(2)}) %collective-permute-start.18) | collective-permute-done | bytes 262176 | tf_op jit(solution)/shard_map/ppermute | solution.py:358
  64.3 3.3 %fourth.1 = (f32[512,128]{1,0:T(8,128)}, f32[512,128]{1,0:T(8,128)S(1)}, f32[4,512,128]{2,1,0:T(8,128)S(1)}) custom-call(f32[512,128]{1,0:T(8,128)S(1)} %get-tuple-element.68.partial, f32[512,128]{1,0:T(8,128)S(1)} %get-tuple-element.66.point, f32[512,128]{1,0:T(8,128)S(1)} %get-tuple-element.70.term, f32[512,128]{1,0:T(8,128)S(1)} %collective-permute-done.17.f1, ...), custom_call_target="tpu_custom_call" | custom-call | flops 6000000000 | bytes 20000000 | tf_op jit(solution)/shard_map/fourth/pallas_call | solution.py:281
  67.6 0.7 collective-permute-start.19
  68.3 0.8 defect.1
  69.1 0.7 collective-permute-start.22
  69.8 0.0 collective-permute-done.20.mine
  69.8 0.1 collective-permute-start.21
  69.9 0.0 collective-permute-done.19.came
  69.9 0.0 collective-permute-done.22.defect
  69.9 1.7 %collective-permute-done.21.other = bf16[4,432,128]{2,1,0:T(8,128)(2,1)S(1)} collective-permute-done((bf16[4,432,128]{2,1,0:T(8,128)(2,1)S(1)}, bf16[4,432,128]{2,1,0:T(8,128)(2,1)S(1)}, u32[]{:S(2)}, u32[]{:S(2)}) %collective-permute-start.21) | collective-permute-done | bytes 442400 | tf_op jit(solution)/shard_map/ppermute | solution.py:372
  71.7 0.7 collective-permute-start.23
  72.3 0.7 collective-permute-start.24
  73.0 0.0 collective-permute-done.23.came
  73.0 0.0 collective-permute-done.24.defect
  73.1 0.7 collective-permute-start.25
  73.8 0.0 collective-permute-done.25.came
  73.8 1.3 %collective-permute-start.26 = (f32[512,128]{1,0:T(8,128)S(1)}, f32[512,128]{1,0:T(8,128)S(1)}, u32[]{:S(2)}, u32[]{:S(2)}) collective-permute-start(f32[512,128]{1,0:T(8,128)S(1)} %get-tuple-element.82.value), channel_id=1, source_target_pairs={{64,96},{128,160},{192,224},{65,97},{129,161},{193,225},{66,98},{1... | collective-permute-start | bytes 786440 | tf_op jit(solution)/shard_map/ppermute | solution.py:315
  75.1 32.2 %collective-permute-done.26.came = f32[512,128]{1,0:T(8,128)S(1)} collective-permute-done((f32[512,128]{1,0:T(8,128)S(1)}, f32[512,128]{1,0:T(8,128)S(1)}, u32[]{:S(2)}, u32[]{:S(2)}) %collective-permute-start.26) | collective-permute-done | bytes 262176 | tf_op jit(solution)/shard_map/ppermute | solution.py:315
  107.3 6.5 %last.1 = f32[4,512,128]{2,1,0:T(8,128)} custom-call(f32[512,128]{1,0:T(8,128)S(1)} %collective-permute-done.26.came, f32[512,128]{1,0:T(8,128)S(1)} %get-tuple-element.83.before, f32[512,128]{1,0:T(8,128)S(1)} %get-tuple-element.82.value, f32[512,128]{1,0:T(8,128)S(1)} %defect.1, f32[4,128]{1,0:T(4,128)S(1)} %copy-done.2, ...), custom_call_target="tpu_custom_call" | custom-call | tf_op jit(solution)/shard_map/last/pallas_call | solution.py:281
  (11 shorter events, 0.1 us)
Async XLA Ops:
  2.4 12.3 %collective-permute-start = (f32[512,128]{1,0:T(8,128)}, f32[512,128]{1,0:T(8,128)S(1)}, u32[]{:S(2)}, u32[]{:S(2)}) collective-permute-start(f32[512,128]{1,0:T(8,128)} %get-tuple-element.44), channel_id=1, source_target_pairs={{0,8},{8,16},{16,24},{24,32},{32,40},{40,48},{48,56},{56,64},{64,7... | collective-permute-start | bytes 786440 | tf_op jit(solution)/shard_map/ppermute | solution.py:309
  2.5 6.3 %collective-permute-start.1 = (bf16[432,128]{1,0:T(8,128)(2,1)}, bf16[432,128]{1,0:T(8,128)(2,1)S(1)}, u32[]{:S(2)}, u32[]{:S(2)}) collective-permute-start(bf16[432,128]{1,0:T(8,128)(2,1)} %get-tuple-element.45), channel_id=1, source_target_pairs={{0,24},{8,0},{16,8},{24,16},{1,25},{9,1},{17,9},{25,17},{2,26},{10... | collective-permute-start | bytes 331784 | tf_op jit(solution)/shard_map/ppermute | solution.py:312
  4.5 8.6 %collective-permute-start.3 = (bf16[432,128]{1,0:T(8,128)(2,1)}, bf16[432,128]{1,0:T(8,128)(2,1)S(1)}, u32[]{:S(2)}, u32[]{:S(2)}) collective-permute-start(bf16[432,128]{1,0:T(8,128)(2,1)} %get-tuple-element.45), channel_id=1, source_target_pairs={{0,8},{8,16},{16,24},{24,0},{1,9},{9,17},{17,25},{25,1},{2,10},{10... | collective-permute-start | bytes 331784 | tf_op jit(solution)/shard_map/ppermute | solution.py:312
  5.8 2.0 %copy-start = (bf16[4,3,3,3,128,128]{5,4,3,2,1,0:T(8,128)(2,1)S(1)}, bf16[4,3,3,3,128,128]{5,4,3,2,1,0:T(8,128)(2,1)}, u32[]{:S(2)}) copy-start(bf16[4,3,3,3,128,128]{5,4,3,2,1,0:T(8,128)(2,1)} %param.6) | copy-start | bytes 10616836
  7.8 6.9 %copy-start.2 = (f32[4,128]{1,0:T(4,128)S(1)}, f32[4,128]{1,0:T(4,128)}, u32[]{:S(2)}) copy-start(f32[4,128]{1,0:T(4,128)} %biases.5) | copy-start | bytes 6148
  8.8 6.0 %collective-permute-start.2 = (bf16[432,128]{1,0:T(8,128)(2,1)S(1)}, bf16[432,128]{1,0:T(8,128)(2,1)S(1)}, u32[]{:S(2)}, u32[]{:S(2)}) collective-permute-start(bf16[432,128]{1,0:T(8,128)(2,1)S(1)} %collective-permute-done.1), channel_id=1, source_target_pairs={{0,24},{8,0},{16,8},{24,16},{1,25},{9,1},{17,9},{25,17},{2,26},{10... | collective-permute-start | bytes 331784 | tf_op jit(solution)/shard_map/ppermute | solution.py:312
  18.0 6.4 %collective-permute-start.4 = (f32[512,128]{1,0:T(8,128)S(1)}, f32[512,128]{1,0:T(8,128)S(1)}, u32[]{:S(2)}, u32[]{:S(2)}) collective-permute-start(f32[512,128]{1,0:T(8,128)S(1)} %first.1), channel_id=1, source_target_pairs={{0,8},{8,16},{16,24},{24,32},{32,40},{40,48},{48,56},{56,64},{64,7... | collective-permute-start | bytes 786440 | tf_op jit(solution)/shard_map/ppermute | solution.py:309
  19.0 13.9 %collective-permute-start.5 = (bf16[3,432,128]{2,1,0:T(8,128)(2,1)S(1)}, bf16[3,432,128]{2,1,0:T(8,128)(2,1)S(1)}, u32[]{:S(2)}, u32[]{:S(2)}) collective-permute-start(bf16[3,432,128]{2,1,0:T(8,128)(2,1)S(1)} %pad_maximum_fusion.p0), channel_id=1, source_target_pairs={{0,2},{2,4},{4,6},{6,0},{1,3},{3,5},{5,7},{7,1},{8,10},{10,12},{12... | collective-permute-start | bytes 995336 | tf_op jit(solution)/shard_map/ppermute | solution.py:336
  20.7 14.5 %collective-permute-start.6 = (bf16[3,432,128]{2,1,0:T(8,128)(2,1)S(1)}, bf16[3,432,128]{2,1,0:T(8,128)(2,1)S(1)}, u32[]{:S(2)}, u32[]{:S(2)}) collective-permute-start(bf16[3,432,128]{2,1,0:T(8,128)(2,1)S(1)} %pad_maximum_fusion.p0), channel_id=1, source_target_pairs={{0,6},{2,0},{4,2},{6,4},{1,7},{3,1},{5,3},{7,5},{8,14},{10,8},{12,... | collective-permute-start | bytes 995336 | tf_op jit(solution)/shard_map/ppermute | solution.py:336
  22.4 14.6 %collective-permute-start.7 = (bf16[3,432,128]{2,1,0:T(8,128)(2,1)S(1)}, bf16[3,432,128]{2,1,0:T(8,128)(2,1)S(1)}, u32[]{:S(2)}, u32[]{:S(2)}) collective-permute-start(bf16[3,432,128]{2,1,0:T(8,128)(2,1)S(1)} %pad_maximum_fusion.p0), channel_id=1, source_target_pairs={{0,4},{2,6},{4,0},{6,2},{1,5},{3,7},{5,1},{7,3},{8,12},{10,14},{12... | collective-permute-start | bytes 995336 | tf_op jit(solution)/shard_map/ppermute | solution.py:336
  27.8 9.7 %collective-permute-start.8 = (f32[512,128]{1,0:T(8,128)S(1)}, f32[512,128]{1,0:T(8,128)S(1)}, u32[]{:S(2)}, u32[]{:S(2)}) collective-permute-start(f32[512,128]{1,0:T(8,128)S(1)} %get-tuple-element.49.m0), channel_id=1, source_target_pairs={{0,16},{8,24},{16,0},{24,8},{1,17},{9,25},{17,1},{25,9},{2,18},{10... | collective-permute-start | bytes 786440 | tf_op jit(solution)/shard_map/ppermute | solution.py:312
  30.4 14.3 %collective-permute-start.9 = (f32[512,128]{1,0:T(8,128)S(1)}, f32[512,128]{1,0:T(8,128)S(1)}, u32[]{:S(2)}, u32[]{:S(2)}) collective-permute-start(f32[512,128]{1,0:T(8,128)S(1)} %get-tuple-element.49.m0), channel_id=1, source_target_pairs={{0,8},{8,16},{16,24},{24,0},{1,9},{9,17},{17,25},{25,1},{2,10},{10... | collective-permute-start | bytes 786440 | tf_op jit(solution)/shard_map/ppermute | solution.py:312
  32.9 11.8 %collective-permute-start.10 = (f32[512,128]{1,0:T(8,128)S(1)}, f32[512,128]{1,0:T(8,128)S(1)}, u32[]{:S(2)}, u32[]{:S(2)}) collective-permute-start(f32[512,128]{1,0:T(8,128)S(1)} %get-tuple-element.49.m0), channel_id=1, source_target_pairs={{0,24},{8,0},{16,8},{24,16},{1,25},{9,1},{17,9},{25,17},{2,26},{10... | collective-permute-start | bytes 786440 | tf_op jit(solution)/shard_map/ppermute | solution.py:312
  44.7 2.6 %collective-permute-start.14 = (bf16[3,432,128]{2,1,0:T(8,128)(2,1)S(1)}, bf16[3,432,128]{2,1,0:T(8,128)(2,1)S(1)}, u32[]{:S(2)}, u32[]{:S(2)}) collective-permute-start(bf16[3,432,128]{2,1,0:T(8,128)(2,1)S(1)} %collective-permute-done.7.p3), channel_id=1, source_target_pairs={{0,1},{1,0},{2,3},{3,2},{4,5},{5,4},{6,7},{7,6},{8,9},{9,8},{10,11... | collective-permute-start | bytes 995336 | tf_op jit(solution)/shard_map/ppermute | solution.py:346
  44.7 2.6 %collective-permute-start.11 = (bf16[3,432,128]{2,1,0:T(8,128)(2,1)S(1)}, bf16[3,432,128]{2,1,0:T(8,128)(2,1)S(1)}, u32[]{:S(2)}, u32[]{:S(2)}) collective-permute-start(bf16[3,432,128]{2,1,0:T(8,128)(2,1)S(1)} %pad_maximum_fusion.p0), channel_id=1, source_target_pairs={{0,1},{1,0},{2,3},{3,2},{4,5},{5,4},{6,7},{7,6},{8,9},{9,8},{10,11... | collective-permute-start | bytes 995336 | tf_op jit(solution)/shard_map/ppermute | solution.py:346
  45.2 2.1 %collective-permute-start.12 = (bf16[3,432,128]{2,1,0:T(8,128)(2,1)S(1)}, bf16[3,432,128]{2,1,0:T(8,128)(2,1)S(1)}, u32[]{:S(2)}, u32[]{:S(2)}) collective-permute-start(bf16[3,432,128]{2,1,0:T(8,128)(2,1)S(1)} %collective-permute-done.5.p1), channel_id=1, source_target_pairs={{0,1},{1,0},{2,3},{3,2},{4,5},{5,4},{6,7},{7,6},{8,9},{9,8},{10,11... | collective-permute-start | bytes 995336 | tf_op jit(solution)/shard_map/ppermute | solution.py:346
  45.2 2.5 %collective-permute-start.13 = (bf16[3,432,128]{2,1,0:T(8,128)(2,1)S(1)}, bf16[3,432,128]{2,1,0:T(8,128)(2,1)S(1)}, u32[]{:S(2)}, u32[]{:S(2)}) collective-permute-start(bf16[3,432,128]{2,1,0:T(8,128)(2,1)S(1)} %collective-permute-done.6.p2), channel_id=1, source_target_pairs={{0,1},{1,0},{2,3},{3,2},{4,5},{5,4},{6,7},{7,6},{8,9},{9,8},{10,11... | collective-permute-start | bytes 995336 | tf_op jit(solution)/shard_map/ppermute | solution.py:346
  45.7 15.2 %copy-start.1 = (f32[1,8,8,8,128]{4,3,2,1,0:T(8,128)S(1)}, f32[1,8,8,8,128]{4,3,2,1,0:T(8,128)}, u32[]{:S(2)}) copy-start(f32[1,8,8,8,128]{4,3,2,1,0:T(8,128)} %param.4) | copy-start | bytes 786436
  45.7 11.4 %collective-permute-start.16 = (f32[512,128]{1,0:T(8,128)S(1)}, f32[512,128]{1,0:T(8,128)S(1)}, u32[]{:S(2)}, u32[]{:S(2)}) collective-permute-start(f32[512,128]{1,0:T(8,128)S(1)} %get-tuple-element.70.term), channel_id=1, source_target_pairs={{0,24},{1,25},{2,26},{3,27},{4,28},{5,29},{6,30},{7,31},{32,56},{3... | collective-permute-start | bytes 786440 | tf_op jit(solution)/shard_map/ppermute | solution.py:348
  50.7 10.2 %collective-permute-start.15 = (f32[512,128]{1,0:T(8,128)S(1)}, f32[512,128]{1,0:T(8,128)S(1)}, u32[]{:S(2)}, u32[]{:S(2)}) collective-permute-start(f32[512,128]{1,0:T(8,128)S(1)} %get-tuple-element.66.point), channel_id=1, source_target_pairs={{0,32},{32,64},{64,96},{96,128},{128,160},{160,192},{192,224},{1,3... | collective-permute-start | bytes 786440 | tf_op jit(solution)/shard_map/ppermute | solution.py:315
  57.2 4.5 %collective-permute-start.17 = (f32[512,128]{1,0:T(8,128)S(1)}, f32[512,128]{1,0:T(8,128)S(1)}, u32[]{:S(2)}, u32[]{:S(2)}) collective-permute-start(f32[512,128]{1,0:T(8,128)S(1)} %get-tuple-element.70.term), channel_id=1, source_target_pairs={{0,8},{1,9},{2,10},{3,11},{4,12},{5,13},{6,14},{7,15},{32,40},{33,... | collective-permute-start | bytes 786440 | tf_op jit(solution)/shard_map/ppermute | solution.py:359
  57.9 6.4 %collective-permute-start.18 = (f32[512,128]{1,0:T(8,128)S(1)}, f32[512,128]{1,0:T(8,128)S(1)}, u32[]{:S(2)}, u32[]{:S(2)}) collective-permute-start(f32[512,128]{1,0:T(8,128)S(1)} %collective-permute-done.16.f3), channel_id=1, source_target_pairs={{24,16},{25,17},{26,18},{27,19},{28,20},{29,21},{30,22},{31,23},{5... | collective-permute-start | bytes 786440 | tf_op jit(solution)/shard_map/ppermute | solution.py:358
  59.2 10.6 %collective-permute-start.20 = (bf16[4,432,128]{2,1,0:T(8,128)(2,1)S(1)}, bf16[4,432,128]{2,1,0:T(8,128)(2,1)S(1)}, u32[]{:S(2)}, u32[]{:S(2)}) collective-permute-start(bf16[4,432,128]{2,1,0:T(8,128)(2,1)S(1)} %get-tuple-element.77), channel_id=1, source_target_pairs={{96,64},{160,128},{97,65},{161,129},{98,66},{162,130},{99,67},{163... | collective-permute-start | bytes 1327112 | tf_op jit(solution)/shard_map/ppermute | solution.py:315
  67.6 2.3 %collective-permute-start.19 = (f32[512,128]{1,0:T(8,128)S(1)}, f32[512,128]{1,0:T(8,128)S(1)}, u32[]{:S(2)}, u32[]{:S(2)}) collective-permute-start(f32[512,128]{1,0:T(8,128)S(1)} %get-tuple-element.73.corner.value), channel_id=1, source_target_pairs={{32,64},{33,65},{34,66},{35,67},{36,68},{37,69},{38,70},{39,71},{4... | collective-permute-start | bytes 786440 | tf_op jit(solution)/shard_map/ppermute | solution.py:315
  69.1 0.8 collective-permute-start.22
  69.8 1.9 %collective-permute-start.21 = (bf16[4,432,128]{2,1,0:T(8,128)(2,1)S(1)}, bf16[4,432,128]{2,1,0:T(8,128)(2,1)S(1)}, u32[]{:S(2)}, u32[]{:S(2)}) collective-permute-start(bf16[4,432,128]{2,1,0:T(8,128)(2,1)S(1)} %collective-permute-done.20.mine), channel_id=1, source_target_pairs={{0,1},{1,0},{2,3},{3,2},{4,5},{5,4},{6,7},{7,6},{8,9},{9,8},{10,11... | collective-permute-start | bytes 1327112 | tf_op jit(solution)/shard_map/ppermute | solution.py:372
  71.7 1.4 %collective-permute-start.23 = (f32[512,128]{1,0:T(8,128)S(1)}, f32[512,128]{1,0:T(8,128)S(1)}, u32[]{:S(2)}, u32[]{:S(2)}) collective-permute-start(f32[512,128]{1,0:T(8,128)S(1)} %next2.1), channel_id=1, source_target_pairs={{64,128},{65,129},{66,130},{67,131},{68,132},{69,133},{70,134},{71... | collective-permute-start | bytes 786440 | tf_op jit(solution)/shard_map/ppermute | solution.py:315
  72.3 0.7 collective-permute-start.24
  73.1 0.7 collective-permute-start.25
  73.8 33.5 %collective-permute-start.26 = (f32[512,128]{1,0:T(8,128)S(1)}, f32[512,128]{1,0:T(8,128)S(1)}, u32[]{:S(2)}, u32[]{:S(2)}) collective-permute-start(f32[512,128]{1,0:T(8,128)S(1)} %get-tuple-element.82.value), channel_id=1, source_target_pairs={{64,96},{128,160},{192,224},{65,97},{129,161},{193,225},{66,98},{1... | collective-permute-start | bytes 786440 | tf_op jit(solution)/shard_map/ppermute | solution.py:315

commit v9 on v8

--- a/solution.py
+++ b/solution.py
@@ -326,14 +326,14 @@
         (barrier((kernels, guess_corner))[0],), "h", [dma(())],
     )
     shares[1] = from_ahead(barrier((shares[0], kept))[0], 1)
-    guess_head, *shares = barrier((guess_head, *shares))
+    guess_head, shares[2] = barrier((guess_head, shares[2]))
     (point,) = call(
         first_kernel, "first", (state,), 4, (guess_head, kept, biases), "vvv",
     )
     head = next_layer(point)
     first_piece = jnp.stack(barrier((point, *shares))[1:])
     pieces = [first_piece] + [
-        lax.ppermute(first_piece, "y", [(i, (i + r) % 4) for i in range(4)]) for r in (1, 3, 2)
+        lax.ppermute(first_piece, "y", [(i, (i + r) % 4) for i in range(4)]) for r in (1, 3)
     ]
     message, term = call(
         second_kernel, "second", (state, state), 1,
@@ -341,11 +341,13 @@
         "vvvv", [buffer],
     )
     m2, m3, m1 = (from_ahead(message, r) for r in (2, 3, 1))
-    pieces, m2, m3 = barrier((pieces, m2, m3))
-    pieces[3], m1 = barrier((pieces[3], m1))
+    pieces[1], message = barrier((pieces[1], message))
+    pieces.append(lax.ppermute(pieces[1], "y", [(i, (i + 1) % 4) for i in range(4)]))
+    pieces, m1, m2, m3 = barrier((pieces, m1, m2, m3))
     pieces += [lax.ppermute(p, "core", [(0, 1), (1, 0)]) for p in pieces]
     term, m3 = barrier((term, m3))
     f3 = lax.ppermute(term, "x", [(0, 3)])
+    f1 = lax.ppermute(term, "x", [(0, 1)])
     stacked = jax.ShapeDtypeStruct((X, ROWS, CH), jnp.float32)
     point, stack, lead, top, part = call(
         third_kernel, "third",
@@ -354,9 +356,8 @@
         3, (message, m1, m2, m3, kept, *pieces), "v" * 13,
     )
     hop = along_z(point, *((i, i + 1) for i in range(Z - 1)))
-    f3, term, _ = barrier((f3, term, point))
-    f2 = lax.ppermute(f3, "x", [(3, 2)])
-    f1 = lax.ppermute(term, "x", [(0, 1)])
+    f1, _ = barrier((f1, point))
+    f2 = lax.ppermute(f1, "x", [(1, 2)])
     next_mine = along_z(part, (3, 2), (5, 4))
     start, partial = call(
         begin_kernel, "begin", (state, state), 2, (inputs, hop, lead), "vvv",

time: 114 us -> 116 us (1.018)
  waiting for transfers between devices: 60.2 us -> 67.2 us
  starting transfers between devices: 27.5 us -> 21.7 us
    ppermute x6, waiting for transfers between devices: 13.6 us -> 23.1 us  [from_ahead(): return lax.ppermute(v, 'x', [(i, (i - r) % X) for i in range(X)])]
    ppermute x6, starting transfers between devices: 9.86 us -> 5.78 us  [from_ahead(): return lax.ppermute(v, 'x', [(i, (i - r) % X) for i in range(X)])]
    ppermute x8, waiting for transfers between devices: 33.3 us -> 37.2 us  [along_z(): return lax.ppermute(v, 'z', pairs)]
    ppermute x1, waiting for transfers between devices: 5.23 us -> 1.68 us  [shards(): f3 = lax.ppermute(term, 'x', [(0, 3)])]
    ppermute x1 -> x2, waiting for transfers between devices: 2.56 us -> 0.01 us  [the longest x1 0.01 us: shards(): lax.ppermute(pieces[1], 'y', [(i, (i + 1) % 4) for i in range(4)])]
    ppermute x3 -> x2, starting transfers between devices: 5.3 us -> 3.31 us  [shards(): lax.ppermute(first_piece, 'y', [(i, (i + r) % 4) for i in range(4)])]
    ppermute x3 -> x2, waiting for transfers between devices: 3.27 us -> 2.24 us  [shards(): lax.ppermute(first_piece, 'y', [(i, (i + r) % 4) for i in range(4)])]
  transfers between devices with their start and end apart: 27 -> 27, of which waited for: 14 -> 12; matrix products, arithmetic and copies ran while one was open for 0% -> 0% of each run, Pallas kernels for 10% -> 13%
where the time goes in v9:
time: 116 us; the launch traced here: 115 us
  waiting for transfers between devices  67.2 us (58%)
  Pallas kernels  23.2 us (20%)
  starting transfers between devices  21.7 us (19%)
  local copies, waits for them, and re-layouts  2.01 us (2%)
    ppermute x8, waiting for transfers between devices, along_z(): return lax.ppermute(v, 'z', pairs)  37.2 us
    pallas_call x14, Pallas kernels, call(): pl.pallas_call(body, name=name, out_shape=outs, in_specs=[specs[p] for p...  23.2 us
    ppermute x6, waiting for transfers between devices, from_ahead(): return lax.ppermute(v, 'x', [(i, (i - r) % X) for i in range(X)])  23.1 us
    ppermute x8, starting transfers between devices, along_z(): return lax.ppermute(v, 'z', pairs)  6.64 us
    ppermute x6, starting transfers between devices, from_ahead(): return lax.ppermute(v, 'x', [(i, (i - r) % X) for i in range(X)])  5.78 us
    ppermute x2, starting transfers between devices, shards(): lax.ppermute(first_piece, 'y', [(i, (i + r) % 4) for i in range(4)])  3.31 us
  transfers between devices with their start and end apart: 27, of which 12 were waited for; matrix products, arithmetic and copies ran while one was open for 0% of the time, Pallas kernels for 13%

profile of v9, /device:TPU:230, one launch (start us, length us, event | category | flops | bytes accessed | tf_op | source)
XLA Modules:
  0.0 115.2 jit_solution(750516814805807721)
XLA Ops:
  0.6 1.8 %prepare.1 = (f32[512,128]{1,0:T(8,128)}, bf16[432,128]{1,0:T(8,128)(2,1)}) custom-call(f32[4,512,128]{2,1,0:T(8,128)} %bitcast.14, f32[512,128]{1,0:T(8,128)} %bitcast.12, bf16[4,8,432,128]{3,2,1,0:T(8,128)(2,1)} %bitcast.10), custom_call_target="tpu_custom_call" | custom-call | tf_op jit(solution)/shard_map/prepare/pallas_call | solution.py:281
  2.4 0.1 collective-permute-start
  2.5 2.0 %collective-permute-start.1 = (bf16[432,128]{1,0:T(8,128)(2,1)}, bf16[432,128]{1,0:T(8,128)(2,1)S(1)}, u32[]{:S(2)}, u32[]{:S(2)}) collective-permute-start(bf16[432,128]{1,0:T(8,128)(2,1)} %get-tuple-element.43), channel_id=1, source_target_pairs={{0,8},{8,16},{16,24},{24,0},{1,9},{9,17},{17,25},{25,1},{2,10},{10... | collective-permute-start | bytes 331784 | tf_op jit(solution)/shard_map/ppermute | solution.py:312
  4.5 0.1 collective-permute-start.2
  4.6 2.0 %copy-done = bf16[4,3,3,3,128,128]{5,4,3,2,1,0:T(8,128)(2,1)S(1)} copy-done((bf16[4,3,3,3,128,128]{5,4,3,2,1,0:T(8,128)(2,1)S(1)}, bf16[4,3,3,3,128,128]{5,4,3,2,1,0:T(8,128)(2,1)}, u32[]{:S(2)}) %copy-start) | copy-done | bytes 3538968
  6.6 0.4 load.1.kernels
  7.0 6.1 %collective-permute-done.1 = bf16[432,128]{1,0:T(8,128)(2,1)S(1)} collective-permute-done((bf16[432,128]{1,0:T(8,128)(2,1)}, bf16[432,128]{1,0:T(8,128)(2,1)S(1)}, u32[]{:S(2)}, u32[]{:S(2)}) %collective-permute-start.1) | collective-permute-done | bytes 110624 | tf_op jit(solution)/shard_map/ppermute | solution.py:312
  13.1 0.0 collective-permute-done.head.guess_head
  13.1 3.3 %first.1 = f32[512,128]{1,0:T(8,128)S(1)} custom-call(f32[512,128]{1,0:T(8,128)S(1)} %collective-permute-done.head.guess_head, bf16[4,8,432,128]{3,2,1,0:T(8,128)(2,1)S(1)} %load.1.kernels, f32[4,128]{1,0:T(4,128)S(1)} %copy-done.2), custom_call_target="tpu_custom_call" | custom-call | tf_op jit(solution)/shard_map/first/pallas_call | solution.py:281
  16.4 1.3 %collective-permute-start.5 = (f32[512,128]{1,0:T(8,128)S(1)}, f32[512,128]{1,0:T(8,128)S(1)}, u32[]{:S(2)}, u32[]{:S(2)}) collective-permute-start(f32[512,128]{1,0:T(8,128)S(1)} %first.1), channel_id=1, source_target_pairs={{0,8},{8,16},{16,24},{24,32},{32,40},{40,48},{48,56},{56,64},{64,7... | collective-permute-start | bytes 786440 | tf_op jit(solution)/shard_map/ppermute | solution.py:309
  17.7 0.0 collective-permute-done.2
  17.7 0.8 collective-permute-start.3
  18.5 5.2 %collective-permute-done.3 = bf16[432,128]{1,0:T(8,128)(2,1)S(1)} collective-permute-done((bf16[432,128]{1,0:T(8,128)(2,1)S(1)}, bf16[432,128]{1,0:T(8,128)(2,1)S(1)}, u32[]{:S(2)}, u32[]{:S(2)}) %collective-permute-start.3) | collective-permute-done | bytes 110624 | tf_op jit(solution)/shard_map/ppermute | solution.py:312
  23.7 1.7 %collective-permute-start.4 = (bf16[3,432,128]{2,1,0:T(8,128)(2,1)S(1)}, bf16[3,432,128]{2,1,0:T(8,128)(2,1)S(1)}, u32[]{:S(2)}, u32[]{:S(2)}) collective-permute-start(bf16[3,432,128]{2,1,0:T(8,128)(2,1)S(1)} %pad_maximum_fusion.p0), channel_id=1, source_target_pairs={{0,2},{2,4},{4,6},{6,0},{1,3},{3,5},{5,7},{7,1},{8,10},{10,12},{12... | collective-permute-start | bytes 995336 | tf_op jit(solution)/shard_map/ppermute | solution.py:336
  25.4 1.7 %collective-permute-start.6 = (bf16[3,432,128]{2,1,0:T(8,128)(2,1)S(1)}, bf16[3,432,128]{2,1,0:T(8,128)(2,1)S(1)}, u32[]{:S(2)}, u32[]{:S(2)}) collective-permute-start(bf16[3,432,128]{2,1,0:T(8,128)(2,1)S(1)} %pad_maximum_fusion.p0), channel_id=1, source_target_pairs={{0,6},{2,0},{4,2},{6,4},{1,7},{3,1},{5,3},{7,5},{8,14},{10,8},{12,... | collective-permute-start | bytes 995336 | tf_op jit(solution)/shard_map/ppermute | solution.py:336
  27.0 0.0 collective-permute-done.5.head
  27.0 3.3 %second.1 = (f32[512,128]{1,0:T(8,128)S(1)}, f32[512,128]{1,0:T(8,128)S(1)}) custom-call(f32[512,128]{1,0:T(8,128)S(1)} %collective-permute-done.5.head, f32[512,128]{1,0:T(8,128)S(1)} %collective-permute-done.head.guess_head, bf16[4,8,432,128]{3,2,1,0:T(8,128)(2,1)S(1)} %load.1.kernels, f32[4,128]{1,0:T(4,128)S(1)} %copy-done.2), custom_call_target="tpu_custom_call" | custom-call | flops 6000000000 | bytes 20000000 | tf_op jit(solution)/shard_map/second/pallas_call | solution.py:281
  30.4 2.2 %collective-permute-done.4.p1 = bf16[3,432,128]{2,1,0:T(8,128)(2,1)S(1)} collective-permute-done((bf16[3,432,128]{2,1,0:T(8,128)(2,1)S(1)}, bf16[3,432,128]{2,1,0:T(8,128)(2,1)S(1)}, u32[]{:S(2)}, u32[]{:S(2)}) %collective-permute-start.4) | collective-permute-done | bytes 331808 | tf_op jit(solution)/shard_map/ppermute | solution.py:336
  32.6 0.7 collective-permute-start.7
  33.3 1.4 %collective-permute-start.10 = (f32[512,128]{1,0:T(8,128)S(1)}, f32[512,128]{1,0:T(8,128)S(1)}, u32[]{:S(2)}, u32[]{:S(2)}) collective-permute-start(f32[512,128]{1,0:T(8,128)S(1)} %get-tuple-element.52.m0), channel_id=1, source_target_pairs={{0,8},{8,16},{16,24},{24,0},{1,9},{9,17},{17,25},{25,1},{2,10},{10... | collective-permute-start | bytes 786440 | tf_op jit(solution)/shard_map/ppermute | solution.py:312
  34.7 0.6 collective-permute-start.8
  35.3 0.9 collective-permute-start.9
  36.2 0.0 collective-permute-done.6.p2
  36.2 8.5 %collective-permute-done.10.m3 = f32[512,128]{1,0:T(8,128)S(1)} collective-permute-done((f32[512,128]{1,0:T(8,128)S(1)}, f32[512,128]{1,0:T(8,128)S(1)}, u32[]{:S(2)}, u32[]{:S(2)}) %collective-permute-start.10) | collective-permute-done | bytes 262176 | tf_op jit(solution)/shard_map/ppermute | solution.py:312
  44.7 3.4 %collective-permute-done.8.m1 = f32[512,128]{1,0:T(8,128)S(1)} collective-permute-done((f32[512,128]{1,0:T(8,128)S(1)}, f32[512,128]{1,0:T(8,128)S(1)}, u32[]{:S(2)}, u32[]{:S(2)}) %collective-permute-start.8) | collective-permute-done | bytes 262176 | tf_op jit(solution)/shard_map/ppermute | solution.py:312
  48.1 0.0 collective-permute-done.9.m2
  48.1 0.0 collective-permute-done.7.p3
  48.1 0.0 collective-permute-start.11
  48.1 0.5 collective-permute-start.12
  48.6 0.1 collective-permute-start.13
  48.7 0.4 collective-permute-start.14
  49.1 0.8 collective-permute-start.16
  49.9 0.0 collective-permute-done.11.o0
  49.9 0.3 collective-permute-done.12.o1
  50.2 0.5 collective-permute-done.13.o2
  50.6 0.5 collective-permute-done.14.o3
  51.1 2.9 %third.1 = (f32[512,128]{1,0:T(8,128)S(1)}, f32[4,512,128]{2,1,0:T(8,128)S(1)}, bf16[4,8,432,128]{3,2,1,0:T(8,128)(2,1)S(1)}, bf16[8,432,128]{2,1,0:T(8,128)(2,1)S(1)}, bf16[4,432,128]{2,1,0:T(8,128)(2,1)S(1)}) custom-call(f32[512,128]{1,0:T(8,128)S(1)} %get-tuple-element.52.m0, f32[512,128]{1,0:T(8,128)S(1)} %collective-permute-done.8.m1, ...), custom_call_target="tpu_custom_call" | custom-call | tf_op jit(solution)/shard_map/third/pallas_call | solution.py:281
  54.0 1.3 %collective-permute-start.15 = (f32[512,128]{1,0:T(8,128)S(1)}, f32[512,128]{1,0:T(8,128)S(1)}, u32[]{:S(2)}, u32[]{:S(2)}) collective-permute-start(f32[512,128]{1,0:T(8,128)S(1)} %get-tuple-element.63.point), channel_id=1, source_target_pairs={{0,32},{32,64},{64,96},{96,128},{128,160},{160,192},{192,224},{1,3... | collective-permute-start | bytes 786440 | tf_op jit(solution)/shard_map/ppermute | solution.py:315
  55.3 1.3 %collective-permute-start.18 = (f32[512,128]{1,0:T(8,128)S(1)}, f32[512,128]{1,0:T(8,128)S(1)}, u32[]{:S(2)}, u32[]{:S(2)}) collective-permute-start(f32[512,128]{1,0:T(8,128)S(1)} %get-tuple-element.66.term), channel_id=1, source_target_pairs={{0,24},{1,25},{2,26},{3,27},{4,28},{5,29},{6,30},{7,31},{32,56},{3... | collective-permute-start | bytes 786440 | tf_op jit(solution)/shard_map/ppermute | solution.py:349
  56.6 0.0 collective-permute-done.16.f1
  56.6 0.7 collective-permute-start.17
  57.3 0.7 collective-permute-start.20
  58.0 6.2 %collective-permute-done.15.hop = f32[512,128]{1,0:T(8,128)S(1)} collective-permute-done((f32[512,128]{1,0:T(8,128)S(1)}, f32[512,128]{1,0:T(8,128)S(1)}, u32[]{:S(2)}, u32[]{:S(2)}) %collective-permute-start.15) | collective-permute-done | bytes 262176 | tf_op jit(solution)/shard_map/ppermute | solution.py:315
  64.2 0.8 begin.1
  65.1 1.7 %collective-permute-done.18.f3 = f32[512,128]{1,0:T(8,128)S(1)} collective-permute-done((f32[512,128]{1,0:T(8,128)S(1)}, f32[512,128]{1,0:T(8,128)S(1)}, u32[]{:S(2)}, u32[]{:S(2)}) %collective-permute-start.18) | collective-permute-done | bytes 262176 | tf_op jit(solution)/shard_map/ppermute | solution.py:349
  66.7 0.0 collective-permute-done.17.f2
  66.8 3.3 %fourth.1 = (f32[512,128]{1,0:T(8,128)}, f32[512,128]{1,0:T(8,128)S(1)}, f32[4,512,128]{2,1,0:T(8,128)S(1)}) custom-call(f32[512,128]{1,0:T(8,128)S(1)} %get-tuple-element.65.partial, f32[512,128]{1,0:T(8,128)S(1)} %get-tuple-element.63.point, f32[512,128]{1,0:T(8,128)S(1)} %get-tuple-element.66.term, f32[512,128]{1,0:T(8,128)S(1)} %collective-permute-done.16.f1, ...), custom_call_target="tpu_custom_call" | custom-call | flops 6000000000 | bytes 20000000 | tf_op jit(solution)/shard_map/fourth/pallas_call | solution.py:281
  70.0 0.7 collective-permute-start.19
  70.7 0.8 defect.1
  71.5 0.7 collective-permute-start.22
  72.2 0.0 collective-permute-done.20.mine
  72.2 0.1 collective-permute-start.21
  72.3 0.0 collective-permute-done.19.came
  72.4 0.0 collective-permute-done.22.defect
  72.4 1.7 %collective-permute-done.21.other = bf16[4,432,128]{2,1,0:T(8,128)(2,1)S(1)} collective-permute-done((bf16[4,432,128]{2,1,0:T(8,128)(2,1)S(1)}, bf16[4,432,128]{2,1,0:T(8,128)(2,1)S(1)}, u32[]{:S(2)}, u32[]{:S(2)}) %collective-permute-start.21) | collective-permute-done | bytes 442400 | tf_op jit(solution)/shard_map/ppermute | solution.py:373
  74.1 0.7 collective-permute-start.23
  74.8 0.7 collective-permute-start.24
  75.5 0.0 collective-permute-done.23.came
  75.5 0.0 collective-permute-done.24.defect
  75.5 0.7 collective-permute-start.25
  76.2 0.0 collective-permute-done.25.came
  76.3 1.3 %collective-permute-start.26 = (f32[512,128]{1,0:T(8,128)S(1)}, f32[512,128]{1,0:T(8,128)S(1)}, u32[]{:S(2)}, u32[]{:S(2)}) collective-permute-start(f32[512,128]{1,0:T(8,128)S(1)} %get-tuple-element.78.value), channel_id=1, source_target_pairs={{64,96},{128,160},{192,224},{65,97},{129,161},{193,225},{66,98},{1... | collective-permute-start | bytes 786440 | tf_op jit(solution)/shard_map/ppermute | solution.py:315
  77.6 30.9 %collective-permute-done.26.came = f32[512,128]{1,0:T(8,128)S(1)} collective-permute-done((f32[512,128]{1,0:T(8,128)S(1)}, f32[512,128]{1,0:T(8,128)S(1)}, u32[]{:S(2)}, u32[]{:S(2)}) %collective-permute-start.26) | collective-permute-done | bytes 262176 | tf_op jit(solution)/shard_map/ppermute | solution.py:315
  108.5 6.5 %last.1 = f32[4,512,128]{2,1,0:T(8,128)} custom-call(f32[512,128]{1,0:T(8,128)S(1)} %collective-permute-done.26.came, f32[512,128]{1,0:T(8,128)S(1)} %get-tuple-element.79.before, f32[512,128]{1,0:T(8,128)S(1)} %get-tuple-element.78.value, f32[512,128]{1,0:T(8,128)S(1)} %defect.1, f32[4,128]{1,0:T(4,128)S(1)} %copy-done.2, ...), custom_call_target="tpu_custom_call" | custom-call | tf_op jit(solution)/shard_map/last/pallas_call | solution.py:281
  (11 shorter events, 0.1 us)
Async XLA Ops:
  2.4 10.7 %collective-permute-start = (f32[512,128]{1,0:T(8,128)}, f32[512,128]{1,0:T(8,128)S(1)}, u32[]{:S(2)}, u32[]{:S(2)}) collective-permute-start(f32[512,128]{1,0:T(8,128)} %get-tuple-element.42), channel_id=1, source_target_pairs={{0,8},{8,16},{16,24},{24,32},{32,40},{40,48},{48,56},{56,64},{64,7... | collective-permute-start | bytes 786440 | tf_op jit(solution)/shard_map/ppermute | solution.py:309
  2.5 10.6 %collective-permute-start.1 = (bf16[432,128]{1,0:T(8,128)(2,1)}, bf16[432,128]{1,0:T(8,128)(2,1)S(1)}, u32[]{:S(2)}, u32[]{:S(2)}) collective-permute-start(bf16[432,128]{1,0:T(8,128)(2,1)} %get-tuple-element.43), channel_id=1, source_target_pairs={{0,8},{8,16},{16,24},{24,0},{1,9},{9,17},{17,25},{25,1},{2,10},{10... | collective-permute-start | bytes 331784 | tf_op jit(solution)/shard_map/ppermute | solution.py:312
  4.5 13.2 %collective-permute-start.2 = (bf16[432,128]{1,0:T(8,128)(2,1)}, bf16[432,128]{1,0:T(8,128)(2,1)S(1)}, u32[]{:S(2)}, u32[]{:S(2)}) collective-permute-start(bf16[432,128]{1,0:T(8,128)(2,1)} %get-tuple-element.43), channel_id=1, source_target_pairs={{0,24},{8,0},{16,8},{24,16},{1,25},{9,1},{17,9},{25,17},{2,26},{10... | collective-permute-start | bytes 331784 | tf_op jit(solution)/shard_map/ppermute | solution.py:312
  4.6 2.0 %copy-start = (bf16[4,3,3,3,128,128]{5,4,3,2,1,0:T(8,128)(2,1)S(1)}, bf16[4,3,3,3,128,128]{5,4,3,2,1,0:T(8,128)(2,1)}, u32[]{:S(2)}) copy-start(bf16[4,3,3,3,128,128]{5,4,3,2,1,0:T(8,128)(2,1)} %param.6) | copy-start | bytes 10616836
  6.6 6.5 %copy-start.2 = (f32[4,128]{1,0:T(4,128)S(1)}, f32[4,128]{1,0:T(4,128)}, u32[]{:S(2)}) copy-start(f32[4,128]{1,0:T(4,128)} %biases.5) | copy-start | bytes 6148
  16.4 10.6 %collective-permute-start.5 = (f32[512,128]{1,0:T(8,128)S(1)}, f32[512,128]{1,0:T(8,128)S(1)}, u32[]{:S(2)}, u32[]{:S(2)}) collective-permute-start(f32[512,128]{1,0:T(8,128)S(1)} %first.1), channel_id=1, source_target_pairs={{0,8},{8,16},{16,24},{24,32},{32,40},{40,48},{48,56},{56,64},{64,7... | collective-permute-start | bytes 786440 | tf_op jit(solution)/shard_map/ppermute | solution.py:309
  17.7 6.0 %collective-permute-start.3 = (bf16[432,128]{1,0:T(8,128)(2,1)S(1)}, bf16[432,128]{1,0:T(8,128)(2,1)S(1)}, u32[]{:S(2)}, u32[]{:S(2)}) collective-permute-start(bf16[432,128]{1,0:T(8,128)(2,1)S(1)} %collective-permute-done.2), channel_id=1, source_target_pairs={{0,24},{8,0},{16,8},{24,16},{1,25},{9,1},{17,9},{25,17},{2,26},{10... | collective-permute-start | bytes 331784 | tf_op jit(solution)/shard_map/ppermute | solution.py:312
  23.7 8.9 %collective-permute-start.4 = (bf16[3,432,128]{2,1,0:T(8,128)(2,1)S(1)}, bf16[3,432,128]{2,1,0:T(8,128)(2,1)S(1)}, u32[]{:S(2)}, u32[]{:S(2)}) collective-permute-start(bf16[3,432,128]{2,1,0:T(8,128)(2,1)S(1)} %pad_maximum_fusion.p0), channel_id=1, source_target_pairs={{0,2},{2,4},{4,6},{6,0},{1,3},{3,5},{5,7},{7,1},{8,10},{10,12},{12... | collective-permute-start | bytes 995336 | tf_op jit(solution)/shard_map/ppermute | solution.py:336
  25.4 10.8 %collective-permute-start.6 = (bf16[3,432,128]{2,1,0:T(8,128)(2,1)S(1)}, bf16[3,432,128]{2,1,0:T(8,128)(2,1)S(1)}, u32[]{:S(2)}, u32[]{:S(2)}) collective-permute-start(bf16[3,432,128]{2,1,0:T(8,128)(2,1)S(1)} %pad_maximum_fusion.p0), channel_id=1, source_target_pairs={{0,6},{2,0},{4,2},{6,4},{1,7},{3,1},{5,3},{7,5},{8,14},{10,8},{12,... | collective-permute-start | bytes 995336 | tf_op jit(solution)/shard_map/ppermute | solution.py:336
  32.6 15.5 %collective-permute-start.7 = (bf16[3,432,128]{2,1,0:T(8,128)(2,1)S(1)}, bf16[3,432,128]{2,1,0:T(8,128)(2,1)S(1)}, u32[]{:S(2)}, u32[]{:S(2)}) collective-permute-start(bf16[3,432,128]{2,1,0:T(8,128)(2,1)S(1)} %collective-permute-done.4.p1), channel_id=1, source_target_pairs={{0,2},{2,4},{4,6},{6,0},{1,3},{3,5},{5,7},{7,1},{8,10},{10,12},{12... | collective-permute-start | bytes 995336 | tf_op jit(solution)/shard_map/ppermute | solution.py:345
  33.3 11.4 %collective-permute-start.10 = (f32[512,128]{1,0:T(8,128)S(1)}, f32[512,128]{1,0:T(8,128)S(1)}, u32[]{:S(2)}, u32[]{:S(2)}) collective-permute-start(f32[512,128]{1,0:T(8,128)S(1)} %get-tuple-element.52.m0), channel_id=1, source_target_pairs={{0,8},{8,16},{16,24},{24,0},{1,9},{9,17},{17,25},{25,1},{2,10},{10... | collective-permute-start | bytes 786440 | tf_op jit(solution)/shard_map/ppermute | solution.py:312
  34.7 13.4 %collective-permute-start.8 = (f32[512,128]{1,0:T(8,128)S(1)}, f32[512,128]{1,0:T(8,128)S(1)}, u32[]{:S(2)}, u32[]{:S(2)}) collective-permute-start(f32[512,128]{1,0:T(8,128)S(1)} %get-tuple-element.52.m0), channel_id=1, source_target_pairs={{0,24},{8,0},{16,8},{24,16},{1,25},{9,1},{17,9},{25,17},{2,26},{10... | collective-permute-start | bytes 786440 | tf_op jit(solution)/shard_map/ppermute | solution.py:312
  35.3 12.8 %collective-permute-start.9 = (f32[512,128]{1,0:T(8,128)S(1)}, f32[512,128]{1,0:T(8,128)S(1)}, u32[]{:S(2)}, u32[]{:S(2)}) collective-permute-start(f32[512,128]{1,0:T(8,128)S(1)} %get-tuple-element.52.m0), channel_id=1, source_target_pairs={{0,16},{8,24},{16,0},{24,8},{1,17},{9,25},{17,1},{25,9},{2,18},{10... | collective-permute-start | bytes 786440 | tf_op jit(solution)/shard_map/ppermute | solution.py:312
  48.1 1.8 %collective-permute-start.11 = (bf16[3,432,128]{2,1,0:T(8,128)(2,1)S(1)}, bf16[3,432,128]{2,1,0:T(8,128)(2,1)S(1)}, u32[]{:S(2)}, u32[]{:S(2)}) collective-permute-start(bf16[3,432,128]{2,1,0:T(8,128)(2,1)S(1)} %pad_maximum_fusion.p0), channel_id=1, source_target_pairs={{0,1},{1,0},{2,3},{3,2},{4,5},{5,4},{6,7},{7,6},{8,9},{9,8},{10,11... | collective-permute-start | bytes 995336 | tf_op jit(solution)/shard_map/ppermute | solution.py:347
  48.1 2.1 %collective-permute-start.12 = (bf16[3,432,128]{2,1,0:T(8,128)(2,1)S(1)}, bf16[3,432,128]{2,1,0:T(8,128)(2,1)S(1)}, u32[]{:S(2)}, u32[]{:S(2)}) collective-permute-start(bf16[3,432,128]{2,1,0:T(8,128)(2,1)S(1)} %collective-permute-done.4.p1), channel_id=1, source_target_pairs={{0,1},{1,0},{2,3},{3,2},{4,5},{5,4},{6,7},{7,6},{8,9},{9,8},{10,11... | collective-permute-start | bytes 995336 | tf_op jit(solution)/shard_map/ppermute | solution.py:347
  48.6 2.1 %collective-permute-start.13 = (bf16[3,432,128]{2,1,0:T(8,128)(2,1)S(1)}, bf16[3,432,128]{2,1,0:T(8,128)(2,1)S(1)}, u32[]{:S(2)}, u32[]{:S(2)}) collective-permute-start(bf16[3,432,128]{2,1,0:T(8,128)(2,1)S(1)} %collective-permute-done.6.p2), channel_id=1, source_target_pairs={{0,1},{1,0},{2,3},{3,2},{4,5},{5,4},{6,7},{7,6},{8,9},{9,8},{10,11... | collective-permute-start | bytes 995336 | tf_op jit(solution)/shard_map/ppermute | solution.py:347
  48.7 2.5 %collective-permute-start.14 = (bf16[3,432,128]{2,1,0:T(8,128)(2,1)S(1)}, bf16[3,432,128]{2,1,0:T(8,128)(2,1)S(1)}, u32[]{:S(2)}, u32[]{:S(2)}) collective-permute-start(bf16[3,432,128]{2,1,0:T(8,128)(2,1)S(1)} %collective-permute-done.7.p3), channel_id=1, source_target_pairs={{0,1},{1,0},{2,3},{3,2},{4,5},{5,4},{6,7},{7,6},{8,9},{9,8},{10,11... | collective-permute-start | bytes 995336 | tf_op jit(solution)/shard_map/ppermute | solution.py:347
  49.1 15.2 %copy-start.1 = (f32[1,8,8,8,128]{4,3,2,1,0:T(8,128)S(1)}, f32[1,8,8,8,128]{4,3,2,1,0:T(8,128)}, u32[]{:S(2)}) copy-start(f32[1,8,8,8,128]{4,3,2,1,0:T(8,128)} %param.4) | copy-start | bytes 786436
  49.1 7.5 %collective-permute-start.16 = (f32[512,128]{1,0:T(8,128)S(1)}, f32[512,128]{1,0:T(8,128)S(1)}, u32[]{:S(2)}, u32[]{:S(2)}) collective-permute-start(f32[512,128]{1,0:T(8,128)S(1)} %get-tuple-element.66.term), channel_id=1, source_target_pairs={{0,8},{1,9},{2,10},{3,11},{4,12},{5,13},{6,14},{7,15},{32,40},{33,... | collective-permute-start | bytes 786440 | tf_op jit(solution)/shard_map/ppermute | solution.py:350
  54.0 10.2 %collective-permute-start.15 = (f32[512,128]{1,0:T(8,128)S(1)}, f32[512,128]{1,0:T(8,128)S(1)}, u32[]{:S(2)}, u32[]{:S(2)}) collective-permute-start(f32[512,128]{1,0:T(8,128)S(1)} %get-tuple-element.63.point), channel_id=1, source_target_pairs={{0,32},{32,64},{64,96},{96,128},{128,160},{160,192},{192,224},{1,3... | collective-permute-start | bytes 786440 | tf_op jit(solution)/shard_map/ppermute | solution.py:315
  55.3 11.5 %collective-permute-start.18 = (f32[512,128]{1,0:T(8,128)S(1)}, f32[512,128]{1,0:T(8,128)S(1)}, u32[]{:S(2)}, u32[]{:S(2)}) collective-permute-start(f32[512,128]{1,0:T(8,128)S(1)} %get-tuple-element.66.term), channel_id=1, source_target_pairs={{0,24},{1,25},{2,26},{3,27},{4,28},{5,29},{6,30},{7,31},{32,56},{3... | collective-permute-start | bytes 786440 | tf_op jit(solution)/shard_map/ppermute | solution.py:349
  56.6 10.1 %collective-permute-start.17 = (f32[512,128]{1,0:T(8,128)S(1)}, f32[512,128]{1,0:T(8,128)S(1)}, u32[]{:S(2)}, u32[]{:S(2)}) collective-permute-start(f32[512,128]{1,0:T(8,128)S(1)} %collective-permute-done.16.f1), channel_id=1, source_target_pairs={{8,16},{9,17},{10,18},{11,19},{12,20},{13,21},{14,22},{15,23},{40,... | collective-permute-start | bytes 786440 | tf_op jit(solution)/shard_map/ppermute | solution.py:360
  57.3 14.9 %collective-permute-start.20 = (bf16[4,432,128]{2,1,0:T(8,128)(2,1)S(1)}, bf16[4,432,128]{2,1,0:T(8,128)(2,1)S(1)}, u32[]{:S(2)}, u32[]{:S(2)}) collective-permute-start(bf16[4,432,128]{2,1,0:T(8,128)(2,1)S(1)} %get-tuple-element.73), channel_id=1, source_target_pairs={{96,64},{160,128},{97,65},{161,129},{98,66},{162,130},{99,67},{163... | collective-permute-start | bytes 1327112 | tf_op jit(solution)/shard_map/ppermute | solution.py:315
  70.0 2.3 %collective-permute-start.19 = (f32[512,128]{1,0:T(8,128)S(1)}, f32[512,128]{1,0:T(8,128)S(1)}, u32[]{:S(2)}, u32[]{:S(2)}) collective-permute-start(f32[512,128]{1,0:T(8,128)S(1)} %get-tuple-element.69.corner.value), channel_id=1, source_target_pairs={{32,64},{33,65},{34,66},{35,67},{36,68},{37,69},{38,70},{39,71},{4... | collective-permute-start | bytes 786440 | tf_op jit(solution)/shard_map/ppermute | solution.py:315
  71.5 0.8 collective-permute-start.22
  72.2 1.9 %collective-permute-start.21 = (bf16[4,432,128]{2,1,0:T(8,128)(2,1)S(1)}, bf16[4,432,128]{2,1,0:T(8,128)(2,1)S(1)}, u32[]{:S(2)}, u32[]{:S(2)}) collective-permute-start(bf16[4,432,128]{2,1,0:T(8,128)(2,1)S(1)} %collective-permute-done.20.mine), channel_id=1, source_target_pairs={{0,1},{1,0},{2,3},{3,2},{4,5},{5,4},{6,7},{7,6},{8,9},{9,8},{10,11... | collective-permute-start | bytes 1327112 | tf_op jit(solution)/shard_map/ppermute | solution.py:373
  74.1 1.4 %collective-permute-start.23 = (f32[512,128]{1,0:T(8,128)S(1)}, f32[512,128]{1,0:T(8,128)S(1)}, u32[]{:S(2)}, u32[]{:S(2)}) collective-permute-start(f32[512,128]{1,0:T(8,128)S(1)} %next2.1), channel_id=1, source_target_pairs={{64,128},{65,129},{66,130},{67,131},{68,132},{69,133},{70,134},{71... | collective-permute-start | bytes 786440 | tf_op jit(solution)/shard_map/ppermute | solution.py:315
  74.8 0.7 collective-permute-start.24
  75.5 0.7 collective-permute-start.25
  76.3 32.2 %collective-permute-start.26 = (f32[512,128]{1,0:T(8,128)S(1)}, f32[512,128]{1,0:T(8,128)S(1)}, u32[]{:S(2)}, u32[]{:S(2)}) collective-permute-start(f32[512,128]{1,0:T(8,128)S(1)} %get-tuple-element.78.value), channel_id=1, source_target_pairs={{64,96},{128,160},{192,224},{65,97},{129,161},{193,225},{66,98},{1... | collective-permute-start | bytes 786440 | tf_op jit(solution)/shard_map/ppermute | solution.py:315

commit v10 on v6

--- a/solution.py
+++ b/solution.py
@@ -317,11 +317,11 @@
     )
     guess_head = next_layer(guess_corner)
     shares = [from_ahead(share, 1), None, from_ahead(share, 3)]
-    shares[1] = from_ahead(shares[0], 1)
     (kept,) = call(
         load_kernel, "load", (jax.ShapeDtypeStruct((4,) + WHOLE, jnp.bfloat16),), 0,
         (barrier((kernels, guess_corner))[0],), "h", [dma(())],
     )
+    shares[1] = from_ahead(barrier((shares[0], kept))[0], 1)
     (point,) = call(
         first_kernel, "first", (state,), 4, (guess_head, kept, biases), "vvv",
     )
@@ -338,7 +338,7 @@
     m2, m3, m1 = (from_ahead(message, r) for r in (2, 3, 1))
     pieces, m2, m3 = barrier((pieces, m2, m3))
     pieces += [lax.ppermute(p, "core", [(0, 1), (1, 0)]) for p in pieces]
-    term, m1, m2, m3 = barrier((term, m1, m2, m3))
+    term, m3 = barrier((term, m3))
     f1, f3 = (lax.ppermute(term, "x", [(0, r)]) for r in (1, 3))
     stacked = jax.ShapeDtypeStruct((X, ROWS, CH), jnp.float32)
     point, stack, lead, top, part = call(
@@ -348,6 +348,7 @@
         3, (message, m1, m2, m3, kept, *pieces), "v" * 13,
     )
     hop = along_z(point, *((i, i + 1) for i in range(Z - 1)))
+    f1, hop_point = barrier((f1, point))
     f2 = lax.ppermute(f1, "x", [(1, 2)])
     next_mine = along_z(part, (3, 2), (5, 4))
     residual, corner, start, stack = call(

time: 111 us -> 108 us (0.973)
  the two profiles are of different devices: /device:TPU:226 before, /device:TPU:250 now
where the time goes in v10:
time: 108 us
  waiting for transfers between devices  57.6 us (53%)
  starting transfers between devices  26.2 us (24%)
  Pallas kernels  20.8 us (19%)
  local copies, waits for them, and re-layouts  2.01 us (2%)
  between operations  1.08 us (1%)
    ppermute x8, waiting for transfers between devices, along_z(): return lax.ppermute(v, 'z', pairs)  34 us
    pallas_call x13, Pallas kernels, call(): pl.pallas_call(body, name=name, out_shape=outs, in_specs=[specs[p] for p...  20.8 us
    ppermute x6, starting transfers between devices, from_ahead(): return lax.ppermute(v, 'x', [(i, (i - r) % X) for i in range(X)])  8.56 us
    ppermute x6, waiting for transfers between devices, from_ahead(): return lax.ppermute(v, 'x', [(i, (i - r) % X) for i in range(X)])  8.32 us
    ppermute x8, starting transfers between devices, along_z(): return lax.ppermute(v, 'z', pairs)  6.64 us
    ppermute x2, waiting for transfers between devices, shards(): f1, f3 = (lax.ppermute(term, 'x', [(0, r)]) for r in (1, 3))  5 us
    ppermute x2, waiting for transfers between devices, next_layer(): lax.ppermute(v, LAYER, [(i, (i + 1) % (X * Z)) for i in range(X * Z)])  4.51 us
    ppermute x3, starting transfers between devices, shards(): lax.ppermute(first_piece, 'y', [(i, (i + r) % 4) for i in range(4)])  3.34 us
  transfers between devices with their start and end apart: 27, of which 12 were waited for; matrix products, arithmetic and copies ran while one was open for 0% of the time, Pallas kernels for 14%

profile of v10, /device:TPU:250, one launch (start us, length us, event | category | flops | bytes accessed | tf_op | source)
XLA Modules:
  0.0 107.7 jit_solution(15097426606103765790)
XLA Ops:
  0.6 1.8 %prepare.1 = (f32[512,128]{1,0:T(8,128)}, bf16[432,128]{1,0:T(8,128)(2,1)}) custom-call(f32[4,512,128]{2,1,0:T(8,128)} %bitcast.14, f32[512,128]{1,0:T(8,128)} %bitcast.12, bf16[4,8,432,128]{3,2,1,0:T(8,128)(2,1)} %bitcast.10), custom_call_target="tpu_custom_call" | custom-call | tf_op jit(solution)/shard_map/prepare/pallas_call | solution.py:277
  2.4 1.6 %collective-permute-start = (f32[512,128]{1,0:T(8,128)}, f32[512,128]{1,0:T(8,128)S(1)}, u32[]{:S(2)}, u32[]{:S(2)}) collective-permute-start(f32[512,128]{1,0:T(8,128)} %get-tuple-element.36), channel_id=1, source_target_pairs={{0,8},{8,16},{16,24},{24,32},{32,40},{40,48},{48,56},{56,64},{64,7... | collective-permute-start | bytes 786440 | tf_op jit(solution)/shard_map/ppermute | solution.py:305
  4.0 0.5 collective-permute-start.3
  4.5 1.5 %collective-permute-start.5 = (bf16[432,128]{1,0:T(8,128)(2,1)}, bf16[432,128]{1,0:T(8,128)(2,1)S(1)}, u32[]{:S(2)}, u32[]{:S(2)}) collective-permute-start(bf16[432,128]{1,0:T(8,128)(2,1)} %get-tuple-element.39), channel_id=1, source_target_pairs={{0,8},{8,16},{16,24},{24,0},{1,9},{9,17},{17,25},{25,1},{2,10},{10... | collective-permute-start | bytes 331784 | tf_op jit(solution)/shard_map/ppermute | solution.py:308
  6.0 2.0 %copy-done = bf16[4,3,3,3,128,128]{5,4,3,2,1,0:T(8,128)(2,1)S(1)} copy-done((bf16[4,3,3,3,128,128]{5,4,3,2,1,0:T(8,128)(2,1)S(1)}, bf16[4,3,3,3,128,128]{5,4,3,2,1,0:T(8,128)(2,1)}, u32[]{:S(2)}) %copy-start) | copy-done | bytes 3538968
  8.0 0.4 load.1.kernels
  8.4 0.5 collective-permute-done.3
  8.9 0.5 collective-permute-start.4
  9.5 2.4 %collective-permute-done.head.guess_head = f32[512,128]{1,0:T(8,128)S(1)} collective-permute-done((f32[512,128]{1,0:T(8,128)}, f32[512,128]{1,0:T(8,128)S(1)}, u32[]{:S(2)}, u32[]{:S(2)}) %collective-permute-start) | collective-permute-done | bytes 262176 | tf_op jit(solution)/shard_map/ppermute | solution.py:305
  11.9 0.0 copy-done.2
  11.9 3.3 %first.1 = f32[512,128]{1,0:T(8,128)S(1)} custom-call(f32[512,128]{1,0:T(8,128)S(1)} %collective-permute-done.head.guess_head, bf16[4,8,432,128]{3,2,1,0:T(8,128)(2,1)S(1)} %load.1.kernels, f32[4,128]{1,0:T(4,128)S(1)} %copy-done.2), custom_call_target="tpu_custom_call" | custom-call | flops 4 | bytes 4 | tf_op jit(solution)/shard_map/first/pallas_call | solution.py:277
  15.2 1.6 %collective-permute-start.1 = (f32[512,128]{1,0:T(8,128)S(1)}, f32[512,128]{1,0:T(8,128)S(1)}, u32[]{:S(2)}, u32[]{:S(2)}) collective-permute-start(f32[512,128]{1,0:T(8,128)S(1)} %first.1), channel_id=1, source_target_pairs={{0,8},{8,16},{16,24},{24,32},{32,40},{40,48},{48,56},{56,64},{64,7... | collective-permute-start | bytes 786440 | tf_op jit(solution)/shard_map/ppermute | solution.py:305
  16.7 0.0 collective-permute-done.5
  16.7 0.0 collective-permute-done.4
  16.8 0.3 collective-permute-start.6
  17.1 1.8 %collective-permute-start.7 = (bf16[3,432,128]{2,1,0:T(8,128)(2,1)S(1)}, bf16[3,432,128]{2,1,0:T(8,128)(2,1)S(1)}, u32[]{:S(2)}, u32[]{:S(2)}) collective-permute-start(bf16[3,432,128]{2,1,0:T(8,128)(2,1)S(1)} %pad_maximum_fusion.p0), channel_id=1, source_target_pairs={{0,6},{2,0},{4,2},{6,4},{1,7},{3,1},{5,3},{7,5},{8,14},{10,8},{12,... | collective-permute-start | bytes 995336 | tf_op jit(solution)/shard_map/ppermute | solution.py:331
  18.9 1.2 %collective-permute-start.8 = (bf16[3,432,128]{2,1,0:T(8,128)(2,1)S(1)}, bf16[3,432,128]{2,1,0:T(8,128)(2,1)S(1)}, u32[]{:S(2)}, u32[]{:S(2)}) collective-permute-start(bf16[3,432,128]{2,1,0:T(8,128)(2,1)S(1)} %pad_maximum_fusion.p0), channel_id=1, source_target_pairs={{0,4},{2,6},{4,0},{6,2},{1,5},{3,7},{5,1},{7,3},{8,12},{10,14},{12... | collective-permute-start | bytes 995336 | tf_op jit(solution)/shard_map/ppermute | solution.py:331
  20.1 2.1 %collective-permute-done.1.head = f32[512,128]{1,0:T(8,128)S(1)} collective-permute-done((f32[512,128]{1,0:T(8,128)S(1)}, f32[512,128]{1,0:T(8,128)S(1)}, u32[]{:S(2)}, u32[]{:S(2)}) %collective-permute-start.1) | collective-permute-done | bytes 262176 | tf_op jit(solution)/shard_map/ppermute | solution.py:305
  22.2 3.3 %second.1 = (f32[512,128]{1,0:T(8,128)S(1)}, f32[512,128]{1,0:T(8,128)S(1)}) custom-call(f32[512,128]{1,0:T(8,128)S(1)} %collective-permute-done.1.head, f32[512,128]{1,0:T(8,128)S(1)} %collective-permute-done.head.guess_head, bf16[4,8,432,128]{3,2,1,0:T(8,128)(2,1)S(1)} %load.1.kernels, f32[4,128]{1,0:T(4,128)S(1)} %copy-done.2), custom_call_target="tpu_custom_call" | custom-call | flops 4 | bytes 4 | tf_op jit(solution)/shard_map/second/pallas_call | solution.py:277
  25.5 1.0 collective-permute-start.10
  26.5 5.0 %collective-permute-start.9 = (f32[512,128]{1,0:T(8,128)S(1)}, f32[512,128]{1,0:T(8,128)S(1)}, u32[]{:S(2)}, u32[]{:S(2)}) collective-permute-start(f32[512,128]{1,0:T(8,128)S(1)} %get-tuple-element.38.m0), channel_id=1, source_target_pairs={{0,16},{8,24},{16,0},{24,8},{1,17},{9,25},{17,1},{25,9},{2,18},{10... | collective-permute-start | bytes 786440 | tf_op jit(solution)/shard_map/ppermute | solution.py:308
  31.5 0.0 collective-permute-done.6.p1
  31.5 0.0 collective-permute-start.2
  31.6 0.9 collective-permute-done.7.p2
  32.5 0.0 collective-permute-done.8.p3
  32.5 4.2 %collective-permute-done.10.m3 = f32[512,128]{1,0:T(8,128)S(1)} collective-permute-done((f32[512,128]{1,0:T(8,128)S(1)}, f32[512,128]{1,0:T(8,128)S(1)}, u32[]{:S(2)}, u32[]{:S(2)}) %collective-permute-start.10) | collective-permute-done | bytes 262176 | tf_op jit(solution)/shard_map/ppermute | solution.py:308
  36.7 1.8 %collective-permute-done.9.m2 = f32[512,128]{1,0:T(8,128)S(1)} collective-permute-done((f32[512,128]{1,0:T(8,128)S(1)}, f32[512,128]{1,0:T(8,128)S(1)}, u32[]{:S(2)}, u32[]{:S(2)}) %collective-permute-start.9) | collective-permute-done | bytes 262176 | tf_op jit(solution)/shard_map/ppermute | solution.py:308
  38.5 0.0 collective-permute-start.11
  38.5 0.5 collective-permute-start.12
  39.1 0.0 collective-permute-start.13
  39.1 0.5 collective-permute-start.14
  39.6 1.8 %collective-permute-done.2.m1 = f32[512,128]{1,0:T(8,128)S(1)} collective-permute-done((f32[512,128]{1,0:T(8,128)S(1)}, f32[512,128]{1,0:T(8,128)S(1)}, u32[]{:S(2)}, u32[]{:S(2)}) %collective-permute-start.2) | collective-permute-done | bytes 262176 | tf_op jit(solution)/shard_map/ppermute | solution.py:308
  41.3 1.3 %collective-permute-start.16 = (f32[512,128]{1,0:T(8,128)S(1)}, f32[512,128]{1,0:T(8,128)S(1)}, u32[]{:S(2)}, u32[]{:S(2)}) collective-permute-start(f32[512,128]{1,0:T(8,128)S(1)} %get-tuple-element.53.term), channel_id=1, source_target_pairs={{0,8},{1,9},{2,10},{3,11},{4,12},{5,13},{6,14},{7,15},{32,40},{33,... | collective-permute-start | bytes 786440 | tf_op jit(solution)/shard_map/ppermute | solution.py:342
  42.6 0.0 collective-permute-done.11.o0
  42.6 0.9 collective-permute-start.18
  43.5 0.0 collective-permute-done.12.o1
  43.5 0.0 collective-permute-done.13.o2
  43.5 0.0 collective-permute-done.14.o3
  43.5 2.9 %third.1 = (f32[512,128]{1,0:T(8,128)S(1)}, f32[4,512,128]{2,1,0:T(8,128)S(1)}, bf16[4,8,432,128]{3,2,1,0:T(8,128)(2,1)S(1)}, bf16[8,432,128]{2,1,0:T(8,128)(2,1)S(1)}, bf16[4,432,128]{2,1,0:T(8,128)(2,1)S(1)}) custom-call(f32[512,128]{1,0:T(8,128)S(1)} %get-tuple-element.38.m0, f32[512,128]{1,0:T(8,128)S(1)} %collective-permute-done.2.m1, ...), custom_call_target="tpu_custom_call" | custom-call | flops 3 | bytes 3 | tf_op jit(solution)/shard_map/third/pallas_call | solution.py:277
  46.4 5.0 %collective-permute-done.16.f1 = f32[512,128]{1,0:T(8,128)S(1)} collective-permute-done((f32[512,128]{1,0:T(8,128)S(1)}, f32[512,128]{1,0:T(8,128)S(1)}, u32[]{:S(2)}, u32[]{:S(2)}) %collective-permute-start.16) | collective-permute-done | bytes 262176 | tf_op jit(solution)/shard_map/ppermute | solution.py:342
  51.4 1.3 %collective-permute-start.17 = (f32[512,128]{1,0:T(8,128)S(1)}, f32[512,128]{1,0:T(8,128)S(1)}, u32[]{:S(2)}, u32[]{:S(2)}) collective-permute-start(f32[512,128]{1,0:T(8,128)S(1)} %collective-permute-done.16.f1), channel_id=1, source_target_pairs={{8,16},{9,17},{10,18},{11,19},{12,20},{13,21},{14,22},{15,23},{40,... | collective-permute-start | bytes 786440 | tf_op jit(solution)/shard_map/ppermute | solution.py:352
  52.7 1.3 %collective-permute-start.15 = (f32[512,128]{1,0:T(8,128)S(1)}, f32[512,128]{1,0:T(8,128)S(1)}, u32[]{:S(2)}, u32[]{:S(2)}) collective-permute-start(f32[512,128]{1,0:T(8,128)S(1)} %get-tuple-element.52.point), channel_id=1, source_target_pairs={{0,32},{32,64},{64,96},{96,128},{128,160},{160,192},{192,224},{1,3... | collective-permute-start | bytes 786440 | tf_op jit(solution)/shard_map/ppermute | solution.py:311
  54.0 0.7 collective-permute-start.20
  54.7 0.0 collective-permute-done.18.f3
  54.7 3.1 %collective-permute-done.17.f2 = f32[512,128]{1,0:T(8,128)S(1)} collective-permute-done((f32[512,128]{1,0:T(8,128)S(1)}, f32[512,128]{1,0:T(8,128)S(1)}, u32[]{:S(2)}, u32[]{:S(2)}) %collective-permute-start.17) | collective-permute-done | bytes 262176 | tf_op jit(solution)/shard_map/ppermute | solution.py:352
  57.8 4.1 %collective-permute-done.15.hop = f32[512,128]{1,0:T(8,128)S(1)} collective-permute-done((f32[512,128]{1,0:T(8,128)S(1)}, f32[512,128]{1,0:T(8,128)S(1)}, u32[]{:S(2)}, u32[]{:S(2)}) %collective-permute-start.15) | collective-permute-done | bytes 262176 | tf_op jit(solution)/shard_map/ppermute | solution.py:311
  62.0 4.1 %fourth.1 = (f32[512,128]{1,0:T(8,128)}, f32[512,128]{1,0:T(8,128)S(1)}, f32[512,128]{1,0:T(8,128)S(1)}, f32[4,512,128]{2,1,0:T(8,128)S(1)}) custom-call(f32[512,128]{1,0:T(8,128)S(1)} %bitcast.13, f32[512,128]{1,0:T(8,128)S(1)} %collective-permute-done.15.hop, f32[512,128]{1,0:T(8,128)S(1)} %get-tuple-element.52.point, ...), custom_call_target="tpu_custom_call" | custom-call | flops 6000000000 | bytes 20000000 | tf_op jit(solution)/shard_map/fourth/pallas_call | solution.py:277
  66.0 0.7 collective-permute-start.19
  66.7 0.8 defect.1
  67.5 0.7 collective-permute-start.22
  68.2 0.0 collective-permute-done.20.mine
  68.2 0.1 collective-permute-start.21
  68.3 0.0 collective-permute-done.19.came
  68.4 0.0 collective-permute-done.22.defect
  68.4 1.7 %collective-permute-done.21.other = bf16[4,432,128]{2,1,0:T(8,128)(2,1)S(1)} collective-permute-done((bf16[4,432,128]{2,1,0:T(8,128)(2,1)S(1)}, bf16[4,432,128]{2,1,0:T(8,128)(2,1)S(1)}, u32[]{:S(2)}, u32[]{:S(2)}) %collective-permute-start.21) | collective-permute-done | bytes 442400 | tf_op jit(solution)/shard_map/ppermute | solution.py:362
  70.1 0.7 collective-permute-start.23
  70.8 0.7 collective-permute-start.24
  71.5 0.0 collective-permute-done.23.came
  71.5 0.0 collective-permute-done.24.defect
  71.5 0.7 collective-permute-start.25
  72.2 0.0 collective-permute-done.25.came
  72.3 1.3 %collective-permute-start.26 = (f32[512,128]{1,0:T(8,128)S(1)}, f32[512,128]{1,0:T(8,128)S(1)}, u32[]{:S(2)}, u32[]{:S(2)}) collective-permute-start(f32[512,128]{1,0:T(8,128)S(1)} %get-tuple-element.66.value), channel_id=1, source_target_pairs={{64,96},{128,160},{192,224},{65,97},{129,161},{193,225},{66,98},{1... | collective-permute-start | bytes 786440 | tf_op jit(solution)/shard_map/ppermute | solution.py:311
  73.6 29.8 %collective-permute-done.26.came = f32[512,128]{1,0:T(8,128)S(1)} collective-permute-done((f32[512,128]{1,0:T(8,128)S(1)}, f32[512,128]{1,0:T(8,128)S(1)}, u32[]{:S(2)}, u32[]{:S(2)}) %collective-permute-start.26) | collective-permute-done | bytes 262176 | tf_op jit(solution)/shard_map/ppermute | solution.py:311
  103.4 4.2 %last.1 = f32[4,512,128]{2,1,0:T(8,128)} custom-call(f32[512,128]{1,0:T(8,128)S(1)} %collective-permute-done.26.came, f32[512,128]{1,0:T(8,128)S(1)} %get-tuple-element.67.before, f32[512,128]{1,0:T(8,128)S(1)} %get-tuple-element.66.value, f32[512,128]{1,0:T(8,128)S(1)} %defect.1, f32[4,128]{1,0:T(4,128)S(1)} %copy-done.2, ...), custom_call_target="tpu_custom_call" | custom-call | flops 6 | bytes 6 | tf_op jit(solution)/shard_map/last/pallas_call | solution.py:277
  (10 shorter events, 0.1 us)
Async XLA Ops:
  2.4 9.5 %collective-permute-start = (f32[512,128]{1,0:T(8,128)}, f32[512,128]{1,0:T(8,128)S(1)}, u32[]{:S(2)}, u32[]{:S(2)}) collective-permute-start(f32[512,128]{1,0:T(8,128)} %get-tuple-element.36), channel_id=1, source_target_pairs={{0,8},{8,16},{16,24},{24,32},{32,40},{40,48},{48,56},{56,64},{64,7... | collective-permute-start | bytes 786440 | tf_op jit(solution)/shard_map/ppermute | solution.py:305
  4.0 5.0 %collective-permute-start.3 = (bf16[432,128]{1,0:T(8,128)(2,1)}, bf16[432,128]{1,0:T(8,128)(2,1)S(1)}, u32[]{:S(2)}, u32[]{:S(2)}) collective-permute-start(bf16[432,128]{1,0:T(8,128)(2,1)} %get-tuple-element.39), channel_id=1, source_target_pairs={{0,24},{8,0},{16,8},{24,16},{1,25},{9,1},{17,9},{25,17},{2,26},{10... | collective-permute-start | bytes 331784 | tf_op jit(solution)/shard_map/ppermute | solution.py:308
  4.5 12.2 %collective-permute-start.5 = (bf16[432,128]{1,0:T(8,128)(2,1)}, bf16[432,128]{1,0:T(8,128)(2,1)S(1)}, u32[]{:S(2)}, u32[]{:S(2)}) collective-permute-start(bf16[432,128]{1,0:T(8,128)(2,1)} %get-tuple-element.39), channel_id=1, source_target_pairs={{0,8},{8,16},{16,24},{24,0},{1,9},{9,17},{17,25},{25,1},{2,10},{10... | collective-permute-start | bytes 331784 | tf_op jit(solution)/shard_map/ppermute | solution.py:308
  6.0 2.0 %copy-start = (bf16[4,3,3,3,128,128]{5,4,3,2,1,0:T(8,128)(2,1)S(1)}, bf16[4,3,3,3,128,128]{5,4,3,2,1,0:T(8,128)(2,1)}, u32[]{:S(2)}) copy-start(bf16[4,3,3,3,128,128]{5,4,3,2,1,0:T(8,128)(2,1)} %param.6) | copy-start | bytes 10616836
  8.0 3.9 %copy-start.2 = (f32[4,128]{1,0:T(4,128)S(1)}, f32[4,128]{1,0:T(4,128)}, u32[]{:S(2)}) copy-start(f32[4,128]{1,0:T(4,128)} %biases.5) | copy-start | bytes 6148
  8.9 7.8 %collective-permute-start.4 = (bf16[432,128]{1,0:T(8,128)(2,1)S(1)}, bf16[432,128]{1,0:T(8,128)(2,1)S(1)}, u32[]{:S(2)}, u32[]{:S(2)}) collective-permute-start(bf16[432,128]{1,0:T(8,128)(2,1)S(1)} %collective-permute-done.3), channel_id=1, source_target_pairs={{0,24},{8,0},{16,8},{24,16},{1,25},{9,1},{17,9},{25,17},{2,26},{10... | collective-permute-start | bytes 331784 | tf_op jit(solution)/shard_map/ppermute | solution.py:308
  15.2 7.1 %collective-permute-start.1 = (f32[512,128]{1,0:T(8,128)S(1)}, f32[512,128]{1,0:T(8,128)S(1)}, u32[]{:S(2)}, u32[]{:S(2)}) collective-permute-start(f32[512,128]{1,0:T(8,128)S(1)} %first.1), channel_id=1, source_target_pairs={{0,8},{8,16},{16,24},{24,32},{32,40},{40,48},{48,56},{56,64},{64,7... | collective-permute-start | bytes 786440 | tf_op jit(solution)/shard_map/ppermute | solution.py:305
  16.8 14.8 %collective-permute-start.6 = (bf16[3,432,128]{2,1,0:T(8,128)(2,1)S(1)}, bf16[3,432,128]{2,1,0:T(8,128)(2,1)S(1)}, u32[]{:S(2)}, u32[]{:S(2)}) collective-permute-start(bf16[3,432,128]{2,1,0:T(8,128)(2,1)S(1)} %pad_maximum_fusion.p0), channel_id=1, source_target_pairs={{0,2},{2,4},{4,6},{6,0},{1,3},{3,5},{5,7},{7,1},{8,10},{10,12},{12... | collective-permute-start | bytes 995336 | tf_op jit(solution)/shard_map/ppermute | solution.py:331
  17.1 15.4 %collective-permute-start.7 = (bf16[3,432,128]{2,1,0:T(8,128)(2,1)S(1)}, bf16[3,432,128]{2,1,0:T(8,128)(2,1)S(1)}, u32[]{:S(2)}, u32[]{:S(2)}) collective-permute-start(bf16[3,432,128]{2,1,0:T(8,128)(2,1)S(1)} %pad_maximum_fusion.p0), channel_id=1, source_target_pairs={{0,6},{2,0},{4,2},{6,4},{1,7},{3,1},{5,3},{7,5},{8,14},{10,8},{12,... | collective-permute-start | bytes 995336 | tf_op jit(solution)/shard_map/ppermute | solution.py:331
  18.9 13.6 %collective-permute-start.8 = (bf16[3,432,128]{2,1,0:T(8,128)(2,1)S(1)}, bf16[3,432,128]{2,1,0:T(8,128)(2,1)S(1)}, u32[]{:S(2)}, u32[]{:S(2)}) collective-permute-start(bf16[3,432,128]{2,1,0:T(8,128)(2,1)S(1)} %pad_maximum_fusion.p0), channel_id=1, source_target_pairs={{0,4},{2,6},{4,0},{6,2},{1,5},{3,7},{5,1},{7,3},{8,12},{10,14},{12... | collective-permute-start | bytes 995336 | tf_op jit(solution)/shard_map/ppermute | solution.py:331
  25.5 11.2 %collective-permute-start.10 = (f32[512,128]{1,0:T(8,128)S(1)}, f32[512,128]{1,0:T(8,128)S(1)}, u32[]{:S(2)}, u32[]{:S(2)}) collective-permute-start(f32[512,128]{1,0:T(8,128)S(1)} %get-tuple-element.38.m0), channel_id=1, source_target_pairs={{0,8},{8,16},{16,24},{24,0},{1,9},{9,17},{17,25},{25,1},{2,10},{10... | collective-permute-start | bytes 786440 | tf_op jit(solution)/shard_map/ppermute | solution.py:308
  26.5 12.0 %collective-permute-start.9 = (f32[512,128]{1,0:T(8,128)S(1)}, f32[512,128]{1,0:T(8,128)S(1)}, u32[]{:S(2)}, u32[]{:S(2)}) collective-permute-start(f32[512,128]{1,0:T(8,128)S(1)} %get-tuple-element.38.m0), channel_id=1, source_target_pairs={{0,16},{8,24},{16,0},{24,8},{1,17},{9,25},{17,1},{25,9},{2,18},{10... | collective-permute-start | bytes 786440 | tf_op jit(solution)/shard_map/ppermute | solution.py:308
  31.5 9.8 %collective-permute-start.2 = (f32[512,128]{1,0:T(8,128)S(1)}, f32[512,128]{1,0:T(8,128)S(1)}, u32[]{:S(2)}, u32[]{:S(2)}) collective-permute-start(f32[512,128]{1,0:T(8,128)S(1)} %get-tuple-element.38.m0), channel_id=1, source_target_pairs={{0,24},{8,0},{16,8},{24,16},{1,25},{9,1},{17,9},{25,17},{2,26},{10... | collective-permute-start | bytes 786440 | tf_op jit(solution)/shard_map/ppermute | solution.py:308
  38.5 4.1 %collective-permute-start.11 = (bf16[3,432,128]{2,1,0:T(8,128)(2,1)S(1)}, bf16[3,432,128]{2,1,0:T(8,128)(2,1)S(1)}, u32[]{:S(2)}, u32[]{:S(2)}) collective-permute-start(bf16[3,432,128]{2,1,0:T(8,128)(2,1)S(1)} %pad_maximum_fusion.p0), channel_id=1, source_target_pairs={{0,1},{1,0},{2,3},{3,2},{4,5},{5,4},{6,7},{7,6},{8,9},{9,8},{10,11... | collective-permute-start | bytes 995336 | tf_op jit(solution)/shard_map/ppermute | solution.py:340
  38.5 4.9 %collective-permute-start.12 = (bf16[3,432,128]{2,1,0:T(8,128)(2,1)S(1)}, bf16[3,432,128]{2,1,0:T(8,128)(2,1)S(1)}, u32[]{:S(2)}, u32[]{:S(2)}) collective-permute-start(bf16[3,432,128]{2,1,0:T(8,128)(2,1)S(1)} %collective-permute-done.6.p1), channel_id=1, source_target_pairs={{0,1},{1,0},{2,3},{3,2},{4,5},{5,4},{6,7},{7,6},{8,9},{9,8},{10,11... | collective-permute-start | bytes 995336 | tf_op jit(solution)/shard_map/ppermute | solution.py:340
  39.1 4.4 %collective-permute-start.13 = (bf16[3,432,128]{2,1,0:T(8,128)(2,1)S(1)}, bf16[3,432,128]{2,1,0:T(8,128)(2,1)S(1)}, u32[]{:S(2)}, u32[]{:S(2)}) collective-permute-start(bf16[3,432,128]{2,1,0:T(8,128)(2,1)S(1)} %collective-permute-done.7.p2), channel_id=1, source_target_pairs={{0,1},{1,0},{2,3},{3,2},{4,5},{5,4},{6,7},{7,6},{8,9},{9,8},{10,11... | collective-permute-start | bytes 995336 | tf_op jit(solution)/shard_map/ppermute | solution.py:340
  39.1 4.5 %collective-permute-start.14 = (bf16[3,432,128]{2,1,0:T(8,128)(2,1)S(1)}, bf16[3,432,128]{2,1,0:T(8,128)(2,1)S(1)}, u32[]{:S(2)}, u32[]{:S(2)}) collective-permute-start(bf16[3,432,128]{2,1,0:T(8,128)(2,1)S(1)} %collective-permute-done.8.p3), channel_id=1, source_target_pairs={{0,1},{1,0},{2,3},{3,2},{4,5},{5,4},{6,7},{7,6},{8,9},{9,8},{10,11... | collective-permute-start | bytes 995336 | tf_op jit(solution)/shard_map/ppermute | solution.py:340
  39.6 22.4 %copy-start.1 = (f32[1,8,8,8,128]{4,3,2,1,0:T(8,128)S(1)}, f32[1,8,8,8,128]{4,3,2,1,0:T(8,128)}, u32[]{:S(2)}) copy-start(f32[1,8,8,8,128]{4,3,2,1,0:T(8,128)} %param.4) | copy-start | bytes 786436
  41.3 10.1 %collective-permute-start.16 = (f32[512,128]{1,0:T(8,128)S(1)}, f32[512,128]{1,0:T(8,128)S(1)}, u32[]{:S(2)}, u32[]{:S(2)}) collective-permute-start(f32[512,128]{1,0:T(8,128)S(1)} %get-tuple-element.53.term), channel_id=1, source_target_pairs={{0,8},{1,9},{2,10},{3,11},{4,12},{5,13},{6,14},{7,15},{32,40},{33,... | collective-permute-start | bytes 786440 | tf_op jit(solution)/shard_map/ppermute | solution.py:342
  42.6 12.1 %collective-permute-start.18 = (f32[512,128]{1,0:T(8,128)S(1)}, f32[512,128]{1,0:T(8,128)S(1)}, u32[]{:S(2)}, u32[]{:S(2)}) collective-permute-start(f32[512,128]{1,0:T(8,128)S(1)} %get-tuple-element.53.term), channel_id=1, source_target_pairs={{0,24},{1,25},{2,26},{3,27},{4,28},{5,29},{6,30},{7,31},{32,56},{3... | collective-permute-start | bytes 786440 | tf_op jit(solution)/shard_map/ppermute | solution.py:342
  51.4 6.4 %collective-permute-start.17 = (f32[512,128]{1,0:T(8,128)S(1)}, f32[512,128]{1,0:T(8,128)S(1)}, u32[]{:S(2)}, u32[]{:S(2)}) collective-permute-start(f32[512,128]{1,0:T(8,128)S(1)} %collective-permute-done.16.f1), channel_id=1, source_target_pairs={{8,16},{9,17},{10,18},{11,19},{12,20},{13,21},{14,22},{15,23},{40,... | collective-permute-start | bytes 786440 | tf_op jit(solution)/shard_map/ppermute | solution.py:352
  52.7 9.2 %collective-permute-start.15 = (f32[512,128]{1,0:T(8,128)S(1)}, f32[512,128]{1,0:T(8,128)S(1)}, u32[]{:S(2)}, u32[]{:S(2)}) collective-permute-start(f32[512,128]{1,0:T(8,128)S(1)} %get-tuple-element.52.point), channel_id=1, source_target_pairs={{0,32},{32,64},{64,96},{96,128},{128,160},{160,192},{192,224},{1,3... | collective-permute-start | bytes 786440 | tf_op jit(solution)/shard_map/ppermute | solution.py:311
  54.0 14.2 %collective-permute-start.20 = (bf16[4,432,128]{2,1,0:T(8,128)(2,1)S(1)}, bf16[4,432,128]{2,1,0:T(8,128)(2,1)S(1)}, u32[]{:S(2)}, u32[]{:S(2)}) collective-permute-start(bf16[4,432,128]{2,1,0:T(8,128)(2,1)S(1)} %get-tuple-element.61), channel_id=1, source_target_pairs={{96,64},{160,128},{97,65},{161,129},{98,66},{162,130},{99,67},{163... | collective-permute-start | bytes 1327112 | tf_op jit(solution)/shard_map/ppermute | solution.py:311
  66.0 2.3 %collective-permute-start.19 = (f32[512,128]{1,0:T(8,128)S(1)}, f32[512,128]{1,0:T(8,128)S(1)}, u32[]{:S(2)}, u32[]{:S(2)}) collective-permute-start(f32[512,128]{1,0:T(8,128)S(1)} %get-tuple-element.57.corner.value), channel_id=1, source_target_pairs={{32,64},{33,65},{34,66},{35,67},{36,68},{37,69},{38,70},{39,71},{4... | collective-permute-start | bytes 786440 | tf_op jit(solution)/shard_map/ppermute | solution.py:311
  67.5 0.8 collective-permute-start.22
  68.2 1.9 %collective-permute-start.21 = (bf16[4,432,128]{2,1,0:T(8,128)(2,1)S(1)}, bf16[4,432,128]{2,1,0:T(8,128)(2,1)S(1)}, u32[]{:S(2)}, u32[]{:S(2)}) collective-permute-start(bf16[4,432,128]{2,1,0:T(8,128)(2,1)S(1)} %collective-permute-done.20.mine), channel_id=1, source_target_pairs={{0,1},{1,0},{2,3},{3,2},{4,5},{5,4},{6,7},{7,6},{8,9},{9,8},{10,11... | collective-permute-start | bytes 1327112 | tf_op jit(solution)/shard_map/ppermute | solution.py:362
  70.1 1.4 %collective-permute-start.23 = (f32[512,128]{1,0:T(8,128)S(1)}, f32[512,128]{1,0:T(8,128)S(1)}, u32[]{:S(2)}, u32[]{:S(2)}) collective-permute-start(f32[512,128]{1,0:T(8,128)S(1)} %next2.1), channel_id=1, source_target_pairs={{64,128},{65,129},{66,130},{67,131},{68,132},{69,133},{70,134},{71... | collective-permute-start | bytes 786440 | tf_op jit(solution)/shard_map/ppermute | solution.py:311
  70.8 0.7 collective-permute-start.24
  71.5 0.7 collective-permute-start.25
  72.3 31.1 %collective-permute-start.26 = (f32[512,128]{1,0:T(8,128)S(1)}, f32[512,128]{1,0:T(8,128)S(1)}, u32[]{:S(2)}, u32[]{:S(2)}) collective-permute-start(f32[512,128]{1,0:T(8,128)S(1)} %get-tuple-element.66.value), channel_id=1, source_target_pairs={{64,96},{128,160},{192,224},{65,97},{129,161},{193,225},{66,98},{1... | collective-permute-start | bytes 786440 | tf_op jit(solution)/shard_map/ppermute | solution.py:311

commit v11 on v10

--- a/solution.py
+++ b/solution.py
@@ -27,15 +27,18 @@
     lhs = jnp.concatenate(
         [s.reshape(ROWS, CH).astype(jnp.bfloat16) for s in (before, t, after)], 1
     )
-    rhs = jnp.concatenate([weights[n * DEEP : (n + 1) * DEEP] for n in range(TAPS)], 1)
-    out = jnp.dot(lhs, rhs, preferred_element_type=jnp.float32)
+    taps = [weights[n * DEEP : (n + 1) * DEEP] for n in range(TAPS)]
+    first, second = (
+        jnp.dot(lhs, jnp.concatenate(part, 1), preferred_element_type=jnp.float32)
+        for part in (taps[:6], taps[6:])
+    )
     edge_y = jnp.zeros((8, 1, 8, CH), jnp.float32)
     edge_x = jnp.zeros((1, 8, 8, CH), jnp.float32)
     total = None
     for dx in range(3):
         for dy in range(3):
             n = dx * 3 + dy
-            part = out[:, n * CH : (n + 1) * CH].reshape(8, 8, 8, CH)
+            part = (first if n < 6 else second)[:, n % 6 * CH : (n % 6 + 1) * CH].reshape(8, 8, 8, CH)
             if dy == 0:
                 part = jnp.concatenate([edge_y, part[:, :7]], 1)
             if dy == 2:

time: 108 us -> 108 us (level)
  no operation moved by 1% of the time
where the time goes in v11:
time: 108 us
  waiting for transfers between devices  57.6 us (53%)
  starting transfers between devices  26.2 us (24%)
  Pallas kernels  20.8 us (19%)
  local copies, waits for them, and re-layouts  2.01 us (2%)
  between operations  1.08 us (1%)
    ppermute x8, waiting for transfers between devices, along_z(): return lax.ppermute(v, 'z', pairs)  34 us
    pallas_call x13, Pallas kernels, call(): pl.pallas_call(body, name=name, out_shape=outs, in_specs=[specs[p] for p...  20.8 us
    ppermute x6, starting transfers between devices, from_ahead(): return lax.ppermute(v, 'x', [(i, (i - r) % X) for i in range(X)])  8.56 us
    ppermute x6, waiting for transfers between devices, from_ahead(): return lax.ppermute(v, 'x', [(i, (i - r) % X) for i in range(X)])  8.32 us
    ppermute x8, starting transfers between devices, along_z(): return lax.ppermute(v, 'z', pairs)  6.64 us
    ppermute x2, waiting for transfers between devices, shards(): f1, f3 = (lax.ppermute(term, 'x', [(0, r)]) for r in (1, 3))  5 us
    ppermute x2, waiting for transfers between devices, next_layer(): lax.ppermute(v, LAYER, [(i, (i + 1) % (X * Z)) for i in range(X * Z)])  4.51 us
    ppermute x3, starting transfers between devices, shards(): lax.ppermute(first_piece, 'y', [(i, (i + r) % 4) for i in range(4)])  3.34 us
  transfers between devices with their start and end apart: 27, of which 12 were waited for; matrix products, arithmetic and copies ran while one was open for 0% of the time, Pallas kernels for 14%

profile of v11, /device:TPU:250, one launch (start us, length us, event | category | flops | bytes accessed | tf_op | source)
XLA Modules:
  0.0 107.7 jit_solution(15097426606103765790)
XLA Ops:
  0.6 1.8 %prepare.1 = (f32[512,128]{1,0:T(8,128)}, bf16[432,128]{1,0:T(8,128)(2,1)}) custom-call(f32[4,512,128]{2,1,0:T(8,128)} %bitcast.14, f32[512,128]{1,0:T(8,128)} %bitcast.12, bf16[4,8,432,128]{3,2,1,0:T(8,128)(2,1)} %bitcast.10), custom_call_target="tpu_custom_call" | custom-call | tf_op jit(solution)/shard_map/prepare/pallas_call | solution.py:280
  2.4 1.6 %collective-permute-start = (f32[512,128]{1,0:T(8,128)}, f32[512,128]{1,0:T(8,128)S(1)}, u32[]{:S(2)}, u32[]{:S(2)}) collective-permute-start(f32[512,128]{1,0:T(8,128)} %get-tuple-element.36), channel_id=1, source_target_pairs={{0,8},{8,16},{16,24},{24,32},{32,40},{40,48},{48,56},{56,64},{64,7... | collective-permute-start | bytes 786440 | tf_op jit(solution)/shard_map/ppermute | solution.py:308
  4.0 0.5 collective-permute-start.3
  4.5 1.5 %collective-permute-start.5 = (bf16[432,128]{1,0:T(8,128)(2,1)}, bf16[432,128]{1,0:T(8,128)(2,1)S(1)}, u32[]{:S(2)}, u32[]{:S(2)}) collective-permute-start(bf16[432,128]{1,0:T(8,128)(2,1)} %get-tuple-element.39), channel_id=1, source_target_pairs={{0,8},{8,16},{16,24},{24,0},{1,9},{9,17},{17,25},{25,1},{2,10},{10... | collective-permute-start | bytes 331784 | tf_op jit(solution)/shard_map/ppermute | solution.py:311
  6.0 2.0 %copy-done = bf16[4,3,3,3,128,128]{5,4,3,2,1,0:T(8,128)(2,1)S(1)} copy-done((bf16[4,3,3,3,128,128]{5,4,3,2,1,0:T(8,128)(2,1)S(1)}, bf16[4,3,3,3,128,128]{5,4,3,2,1,0:T(8,128)(2,1)}, u32[]{:S(2)}) %copy-start) | copy-done | bytes 3538968
  8.0 0.4 load.1.kernels
  8.4 0.5 collective-permute-done.3
  8.9 0.5 collective-permute-start.4
  9.5 2.4 %collective-permute-done.head.guess_head = f32[512,128]{1,0:T(8,128)S(1)} collective-permute-done((f32[512,128]{1,0:T(8,128)}, f32[512,128]{1,0:T(8,128)S(1)}, u32[]{:S(2)}, u32[]{:S(2)}) %collective-permute-start) | collective-permute-done | bytes 262176 | tf_op jit(solution)/shard_map/ppermute | solution.py:308
  11.9 0.0 copy-done.2
  11.9 3.3 %first.1 = f32[512,128]{1,0:T(8,128)S(1)} custom-call(f32[512,128]{1,0:T(8,128)S(1)} %collective-permute-done.head.guess_head, bf16[4,8,432,128]{3,2,1,0:T(8,128)(2,1)S(1)} %load.1.kernels, f32[4,128]{1,0:T(4,128)S(1)} %copy-done.2), custom_call_target="tpu_custom_call" | custom-call | flops 4 | bytes 4 | tf_op jit(solution)/shard_map/first/pallas_call | solution.py:280
  15.2 1.6 %collective-permute-start.1 = (f32[512,128]{1,0:T(8,128)S(1)}, f32[512,128]{1,0:T(8,128)S(1)}, u32[]{:S(2)}, u32[]{:S(2)}) collective-permute-start(f32[512,128]{1,0:T(8,128)S(1)} %first.1), channel_id=1, source_target_pairs={{0,8},{8,16},{16,24},{24,32},{32,40},{40,48},{48,56},{56,64},{64,7... | collective-permute-start | bytes 786440 | tf_op jit(solution)/shard_map/ppermute | solution.py:308
  16.7 0.0 collective-permute-done.5
  16.7 0.0 collective-permute-done.4
  16.8 0.3 collective-permute-start.6
  17.1 1.8 %collective-permute-start.7 = (bf16[3,432,128]{2,1,0:T(8,128)(2,1)S(1)}, bf16[3,432,128]{2,1,0:T(8,128)(2,1)S(1)}, u32[]{:S(2)}, u32[]{:S(2)}) collective-permute-start(bf16[3,432,128]{2,1,0:T(8,128)(2,1)S(1)} %pad_maximum_fusion.p0), channel_id=1, source_target_pairs={{0,6},{2,0},{4,2},{6,4},{1,7},{3,1},{5,3},{7,5},{8,14},{10,8},{12,... | collective-permute-start | bytes 995336 | tf_op jit(solution)/shard_map/ppermute | solution.py:334
  18.9 1.2 %collective-permute-start.8 = (bf16[3,432,128]{2,1,0:T(8,128)(2,1)S(1)}, bf16[3,432,128]{2,1,0:T(8,128)(2,1)S(1)}, u32[]{:S(2)}, u32[]{:S(2)}) collective-permute-start(bf16[3,432,128]{2,1,0:T(8,128)(2,1)S(1)} %pad_maximum_fusion.p0), channel_id=1, source_target_pairs={{0,4},{2,6},{4,0},{6,2},{1,5},{3,7},{5,1},{7,3},{8,12},{10,14},{12... | collective-permute-start | bytes 995336 | tf_op jit(solution)/shard_map/ppermute | solution.py:334
  20.1 2.1 %collective-permute-done.1.head = f32[512,128]{1,0:T(8,128)S(1)} collective-permute-done((f32[512,128]{1,0:T(8,128)S(1)}, f32[512,128]{1,0:T(8,128)S(1)}, u32[]{:S(2)}, u32[]{:S(2)}) %collective-permute-start.1) | collective-permute-done | bytes 262176 | tf_op jit(solution)/shard_map/ppermute | solution.py:308
  22.2 3.3 %second.1 = (f32[512,128]{1,0:T(8,128)S(1)}, f32[512,128]{1,0:T(8,128)S(1)}) custom-call(f32[512,128]{1,0:T(8,128)S(1)} %collective-permute-done.1.head, f32[512,128]{1,0:T(8,128)S(1)} %collective-permute-done.head.guess_head, bf16[4,8,432,128]{3,2,1,0:T(8,128)(2,1)S(1)} %load.1.kernels, f32[4,128]{1,0:T(4,128)S(1)} %copy-done.2), custom_call_target="tpu_custom_call" | custom-call | flops 4 | bytes 4 | tf_op jit(solution)/shard_map/second/pallas_call | solution.py:280
  25.5 1.0 collective-permute-start.10
  26.5 5.0 %collective-permute-start.9 = (f32[512,128]{1,0:T(8,128)S(1)}, f32[512,128]{1,0:T(8,128)S(1)}, u32[]{:S(2)}, u32[]{:S(2)}) collective-permute-start(f32[512,128]{1,0:T(8,128)S(1)} %get-tuple-element.38.m0), channel_id=1, source_target_pairs={{0,16},{8,24},{16,0},{24,8},{1,17},{9,25},{17,1},{25,9},{2,18},{10... | collective-permute-start | bytes 786440 | tf_op jit(solution)/shard_map/ppermute | solution.py:311
  31.5 0.0 collective-permute-done.6.p1
  31.5 0.0 collective-permute-start.2
  31.6 0.9 collective-permute-done.7.p2
  32.5 0.0 collective-permute-done.8.p3
  32.5 4.2 %collective-permute-done.10.m3 = f32[512,128]{1,0:T(8,128)S(1)} collective-permute-done((f32[512,128]{1,0:T(8,128)S(1)}, f32[512,128]{1,0:T(8,128)S(1)}, u32[]{:S(2)}, u32[]{:S(2)}) %collective-permute-start.10) | collective-permute-done | bytes 262176 | tf_op jit(solution)/shard_map/ppermute | solution.py:311
  36.7 1.8 %collective-permute-done.9.m2 = f32[512,128]{1,0:T(8,128)S(1)} collective-permute-done((f32[512,128]{1,0:T(8,128)S(1)}, f32[512,128]{1,0:T(8,128)S(1)}, u32[]{:S(2)}, u32[]{:S(2)}) %collective-permute-start.9) | collective-permute-done | bytes 262176 | tf_op jit(solution)/shard_map/ppermute | solution.py:311
  38.5 0.0 collective-permute-start.11
  38.5 0.5 collective-permute-start.12
  39.1 0.0 collective-permute-start.13
  39.1 0.5 collective-permute-start.14
  39.6 1.8 %collective-permute-done.2.m1 = f32[512,128]{1,0:T(8,128)S(1)} collective-permute-done((f32[512,128]{1,0:T(8,128)S(1)}, f32[512,128]{1,0:T(8,128)S(1)}, u32[]{:S(2)}, u32[]{:S(2)}) %collective-permute-start.2) | collective-permute-done | bytes 262176 | tf_op jit(solution)/shard_map/ppermute | solution.py:311
  41.3 1.3 %collective-permute-start.16 = (f32[512,128]{1,0:T(8,128)S(1)}, f32[512,128]{1,0:T(8,128)S(1)}, u32[]{:S(2)}, u32[]{:S(2)}) collective-permute-start(f32[512,128]{1,0:T(8,128)S(1)} %get-tuple-element.53.term), channel_id=1, source_target_pairs={{0,8},{1,9},{2,10},{3,11},{4,12},{5,13},{6,14},{7,15},{32,40},{33,... | collective-permute-start | bytes 786440 | tf_op jit(solution)/shard_map/ppermute | solution.py:345
  42.6 0.0 collective-permute-done.11.o0
  42.6 0.9 collective-permute-start.18
  43.5 0.0 collective-permute-done.12.o1
  43.5 0.0 collective-permute-done.13.o2
  43.5 0.0 collective-permute-done.14.o3
  43.5 2.9 %third.1 = (f32[512,128]{1,0:T(8,128)S(1)}, f32[4,512,128]{2,1,0:T(8,128)S(1)}, bf16[4,8,432,128]{3,2,1,0:T(8,128)(2,1)S(1)}, bf16[8,432,128]{2,1,0:T(8,128)(2,1)S(1)}, bf16[4,432,128]{2,1,0:T(8,128)(2,1)S(1)}) custom-call(f32[512,128]{1,0:T(8,128)S(1)} %get-tuple-element.38.m0, f32[512,128]{1,0:T(8,128)S(1)} %collective-permute-done.2.m1, ...), custom_call_target="tpu_custom_call" | custom-call | flops 3 | bytes 3 | tf_op jit(solution)/shard_map/third/pallas_call | solution.py:280
  46.4 5.0 %collective-permute-done.16.f1 = f32[512,128]{1,0:T(8,128)S(1)} collective-permute-done((f32[512,128]{1,0:T(8,128)S(1)}, f32[512,128]{1,0:T(8,128)S(1)}, u32[]{:S(2)}, u32[]{:S(2)}) %collective-permute-start.16) | collective-permute-done | bytes 262176 | tf_op jit(solution)/shard_map/ppermute | solution.py:345
  51.4 1.3 %collective-permute-start.17 = (f32[512,128]{1,0:T(8,128)S(1)}, f32[512,128]{1,0:T(8,128)S(1)}, u32[]{:S(2)}, u32[]{:S(2)}) collective-permute-start(f32[512,128]{1,0:T(8,128)S(1)} %collective-permute-done.16.f1), channel_id=1, source_target_pairs={{8,16},{9,17},{10,18},{11,19},{12,20},{13,21},{14,22},{15,23},{40,... | collective-permute-start | bytes 786440 | tf_op jit(solution)/shard_map/ppermute | solution.py:355
  52.7 1.3 %collective-permute-start.15 = (f32[512,128]{1,0:T(8,128)S(1)}, f32[512,128]{1,0:T(8,128)S(1)}, u32[]{:S(2)}, u32[]{:S(2)}) collective-permute-start(f32[512,128]{1,0:T(8,128)S(1)} %get-tuple-element.52.point), channel_id=1, source_target_pairs={{0,32},{32,64},{64,96},{96,128},{128,160},{160,192},{192,224},{1,3... | collective-permute-start | bytes 786440 | tf_op jit(solution)/shard_map/ppermute | solution.py:314
  54.0 0.7 collective-permute-start.20
  54.7 0.0 collective-permute-done.18.f3
  54.7 3.1 %collective-permute-done.17.f2 = f32[512,128]{1,0:T(8,128)S(1)} collective-permute-done((f32[512,128]{1,0:T(8,128)S(1)}, f32[512,128]{1,0:T(8,128)S(1)}, u32[]{:S(2)}, u32[]{:S(2)}) %collective-permute-start.17) | collective-permute-done | bytes 262176 | tf_op jit(solution)/shard_map/ppermute | solution.py:355
  57.8 4.1 %collective-permute-done.15.hop = f32[512,128]{1,0:T(8,128)S(1)} collective-permute-done((f32[512,128]{1,0:T(8,128)S(1)}, f32[512,128]{1,0:T(8,128)S(1)}, u32[]{:S(2)}, u32[]{:S(2)}) %collective-permute-start.15) | collective-permute-done | bytes 262176 | tf_op jit(solution)/shard_map/ppermute | solution.py:314
  62.0 4.1 %fourth.1 = (f32[512,128]{1,0:T(8,128)}, f32[512,128]{1,0:T(8,128)S(1)}, f32[512,128]{1,0:T(8,128)S(1)}, f32[4,512,128]{2,1,0:T(8,128)S(1)}) custom-call(f32[512,128]{1,0:T(8,128)S(1)} %bitcast.13, f32[512,128]{1,0:T(8,128)S(1)} %collective-permute-done.15.hop, f32[512,128]{1,0:T(8,128)S(1)} %get-tuple-element.52.point, ...), custom_call_target="tpu_custom_call" | custom-call | flops 6000000000 | bytes 20000000 | tf_op jit(solution)/shard_map/fourth/pallas_call | solution.py:280
  66.0 0.7 collective-permute-start.19
  66.7 0.8 defect.1
  67.5 0.7 collective-permute-start.22
  68.2 0.0 collective-permute-done.20.mine
  68.2 0.1 collective-permute-start.21
  68.3 0.0 collective-permute-done.19.came
  68.4 0.0 collective-permute-done.22.defect
  68.4 1.7 %collective-permute-done.21.other = bf16[4,432,128]{2,1,0:T(8,128)(2,1)S(1)} collective-permute-done((bf16[4,432,128]{2,1,0:T(8,128)(2,1)S(1)}, bf16[4,432,128]{2,1,0:T(8,128)(2,1)S(1)}, u32[]{:S(2)}, u32[]{:S(2)}) %collective-permute-start.21) | collective-permute-done | bytes 442400 | tf_op jit(solution)/shard_map/ppermute | solution.py:365
  70.1 0.7 collective-permute-start.23
  70.8 0.7 collective-permute-start.24
  71.5 0.0 collective-permute-done.23.came
  71.5 0.0 collective-permute-done.24.defect
  71.5 0.7 collective-permute-start.25
  72.2 0.0 collective-permute-done.25.came
  72.3 1.3 %collective-permute-start.26 = (f32[512,128]{1,0:T(8,128)S(1)}, f32[512,128]{1,0:T(8,128)S(1)}, u32[]{:S(2)}, u32[]{:S(2)}) collective-permute-start(f32[512,128]{1,0:T(8,128)S(1)} %get-tuple-element.66.value), channel_id=1, source_target_pairs={{64,96},{128,160},{192,224},{65,97},{129,161},{193,225},{66,98},{1... | collective-permute-start | bytes 786440 | tf_op jit(solution)/shard_map/ppermute | solution.py:314
  73.6 29.8 %collective-permute-done.26.came = f32[512,128]{1,0:T(8,128)S(1)} collective-permute-done((f32[512,128]{1,0:T(8,128)S(1)}, f32[512,128]{1,0:T(8,128)S(1)}, u32[]{:S(2)}, u32[]{:S(2)}) %collective-permute-start.26) | collective-permute-done | bytes 262176 | tf_op jit(solution)/shard_map/ppermute | solution.py:314
  103.4 4.2 %last.1 = f32[4,512,128]{2,1,0:T(8,128)} custom-call(f32[512,128]{1,0:T(8,128)S(1)} %collective-permute-done.26.came, f32[512,128]{1,0:T(8,128)S(1)} %get-tuple-element.67.before, f32[512,128]{1,0:T(8,128)S(1)} %get-tuple-element.66.value, f32[512,128]{1,0:T(8,128)S(1)} %defect.1, f32[4,128]{1,0:T(4,128)S(1)} %copy-done.2, ...), custom_call_target="tpu_custom_call" | custom-call | flops 6 | bytes 6 | tf_op jit(solution)/shard_map/last/pallas_call | solution.py:280
  (10 shorter events, 0.1 us)
Async XLA Ops:
  2.4 9.5 %collective-permute-start = (f32[512,128]{1,0:T(8,128)}, f32[512,128]{1,0:T(8,128)S(1)}, u32[]{:S(2)}, u32[]{:S(2)}) collective-permute-start(f32[512,128]{1,0:T(8,128)} %get-tuple-element.36), channel_id=1, source_target_pairs={{0,8},{8,16},{16,24},{24,32},{32,40},{40,48},{48,56},{56,64},{64,7... | collective-permute-start | bytes 786440 | tf_op jit(solution)/shard_map/ppermute | solution.py:308
  4.0 5.0 %collective-permute-start.3 = (bf16[432,128]{1,0:T(8,128)(2,1)}, bf16[432,128]{1,0:T(8,128)(2,1)S(1)}, u32[]{:S(2)}, u32[]{:S(2)}) collective-permute-start(bf16[432,128]{1,0:T(8,128)(2,1)} %get-tuple-element.39), channel_id=1, source_target_pairs={{0,24},{8,0},{16,8},{24,16},{1,25},{9,1},{17,9},{25,17},{2,26},{10... | collective-permute-start | bytes 331784 | tf_op jit(solution)/shard_map/ppermute | solution.py:311
  4.5 12.2 %collective-permute-start.5 = (bf16[432,128]{1,0:T(8,128)(2,1)}, bf16[432,128]{1,0:T(8,128)(2,1)S(1)}, u32[]{:S(2)}, u32[]{:S(2)}) collective-permute-start(bf16[432,128]{1,0:T(8,128)(2,1)} %get-tuple-element.39), channel_id=1, source_target_pairs={{0,8},{8,16},{16,24},{24,0},{1,9},{9,17},{17,25},{25,1},{2,10},{10... | collective-permute-start | bytes 331784 | tf_op jit(solution)/shard_map/ppermute | solution.py:311
  6.0 2.0 %copy-start = (bf16[4,3,3,3,128,128]{5,4,3,2,1,0:T(8,128)(2,1)S(1)}, bf16[4,3,3,3,128,128]{5,4,3,2,1,0:T(8,128)(2,1)}, u32[]{:S(2)}) copy-start(bf16[4,3,3,3,128,128]{5,4,3,2,1,0:T(8,128)(2,1)} %param.6) | copy-start | bytes 10616836
  8.0 3.9 %copy-start.2 = (f32[4,128]{1,0:T(4,128)S(1)}, f32[4,128]{1,0:T(4,128)}, u32[]{:S(2)}) copy-start(f32[4,128]{1,0:T(4,128)} %biases.5) | copy-start | bytes 6148
  8.9 7.8 %collective-permute-start.4 = (bf16[432,128]{1,0:T(8,128)(2,1)S(1)}, bf16[432,128]{1,0:T(8,128)(2,1)S(1)}, u32[]{:S(2)}, u32[]{:S(2)}) collective-permute-start(bf16[432,128]{1,0:T(8,128)(2,1)S(1)} %collective-permute-done.3), channel_id=1, source_target_pairs={{0,24},{8,0},{16,8},{24,16},{1,25},{9,1},{17,9},{25,17},{2,26},{10... | collective-permute-start | bytes 331784 | tf_op jit(solution)/shard_map/ppermute | solution.py:311
  15.2 7.1 %collective-permute-start.1 = (f32[512,128]{1,0:T(8,128)S(1)}, f32[512,128]{1,0:T(8,128)S(1)}, u32[]{:S(2)}, u32[]{:S(2)}) collective-permute-start(f32[512,128]{1,0:T(8,128)S(1)} %first.1), channel_id=1, source_target_pairs={{0,8},{8,16},{16,24},{24,32},{32,40},{40,48},{48,56},{56,64},{64,7... | collective-permute-start | bytes 786440 | tf_op jit(solution)/shard_map/ppermute | solution.py:308
  16.8 14.8 %collective-permute-start.6 = (bf16[3,432,128]{2,1,0:T(8,128)(2,1)S(1)}, bf16[3,432,128]{2,1,0:T(8,128)(2,1)S(1)}, u32[]{:S(2)}, u32[]{:S(2)}) collective-permute-start(bf16[3,432,128]{2,1,0:T(8,128)(2,1)S(1)} %pad_maximum_fusion.p0), channel_id=1, source_target_pairs={{0,2},{2,4},{4,6},{6,0},{1,3},{3,5},{5,7},{7,1},{8,10},{10,12},{12... | collective-permute-start | bytes 995336 | tf_op jit(solution)/shard_map/ppermute | solution.py:334
  17.1 15.4 %collective-permute-start.7 = (bf16[3,432,128]{2,1,0:T(8,128)(2,1)S(1)}, bf16[3,432,128]{2,1,0:T(8,128)(2,1)S(1)}, u32[]{:S(2)}, u32[]{:S(2)}) collective-permute-start(bf16[3,432,128]{2,1,0:T(8,128)(2,1)S(1)} %pad_maximum_fusion.p0), channel_id=1, source_target_pairs={{0,6},{2,0},{4,2},{6,4},{1,7},{3,1},{5,3},{7,5},{8,14},{10,8},{12,... | collective-permute-start | bytes 995336 | tf_op jit(solution)/shard_map/ppermute | solution.py:334
  18.9 13.6 %collective-permute-start.8 = (bf16[3,432,128]{2,1,0:T(8,128)(2,1)S(1)}, bf16[3,432,128]{2,1,0:T(8,128)(2,1)S(1)}, u32[]{:S(2)}, u32[]{:S(2)}) collective-permute-start(bf16[3,432,128]{2,1,0:T(8,128)(2,1)S(1)} %pad_maximum_fusion.p0), channel_id=1, source_target_pairs={{0,4},{2,6},{4,0},{6,2},{1,5},{3,7},{5,1},{7,3},{8,12},{10,14},{12... | collective-permute-start | bytes 995336 | tf_op jit(solution)/shard_map/ppermute | solution.py:334
  25.5 11.2 %collective-permute-start.10 = (f32[512,128]{1,0:T(8,128)S(1)}, f32[512,128]{1,0:T(8,128)S(1)}, u32[]{:S(2)}, u32[]{:S(2)}) collective-permute-start(f32[512,128]{1,0:T(8,128)S(1)} %get-tuple-element.38.m0), channel_id=1, source_target_pairs={{0,8},{8,16},{16,24},{24,0},{1,9},{9,17},{17,25},{25,1},{2,10},{10... | collective-permute-start | bytes 786440 | tf_op jit(solution)/shard_map/ppermute | solution.py:311
  26.5 12.0 %collective-permute-start.9 = (f32[512,128]{1,0:T(8,128)S(1)}, f32[512,128]{1,0:T(8,128)S(1)}, u32[]{:S(2)}, u32[]{:S(2)}) collective-permute-start(f32[512,128]{1,0:T(8,128)S(1)} %get-tuple-element.38.m0), channel_id=1, source_target_pairs={{0,16},{8,24},{16,0},{24,8},{1,17},{9,25},{17,1},{25,9},{2,18},{10... | collective-permute-start | bytes 786440 | tf_op jit(solution)/shard_map/ppermute | solution.py:311
  31.5 9.8 %collective-permute-start.2 = (f32[512,128]{1,0:T(8,128)S(1)}, f32[512,128]{1,0:T(8,128)S(1)}, u32[]{:S(2)}, u32[]{:S(2)}) collective-permute-start(f32[512,128]{1,0:T(8,128)S(1)} %get-tuple-element.38.m0), channel_id=1, source_target_pairs={{0,24},{8,0},{16,8},{24,16},{1,25},{9,1},{17,9},{25,17},{2,26},{10... | collective-permute-start | bytes 786440 | tf_op jit(solution)/shard_map/ppermute | solution.py:311
  38.5 4.1 %collective-permute-start.11 = (bf16[3,432,128]{2,1,0:T(8,128)(2,1)S(1)}, bf16[3,432,128]{2,1,0:T(8,128)(2,1)S(1)}, u32[]{:S(2)}, u32[]{:S(2)}) collective-permute-start(bf16[3,432,128]{2,1,0:T(8,128)(2,1)S(1)} %pad_maximum_fusion.p0), channel_id=1, source_target_pairs={{0,1},{1,0},{2,3},{3,2},{4,5},{5,4},{6,7},{7,6},{8,9},{9,8},{10,11... | collective-permute-start | bytes 995336 | tf_op jit(solution)/shard_map/ppermute | solution.py:343
  38.5 4.9 %collective-permute-start.12 = (bf16[3,432,128]{2,1,0:T(8,128)(2,1)S(1)}, bf16[3,432,128]{2,1,0:T(8,128)(2,1)S(1)}, u32[]{:S(2)}, u32[]{:S(2)}) collective-permute-start(bf16[3,432,128]{2,1,0:T(8,128)(2,1)S(1)} %collective-permute-done.6.p1), channel_id=1, source_target_pairs={{0,1},{1,0},{2,3},{3,2},{4,5},{5,4},{6,7},{7,6},{8,9},{9,8},{10,11... | collective-permute-start | bytes 995336 | tf_op jit(solution)/shard_map/ppermute | solution.py:343
  39.1 4.4 %collective-permute-start.13 = (bf16[3,432,128]{2,1,0:T(8,128)(2,1)S(1)}, bf16[3,432,128]{2,1,0:T(8,128)(2,1)S(1)}, u32[]{:S(2)}, u32[]{:S(2)}) collective-permute-start(bf16[3,432,128]{2,1,0:T(8,128)(2,1)S(1)} %collective-permute-done.7.p2), channel_id=1, source_target_pairs={{0,1},{1,0},{2,3},{3,2},{4,5},{5,4},{6,7},{7,6},{8,9},{9,8},{10,11... | collective-permute-start | bytes 995336 | tf_op jit(solution)/shard_map/ppermute | solution.py:343
  39.1 4.5 %collective-permute-start.14 = (bf16[3,432,128]{2,1,0:T(8,128)(2,1)S(1)}, bf16[3,432,128]{2,1,0:T(8,128)(2,1)S(1)}, u32[]{:S(2)}, u32[]{:S(2)}) collective-permute-start(bf16[3,432,128]{2,1,0:T(8,128)(2,1)S(1)} %collective-permute-done.8.p3), channel_id=1, source_target_pairs={{0,1},{1,0},{2,3},{3,2},{4,5},{5,4},{6,7},{7,6},{8,9},{9,8},{10,11... | collective-permute-start | bytes 995336 | tf_op jit(solution)/shard_map/ppermute | solution.py:343
  39.6 22.4 %copy-start.1 = (f32[1,8,8,8,128]{4,3,2,1,0:T(8,128)S(1)}, f32[1,8,8,8,128]{4,3,2,1,0:T(8,128)}, u32[]{:S(2)}) copy-start(f32[1,8,8,8,128]{4,3,2,1,0:T(8,128)} %param.4) | copy-start | bytes 786436
  41.3 10.1 %collective-permute-start.16 = (f32[512,128]{1,0:T(8,128)S(1)}, f32[512,128]{1,0:T(8,128)S(1)}, u32[]{:S(2)}, u32[]{:S(2)}) collective-permute-start(f32[512,128]{1,0:T(8,128)S(1)} %get-tuple-element.53.term), channel_id=1, source_target_pairs={{0,8},{1,9},{2,10},{3,11},{4,12},{5,13},{6,14},{7,15},{32,40},{33,... | collective-permute-start | bytes 786440 | tf_op jit(solution)/shard_map/ppermute | solution.py:345
  42.6 12.1 %collective-permute-start.18 = (f32[512,128]{1,0:T(8,128)S(1)}, f32[512,128]{1,0:T(8,128)S(1)}, u32[]{:S(2)}, u32[]{:S(2)}) collective-permute-start(f32[512,128]{1,0:T(8,128)S(1)} %get-tuple-element.53.term), channel_id=1, source_target_pairs={{0,24},{1,25},{2,26},{3,27},{4,28},{5,29},{6,30},{7,31},{32,56},{3... | collective-permute-start | bytes 786440 | tf_op jit(solution)/shard_map/ppermute | solution.py:345
  51.4 6.4 %collective-permute-start.17 = (f32[512,128]{1,0:T(8,128)S(1)}, f32[512,128]{1,0:T(8,128)S(1)}, u32[]{:S(2)}, u32[]{:S(2)}) collective-permute-start(f32[512,128]{1,0:T(8,128)S(1)} %collective-permute-done.16.f1), channel_id=1, source_target_pairs={{8,16},{9,17},{10,18},{11,19},{12,20},{13,21},{14,22},{15,23},{40,... | collective-permute-start | bytes 786440 | tf_op jit(solution)/shard_map/ppermute | solution.py:355
  52.7 9.2 %collective-permute-start.15 = (f32[512,128]{1,0:T(8,128)S(1)}, f32[512,128]{1,0:T(8,128)S(1)}, u32[]{:S(2)}, u32[]{:S(2)}) collective-permute-start(f32[512,128]{1,0:T(8,128)S(1)} %get-tuple-element.52.point), channel_id=1, source_target_pairs={{0,32},{32,64},{64,96},{96,128},{128,160},{160,192},{192,224},{1,3... | collective-permute-start | bytes 786440 | tf_op jit(solution)/shard_map/ppermute | solution.py:314
  54.0 14.2 %collective-permute-start.20 = (bf16[4,432,128]{2,1,0:T(8,128)(2,1)S(1)}, bf16[4,432,128]{2,1,0:T(8,128)(2,1)S(1)}, u32[]{:S(2)}, u32[]{:S(2)}) collective-permute-start(bf16[4,432,128]{2,1,0:T(8,128)(2,1)S(1)} %get-tuple-element.61), channel_id=1, source_target_pairs={{96,64},{160,128},{97,65},{161,129},{98,66},{162,130},{99,67},{163... | collective-permute-start | bytes 1327112 | tf_op jit(solution)/shard_map/ppermute | solution.py:314
  66.0 2.3 %collective-permute-start.19 = (f32[512,128]{1,0:T(8,128)S(1)}, f32[512,128]{1,0:T(8,128)S(1)}, u32[]{:S(2)}, u32[]{:S(2)}) collective-permute-start(f32[512,128]{1,0:T(8,128)S(1)} %get-tuple-element.57.corner.value), channel_id=1, source_target_pairs={{32,64},{33,65},{34,66},{35,67},{36,68},{37,69},{38,70},{39,71},{4... | collective-permute-start | bytes 786440 | tf_op jit(solution)/shard_map/ppermute | solution.py:314
  67.5 0.8 collective-permute-start.22
  68.2 1.9 %collective-permute-start.21 = (bf16[4,432,128]{2,1,0:T(8,128)(2,1)S(1)}, bf16[4,432,128]{2,1,0:T(8,128)(2,1)S(1)}, u32[]{:S(2)}, u32[]{:S(2)}) collective-permute-start(bf16[4,432,128]{2,1,0:T(8,128)(2,1)S(1)} %collective-permute-done.20.mine), channel_id=1, source_target_pairs={{0,1},{1,0},{2,3},{3,2},{4,5},{5,4},{6,7},{7,6},{8,9},{9,8},{10,11... | collective-permute-start | bytes 1327112 | tf_op jit(solution)/shard_map/ppermute | solution.py:365
  70.1 1.4 %collective-permute-start.23 = (f32[512,128]{1,0:T(8,128)S(1)}, f32[512,128]{1,0:T(8,128)S(1)}, u32[]{:S(2)}, u32[]{:S(2)}) collective-permute-start(f32[512,128]{1,0:T(8,128)S(1)} %next2.1), channel_id=1, source_target_pairs={{64,128},{65,129},{66,130},{67,131},{68,132},{69,133},{70,134},{71... | collective-permute-start | bytes 786440 | tf_op jit(solution)/shard_map/ppermute | solution.py:314
  70.8 0.7 collective-permute-start.24
  71.5 0.7 collective-permute-start.25
  72.3 31.1 %collective-permute-start.26 = (f32[512,128]{1,0:T(8,128)S(1)}, f32[512,128]{1,0:T(8,128)S(1)}, u32[]{:S(2)}, u32[]{:S(2)}) collective-permute-start(f32[512,128]{1,0:T(8,128)S(1)} %get-tuple-element.66.value), channel_id=1, source_target_pairs={{64,96},{128,160},{192,224},{65,97},{129,161},{193,225},{66,98},{1... | collective-permute-start | bytes 786440 | tf_op jit(solution)/shard_map/ppermute | solution.py:314
